TPU v7x, 32 devices: a whole 2x2x4 slice. The times are simulated.
32 devices in a mesh: seq: 8 (over y, x, core), head: 4 (over z).
Axes of the slice: x: 2, y: 2, z: 4, core: 2. Of those that a mesh axis runs over, the one named last changes fastest.
Arguments:
- inputs: bfloat16 [8192, 2048], P(('seq', 'head')), may hold values from -6 to 6
- out_grad: bfloat16 [8192, 2048], P(('seq', 'head')), may hold values from -6 to 6
- q_weight: bfloat16 [2048, 2048], P('seq', 'head'), may hold values from -0.125 to 0.125
- q_bias: bfloat16 [2048], P(('seq', 'head')), may hold values from -4 to 4
- kv_weight: bfloat16 [2048, 512], P(('seq', 'head')), may hold values from -0.125 to 0.125
- kv_bias: bfloat16 [512], P(('seq', 'head')), may hold values from -4 to 4
- out_weight: bfloat16 [2048, 2048], P('head', 'seq'), may hold values from -0.75 to 0.75
- attn_gain: bfloat16 [2048], P(('seq', 'head')), may hold values from 0.5 to 1.5
- ffn_gain: bfloat16 [2048], P(('seq', 'head')), may hold values from 0.5 to 1.5
- gate_weight: bfloat16 [2048, 11008], P('seq', 'head'), may hold values from -0.125 to 0.125
- up_weight: bfloat16 [2048, 11008], P('seq', 'head'), may hold values from -0.125 to 0.125
- down_weight: bfloat16 [11008, 2048], P('head', 'seq'), may hold values from -0.0546875 to 0.0546875
- block_order: int32 [16], replicated, may hold values from 0 to 15, as said below
- long_docs: int32 [8], replicated, may hold values from 1 to 3584, 7168 in all
- short_docs: int32 [4], replicated, may hold values from 1 to 512, 1024 in all
Outputs:
- output: float32 [8192, 2048], P(('seq', 'head'))
- input_grad: float32 [8192, 2048], P(('seq', 'head'))
- q_weight_grad: float32 [2048, 2048], P('seq', 'head')
- q_bias_grad: float32 [2048], P(('seq', 'head'))
- kv_weight_grad: float32 [2048, 512], P(('seq', 'head'))
- kv_bias_grad: float32 [512], P(('seq', 'head'))
- out_weight_grad: float32 [2048, 2048], P('head', 'seq')
- attn_gain_grad: float32 [2048], P(('seq', 'head'))
- ffn_gain_grad: float32 [2048], P(('seq', 'head'))
- gate_weight_grad: float32 [2048, 11008], P('seq', 'head')
- up_weight_grad: float32 [2048, 11008], P('seq', 'head')
- down_weight_grad: float32 [11008, 2048], P('head', 'seq')
Inputs may be any that keep to these rules, and one draw needn't show every extreme that they name: `block_order`: a permutation of the blocks in which storage blocks 2k and 2k + 1 hold a block b < 8 and the block 15 - b. `long_docs`: lay the first row end to end; the largest is 3584. `short_docs`: lay the second row end to end; the largest is 512.
All inputs are finite; a program needn't handle non-finite values.
Results may differ from a plain program's by a relative error of at most 0.023.
Values may be sent and summed in bfloat16 or wider, within the bound.
No kernel may reach another device: no remote copies, remote signals or barrier semaphores. Data moves between devices by JAX's collectives and lax.ppermute only.
A program may use at most 256 MiB of HBM per device.

v0:
```python
import jax
import jax.numpy as jnp
from jax import lax
from jax.sharding import PartitionSpec as P

HEADS = 16
KV = 2
HD = 128
BLK = 512


EPSILON = 1e-06
ROPE_BASE = 1000000.0
NEGATIVE = -1e30


def contract(left_side, right_side, left_dim, right_dim):
    return lax.dot_general(
        left_side,
        right_side,
        (((left_dim,), (right_dim,)), ((), ())),
        preferred_element_type=jnp.float32,
    )


def stream_layout(block_order, long_docs, short_docs):
    within = jnp.arange(BLK, dtype=jnp.int32)
    stream_index = (block_order[:, None] * BLK + within[None, :]).reshape(-1)
    long_ends = jnp.cumsum(long_docs)
    short_ends = jnp.cumsum(short_docs)
    long_total = long_ends[-1]
    second_row = stream_index >= long_total
    position = jnp.where(second_row, stream_index - long_total, stream_index)
    first_doc = jnp.sum((position[:, None] >= long_ends[None, :]).astype(jnp.int32), axis=1)
    second_doc = (
        jnp.sum((position[:, None] >= short_ends[None, :]).astype(jnp.int32), axis=1)
        + long_docs.shape[0]
    )
    document = jnp.where(second_row, second_doc, first_doc)
    return (stream_index, position, document)


def rope_tables(position):
    half_width = HD // 2
    inverse = ROPE_BASE ** (-(jnp.arange(half_width, dtype=jnp.float32) * 2.0 / HD))
    angles = position.astype(jnp.float32)[:, None] * inverse[None, :]
    angles = jnp.concatenate([angles, angles], axis=1)
    return (jnp.cos(angles), jnp.sin(angles))


def rotate(values, cosine, sine_table):
    half_width = values.shape[-1] // 2
    turned = jnp.concatenate([-values[..., half_width:], values[..., :half_width]], axis=-1)
    return values * cosine + turned * sine_table


def norm_forward(values, gain_vector):
    rms_scale = lax.rsqrt(jnp.mean(values * values, axis=1, keepdims=True) + EPSILON)
    return (values * rms_scale * gain_vector, rms_scale)


def norm_backward(values, rms_scale, gain_vector, gradient):
    weighted = gradient * gain_vector
    gain_grad = jnp.sum(gradient * values * rms_scale, axis=0)
    inner_mean = jnp.mean(weighted * values, axis=1, keepdims=True)
    return (rms_scale * weighted - values * rms_scale**3 * inner_mean, gain_grad)


def keep_state(carried):
    return carried


def block_tools(queries, query_stream, query_doc):
    factor = HD ** (-0.5)

    def permitted(block_stream, block_doc):
        return (query_doc[:, None] == block_doc[None, :]) & (
            block_stream[None, :] <= query_stream[:, None]
        )

    def scored(key_block):
        return (
            jnp.einsum("qhd,kd->hqk", queries, key_block, preferred_element_type=jnp.float32)
            * factor
        )

    return (permitted, scored, factor)


def attention_forward(
    queries, key_blocks, value_blocks, query_stream, query_doc, key_stream, key_doc
):
    heads_local = queries.shape[1]
    row_count = queries.shape[0]
    permitted, scored, factor = block_tools(queries, query_stream, query_doc)

    def stats_step(carried, portion):
        key_block, block_stream, block_doc = portion
        allowed = permitted(block_stream, block_doc)

        def stats_visited(current):
            row_top, row_total = current
            masked = jnp.where(allowed[None], scored(key_block), NEGATIVE)
            new_top = jnp.maximum(row_top, jnp.max(masked, axis=2))
            weights = jnp.where(allowed[None], jnp.exp(masked - new_top[:, :, None]), 0.0)
            return (new_top, row_total * jnp.exp(row_top - new_top) + jnp.sum(weights, axis=2))

        return (lax.cond(jnp.any(allowed), stats_visited, keep_state, carried), None)

    start_top = jnp.full((heads_local, row_count), NEGATIVE, jnp.float32)
    start_total = jnp.zeros((heads_local, row_count), jnp.float32)
    (row_top, row_total), unused_out = lax.scan(
        stats_step, (start_top, start_total), (key_blocks, key_stream, key_doc)
    )
    log_total = row_top + jnp.log(row_total)

    def value_step(summed, portion):
        key_block, value_block, block_stream, block_doc = portion
        allowed = permitted(block_stream, block_doc)

        def value_visited(current):
            probabilities = jnp.where(
                allowed[None], jnp.exp(scored(key_block) - log_total[:, :, None]), 0.0
            ).astype(jnp.bfloat16)
            return current + jnp.einsum(
                "hqk,kd->qhd", probabilities, value_block, preferred_element_type=jnp.float32
            )

        return (lax.cond(jnp.any(allowed), value_visited, keep_state, summed), None)

    start_sum = jnp.zeros((row_count, heads_local, HD), jnp.float32)
    summed, unused_too = lax.scan(
        value_step, start_sum, (key_blocks, value_blocks, key_stream, key_doc)
    )
    return (summed, log_total)


def attention_backward(
    queries,
    key_blocks,
    value_blocks,
    query_stream,
    query_doc,
    key_stream,
    key_doc,
    log_total,
    d_mixed,
    row_delta,
):
    permitted, scored, factor = block_tools(queries, query_stream, query_doc)

    def back_step(grad_queries, portion):
        key_block, value_block, block_stream, block_doc = portion
        allowed = permitted(block_stream, block_doc)

        def back_visited(current):
            probabilities = jnp.where(
                allowed[None], jnp.exp(scored(key_block) - log_total[:, :, None]), 0.0
            )
            d_probs = jnp.einsum(
                "qhd,kd->hqk", d_mixed, value_block, preferred_element_type=jnp.float32
            )
            d_scores = (probabilities * (d_probs - row_delta[:, :, None]) * factor).astype(
                jnp.bfloat16
            )
            new_grad = current + jnp.einsum(
                "hqk,kd->qhd", d_scores, key_block, preferred_element_type=jnp.float32
            )
            d_keys = jnp.einsum(
                "hqk,qhd->kd", d_scores, queries, preferred_element_type=jnp.float32
            )
            d_values = jnp.einsum(
                "hqk,qhd->kd",
                probabilities.astype(jnp.bfloat16),
                d_mixed,
                preferred_element_type=jnp.float32,
            )
            return (new_grad, jnp.concatenate([d_keys, d_values], axis=1))

        def skipped(current):
            return (current, jnp.zeros((key_block.shape[0], 2 * HD), jnp.float32))

        return lax.cond(jnp.any(allowed), back_visited, skipped, grad_queries)

    start_grad = jnp.zeros(queries.shape, jnp.float32)
    grad_queries, key_grads = lax.scan(
        back_step, start_grad, (key_blocks, value_blocks, key_stream, key_doc)
    )
    return (grad_queries, key_grads.reshape(-1, 2 * HD))


def gather_normed(normed, out_grad):
    return (
        lax.all_gather(normed, "head", axis=0, tiled=True),
        lax.all_gather(out_grad, "head", axis=0, tiled=True),
    )


def gather_ffn(normed2):
    return lax.all_gather(normed2, "head", axis=0, tiled=True)


def gather_keys(kv_rows):
    return lax.all_gather(kv_rows, ("seq", "head"), axis=0, tiled=True)


def local(
    inputs,
    out_grad,
    q_weight,
    q_bias,
    kv_weight,
    kv_bias,
    out_weight,
    attn_gain,
    ffn_gain,
    gate_weight,
    up_weight,
    down_weight,
    block_order,
    long_docs,
    short_docs,
):
    head_count = lax.axis_size("head")
    seq_index = lax.axis_index("seq")
    head_index = lax.axis_index("head")
    local_rows = inputs.shape[0]
    span_rows = local_rows * head_count
    heads_local = q_weight.shape[1] // HD
    group_index = head_index * heads_local // (HEADS // KV)
    block_count = block_order.shape[0]
    q_full, out_full, gate_full, up_full, down_full = (
        lax.all_gather(q_weight, "seq", axis=0, tiled=True),
        lax.all_gather(out_weight, "seq", axis=1, tiled=True),
        lax.all_gather(gate_weight, "seq", axis=0, tiled=True),
        lax.all_gather(up_weight, "seq", axis=0, tiled=True),
        lax.all_gather(down_weight, "seq", axis=1, tiled=True),
    )
    kv_full, q_bias_full, kv_bias_full, attn_gain_full, ffn_gain_full = (
        lax.all_gather(kv_weight, ("seq", "head"), axis=0, tiled=True),
        lax.all_gather(q_bias, ("seq", "head"), axis=0, tiled=True),
        lax.all_gather(kv_bias, ("seq", "head"), axis=0, tiled=True),
        lax.all_gather(attn_gain, ("seq", "head"), axis=0, tiled=True),
        lax.all_gather(ffn_gain, ("seq", "head"), axis=0, tiled=True),
    )
    q_width = q_full.shape[1]
    q_bias_local = lax.dynamic_slice_in_dim(q_bias_full, head_index * q_width, q_width).astype(
        jnp.float32
    )
    attn_gain32 = attn_gain_full.astype(jnp.float32)
    ffn_gain32 = ffn_gain_full.astype(jnp.float32)
    stream_index, position, document = stream_layout(block_order, long_docs, short_docs)
    span_start = seq_index * span_rows
    local_start = span_start + head_index * local_rows
    query_stream = lax.dynamic_slice_in_dim(stream_index, span_start, span_rows)
    query_doc = lax.dynamic_slice_in_dim(document, span_start, span_rows)
    query_cos, query_sin = rope_tables(lax.dynamic_slice_in_dim(position, span_start, span_rows))
    local_cos, local_sin = rope_tables(lax.dynamic_slice_in_dim(position, local_start, local_rows))
    key_stream = stream_index.reshape(block_count, BLK)
    key_doc = document.reshape(block_count, BLK)
    residual = inputs.astype(jnp.float32)
    normed32, attn_scale = norm_forward(residual, attn_gain32)
    normed = normed32.astype(jnp.bfloat16)
    gathered, grad_gathered = gather_normed(normed, out_grad)
    query_raw = jnp.dot(gathered, q_full, preferred_element_type=jnp.float32) + q_bias_local
    queries = rotate(
        query_raw.reshape(span_rows, heads_local, HD), query_cos[:, None, :], query_sin[:, None, :]
    ).astype(jnp.bfloat16)
    kv_raw = jnp.dot(normed, kv_full, preferred_element_type=jnp.float32) + kv_bias_full.astype(
        jnp.float32
    )
    key_part = rotate(
        kv_raw[:, : KV * HD].reshape(local_rows, KV, HD),
        local_cos[:, None, :],
        local_sin[:, None, :],
    )
    kv_rows = jnp.concatenate(
        [key_part.reshape(local_rows, KV * HD), kv_raw[:, KV * HD :]], axis=1
    ).astype(jnp.bfloat16)
    kv_all = gather_keys(kv_rows)

    def own_group(kv_whole):
        key_cols = lax.dynamic_slice_in_dim(kv_whole, group_index * HD, HD, 1)
        value_cols = lax.dynamic_slice_in_dim(kv_whole, KV * HD + group_index * HD, HD, 1)
        return (key_cols.reshape(block_count, BLK, HD), value_cols.reshape(block_count, BLK, HD))

    key_blocks, value_blocks = own_group(kv_all)
    mixed_sum, log_total = attention_forward(
        queries, key_blocks, value_blocks, query_stream, query_doc, key_stream, key_doc
    )
    mixed_heads = mixed_sum.astype(jnp.bfloat16).reshape(span_rows, q_width)
    attn_terms = jnp.dot(mixed_heads, out_full, preferred_element_type=jnp.float32)
    hidden = residual + lax.psum_scatter(
        attn_terms.astype(jnp.bfloat16), "head", scatter_dimension=0, tiled=True
    ).astype(jnp.float32)
    normed2_32, ffn_scale = norm_forward(hidden, ffn_gain32)
    normed2 = normed2_32.astype(jnp.bfloat16)
    gathered2 = gather_ffn(normed2)
    gate_value = jnp.dot(gathered2, gate_full, preferred_element_type=jnp.float32)
    up_value = jnp.dot(gathered2, up_full, preferred_element_type=jnp.float32)
    activation = (jax.nn.silu(gate_value) * up_value).astype(jnp.bfloat16)
    ffn_terms = jnp.dot(activation, down_full, preferred_element_type=jnp.float32)
    output = hidden + lax.psum_scatter(
        ffn_terms.astype(jnp.bfloat16), "head", scatter_dimension=0, tiled=True
    ).astype(jnp.float32)
    gathered, grad_gathered = gather_normed(normed, out_grad)
    gathered2 = gather_ffn(normed2)
    key_blocks, value_blocks = own_group(gather_keys(kv_rows))
    cotangent = out_grad.astype(jnp.float32)
    down_grad = contract(activation, grad_gathered, 0, 0)
    d_activation = contract(grad_gathered, down_full, 1, 1)
    sigmoid_gate = jax.nn.sigmoid(gate_value)
    d_gate = (
        d_activation * up_value * sigmoid_gate * (1.0 + gate_value * (1.0 - sigmoid_gate))
    ).astype(jnp.bfloat16)
    d_up = (d_activation * gate_value * sigmoid_gate).astype(jnp.bfloat16)
    gate_grad = contract(gathered2, d_gate, 0, 0)
    up_grad = contract(gathered2, d_up, 0, 0)
    ffn_input_terms = contract(d_gate, gate_full, 1, 1) + contract(d_up, up_full, 1, 1)
    d_normed2 = lax.psum_scatter(
        ffn_input_terms.astype(jnp.bfloat16), "head", scatter_dimension=0, tiled=True
    ).astype(jnp.float32)
    d_hidden_norm, ffn_gain_grad = norm_backward(hidden, ffn_scale, ffn_gain32, d_normed2)
    d_hidden = cotangent + d_hidden_norm
    attn_gathered = lax.all_gather(d_hidden.astype(jnp.bfloat16), "head", axis=0, tiled=True)
    out_weight_part = contract(mixed_heads, attn_gathered, 0, 0)
    d_mixed = contract(attn_gathered, out_full, 1, 1).astype(jnp.bfloat16)
    d_mixed_heads = d_mixed.reshape(span_rows, heads_local, HD)
    row_delta = jnp.sum(
        d_mixed_heads.astype(jnp.float32)
        * mixed_heads.reshape(span_rows, heads_local, HD).astype(jnp.float32),
        axis=2,
    ).T
    grad_queries, key_grads = attention_backward(
        queries,
        key_blocks,
        value_blocks,
        query_stream,
        query_doc,
        key_stream,
        key_doc,
        log_total,
        d_mixed_heads,
        row_delta,
    )
    placed = jnp.zeros((key_grads.shape[0], 2 * KV * HD), jnp.float32)
    placed = lax.dynamic_update_slice_in_dim(placed, key_grads[:, :HD], group_index * HD, 1)
    placed = lax.dynamic_update_slice_in_dim(
        placed, key_grads[:, HD:], KV * HD + group_index * HD, 1
    )
    kv_grad_rows = lax.psum_scatter(placed, ("seq", "head"), scatter_dimension=0, tiled=True)
    key_back = rotate(
        kv_grad_rows[:, : KV * HD].reshape(local_rows, KV, HD),
        local_cos[:, None, :],
        -local_sin[:, None, :],
    )
    d_kv = jnp.concatenate(
        [key_back.reshape(local_rows, KV * HD), kv_grad_rows[:, KV * HD :]], axis=1
    ).astype(jnp.bfloat16)
    kv_weight_part = contract(normed, d_kv, 0, 0)
    kv_bias_part = jnp.sum(d_kv.astype(jnp.float32), axis=0)
    d_queries = (
        rotate(grad_queries, query_cos[:, None, :], -query_sin[:, None, :])
        .reshape(span_rows, q_width)
        .astype(jnp.bfloat16)
    )
    q_weight_part = contract(gathered, d_queries, 0, 0)
    q_bias_part = jnp.sum(d_queries.astype(jnp.float32), axis=0)
    q_bias_placed = lax.dynamic_update_slice_in_dim(
        jnp.zeros((q_bias_full.shape[0],), jnp.float32), q_bias_part, head_index * q_width, 0
    )
    query_input_terms = contract(d_queries, q_full, 1, 1)
    d_normed = lax.psum_scatter(
        query_input_terms.astype(jnp.bfloat16), "head", scatter_dimension=0, tiled=True
    ).astype(jnp.float32) + contract(d_kv, kv_full, 1, 1)
    d_input_norm, attn_gain_grad = norm_backward(residual, attn_scale, attn_gain32, d_normed)
    input_grad = d_hidden + d_input_norm
    weight_sums = (
        lax.psum_scatter(
            q_weight_part.astype(jnp.bfloat16), "seq", scatter_dimension=0, tiled=True
        ).astype(jnp.float32),
        lax.psum_scatter(
            out_weight_part.astype(jnp.bfloat16), "seq", scatter_dimension=1, tiled=True
        ).astype(jnp.float32),
        lax.psum_scatter(
            gate_grad.astype(jnp.bfloat16), "seq", scatter_dimension=0, tiled=True
        ).astype(jnp.float32),
        lax.psum_scatter(
            up_grad.astype(jnp.bfloat16), "seq", scatter_dimension=0, tiled=True
        ).astype(jnp.float32),
        lax.psum_scatter(
            down_grad.astype(jnp.bfloat16), "seq", scatter_dimension=1, tiled=True
        ).astype(jnp.float32),
    )
    small_sums = (
        lax.psum_scatter(kv_weight_part, ("seq", "head"), scatter_dimension=0, tiled=True),
        lax.psum_scatter(q_bias_placed, ("seq", "head"), scatter_dimension=0, tiled=True),
        lax.psum_scatter(kv_bias_part, ("seq", "head"), scatter_dimension=0, tiled=True),
        lax.psum_scatter(attn_gain_grad, ("seq", "head"), scatter_dimension=0, tiled=True),
        lax.psum_scatter(ffn_gain_grad, ("seq", "head"), scatter_dimension=0, tiled=True),
    )
    return (
        output,
        input_grad,
        weight_sums[0],
        small_sums[1],
        small_sums[0],
        small_sums[2],
        weight_sums[1],
        small_sums[3],
        small_sums[4],
        weight_sums[2],
        weight_sums[3],
        weight_sums[4],
    )


def solution(mesh):
    in_specs = (
        P(("seq", "head"), None),
        P(("seq", "head"), None),
        P("seq", "head"),
        P(("seq", "head")),
        P(("seq", "head"), None),
        P(("seq", "head")),
        P("head", "seq"),
        P(("seq", "head")),
        P(("seq", "head")),
        P("seq", "head"),
        P("seq", "head"),
        P("head", "seq"),
        P(),
        P(),
        P(),
    )
    out_specs = (
        P(("seq", "head"), None),
        P(("seq", "head"), None),
        P("seq", "head"),
        P(("seq", "head")),
        P(("seq", "head"), None),
        P(("seq", "head")),
        P("head", "seq"),
        P(("seq", "head")),
        P(("seq", "head")),
        P("seq", "head"),
        P("seq", "head"),
        P("head", "seq"),
    )
    return jax.shard_map(local, mesh=mesh, in_specs=in_specs, out_specs=out_specs, check_vma=False)
```

profile of v0, /device:TPU:0, one launch (start us, length us, event | category | flops | bytes accessed | tf_op | source)
XLA Modules:
  0.0 2410.3 jit_solution(1585051232831510738)
XLA Ops:
  12.1 42.3 %all-reduce.9 = (bf16[2048]{0:T(1024)(128)(2,1)S(1)}, bf16[512]{0:T(512)(128)(2,1)S(1)}, bf16[2048]{0:T(1024)(128)(2,1)S(1)}, bf16[2048]{0:T(1024)(128)(2,1)S(1)}) all-reduce(bf16[2048]{0:T(1024)(128)(2,1)S(1)} %dynamic-update-slice, bf16[512]{0:T(512)(128)(2,1)S(1)} %dynamic-update-slice.1, ...), channel_id=1, replica_groups=mesh['seq'=8,'head'=4] {'seq','head'}, use_global_device_ids=true, to_apply=%add | all-reduce | flops 6656 | bytes 26624
  62.8 7.4 all-gather.12.cloned.1.call-done
  80.9 17.9 all-gather.18.cloned.1.call-done
  98.9 82.9 %all-gather.16.cloned.1.call-done = bf16[1024,2048]{1,0:T(8,128)(2,1)} async-done(((bf16[256,2048]{1,0:T(8,128)(2,1)}), bf16[1024,2048]{1,0:T(8,128)(2,1)}) %all-gather.16.cloned.1.call-update) | async-done | bytes 4194320 | tf_op jit(solution)/shard_map/all_gather | solution.py:194
  181.8 5.2 convolution_add_fusion.1
  188.6 72.5 %all-gather.14.cloned.1.call-done = bf16[8192,512]{1,0:T(8,128)(2,1)} async-done(((bf16[256,512]{1,0:T(8,128)(2,1)}), bf16[8192,512]{1,0:T(8,128)(2,1)}) %all-gather.14.cloned.1.call-update) | async-done | bytes 8388624 | tf_op jit(solution)/shard_map/all_gather | solution.py:204
  265.6 64.1 %while.40 = (s32[]{:T(128)}, f32[4,1024]{1,0:T(4,128)S(1)}, f32[4,1024]{1,0:T(4,128)S(1)}, s32[1024]{0:T(1024)S(1)}, s32[16,512]{1,0:T(8,128)S(1)}, /*index=5*/s...) while((s32[]{:T(128)}, f32[4,1024]{1,0:T(4,128)S(1)}, ...), condition=%wide.region_11.12_spmd, body=%wide.region_5.11_spmd.sunk | while | flops 555753472 | bytes 19763912 | solution.py:112
  267.6 4.7 conditional.6
  331.2 73.0 %while.41 = (s32[]{:T(128)}, f32[1024,4,128]{2,0,1:T(8,128)}, s32[1024]{0:T(1024)S(1)}, s32[16,512]{1,0:T(8,128)S(1)}, s32[16,512]{1,0:T(8,128)S(1)}, /*index=5*...) while((s32[]{:T(128)}, f32[1024,4,128]{2,0,1:T(8,128)}, ...), condition=%wide.region_16.17_spmd, body=%wide.region_12.16_spmd.sunk | while | flops 1084751872 | bytes 6591671 | solution.py:132
  333.1 6.0 conditional.7
  333.1 6.0 bitcast_add_fusion
  341.0 6.0 conditional.7
  341.0 6.0 bitcast_add_fusion
  356.8 6.0 conditional.7
  356.8 6.0 bitcast_add_fusion
  364.7 6.0 conditional.7
  364.7 6.0 bitcast_add_fusion
  376.5 6.0 conditional.7
  376.5 6.0 bitcast_add_fusion
  386.4 6.0 conditional.7
  386.4 6.0 bitcast_add_fusion
  394.3 6.0 conditional.7
  394.3 6.0 bitcast_add_fusion
  407.4 5.9 convolution_convert_fusion.4
  414.2 95.9 %reduce-scatter.12.cloned.1.call-done = bf16[256,2048]{1,0:T(8,128)(2,1)} async-done(((bf16[1024,2048]{1,0:T(8,128)(2,1)}), bf16[256,2048]{1,0:T(8,128)(2,1)}) %reduce-scatter.12.cloned.1.call-update) | async-done | bytes 1048592 | tf_op jit(solution)/shard_map/reduce_scatter | solution.py:293
  516.5 64.9 %all-gather.24.cloned.1.call-done = bf16[2048,2752]{0,1:T(8,128)(2,1)} async-done(((bf16[256,2752]{0,1:T(8,128)(2,1)}), bf16[2048,2752]{0,1:T(8,128)(2,1)}) %all-gather.24.cloned.1.call-update) | async-done | bytes 11272208 | tf_op jit(solution)/shard_map/all_gather | solution.py:235
  581.4 83.0 %all-gather.22.cloned.1.call-done = bf16[1024,2048]{1,0:T(8,128)(2,1)} async-done(((bf16[256,2048]{1,0:T(8,128)(2,1)}), bf16[1024,2048]{1,0:T(8,128)(2,1)}) %all-gather.22.cloned.1.call-update) | async-done | bytes 4194320 | tf_op jit(solution)/shard_map/all_gather | solution.py:200
  664.4 17.5 fusion.86
  681.9 51.9 %all-gather.26.cloned.1.call-done = bf16[2048,2752]{0,1:T(8,128)(2,1)} async-done(((bf16[256,2752]{0,1:T(8,128)(2,1)}), bf16[2048,2752]{0,1:T(8,128)(2,1)}) %all-gather.26.cloned.1.call-update) | async-done | bytes 11272208 | tf_op jit(solution)/shard_map/all_gather | solution.py:236
  733.8 17.4 fusion.87
  751.2 64.8 %all-gather.30.cloned.1.call-done = bf16[1024,2048]{1,0:T(8,128)(2,1)} async-done(((bf16[256,2048]{1,0:T(8,128)(2,1)}), bf16[1024,2048]{1,0:T(8,128)(2,1)}) %all-gather.30.cloned.1.call-update) | async-done | bytes 4194320 | tf_op jit(solution)/shard_map/all_gather | solution.py:195
  816.1 69.3 %all-gather.28.cloned.1.call-done = bf16[2752,2048]{1,0:T(8,128)(2,1)} async-done(((bf16[2752,256]{1,0:T(8,128)(2,1)}), bf16[2752,2048]{1,0:T(8,128)(2,1)}) %all-gather.28.cloned.1.call-update) | async-done | bytes 11272208 | tf_op jit(solution)/shard_map/all_gather | solution.py:237
  885.4 24.2 %multiply_convert_fusion = (bf16[1024,2752]{0,1:T(8,128)(2,1)}, bf16[1024,2752]{0,1:T(8,128)(2,1)S(1)}, bf16[1024,2752]{0,1:T(8,128)(2,1)}) fusion(f32[1024,2752]{0,1:T(8,128)} %fusion.86, f32[1024,2752]{0,1:T(8,128)} %fusion.87, bf16[1024,2048]{1,0:T(8,128)(2,1)} %all-gather.30.cloned.1.call-done, bf16[2752,2048]{1,0:T(8,128)(2,1)} %all-gather.28.cloned.1.call-done), kind=kOutput, calls=%fused_computation.62 | convolution fusion | flops 11587813376 | bytes 54919168 | tf_op jit(solution)/shard_map/dot_general | solution.py:18
  909.6 19.7 fusion.88
  929.4 17.3 add_convert_fusion
  946.8 76.9 %reduce-scatter.16.cloned.1.call-done = bf16[256,2048]{1,0:T(8,128)(2,1)} async-done(((bf16[1024,2048]{1,0:T(8,128)(2,1)}), bf16[256,2048]{1,0:T(8,128)(2,1)}) %reduce-scatter.16.cloned.1.call-update) | async-done | bytes 1048592 | tf_op jit(solution)/shard_map/reduce_scatter | solution.py:320
  1030.1 81.1 %all-gather.32.cloned.1.call-done = bf16[1024,2048]{1,0:T(8,128)(2,1)} async-done(((bf16[256,2048]{1,0:T(8,128)(2,1)}), bf16[1024,2048]{1,0:T(8,128)(2,1)}) %all-gather.32.cloned.1.call-update) | async-done | bytes 4194320 | tf_op jit(solution)/shard_map/all_gather | solution.py:325
  1111.3 6.4 multiply_reduce_fusion
  1117.9 219.6 %while.42 = (s32[]{:T(128)}, f32[1024,4,128]{2,0,1:T(8,128)S(1)}, f32[16,512,256]{2,1,0:T(8,128)}, s32[1024]{0:T(1024)S(1)}, s32[16,512]{1,0:T(8,128)}, /*index=...) while((s32[]{:T(128)}, f32[1024,4,128]{2,0,1:T(8,128)S(1)}, ...), condition=%wide.region_27.28_spmd, body=%wide.region_23.27_spmd.sunk | while | flops 2710175744 | bytes 58136864 | solution.py:186
  1121.2 13.6 conditional.8
  1142.1 13.6 conditional.8
  1195.6 13.6 conditional.8
  1216.5 13.6 conditional.8
  1253.7 13.6 conditional.8
  1282.8 13.6 conditional.8
  1303.7 13.6 conditional.8
  1337.5 8.0 broadcast_in_dim.121
  1350.7 17.5 convolution_convert_fusion.1
  1368.3 17.5 convolution_convert_fusion
  1386.1 17.6 convolution_convert_fusion.2
  1413.6 5.8 convolution_convert_fusion.6
  1419.7 6.0 convolution_convert_fusion.3
  1425.8 18.3 convolution_convert_fusion.5
  1444.2 291.8 %reduce-scatter.20.cloned.1.call-done = f32[256,512]{1,0:T(8,128)} async-done(((f32[8192,512]{1,0:T(8,128)}), f32[256,512]{1,0:T(8,128)}) %reduce-scatter.20.cloned.1.call-update) | async-done | bytes 524304 | tf_op jit(solution)/shard_map/reduce_scatter | solution.py:351
  1742.6 81.2 %reduce-scatter.28.cloned.1.call-done = bf16[256,2752]{0,1:T(8,128)(2,1)} async-done(((bf16[2048,2752]{0,1:T(8,128)(2,1)}), bf16[256,2752]{0,1:T(8,128)(2,1)}) %reduce-scatter.28.cloned.1.call-update) | async-done | bytes 1409040 | tf_op jit(solution)/shard_map/reduce_scatter | solution.py:385
  1827.0 86.2 %reduce-scatter.30.cloned.1.call-done = bf16[256,2752]{0,1:T(8,128)(2,1)} async-done(((bf16[2048,2752]{0,1:T(8,128)(2,1)}), bf16[256,2752]{0,1:T(8,128)(2,1)}) %reduce-scatter.30.cloned.1.call-update) | async-done | bytes 1409040 | tf_op jit(solution)/shard_map/reduce_scatter | solution.py:388
  1916.3 85.7 %reduce-scatter.32.cloned.1.call-done = bf16[2752,256]{1,0:T(8,128)(2,1)} async-done(((bf16[2752,2048]{1,0:T(8,128)(2,1)}), bf16[2752,256]{1,0:T(8,128)(2,1)}) %reduce-scatter.32.cloned.1.call-update) | async-done | bytes 1409040 | tf_op jit(solution)/shard_map/reduce_scatter | solution.py:391
  2005.1 42.2 %reduce-scatter.22.cloned.1.call-done = bf16[256,512]{1,0:T(8,128)(2,1)} async-done(((bf16[2048,512]{1,0:T(8,128)(2,1)}), bf16[256,512]{1,0:T(8,128)(2,1)}) %reduce-scatter.22.cloned.1.call-update) | async-done | bytes 262160 | tf_op jit(solution)/shard_map/reduce_scatter | solution.py:379
  2049.2 43.2 %reduce-scatter.26.cloned.1.call-done = bf16[512,256]{1,0:T(8,128)(2,1)} async-done(((bf16[512,2048]{1,0:T(8,128)(2,1)}), bf16[512,256]{1,0:T(8,128)(2,1)}) %reduce-scatter.26.cloned.1.call-update) | async-done | bytes 262160 | tf_op jit(solution)/shard_map/reduce_scatter | solution.py:382
  2094.3 77.2 %reduce-scatter.18.cloned.1.call-done = bf16[256,2048]{1,0:T(8,128)(2,1)} async-done(((bf16[1024,2048]{1,0:T(8,128)(2,1)}), bf16[256,2048]{1,0:T(8,128)(2,1)}) %reduce-scatter.18.cloned.1.call-update) | async-done | bytes 1048592 | tf_op jit(solution)/shard_map/reduce_scatter | solution.py:373
  2175.6 45.4 %all-reduce.8 = (f32[2048]{0:T(1024)S(1)}, f32[512]{0:T(512)S(1)}, f32[2048]{0:T(1024)S(1)}, f32[2048]{0:T(1024)S(1)}) all-reduce(f32[2048]{0:T(1024)S(1)} %bitcast_dynamic-update-slice_fusion, f32[512]{0:T(512)S(1)} %convert_reduce_fusion.1, ...), channel_id=8, replica_groups=mesh['seq'=8,'head'=4] {'seq','head'}, use_global_device_ids=true, to_apply=%region_33.34.clone | all-reduce | flops 6656 | bytes 53248
  2223.3 28.8 %reduce-scatter.14.cloned.1.call-done = bf16[256,2048]{1,0:T(8,128)(2,1)} async-done(((bf16[1024,2048]{1,0:T(8,128)(2,1)}), bf16[256,2048]{1,0:T(8,128)(2,1)}) %reduce-scatter.14.cloned.1.call-update) | async-done | bytes 1048592 | tf_op jit(solution)/shard_map/reduce_scatter | solution.py:303
  2252.2 5.7 fusion.61
  2257.9 145.2 %reduce-scatter.24.cloned.1.call-done = f32[64,512]{1,0:T(8,128)} async-done(((f32[2048,512]{1,0:T(8,128)}), f32[64,512]{1,0:T(8,128)}) %reduce-scatter.24.cloned.1.call-update) | async-done | bytes 131088 | tf_op jit(solution)/shard_map/reduce_scatter | solution.py:396
  (504 shorter events, 407.5 us)
Async XLA Ops:
  7.2 52.6 %copy-start.44 = (s32[8]{0:T(128)S(1)}, s32[8]{0:T(128)}, u32[]{:S(2)}) copy-start(s32[8]{0:T(128)} %param.40) | copy-start | bytes 100
  7.2 53.4 %copy-start.45 = (s32[16]{0:T(128)S(1)}, s32[16]{0:T(128)}, u32[]{:S(2)}) copy-start(s32[16]{0:T(128)} %param.39) | copy-start | bytes 196
  7.2 63.0 %all-gather.12.cloned.1.call-start = ((), (), s32[]{:S(2)}) async-start(), calls=%async_computation.11 | async-start | bytes 2162688 | tf_op jit(solution)/shard_map/all_gather | solution.py:240
  7.9 90.9 %all-gather.18.cloned.1.call-start = ((), (), s32[]{:S(2)}) async-start(), calls=%async_computation.14 | async-start | bytes 2359296 | tf_op jit(solution)/shard_map/all_gather | solution.py:233
  8.7 173.1 %all-gather.16.cloned.1.call-start = ((), (), s32[]{:S(2)}) async-start(), calls=%async_computation.13 | async-start | bytes 5242880 | tf_op jit(solution)/shard_map/all_gather | solution.py:194
  59.7 201.4 %all-gather.14.cloned.1.call-start = ((), (), s32[]{:S(2)}) async-start(), calls=%async_computation.12 | async-start | bytes 8650752 | tf_op jit(solution)/shard_map/all_gather | solution.py:204
  62.8 14.1 copy-start.46
  75.3 331.1 %all-gather.20.cloned.1.call-start = ((), (), s32[]{:S(2)}) async-start(), calls=%async_computation.15 | async-start | bytes 2359296 | tf_op jit(solution)/shard_map/all_gather | solution.py:234
  75.9 434.2 %reduce-scatter.12.cloned.1.call-start = ((), (), s32[]{:S(2)}) async-start(), calls=%async_computation.16 | async-start | bytes 5242880 | tf_op jit(solution)/shard_map/reduce_scatter | solution.py:293
  80.1 107.2 %copy-start.12 = (f32[1024,128]{0,1:T(8,128)}, f32[1024,128]{0,1:T(8,128)S(1)}, u32[]{:S(2)}) copy-start(f32[1024,128]{0,1:T(8,128)S(1)} %get-tuple-element.553) | copy-start | bytes 1572868
  188.0 77.7 %copy-start = (bf16[1024,4,128]{0,2,1:T(8,128)(2,1)}, bf16[1024,4,128]{0,2,1:T(8,128)(2,1)S(1)}, u32[]{:S(2)}) copy-start(bf16[1024,4,128]{0,2,1:T(8,128)(2,1)S(1)} %fusion.66) | copy-start | bytes 3145732
  404.2 9.1 copy-start.17
  404.2 9.1 copy-start.19
  404.2 9.1 copy-start.26
  404.3 9.1 copy-start.27
  404.3 9.1 copy-start.33
  413.4 96.8 %copy-start.2 = (bf16[256,2048]{1,0:T(8,128)(2,1)S(1)}, bf16[256,2048]{1,0:T(8,128)(2,1)}, u32[]{:S(2)}) copy-start(bf16[256,2048]{1,0:T(8,128)(2,1)} %param.27) | copy-start | bytes 3145732
  413.4 168.0 %all-gather.24.cloned.1.call-start = ((), (), s32[]{:S(2)}) async-start(), calls=%async_computation.18 | async-start | bytes 12681216 | tf_op jit(solution)/shard_map/all_gather | solution.py:235
  414.2 250.3 %all-gather.22.cloned.1.call-start = ((), (), s32[]{:S(2)}) async-start(), calls=%async_computation.17 | async-start | bytes 5242880 | tf_op jit(solution)/shard_map/all_gather | solution.py:200
  414.2 612.0 %copy-start.24 = (f32[2048]{0:T(1024)}, f32[2048]{0:T(1024)S(1)}, u32[]{:S(2)}) copy-start(f32[2048]{0:T(1024)S(1)} %convert_element_type.170) | copy-start | bytes 24580
  511.8 514.4 %copy-start.31 = (f32[256]{0:T(256)}, f32[256]{0:T(256)S(1)}, u32[]{:S(2)}) copy-start(f32[256]{0:T(256)S(1)} %get-tuple-element.562) | copy-start | bytes 3076
  511.8 514.4 %copy-start.37 = (f32[256]{0:T(256)}, f32[256]{0:T(256)S(1)}, u32[]{:S(2)}) copy-start(f32[256]{0:T(256)S(1)} %get-tuple-element.561) | copy-start | bytes 3076
  514.4 219.4 %all-gather.26.cloned.1.call-start = ((), (), s32[]{:S(2)}) async-start(), calls=%async_computation.19 | async-start | bytes 12681216 | tf_op jit(solution)/shard_map/all_gather | solution.py:236
  515.2 300.9 %all-gather.30.cloned.1.call-start = ((), (), s32[]{:S(2)}) async-start(), calls=%async_computation.22 | async-start | bytes 5242880 | tf_op jit(solution)/shard_map/all_gather | solution.py:195
  515.7 369.7 %all-gather.28.cloned.1.call-start = ((), (), s32[]{:S(2)}) async-start(), calls=%async_computation.20 | async-start | bytes 12681216 | tf_op jit(solution)/shard_map/all_gather | solution.py:237
  516.5 507.1 %reduce-scatter.16.cloned.1.call-start = ((), (), s32[]{:S(2)}) async-start(), calls=%async_computation.23 | async-start | bytes 5242880 | tf_op jit(solution)/shard_map/reduce_scatter | solution.py:320
  909.6 19.7 copy-start.48
  909.6 19.7 copy-start.42
  946.7 76.9 %copy-start.4 = (bf16[256,2048]{1,0:T(8,128)(2,1)S(1)}, bf16[256,2048]{1,0:T(8,128)(2,1)}, u32[]{:S(2)}) copy-start(bf16[256,2048]{1,0:T(8,128)(2,1)} %reduce-scatter.12.cloned.1.call-done) | copy-start | bytes 3145732
  946.7 80.1 %copy-start.9 = (bf16[256,2048]{1,0:T(8,128)(2,1)S(1)}, bf16[256,2048]{1,0:T(8,128)(2,1)}, u32[]{:S(2)}) copy-start(bf16[256,2048]{1,0:T(8,128)(2,1)} %param.28) | copy-start | bytes 3145732
  946.7 164.5 %all-gather.32.cloned.1.call-start = ((), (), s32[]{:S(2)}) async-start(), calls=%async_computation.24 | async-start | bytes 5242880 | tf_op jit(solution)/shard_map/all_gather | solution.py:325
  1029.8 706.1 %reduce-scatter.20.cloned.1.call-start = ((), (), s32[]{:S(2)}) async-start(), calls=%async_computation.26 | async-start | bytes 17301504 | tf_op jit(solution)/shard_map/reduce_scatter | solution.py:351
  1030.1 87.7 %copy-start.1 = (bf16[1024,4,128]{0,2,1:T(8,128)(2,1)S(1)}, bf16[1024,4,128]{0,2,1:T(8,128)(2,1)}, u32[]{:S(2)}) copy-start(bf16[1024,4,128]{0,2,1:T(8,128)(2,1)} %copy-done) | copy-start | bytes 3145732
  1030.1 87.7 %copy-start.18 = (s32[1024]{0:T(1024)S(1)}, s32[1024]{0:T(1024)}, u32[]{:S(2)}) copy-start(s32[1024]{0:T(1024)} %copy-done.17) | copy-start | bytes 12292
  1030.1 87.7 %copy-start.20 = (s32[1024]{0:T(1024)S(1)}, s32[1024]{0:T(1024)}, u32[]{:S(2)}) copy-start(s32[1024]{0:T(1024)} %copy-done.19) | copy-start | bytes 12292
  1030.1 87.7 %copy-start.34 = (f32[4,1024]{1,0:T(4,128)S(1)}, f32[4,1024]{1,0:T(4,128)}, u32[]{:S(2)}) copy-start(f32[4,1024]{1,0:T(4,128)} %copy-done.33) | copy-start | bytes 49156
  1142.2 2.3 copy-start.8
  1216.5 2.3 copy-start.8
  1337.5 8.0 copy-start.11
  1350.2 473.6 %reduce-scatter.28.cloned.1.call-start = ((), (), s32[]{:S(2)}) async-start(), calls=%async_computation.30 | async-start | bytes 12681216 | tf_op jit(solution)/shard_map/reduce_scatter | solution.py:385
  1368.2 544.9 %reduce-scatter.30.cloned.1.call-start = ((), (), s32[]{:S(2)}) async-start(), calls=%async_computation.31 | async-start | bytes 12681216 | tf_op jit(solution)/shard_map/reduce_scatter | solution.py:388
  1385.9 616.1 %reduce-scatter.32.cloned.1.call-start = ((), (), s32[]{:S(2)}) async-start(), calls=%async_computation.32 | async-start | bytes 12681216 | tf_op jit(solution)/shard_map/reduce_scatter | solution.py:391
  1403.7 643.6 %reduce-scatter.22.cloned.1.call-start = ((), (), s32[]{:S(2)}) async-start(), calls=%async_computation.27 | async-start | bytes 2359296 | tf_op jit(solution)/shard_map/reduce_scatter | solution.py:379
  1403.7 3.8 copy-start.13
  1403.7 3.8 copy-start.16
  1409.8 3.8 copy-start.22
  1413.5 678.9 %reduce-scatter.26.cloned.1.call-start = ((), (), s32[]{:S(2)}) async-start(), calls=%async_computation.29 | async-start | bytes 2359296 | tf_op jit(solution)/shard_map/reduce_scatter | solution.py:382
  1419.5 752.0 %reduce-scatter.18.cloned.1.call-start = ((), (), s32[]{:S(2)}) async-start(), calls=%async_computation.25 | async-start | bytes 5242880 | tf_op jit(solution)/shard_map/reduce_scatter | solution.py:373
  1425.8 826.4 %reduce-scatter.14.cloned.1.call-start = ((), (), s32[]{:S(2)}) async-start(), calls=%async_computation.21 | async-start | bytes 5242880 | tf_op jit(solution)/shard_map/reduce_scatter | solution.py:303
  1444.1 294.3 %copy-start.23 = (f32[256,128]{1,0:T(8,128)S(1)}, f32[256,128]{1,0:T(8,128)}, u32[]{:S(2)}) copy-start(f32[256,128]{1,0:T(8,128)} %get-tuple-element.556) | copy-start | bytes 393220
  1444.1 294.6 %copy-start.15 = (f32[256,2,128]{2,1,0:T(2,128)S(1)}, f32[256,2,128]{2,1,0:T(2,128)}, u32[]{:S(2)}) copy-start(f32[256,2,128]{2,1,0:T(2,128)} %copy-done.14) | copy-start | bytes 786436
  1444.1 295.7 %copy-start.7 = (bf16[256,2048]{1,0:T(8,128)(2,1)S(1)}, bf16[256,2048]{1,0:T(8,128)(2,1)}, u32[]{:S(2)}) copy-start(bf16[256,2048]{1,0:T(8,128)(2,1)} %fusion.58) | copy-start | bytes 3145732
  1444.1 959.0 %reduce-scatter.24.cloned.1.call-start = ((), (), s32[]{:S(2)}) async-start(), calls=%async_computation.28 | async-start | bytes 4325376 | tf_op jit(solution)/shard_map/reduce_scatter | solution.py:396
  1827.0 344.5 %copy-start.3 = (bf16[256,2048]{1,0:T(8,128)(2,1)S(1)}, bf16[256,2048]{1,0:T(8,128)(2,1)}, u32[]{:S(2)}) copy-start(bf16[256,2048]{1,0:T(8,128)(2,1)} %param.27) | copy-start | bytes 3145732
  1827.0 344.5 %copy-start.29 = (f32[2048]{0:T(1024)S(1)}, f32[2048]{0:T(1024)}, u32[]{:S(2)}) copy-start(f32[2048]{0:T(1024)} %copy-done.28) | copy-start | bytes 24580
  1827.0 344.5 %copy-start.36 = (f32[256]{0:T(256)S(1)}, f32[256]{0:T(256)}, u32[]{:S(2)}) copy-start(f32[256]{0:T(256)} %copy-done.35) | copy-start | bytes 3076
  2049.1 126.5 %copy-start.30 = (f32[2048]{0:T(1024)S(1)}, f32[2048]{0:T(1024)}, u32[]{:S(2)}) copy-start(f32[2048]{0:T(1024)} %get-tuple-element.446) | copy-start | bytes 24580
  2049.1 203.0 %copy-start.5 = (bf16[256,2048]{1,0:T(8,128)(2,1)S(1)}, bf16[256,2048]{1,0:T(8,128)(2,1)}, u32[]{:S(2)}) copy-start(bf16[256,2048]{1,0:T(8,128)(2,1)} %reduce-scatter.12.cloned.1.call-done) | copy-start | bytes 3145732
  2049.1 203.0 %copy-start.10 = (bf16[256,2048]{1,0:T(8,128)(2,1)S(1)}, bf16[256,2048]{1,0:T(8,128)(2,1)}, u32[]{:S(2)}) copy-start(bf16[256,2048]{1,0:T(8,128)(2,1)} %param.28) | copy-start | bytes 3145732
  2049.1 203.0 %copy-start.25 = (f32[2048]{0:T(1024)S(1)}, f32[2048]{0:T(1024)}, u32[]{:S(2)}) copy-start(f32[2048]{0:T(1024)} %copy-done.24) | copy-start | bytes 24580
  2049.1 203.0 %copy-start.32 = (f32[256]{0:T(256)S(1)}, f32[256]{0:T(256)}, u32[]{:S(2)}) copy-start(f32[256]{0:T(256)} %copy-done.31) | copy-start | bytes 3076
  2049.1 203.0 %copy-start.38 = (f32[256]{0:T(256)S(1)}, f32[256]{0:T(256)}, u32[]{:S(2)}) copy-start(f32[256]{0:T(256)} %copy-done.37) | copy-start | bytes 3076
  2049.2 203.0 %copy-start.40 = (f32[256]{0:T(256)S(1)}, f32[256]{0:T(256)}, u32[]{:S(2)}) copy-start(f32[256]{0:T(256)} %copy-done.39) | copy-start | bytes 3076
  2049.2 203.0 %copy-start.41 = (f32[256]{0:T(256)S(1)}, f32[256]{0:T(256)}, u32[]{:S(2)}) copy-start(f32[256]{0:T(256)} %get-tuple-element.559) | copy-start | bytes 3076
  (19 other events, 37.0 us)
Sparse Core Ops, SparseCore 0:
  11.0 59.1 all-gather.11
  72.1 26.7 all-gather.17
  101.0 80.7 all-gather.15
  185.2 75.9 all-gather.13
  262.8 26.7 all-gather.19
  413.5 96.5 reduce-scatter.11
  512.2 69.2 all-gather.23
  583.6 80.7 all-gather.21
  666.5 67.2 all-gather.25
  735.3 80.7 all-gather.29
  818.1 67.2 all-gather.27
  946.8 76.7 reduce-scatter.15
  1029.9 81.2 all-gather.31
  1350.4 385.5 reduce-scatter.19
  1739.4 84.4 reduce-scatter.27
  1827.8 85.3 reduce-scatter.29
  1916.6 85.3 reduce-scatter.31
  2006.1 41.2 reduce-scatter.21
  2051.2 41.2 reduce-scatter.25
  2094.7 76.7 reduce-scatter.17
  2173.8 78.3 reduce-scatter.13
  2255.1 148.0 reduce-scatter.23
where the time goes:
time: 2420 us; the launch traced here: 2410 us
  waiting for transfers between devices  1650 us (68%)
  matrix products  358 us (15%)
  other arithmetic  139 us (6%)
  local copies, waits for them, and re-layouts  120 us (5%)
  blocking collectives  87.7 us (4%)
  loops' own time  33.5 us (1%)
    reduce_scatter x1, waiting for transfers between devices, local(): lax.psum_scatter(placed, ('seq', 'head'), scatter_dimension=0, tiled=True)  292 us
    reduce_scatter x1, waiting for transfers between devices, local(): lax.psum_scatter(kv_weight_part, ('seq', 'head'), scatter_dimension=0, ti...  145 us
    dot_general x12, matrix products, contract(): lax.dot_general(left_side, right_side, (((left_dim,), (right_dim,)), ((),...  143 us
    reduce_scatter x1, waiting for transfers between devices, local(): lax.psum_scatter(attn_terms.astype(jnp.bfloat16), 'head', scatter_dimensi...  95.9 us
    unnamed x2, blocking collectives  87.7 us
    reduce_scatter x1, waiting for transfers between devices, local(): lax.psum_scatter(up_grad.astype(jnp.bfloat16), 'seq', scatter_dimension=0...  86.2 us
    reduce_scatter x1, waiting for transfers between devices, local(): lax.psum_scatter(down_grad.astype(jnp.bfloat16), 'seq', scatter_dimension...  85.7 us
    all_gather x1, waiting for transfers between devices, gather_ffn(): return lax.all_gather(normed2, 'head', axis=0, tiled=True)  83 us
  transfers between devices with their start and end apart: 22, of which 21 were waited for; matrix products, arithmetic and copies ran while one was open for 13% of the time, Pallas kernels for 0%

commit v1 on v0

v1 whole, which is shorter than its diff:
```python
import functools

import jax
import jax.numpy as jnp
from jax import lax
from jax.experimental import pallas as pl
from jax.experimental.pallas import tpu as pltpu
from jax.sharding import PartitionSpec as P

HEADS = 16
KV = 2
HD = 128
BLK = 512
GROUP = HEADS // KV
TILE = 512
BATCH = 8

EPSILON = 1e-06
ROPE_BASE = 1000000.0
NEGATIVE = -1e30
SCALE = HD**-0.5
LOG2E = 1.4426950408889634

F32 = jnp.float32
BF16 = jnp.bfloat16

RELATIVE = (0, 2, 4, 6, 1, 3, 5, 7)
SLOTS = ((0, 1, 2, 3), (1, 0, 2, 3), (2, 3, 1, 0), (3, 2, 1, 0))


def contract(left_side, right_side, left_dim, right_dim):
    return lax.dot_general(
        left_side,
        right_side,
        (((left_dim,), (right_dim,)), ((), ())),
        preferred_element_type=F32,
    )


class SeqAxis:
    def __init__(self):
        self.size = lax.axis_size("seq")
        self.me = lax.axis_index("seq")
        self.fast = self.size == 8

    def owner(self, position):
        return self.me ^ RELATIVE[position] if self.fast else position

    def swap(self, value, bit):
        return lax.ppermute(value, "seq", [(i, i ^ bit) for i in range(self.size)])

    def gather(self, value):
        if not self.fast:
            whole = lax.all_gather(value, "seq", axis=0, tiled=False)
            return [whole[i] for i in range(self.size)]
        half = value.shape[0] // 2
        along_x = self.swap(value, 2)
        along_y = self.swap(value, 4)
        corner = jnp.concatenate(
            [self.swap(along_y[:half], 2), self.swap(along_x[half:], 4)], axis=0
        )
        chip = [value, along_x, along_y, corner]
        return chip + [self.swap(item, 1) for item in chip]

    def reduce(self, even, odd, axis):
        if not self.fast:
            whole = jnp.concatenate([even, odd], axis=axis).astype(BF16)
            return lax.psum_scatter(whole, "seq", scatter_dimension=axis, tiled=True).astype(F32)
        width = even.shape[axis] // 4
        chip = (even + self.swap(odd.astype(BF16), 1).astype(F32)).astype(BF16)
        here, to_x, to_y, corner = (
            lax.slice_in_dim(chip, i * width, (i + 1) * width, axis=axis) for i in range(4)
        )
        half = corner.shape[0] // 2
        for_y = self.swap(corner[:half], 2)
        for_x = self.swap(corner[half:], 4)
        to_x = jnp.concatenate([to_x[:half], to_x[half:] + for_x], axis=0)
        to_y = jnp.concatenate([to_y[:half] + for_y, to_y[half:]], axis=0)
        return here.astype(F32) + self.swap(to_x, 2).astype(F32) + self.swap(to_y, 4).astype(F32)


class HeadAxis:
    def __init__(self):
        self.size = lax.axis_size("head")
        self.me = lax.axis_index("head")
        self.fast = self.size == 4
        self.inner = (self.me == 1) | (self.me == 2)

    def owners(self):
        if self.fast:
            return jnp.array(SLOTS, jnp.int32)[self.me]
        return jnp.arange(self.size, dtype=jnp.int32)

    def send(self, value, pairs):
        return lax.ppermute(value, "head", pairs)

    def gather(self, value):
        if not self.fast:
            whole = lax.all_gather(value, "head", axis=0, tiled=False)
            return [whole[i] for i in range(self.size)]
        pair = [(0, 1), (1, 0), (2, 3), (3, 2)]
        middle = [(1, 2), (2, 1)]
        outward = [(1, 0), (2, 3)]
        slot1 = self.send(value, pair)
        near = self.send(value, middle)
        far = self.send(slot1, middle)
        slot2 = jnp.where(self.inner, near, self.send(near, outward))
        slot3 = jnp.where(self.inner, far, self.send(far, outward))
        return [value, slot1, slot2, slot3]

    def reduce(self, pieces):
        if not self.fast:
            whole = jnp.stack(pieces).astype(BF16)
            return lax.psum_scatter(whole, "head", scatter_dimension=0, tiled=False).astype(F32)
        pair = [(0, 1), (1, 0), (2, 3), (3, 2)]
        middle = [(1, 2), (2, 1)]
        inward = [(0, 1), (3, 2)]
        own, slot1, slot2, slot3 = pieces
        far = slot3 + self.send(slot3.astype(BF16), inward)
        near = slot2 + self.send(slot2.astype(BF16), inward)
        next_door = slot1 + self.send(far.astype(BF16), middle)
        return (
            own.astype(F32)
            + self.send(next_door.astype(BF16), pair).astype(F32)
            + self.send(near.astype(BF16), middle).astype(F32)
        )


def place(pieces, owners, axis):
    width = pieces[0].shape[axis]
    shape = list(pieces[0].shape)
    shape[axis] = width * len(pieces)
    whole = jnp.zeros(shape, pieces[0].dtype)
    for slot, item in enumerate(pieces):
        whole = lax.dynamic_update_slice_in_dim(whole, item, owners[slot] * width, axis)
    return whole


def take(whole, owners, axis):
    count = owners.shape[0]
    width = whole.shape[axis] // count
    return [
        lax.dynamic_slice_in_dim(whole, owners[slot] * width, width, axis) for slot in range(count)
    ]


def vmem():
    return pl.BlockSpec(memory_space=pltpu.VMEM)


def smem():
    return pl.BlockSpec(memory_space=pltpu.SMEM)


def shuffle_kernel(order_ref, in_ref, out_ref):
    out_ref[...] = in_ref[...]


def shuffle(values, order):
    count = order.shape[0]
    rows, width = values.shape[0], values.shape[1] // count
    return pl.pallas_call(
        shuffle_kernel,
        out_shape=jax.ShapeDtypeStruct(values.shape, values.dtype),
        grid_spec=pltpu.PrefetchScalarGridSpec(
            num_scalar_prefetch=1,
            grid=(count,),
            in_specs=[pl.BlockSpec((rows, width), lambda i, order_ref: (0, order_ref[i]))],
            out_specs=pl.BlockSpec((rows, width), lambda i, order_ref: (0, i)),
        ),
        cost_estimate=pl.CostEstimate(flops=0, transcendentals=0, bytes_accessed=2 * values.nbytes if hasattr(values, "nbytes") else 0),
        name="shuffle",
    )(order, values)


def turn(values, cosine, sine):
    return values * cosine + pltpu.roll(values, HD // 2, 1) * sine


def allowed_bias(tile, stream, first, shape):
    key = tile * TILE + lax.broadcasted_iota(jnp.int32, shape, 0)
    return jnp.where((key >= first) & (key <= stream), 0.0, NEGATIVE)


def forward_kernel(
    offset_ref, bound_ref, raw_ref, cos_ref, sin_ref, stream_ref, first_ref, kv_ref,
    query_ref, mixed_ref, lse_ref,
    top_ref, total_ref, sum_ref, bias_ref, turned_ref,
):
    rows = raw_ref.shape[0]
    cosine, sine = cos_ref[...], sin_ref[...]
    for h in range(HEADS):
        query_ref[h] = turn(raw_ref[:, h * HD : (h + 1) * HD], cosine, sine).astype(BF16)
    top_ref[...] = jnp.full(top_ref.shape, NEGATIVE, F32)
    total_ref[...] = jnp.zeros(total_ref.shape, F32)
    sum_ref[...] = jnp.zeros(sum_ref.shape, F32)

    def visit(tile, carry):
        start = pl.multiple_of(offset_ref[tile], TILE)
        bias_ref[...] = allowed_bias(tile, stream_ref[...], first_ref[...], bias_ref.shape)
        for g in range(KV):
            turned_ref[g] = kv_ref[pl.ds(start, TILE), (KV + g) * HD : (KV + g + 1) * HD].T
        for g in range(KV):
            keys = kv_ref[pl.ds(start, TILE), g * HD : (g + 1) * HD]

            def some(i, carry):
                heads = [g * GROUP + i * BATCH + b for b in range(BATCH)]
                old = [top_ref[h] for h in heads]
                total = [total_ref[h] for h in heads]
                summed = [sum_ref[h] for h in heads]
                scores = [contract(keys, query_ref[h], 1, 1) for h in heads]
                bias = bias_ref[...]
                turned = turned_ref[g]
                new, fresh, fades = [], [], []
                for b in range(BATCH):
                    score = scores[b] * (SCALE * LOG2E) + bias
                    peak = jnp.maximum(old[b], jnp.max(score, axis=0, keepdims=True))
                    weights = jnp.exp2(score - peak)
                    fade = jnp.exp2(old[b] - peak)
                    new.append(peak)
                    fades.append(fade)
                    total[b] = total[b] * fade + jnp.sum(weights, axis=0, keepdims=True)
                    fresh.append(contract(turned, weights.astype(BF16), 1, 0))
                for b, h in enumerate(heads):
                    top_ref[h] = new[b]
                    total_ref[h] = total[b]
                    sum_ref[h] = summed[b] * fades[b] + fresh[b]
                return carry

            lax.fori_loop(0, GROUP // BATCH, some, 0)
        return carry

    lax.fori_loop(bound_ref[0], bound_ref[1] + 1, visit, 0)
    for h in range(HEADS):
        lse_ref[h] = top_ref[h] + jnp.log2(total_ref[h])
        mixed_ref[:, h * HD : (h + 1) * HD] = (sum_ref[h] / total_ref[h]).T.astype(BF16)


def attention_forward(offsets, bounds, query_raw, cosine, sine, stream, first, kv_all):
    rows = query_raw.shape[0]
    return pl.pallas_call(
        forward_kernel,
        out_shape=(
            jax.ShapeDtypeStruct((HEADS, rows, HD), BF16),
            jax.ShapeDtypeStruct((rows, HEADS * HD), BF16),
            jax.ShapeDtypeStruct((HEADS, 1, rows), F32),
        ),
        in_specs=[smem(), smem()] + [vmem()] * 6,
        out_specs=[vmem()] * 3,
        scratch_shapes=[
            pltpu.VMEM((HEADS, 1, rows), F32),
            pltpu.VMEM((HEADS, 1, rows), F32),
            pltpu.VMEM((HEADS, HD, rows), F32),
            pltpu.VMEM((TILE, rows), F32),
            pltpu.VMEM((KV, HD, TILE), BF16),
        ],
        compiler_params=pltpu.CompilerParams(vmem_limit_bytes=48 << 20),
        cost_estimate=pl.CostEstimate(
            flops=4 * HEADS * rows * HD * 2048,
            transcendentals=HEADS * rows * 2048,
            bytes_accessed=kv_all.size * 2 + query_raw.size * 8,
        ),
        name="attention_forward",
    )(offsets, bounds, query_raw, cosine, sine, stream, first, kv_all)


def backward_kernel(
    offset_ref, bound_ref, query_ref, cos_ref, sin_ref, stream_ref, first_ref, kv_ref,
    mixed_ref, grad_ref, lse_ref,
    d_query_ref, d_kv_ref,
    delta_ref, head_grad_ref, sum_ref, bias_ref, turned_ref, d_tile_ref,
):
    rows = mixed_ref.shape[0]
    for h in range(HEADS):
        part = grad_ref[:, h * HD : (h + 1) * HD]
        head_grad_ref[h] = part
        product = part.astype(F32) * mixed_ref[:, h * HD : (h + 1) * HD].astype(F32)
        delta_ref[h] = lax.dot_general(
            jnp.ones((8, HD), F32),
            product,
            (((1,), (1,)), ((), ())),
            precision=lax.Precision.HIGHEST,
            preferred_element_type=F32,
        )[:1]
    sum_ref[...] = jnp.zeros(sum_ref.shape, F32)
    d_kv_ref[...] = jnp.zeros(d_kv_ref.shape, BF16)

    def visit(tile, carry):
        start = pl.multiple_of(offset_ref[tile], TILE)
        bias_ref[...] = allowed_bias(tile, stream_ref[...], first_ref[...], bias_ref.shape)
        d_tile_ref[...] = jnp.zeros(d_tile_ref.shape, F32)
        for g in range(KV):
            turned_ref[g] = kv_ref[pl.ds(start, TILE), g * HD : (g + 1) * HD].T
        for g in range(KV):
            keys = kv_ref[pl.ds(start, TILE), g * HD : (g + 1) * HD]
            values = kv_ref[pl.ds(start, TILE), (KV + g) * HD : (KV + g + 1) * HD]

            def some(i, carry):
                heads = [g * GROUP + i * BATCH + b for b in range(BATCH)]
                query = [query_ref[h] for h in heads]
                head_grad = [head_grad_ref[h] for h in heads]
                summed = [sum_ref[h] for h in heads]
                bias = bias_ref[...]
                turned = turned_ref[g]
                d_keys, d_values = d_tile_ref[g], d_tile_ref[KV + g]
                for b, h in enumerate(heads):
                    scores = contract(keys, query[b], 1, 1) * (SCALE * LOG2E) + bias
                    weights = jnp.exp2(scores - lse_ref[h])
                    d_weights = contract(values, head_grad[b], 1, 1)
                    d_scores = (weights * (d_weights - delta_ref[h])).astype(BF16)
                    d_keys += contract(d_scores, query[b], 1, 0)
                    d_values += contract(weights.astype(BF16), head_grad[b], 1, 0)
                    summed[b] += contract(turned, d_scores, 1, 0)
                for b, h in enumerate(heads):
                    sum_ref[h] = summed[b]
                d_tile_ref[g] = d_keys
                d_tile_ref[KV + g] = d_values
                return carry

            lax.fori_loop(0, GROUP // BATCH, some, 0)
        for g in range(KV):
            d_kv_ref[pl.ds(start, TILE), g * HD : (g + 1) * HD] = (
                d_tile_ref[g] * SCALE
            ).astype(BF16)
            d_kv_ref[pl.ds(start, TILE), (KV + g) * HD : (KV + g + 1) * HD] = d_tile_ref[
                KV + g
            ].astype(BF16)
        return carry

    lax.fori_loop(bound_ref[0], bound_ref[1] + 1, visit, 0)
    cosine, sine = cos_ref[...], -sin_ref[...]
    for h in range(HEADS):
        d_query_ref[:, h * HD : (h + 1) * HD] = turn(
            sum_ref[h].T * SCALE, cosine, sine
        ).astype(BF16)


def attention_backward(
    offsets, bounds, queries, cosine, sine, stream, first, kv_all, mixed, d_mixed, lse
):
    rows = mixed.shape[0]
    return pl.pallas_call(
        backward_kernel,
        out_shape=(
            jax.ShapeDtypeStruct((rows, HEADS * HD), BF16),
            jax.ShapeDtypeStruct(kv_all.shape, BF16),
        ),
        in_specs=[smem(), smem()] + [vmem()] * 9,
        out_specs=[vmem()] * 2,
        scratch_shapes=[
            pltpu.VMEM((HEADS, 1, rows), F32),
            pltpu.VMEM((HEADS, rows, HD), BF16),
            pltpu.VMEM((HEADS, HD, rows), F32),
            pltpu.VMEM((TILE, rows), F32),
            pltpu.VMEM((KV, HD, TILE), BF16),
            pltpu.VMEM((2 * KV, TILE, HD), F32),
        ],
        compiler_params=pltpu.CompilerParams(vmem_limit_bytes=56 << 20),
        cost_estimate=pl.CostEstimate(
            flops=10 * HEADS * rows * HD * 2048,
            transcendentals=HEADS * rows * 2048,
            bytes_accessed=kv_all.size * 4 + mixed.size * 8,
        ),
        name="attention_backward",
    )(offsets, bounds, queries, cosine, sine, stream, first, kv_all, mixed, d_mixed, lse)


def ffn_kernel(normed_ref, grad_ref, gate_ref, up_ref, down_ref, act_ref, d_gate_ref, d_up_ref):
    step = 256

    def chunk(i, carry):
        at = pl.ds(pl.multiple_of(i * step, step), step)
        normed = normed_ref[at, :]
        gate = contract(normed, gate_ref[...], 1, 0)
        up = contract(normed, up_ref[...], 1, 0)
        d_act = contract(grad_ref[at, :], down_ref[...], 1, 1)
        sigmoid = jax.nn.sigmoid(gate)
        silu = gate * sigmoid
        act_ref[at, :] = (silu * up).astype(BF16)
        d_up_ref[at, :] = (d_act * silu).astype(BF16)
        d_gate_ref[at, :] = (d_act * up * (sigmoid + silu * (1.0 - sigmoid))).astype(BF16)
        return carry

    lax.fori_loop(0, normed_ref.shape[0] // step, chunk, 0)


def ffn_middle(normed, grad, gate, up, down):
    rows, depth = normed.shape
    units = gate.shape[1]
    width = 256
    whole = pl.BlockSpec((rows, depth), lambda i: (0, 0), pipeline_mode=pl.Buffered(1))
    columns = pl.BlockSpec((depth, width), lambda i: (0, i))
    out = pl.BlockSpec((rows, width), lambda i: (0, i))
    return pl.pallas_call(
        ffn_kernel,
        out_shape=(jax.ShapeDtypeStruct((rows, units), BF16),) * 3,
        grid=(pl.cdiv(units, width),),
        in_specs=[whole, whole, columns, columns, pl.BlockSpec((width, depth), lambda i: (i, 0))],
        out_specs=[out] * 3,
        compiler_params=pltpu.CompilerParams(vmem_limit_bytes=48 << 20),
        cost_estimate=pl.CostEstimate(
            flops=6 * rows * depth * units,
            transcendentals=rows * units,
            bytes_accessed=2 * (3 * depth * units + 3 * rows * units + 2 * rows * depth),
        ),
        name="ffn_middle",
    )(normed, grad, gate, up, down)


def back_kernel(d_gate_ref, d_up_ref, gate_ref, up_ref, out_ref):
    out_ref[...] = (
        contract(d_gate_ref[...], gate_ref[...], 1, 1) + contract(d_up_ref[...], up_ref[...], 1, 1)
    ).astype(BF16)


def ffn_back(d_gate, d_up, gate, up):
    rows, units = d_gate.shape
    depth = gate.shape[0]
    width = 256
    whole = pl.BlockSpec((rows, units), lambda i: (0, 0), pipeline_mode=pl.Buffered(1))
    part = pl.BlockSpec((width, units), lambda i: (i, 0))
    return pl.pallas_call(
        back_kernel,
        out_shape=jax.ShapeDtypeStruct((rows, depth), BF16),
        grid=(depth // width,),
        in_specs=[whole, whole, part, part],
        out_specs=pl.BlockSpec((rows, width), lambda i: (0, i)),
        compiler_params=pltpu.CompilerParams(vmem_limit_bytes=48 << 20),
        cost_estimate=pl.CostEstimate(
            flops=4 * rows * depth * units,
            transcendentals=0,
            bytes_accessed=2 * (2 * depth * units + 2 * rows * units + rows * depth),
        ),
        name="ffn_back",
    )(d_gate, d_up, gate, up)


def rope_tables(position):
    half_width = HD // 2
    inverse = ROPE_BASE ** (-(jnp.arange(half_width, dtype=F32) * 2.0 / HD))
    angles = position.astype(F32)[:, None] * inverse[None, :]
    cosine, sine = jnp.cos(angles), jnp.sin(angles)
    return (
        jnp.concatenate([cosine, cosine], axis=1),
        jnp.concatenate([-sine, sine], axis=1),
    )


def rotate(values, cosine, sine):
    half_width = values.shape[-1] // 2
    swapped = jnp.concatenate([values[..., half_width:], values[..., :half_width]], axis=-1)
    return values * cosine + swapped * sine


def norm_forward(values, gain_vector):
    rms_scale = lax.rsqrt(jnp.mean(values * values, axis=1, keepdims=True) + EPSILON)
    return (values * rms_scale * gain_vector, rms_scale)


def norm_backward(values, rms_scale, gain_vector, gradient):
    weighted = gradient * gain_vector
    gain_grad = jnp.sum(gradient * values * rms_scale, axis=0)
    inner_mean = jnp.mean(weighted * values, axis=1, keepdims=True)
    return (rms_scale * weighted - values * rms_scale**3 * inner_mean, gain_grad)


def local(
    inputs,
    out_grad,
    q_weight,
    q_bias,
    kv_weight,
    kv_bias,
    out_weight,
    attn_gain,
    ffn_gain,
    gate_weight,
    up_weight,
    down_weight,
    block_order,
    long_docs,
    short_docs,
):
    seq, head = SeqAxis(), HeadAxis()
    owners = head.owners()
    local_rows, depth = inputs.shape
    span_rows = local_rows * head.size
    block_count = block_order.shape[0]
    wide = KV * HD * 2
    seq_order = jnp.stack([jnp.asarray(seq.owner(p), jnp.int32) for p in range(seq.size)])
    seq_place = jnp.argsort(seq_order).astype(jnp.int32)

    kv_rows_each = kv_weight.shape[0]
    sizes = [q_bias.shape[0], kv_bias.shape[0], attn_gain.shape[0], ffn_gain.shape[0]]
    padded = -(-(kv_rows_each + 1) // 16) * 16
    strip = jnp.concatenate([q_bias, kv_bias, attn_gain, ffn_gain])
    strip = jnp.pad(strip, (0, wide - strip.shape[0]))[None, :]
    pack = jnp.concatenate(
        [kv_weight, strip, jnp.zeros((padded - kv_rows_each - 1, wide), BF16)], axis=0
    )
    pack_span = place(head.gather(pack), owners, 0)
    pack_all = jnp.stack(seq.gather(pack_span)).reshape(seq.size, head.size, padded, wide)
    kv_full = pack_all[:, :, :kv_rows_each].reshape(depth, wide)
    strips = pack_all[:, :, kv_rows_each].astype(F32)

    def part_of(i):
        start = sum(sizes[:i])
        return strips[:, :, start : start + sizes[i]].reshape(seq.size, -1)

    q_bias_full = part_of(0)[seq_place].reshape(1, -1)
    kv_bias_full = part_of(1)[seq_place].reshape(1, -1)
    attn_gain32 = part_of(2).reshape(1, -1)
    ffn_gain32 = part_of(3).reshape(1, -1)

    q_full = jnp.concatenate(seq.gather(place(head.gather(q_weight), owners, 1)), axis=0)

    starts = jnp.concatenate(
        [
            jnp.cumsum(long_docs) - long_docs,
            jnp.sum(long_docs) + jnp.cumsum(short_docs) - short_docs,
        ]
    )
    row_start = (seq.me * head.size + head.me) * local_rows
    stream = (
        block_order[row_start // BLK] * BLK
        + row_start % BLK
        + jnp.arange(local_rows, dtype=jnp.int32)
    )
    long_total = jnp.sum(long_docs)
    position = jnp.where(stream >= long_total, stream - long_total, stream)
    first = jnp.max(jnp.where(starts[None, :] <= stream[:, None], starts[None, :], 0), axis=1)
    cosine, sine = rope_tables(position)
    storage = jnp.argsort(block_order).astype(jnp.int32)
    span_blocks = span_rows // BLK
    base = seq_place[storage // span_blocks] * span_rows + storage % span_blocks * BLK
    per_block = BLK // TILE
    offsets = (base[:, None] + jnp.arange(per_block, dtype=jnp.int32)[None, :] * TILE).reshape(-1)
    bounds = jnp.stack([first[0] // TILE, stream[-1] // TILE]).astype(jnp.int32)
    stream_row, first_row = stream[None, :], first[None, :]

    residual = shuffle(inputs, seq_order).astype(F32)
    cotangent16 = shuffle(out_grad, seq_order)
    normed32, attn_scale = norm_forward(residual, attn_gain32)
    normed = normed32.astype(BF16)
    kv_raw = jnp.dot(normed, kv_full, preferred_element_type=F32) + kv_bias_full
    key_part = rotate(
        kv_raw[:, : KV * HD].reshape(local_rows, KV, HD), cosine[:, None, :], sine[:, None, :]
    )
    kv_rows = jnp.concatenate(
        [key_part.reshape(local_rows, KV * HD), kv_raw[:, KV * HD :]], axis=1
    ).astype(BF16)
    kv_all = jnp.concatenate(seq.gather(place(head.gather(kv_rows), owners, 0)), axis=0)
    query_raw = jnp.dot(normed, q_full, preferred_element_type=F32) + q_bias_full
    queries, mixed, lse = attention_forward(
        offsets, bounds, query_raw, cosine, sine, stream_row, first_row, kv_all
    )
    out_full = jnp.concatenate(seq.gather(place(head.gather(out_weight), owners, 0)), axis=1)
    hidden = residual + jnp.dot(mixed, out_full, preferred_element_type=F32)
    normed2_32, ffn_scale = norm_forward(hidden, ffn_gain32)
    normed2 = normed2_32.astype(BF16)

    gate_full = jnp.concatenate(seq.gather(gate_weight), axis=0)
    up_full = jnp.concatenate(seq.gather(up_weight), axis=0)
    down_full = jnp.concatenate(seq.gather(down_weight), axis=1)
    grad_all = jnp.concatenate(head.gather(cotangent16), axis=0)
    normed2_all = jnp.concatenate(head.gather(normed2), axis=0)
    act, d_gate, d_up = ffn_middle(normed2_all, grad_all, gate_full, up_full, down_full)

    def slots(whole):
        return [whole[i * local_rows : (i + 1) * local_rows] for i in range(head.size)]

    d_normed2 = head.reduce(slots(ffn_back(d_gate, d_up, gate_full, up_full)))
    ffn_terms = jnp.dot(act, down_full, preferred_element_type=F32).astype(BF16)
    output = hidden + head.reduce(slots(ffn_terms))
    output = shuffle(output, seq_place)
    half = depth // 2
    gate_grad = seq.reduce(
        contract(normed2_all[:, :half], d_gate, 0, 0),
        contract(normed2_all[:, half:], d_gate, 0, 0),
        0,
    )
    up_grad = seq.reduce(
        contract(normed2_all[:, :half], d_up, 0, 0),
        contract(normed2_all[:, half:], d_up, 0, 0),
        0,
    )
    down_grad = seq.reduce(
        contract(act, grad_all[:, :half], 0, 0), contract(act, grad_all[:, half:], 0, 0), 1
    )

    cotangent = cotangent16.astype(F32)
    d_hidden_norm, ffn_gain_grad = norm_backward(hidden, ffn_scale, ffn_gain32, d_normed2)
    d_hidden = cotangent + d_hidden_norm
    d_attn = d_hidden.astype(BF16)
    d_mixed = contract(d_attn, out_full, 1, 1).astype(BF16)
    d_queries, d_kv_all = attention_backward(
        offsets, bounds, queries, cosine, sine, stream_row, first_row, kv_all, mixed, d_mixed, lse
    )
    middle = d_kv_all.shape[0] // 2
    d_kv_span = seq.reduce(d_kv_all[:middle].astype(F32), d_kv_all[middle:], 0).astype(BF16)
    d_kv_own = head.reduce(take(d_kv_span, owners, 0))
    key_back = rotate(
        d_kv_own[:, : KV * HD].reshape(local_rows, KV, HD), cosine[:, None, :], -sine[:, None, :]
    )
    d_kv = jnp.concatenate(
        [key_back.reshape(local_rows, KV * HD), d_kv_own[:, KV * HD :]], axis=1
    ).astype(BF16)
    d_normed = contract(d_queries, q_full, 1, 1) + contract(d_kv, kv_full, 1, 1)
    d_input_norm, attn_gain_grad = norm_backward(residual, attn_scale, attn_gain32, d_normed)
    input_grad = shuffle(d_hidden + d_input_norm, seq_place)

    def head_sum(value, axis):
        return head.reduce(take(value.astype(BF16), owners, axis))

    out_weight_grad = head_sum(
        seq.reduce(
            contract(mixed, d_attn[:, :half], 0, 0), contract(mixed, d_attn[:, half:], 0, 0), 1
        ),
        0,
    )
    q_weight_grad = head_sum(
        seq.reduce(
            contract(normed[:, :half], d_queries, 0, 0),
            contract(normed[:, half:], d_queries, 0, 0),
            0,
        ),
        1,
    )
    kv_part = contract(normed, d_kv, 0, 0).reshape(seq.size, head.size, kv_rows_each, wide)
    q_bias_part = jnp.sum(d_queries.astype(F32), axis=0).reshape(seq.size, -1)[seq_order]
    kv_bias_part = jnp.sum(d_kv.astype(F32), axis=0).reshape(seq.size, -1)[seq_order]
    strips = jnp.concatenate(
        [
            item.reshape(seq.size, head.size, 1, -1)
            for item in (q_bias_part, kv_bias_part, attn_gain_grad, ffn_gain_grad)
        ],
        axis=3,
    )
    strips = jnp.pad(
        strips,
        ((0, 0), (0, 0), (0, padded - kv_rows_each - 1), (0, wide - strips.shape[3])),
    )
    small = jnp.concatenate([kv_part, strips], axis=2).reshape(-1, wide)
    middle = small.shape[0] // 2
    small = head_sum(seq.reduce(small[:middle], small[middle:], 0), 0)
    kv_weight_grad = small[:kv_rows_each]
    tail = small[kv_rows_each]
    cuts = [sum(sizes[:i]) for i in range(5)]
    q_bias_grad, kv_bias_grad, attn_grad, ffn_grad = (
        tail[cuts[i] : cuts[i + 1]] for i in range(4)
    )
    return (
        output,
        input_grad,
        q_weight_grad,
        q_bias_grad,
        kv_weight_grad,
        kv_bias_grad,
        out_weight_grad,
        attn_grad,
        ffn_grad,
        gate_grad,
        up_grad,
        down_grad,
    )


def solution(mesh):
    in_specs = (
        P(("seq", "head"), None),
        P(("seq", "head"), None),
        P("seq", "head"),
        P(("seq", "head")),
        P(("seq", "head"), None),
        P(("seq", "head")),
        P("head", "seq"),
        P(("seq", "head")),
        P(("seq", "head")),
        P("seq", "head"),
        P("seq", "head"),
        P("head", "seq"),
        P(),
        P(),
        P(),
    )
    out_specs = (
        P(("seq", "head"), None),
        P(("seq", "head"), None),
        P("seq", "head"),
        P(("seq", "head")),
        P(("seq", "head"), None),
        P(("seq", "head")),
        P("head", "seq"),
        P(("seq", "head")),
        P(("seq", "head")),
        P("seq", "head"),
        P("seq", "head"),
        P("head", "seq"),
    )
    return jax.shard_map(local, mesh=mesh, in_specs=in_specs, out_specs=out_specs, check_vma=False)
```

time: 2420 us -> 1270 us (0.52)
  waiting for transfers between devices: 1650 us -> 437 us
  matrix products: 358 us -> 126 us
  starting transfers between devices: 1.89 us -> 225 us
  Pallas kernels: 0 us -> 155 us
  blocking collectives: 87.7 us -> 0 us
  local copies, waits for them, and re-layouts: 120 us -> 197 us
  other arithmetic: 139 us -> 93.2 us
  loops' own time: 33.5 us -> 0 us
    reduce_scatter x11 -> x0, waiting for transfers between devices: 1050 us -> none  [the longest x1 292 us: local(): lax.psum_scatter(placed, ('seq', 'head'), scatter_dimension=0, tiled=True)]
    all_gather x11 -> x0, waiting for transfers between devices: 596 us -> none  [the longest x1 83 us: gather_ffn(): return lax.all_gather(normed2, 'head', axis=0, tiled=True)]
    ppermute x0 -> x151, waiting for transfers between devices: none -> 437 us  [the longest x91 257 us: swap(): return lax.ppermute(value, 'seq', [(i, i ^ bit) for i in range(self.size)])]
    ppermute x0 -> x151, starting transfers between devices: none -> 225 us  [the longest x60 135 us: send(): return lax.ppermute(value, 'head', pairs)]
    dot_general x55 -> x4, matrix products: 215 us -> 31.2 us  [the longest x1 16.6 us: local(): ffn_terms = jnp.dot(act, down_full, preferred_element_type=F32).astype(BF16)]
    pallas_call x0 -> x8, Pallas kernels: none -> 155 us  [the longest x1 50.2 us: ffn_middle(): pl.pallas_call(ffn_kernel, out_shape=(jax.ShapeDtypeStruct((rows, units),...]
    unnamed x2 -> x0, blocking collectives: 87.7 us -> none
    unnamed x107 -> x212, local copies, waits for them, and re-layouts: 10.5 us -> 93.2 us
  transfers between devices with their start and end apart: 22 -> 151, of which waited for: 21 -> 52; matrix products, arithmetic and copies ran while one was open for 13% -> 31% of each run, Pallas kernels for 0% -> 6%
where the time goes in v1:
time: 1270 us; the launch traced here: 1250 us
  waiting for transfers between devices  437 us (34%)
  starting transfers between devices  225 us (18%)
  local copies, waits for them, and re-layouts  197 us (16%)
  Pallas kernels  155 us (12%)
  matrix products  126 us (10%)
  other arithmetic  93.2 us (7%)
  between operations  16.6 us (1%)
    ppermute x91, waiting for transfers between devices, swap(): return lax.ppermute(value, 'seq', [(i, i ^ bit) for i in range(self.size)])  257 us
    ppermute x60, waiting for transfers between devices, send(): return lax.ppermute(value, 'head', pairs)  180 us
    ppermute x60, starting transfers between devices, send(): return lax.ppermute(value, 'head', pairs)  135 us
    dot_general x14, matrix products, contract(): lax.dot_general(left_side, right_side, (((left_dim,), (right_dim,)), ((),...  95.1 us
    unnamed x212, local copies, waits for them, and re-layouts  93.2 us
    ppermute x91, starting transfers between devices, swap(): return lax.ppermute(value, 'seq', [(i, i ^ bit) for i in range(self.size)])  90.5 us
    pallas_call x1, Pallas kernels, ffn_middle(): pl.pallas_call(ffn_kernel, out_shape=(jax.ShapeDtypeStruct((rows, units),...  50.2 us
    ppermute x16, local copies, waits for them, and re-layouts, swap(): return lax.ppermute(value, 'seq', [(i, i ^ bit) for i in range(self.size)])  38.5 us
  transfers between devices with their start and end apart: 151, of which 52 were waited for; matrix products, arithmetic and copies ran while one was open for 31% of the time, Pallas kernels for 6%

profile of v1, /device:TPU:0, one launch (start us, length us, event | category | flops | bytes accessed | tf_op | source)
XLA Modules:
  0.0 1251.0 jit_solution(3014475840934252887)
XLA Ops:
  2.0 5.2 collective-permute-start.13
  40.5 6.1 shuffle.4
  48.7 5.9 shuffle.5
  70.4 8.9 collective-permute-start.39
  81.1 5.0 collective-permute-done.4
  103.6 19.6 %collective-permute-done.6 = bf16[320,512]{1,0:T(8,128)(2,1)S(1)} collective-permute-done((bf16[320,512]{1,0:T(8,128)(2,1)S(1)}, bf16[320,512]{1,0:T(8,128)(2,1)S(1)}, u32[]{:S(2)}, u32[]{:S(2)}) %collective-permute-start.6) | collective-permute-done | bytes 327712 | tf_op jit(solution)/shard_map/ppermute | solution.py:50
  131.5 5.5 collective-permute-done.43
  161.7 42.5 %collective-permute-done.70 = bf16[256,2752]{0,1:T(8,128)(2,1)} collective-permute-done((bf16[256,2752]{0,1:T(8,128)(2,1)}, bf16[256,2752]{0,1:T(8,128)(2,1)}, u32[]{:S(2)}, u32[]{:S(2)}) %collective-permute-start.70) | collective-permute-done | bytes 1409056 | tf_op jit(solution)/shard_map/ppermute | solution.py:50
  225.5 18.6 %collective-permute-done.78 = bf16[2752,256]{1,0:T(8,128)(2,1)} collective-permute-done((bf16[2752,256]{1,0:T(8,128)(2,1)}, bf16[2752,256]{1,0:T(8,128)(2,1)}, u32[]{:S(2)}, u32[]{:S(2)}) %collective-permute-start.78) | collective-permute-done | bytes 1409056 | tf_op jit(solution)/shard_map/ppermute | solution.py:50
  282.7 5.5 collective-permute-done.18
  303.5 8.6 collective-permute-done.30
  318.8 12.2 collective-permute-done.73
  367.6 5.4 collective-permute-done.46
  377.3 6.6 collective-permute-done.20
  405.8 11.1 collective-permute-done.57
  435.1 7.4 collective-permute-done.32
  450.2 6.0 collective-permute-done.33
  458.4 5.7 convolution_add_fusion.1.raw_ref
  473.0 17.5 %attention_forward.1 = (bf16[16,256,128]{2,1,0:T(8,128)(2,1)S(1)}, bf16[256,2048]{1,0:T(8,128)(2,1)S(1)}, f32[16,1,256]{2,1,0:T(1,128)S(1)}) custom-call(s32[16]{0:T(128)S(1)} %fusion.36.offset_ref, s32[2]{0:T(128)S(1)} %pad_add_fusion.1.bound_ref, f32[256,2048]{1,0:T(8,128)S(1)} %convolution_add_fusion.1.raw_ref, ...), custom_call_target="tpu_custom_call" | custom-call | flops 4294967296 | bytes 12582912 | tf_op jit(solution)/shard_map/attention_forward/pallas_call | solution.py:241
  490.6 6.6 multiply_reduce_fusion.2
  507.2 11.6 collective-permute-done.52
  538.5 18.1 %collective-permute-done.54 = bf16[256,2048]{1,0:T(8,128)(2,1)S(1)} collective-permute-done((bf16[256,2048]{1,0:T(8,128)(2,1)}, bf16[256,2048]{1,0:T(8,128)(2,1)S(1)}, u32[]{:S(2)}, u32[]{:S(2)}) %collective-permute-start.54) | collective-permute-done | bytes 1048608 | tf_op jit(solution)/shard_map/ppermute | solution.py:95
  556.7 22.4 %collective-permute-done.56 = bf16[256,2048]{1,0:T(8,128)(2,1)S(1)} collective-permute-done((bf16[256,2048]{1,0:T(8,128)(2,1)}, bf16[256,2048]{1,0:T(8,128)(2,1)S(1)}, u32[]{:S(2)}, u32[]{:S(2)}) %collective-permute-start.56) | collective-permute-done | bytes 1048608 | tf_op jit(solution)/shard_map/ppermute | solution.py:95
  581.0 50.2 %ffn_middle.1 = (bf16[1024,2752]{1,0:T(8,128)(2,1)}, bf16[1024,2752]{1,0:T(8,128)(2,1)}, bf16[1024,2752]{1,0:T(8,128)(2,1)}) custom-call(bf16[1024,2048]{1,0:T(8,128)(2,1)S(1)} %pad_maximum_fusion.normed_ref, bf16[1024,2048]{1,0:T(8,128)(2,1)} %pad_maximum_fusion.1.grad_ref, bf16[2048,2752]{1,0:T(8,128)(2,1)} %constant_dynamic-update-slice_fusion.36.gate_ref, ...), custom_call_target="tpu_custom_call" | custom-call | flops 34628173824 | bytes 59113472 | tf_op jit(solution)/shard_map/ffn_middle/pallas_call | solution.py:394
  631.2 16.6 %convolution_convert_fusion.3 = bf16[1024,2048]{1,0:T(8,128)(2,1)S(1)} fusion(bf16[1024,2752]{1,0:T(8,128)(2,1)} %get-tuple-element.25, bf16[2752,2048]{1,0:T(8,128)(2,1)} %constant_dynamic-update-slice_fusion.54.down_ref), kind=kOutput, calls=%fused_computation.24 | convolution fusion | flops 11544821760 | bytes 21102592 | tf_op jit(solution)/shard_map/dot_general | solution.py:573
  648.9 31.6 %ffn_back.1 = bf16[1024,2048]{1,0:T(8,128)(2,1)S(1)} custom-call(bf16[1024,2752]{1,0:T(8,128)(2,1)} %get-tuple-element.26.d_gate_ref, bf16[1024,2752]{1,0:T(8,128)(2,1)} %get-tuple-element.27.d_up_ref, bf16[2048,2752]{1,0:T(8,128)(2,1)} %constant_dynamic-update-slice_fusion.36.gate_ref, bf16[2048,2752]{1,0:T(8,128)(2,1)} %constant_dynamic-update-slice_fusion.45.up_ref), custom_call_target="tpu_custom_call" | custom-call | flops 23085449216 | bytes 38010880 | tf_op jit(solution)/shard_map/ffn_back/pallas_call | solution.py:422
  684.8 10.9 convolution_convert_fusion
  695.7 11.3 collective-permute-done.91
  707.9 7.1 collective-permute-start.94
  715.0 14.6 %collective-permute-done.86 = bf16[256,2048]{1,0:T(8,128)(2,1)S(1)} collective-permute-done((bf16[256,2048]{1,0:T(8,128)(2,1)}, bf16[256,2048]{1,0:T(8,128)(2,1)S(1)}, u32[]{:S(2)}, u32[]{:S(2)}) %collective-permute-start.86) | collective-permute-done | bytes 1048608 | tf_op jit(solution)/shard_map/ppermute | solution.py:95
  730.5 6.0 collective-permute-start.89
  736.5 10.6 convolution_convert_fusion.1
  747.1 4.9 collective-permute-done.94
  757.7 16.7 %collective-permute-done.89 = bf16[256,2048]{1,0:T(8,128)(2,1)S(1)} collective-permute-done((bf16[256,2048]{1,0:T(8,128)(2,1)S(1)}, bf16[256,2048]{1,0:T(8,128)(2,1)S(1)}, u32[]{:S(2)}, u32[]{:S(2)}) %collective-permute-start.89) | collective-permute-done | bytes 1048608 | tf_op jit(solution)/shard_map/ppermute | solution.py:95
  780.5 10.6 convolution_convert_fusion.2
  791.0 5.9 collective-permute-done.93
  799.2 18.4 %collective-permute-done.88 = bf16[256,2048]{1,0:T(8,128)(2,1)} collective-permute-done((bf16[256,2048]{1,0:T(8,128)(2,1)}, bf16[256,2048]{1,0:T(8,128)(2,1)}, u32[]{:S(2)}, u32[]{:S(2)}) %collective-permute-start.88) | collective-permute-done | bytes 1048608 | tf_op jit(solution)/shard_map/ppermute | solution.py:95
  817.6 7.1 fusion.41
  827.9 6.7 convolution_convert_fusion.6.grad_ref
  834.7 31.3 %attention_backward.1 = (bf16[256,2048]{1,0:T(8,128)(2,1)}, bf16[8192,512]{1,0:T(8,128)(2,1)}) custom-call(s32[16]{0:T(128)} %copy-done.9, s32[2]{0:T(128)} %copy-done.10, bf16[16,256,128]{2,1,0:T(8,128)(2,1)} %copy-done.11, f32[256,128]{1,0:T(8,128)} %copy-done.5, f32[256,128]{1,0:T(8,128)} %copy-done.6, s32[1,256]{1,0:T(1,128)} %copy-done.8, ...), custom_call_target="tpu_custom_call" | custom-call | flops 10737418240 | bytes 20971520 | tf_op jit(solution)/shard_map/attention_backward/pallas_call | solution.py:342
  868.7 6.3 shuffle.6
  875.0 4.6 slice.484
  882.2 11.7 add_convert_fusion.1
  896.9 18.3 %collective-permute-start.144 = (bf16[128,2752]{0,1:T(8,128)(2,1)}, bf16[128,2752]{0,1:T(8,128)(2,1)}, u32[]{:S(2)}, u32[]{:S(2)}) collective-permute-start(bf16[128,2752]{0,1:T(8,128)(2,1)} %get-tuple-element.48), channel_id=1, source_target_pairs={{0,8},{4,12},{8,0},{12,4},{16,24},{20,28},{24,16},{28,20},{1,9},{5... | collective-permute-start | bytes 2113544 | tf_op jit(solution)/shard_map/ppermute | solution.py:50
  915.2 10.1 add_convert_fusion
  932.6 12.2 add_convert_fusion.2
  955.5 9.2 collective-permute-done.139
  972.4 9.3 collective-permute-done.149
  995.5 4.7 add_convert_fusion.5
  1004.3 11.5 collective-permute-done.145
  1024.1 13.5 %collective-permute-done.99 = bf16[512,512]{1,0:T(8,128)(2,1)S(1)} collective-permute-done((bf16[512,512]{1,0:T(8,128)(2,1)S(1)}, bf16[512,512]{1,0:T(8,128)(2,1)S(1)}, u32[]{:S(2)}, u32[]{:S(2)}) %collective-permute-start.99) | collective-permute-done | bytes 524320 | tf_op jit(solution)/shard_map/ppermute | solution.py:50
  1039.2 27.2 %collective-permute-done.97 = bf16[512,512]{1,0:T(8,128)(2,1)S(1)} collective-permute-done((bf16[512,512]{1,0:T(8,128)(2,1)S(1)}, bf16[512,512]{1,0:T(8,128)(2,1)S(1)}, u32[]{:S(2)}, u32[]{:S(2)}) %collective-permute-start.97) | collective-permute-done | bytes 524320 | tf_op jit(solution)/shard_map/ppermute | solution.py:50
  1071.5 9.7 collective-permute-done.107
  1082.7 21.0 %collective-permute-done.100 = bf16[1024,512]{1,0:T(8,128)(2,1)S(1)} collective-permute-done((bf16[1024,512]{1,0:T(8,128)(2,1)S(1)}, bf16[1024,512]{1,0:T(8,128)(2,1)S(1)}, u32[]{:S(2)}, u32[]{:S(2)}) %collective-permute-start.100) | collective-permute-done | bytes 1048608 | tf_op jit(solution)/shard_map/ppermute | solution.py:50
  1113.8 12.3 collective-permute-done.130
  1128.7 11.4 collective-permute-start.131
  1140.2 5.8 collective-permute-done.110
  1151.0 5.4 collective-permute-done.104
  1161.3 8.8 collective-permute-start.111
  1175.9 8.1 fusion.11
  1193.2 5.1 collective-permute-start.134
  1217.9 8.3 collective-permute-start.121
  1231.0 7.9 collective-permute-start.124
  1242.6 6.3 shuffle.7
  (696 shorter events, 463.2 us)
Async XLA Ops:
  0.6 87.0 %collective-permute-start.14 = (bf16[256,512]{1,0:T(8,128)(2,1)}, bf16[256,512]{1,0:T(8,128)(2,1)}, u32[]{:S(2)}, u32[]{:S(2)}) collective-permute-start(bf16[256,512]{1,0:T(8,128)(2,1)} %param.18), channel_id=1, source_target_pairs={{1,2},{2,1},{5,6},{6,5},{9,10},{10,9},{13,14},{14,13},{17,18},{18,... | collective-permute-start | bytes 786440 | tf_op jit(solution)/shard_map/ppermute | solution.py:95
  2.0 87.0 %collective-permute-start.13 = (bf16[256,512]{1,0:T(8,128)(2,1)}, bf16[256,512]{1,0:T(8,128)(2,1)}, u32[]{:S(2)}, u32[]{:S(2)}) collective-permute-start(bf16[256,512]{1,0:T(8,128)(2,1)} %param.18), channel_id=1, source_target_pairs={{0,1},{1,0},{2,3},{3,2},{4,5},{5,4},{6,7},{7,6},{8,9},{9,8},{10,11... | collective-permute-start | bytes 786440 | tf_op jit(solution)/shard_map/ppermute | solution.py:95
  11.6 55.9 %collective-permute-start = (bf16[80,512]{1,0:T(8,128)(2,1)}, bf16[80,512]{1,0:T(8,128)(2,1)}, u32[]{:S(2)}, u32[]{:S(2)}) collective-permute-start(bf16[80,512]{1,0:T(8,128)(2,1)} %get-tuple-element.108), channel_id=1, source_target_pairs={{0,1},{1,0},{2,3},{3,2},{4,5},{5,4},{6,7},{7,6},{8,9},{9,8},{10,11... | collective-permute-start | bytes 245768 | tf_op jit(solution)/shard_map/ppermute | solution.py:95
  11.7 56.5 %collective-permute-start.1 = (bf16[80,512]{1,0:T(8,128)(2,1)}, bf16[80,512]{1,0:T(8,128)(2,1)}, u32[]{:S(2)}, u32[]{:S(2)}) collective-permute-start(bf16[80,512]{1,0:T(8,128)(2,1)} %get-tuple-element.108), channel_id=1, source_target_pairs={{1,2},{2,1},{5,6},{6,5},{9,10},{10,9},{13,14},{14,13},{17,18},{18,... | collective-permute-start | bytes 245768 | tf_op jit(solution)/shard_map/ppermute | solution.py:95
  12.9 77.9 %collective-permute-start.40 = (bf16[512,256]{1,0:T(8,128)(2,1)}, bf16[512,256]{1,0:T(8,128)(2,1)}, u32[]{:S(2)}, u32[]{:S(2)}) collective-permute-start(bf16[512,256]{1,0:T(8,128)(2,1)} %param.22), channel_id=1, source_target_pairs={{1,2},{2,1},{5,6},{6,5},{9,10},{10,9},{13,14},{14,13},{17,18},{18,... | collective-permute-start | bytes 786440 | tf_op jit(solution)/shard_map/ppermute | solution.py:95
  86.1 128.1 %collective-permute-start.63 = (bf16[256,2752]{0,1:T(8,128)(2,1)}, bf16[256,2752]{0,1:T(8,128)(2,1)}, u32[]{:S(2)}, u32[]{:S(2)}) collective-permute-start(bf16[256,2752]{0,1:T(8,128)(2,1)} %param.25), channel_id=1, source_target_pairs={{0,16},{4,20},{8,24},{12,28},{16,0},{20,4},{24,8},{28,12},{1,17},{... | collective-permute-start | bytes 4227080 | tf_op jit(solution)/shard_map/ppermute | solution.py:50
  89.0 41.9 %collective-permute-start.9 = (bf16[320,512]{1,0:T(8,128)(2,1)S(1)}, bf16[320,512]{1,0:T(8,128)(2,1)S(1)}, u32[]{:S(2)}, u32[]{:S(2)}) collective-permute-start(bf16[320,512]{1,0:T(8,128)(2,1)S(1)} %select_dynamic-update-slice_fusion.6), channel_id=1, source_target_pairs={{0,4},{4,0},{8,12},{12,8},{16,20},{20,16},{24,28},{28,24},{1,5},{5... | collective-permute-start | bytes 983048 | tf_op jit(solution)/shard_map/ppermute | solution.py:50
  90.8 32.4 %collective-permute-start.6 = (bf16[320,512]{1,0:T(8,128)(2,1)S(1)}, bf16[320,512]{1,0:T(8,128)(2,1)S(1)}, u32[]{:S(2)}, u32[]{:S(2)}) collective-permute-start(bf16[320,512]{1,0:T(8,128)(2,1)S(1)} %select_dynamic-update-slice_fusion.6), channel_id=1, source_target_pairs={{0,16},{4,20},{8,24},{12,28},{16,0},{20,4},{24,8},{28,12},{1,17},{... | collective-permute-start | bytes 983048 | tf_op jit(solution)/shard_map/ppermute | solution.py:50
  96.2 29.3 %collective-permute-start.5 = (bf16[320,512]{1,0:T(8,128)(2,1)S(1)}, bf16[320,512]{1,0:T(8,128)(2,1)S(1)}, u32[]{:S(2)}, u32[]{:S(2)}) collective-permute-start(bf16[320,512]{1,0:T(8,128)(2,1)S(1)} %select_dynamic-update-slice_fusion.6), channel_id=1, source_target_pairs={{0,8},{4,12},{8,0},{12,4},{16,24},{20,28},{24,16},{28,20},{1,9},{5... | collective-permute-start | bytes 983048 | tf_op jit(solution)/shard_map/ppermute | solution.py:50
  140.1 69.9 %collective-permute-start.62 = (bf16[256,2752]{0,1:T(8,128)(2,1)}, bf16[256,2752]{0,1:T(8,128)(2,1)}, u32[]{:S(2)}, u32[]{:S(2)}) collective-permute-start(bf16[256,2752]{0,1:T(8,128)(2,1)} %param.25), channel_id=1, source_target_pairs={{0,8},{4,12},{8,0},{12,4},{16,24},{20,28},{24,16},{28,20},{1,9},{5... | collective-permute-start | bytes 4227080 | tf_op jit(solution)/shard_map/ppermute | solution.py:50
  142.2 63.7 %collective-permute-start.71 = (bf16[256,2752]{0,1:T(8,128)(2,1)}, bf16[256,2752]{0,1:T(8,128)(2,1)}, u32[]{:S(2)}, u32[]{:S(2)}) collective-permute-start(bf16[256,2752]{0,1:T(8,128)(2,1)} %param.26), channel_id=1, source_target_pairs={{0,16},{4,20},{8,24},{12,28},{16,0},{20,4},{24,8},{28,12},{1,17},{... | collective-permute-start | bytes 4227080 | tf_op jit(solution)/shard_map/ppermute | solution.py:50
  143.8 60.4 %collective-permute-start.70 = (bf16[256,2752]{0,1:T(8,128)(2,1)}, bf16[256,2752]{0,1:T(8,128)(2,1)}, u32[]{:S(2)}, u32[]{:S(2)}) collective-permute-start(bf16[256,2752]{0,1:T(8,128)(2,1)} %param.26), channel_id=1, source_target_pairs={{0,8},{4,12},{8,0},{12,4},{16,24},{20,28},{24,16},{28,20},{1,9},{5... | collective-permute-start | bytes 4227080 | tf_op jit(solution)/shard_map/ppermute | solution.py:50
  161.7 61.7 %collective-permute-start.66 = (bf16[256,2752]{0,1:T(8,128)(2,1)}, bf16[256,2752]{0,1:T(8,128)(2,1)}, u32[]{:S(2)}, u32[]{:S(2)}) collective-permute-start(bf16[256,2752]{0,1:T(8,128)(2,1)} %param.25), channel_id=1, source_target_pairs={{0,4},{4,0},{8,12},{12,8},{16,20},{20,16},{24,28},{28,24},{1,5},{5... | collective-permute-start | bytes 4227080 | tf_op jit(solution)/shard_map/ppermute | solution.py:50
  205.9 42.3 %collective-permute-start.79 = (bf16[2752,256]{1,0:T(8,128)(2,1)}, bf16[2752,256]{1,0:T(8,128)(2,1)}, u32[]{:S(2)}, u32[]{:S(2)}) collective-permute-start(bf16[2752,256]{1,0:T(8,128)(2,1)} %param.27), channel_id=1, source_target_pairs={{0,16},{4,20},{8,24},{12,28},{16,0},{20,4},{24,8},{28,12},{1,17},{... | collective-permute-start | bytes 4227080 | tf_op jit(solution)/shard_map/ppermute | solution.py:50
  210.0 34.0 %collective-permute-start.78 = (bf16[2752,256]{1,0:T(8,128)(2,1)}, bf16[2752,256]{1,0:T(8,128)(2,1)}, u32[]{:S(2)}, u32[]{:S(2)}) collective-permute-start(bf16[2752,256]{1,0:T(8,128)(2,1)} %param.27), channel_id=1, source_target_pairs={{0,8},{4,12},{8,0},{12,4},{16,24},{20,28},{24,16},{28,20},{1,9},{5... | collective-permute-start | bytes 4227080 | tf_op jit(solution)/shard_map/ppermute | solution.py:50
  221.8 53.8 %collective-permute-start.44 = (bf16[2048,256]{1,0:T(8,128)(2,1)}, bf16[2048,256]{1,0:T(8,128)(2,1)}, u32[]{:S(2)}, u32[]{:S(2)}) collective-permute-start(bf16[2048,256]{1,0:T(8,128)(2,1)} %select_dynamic-update-slice_fusion), channel_id=1, source_target_pairs={{0,8},{4,12},{8,0},{12,4},{16,24},{20,28},{24,16},{28,20},{1,9},{5... | collective-permute-start | bytes 3145736 | tf_op jit(solution)/shard_map/ppermute | solution.py:50
  223.3 55.3 %collective-permute-start.58 = (bf16[256,2048]{1,0:T(8,128)(2,1)S(1)}, bf16[256,2048]{1,0:T(8,128)(2,1)}, u32[]{:S(2)}, u32[]{:S(2)}) collective-permute-start(bf16[256,2048]{1,0:T(8,128)(2,1)S(1)} %copy-done.21), channel_id=1, source_target_pairs={{1,2},{2,1},{5,6},{6,5},{9,10},{10,9},{13,14},{14,13},{17,18},{18,... | collective-permute-start | bytes 3145736 | tf_op jit(solution)/shard_map/ppermute | solution.py:95
  225.0 53.6 %collective-permute-start.45 = (bf16[2048,256]{1,0:T(8,128)(2,1)}, bf16[2048,256]{1,0:T(8,128)(2,1)}, u32[]{:S(2)}, u32[]{:S(2)}) collective-permute-start(bf16[2048,256]{1,0:T(8,128)(2,1)} %select_dynamic-update-slice_fusion), channel_id=1, source_target_pairs={{0,16},{4,20},{8,24},{12,28},{16,0},{20,4},{24,8},{28,12},{1,17},{... | collective-permute-start | bytes 3145736 | tf_op jit(solution)/shard_map/ppermute | solution.py:50
  248.2 49.3 %collective-permute-start.19 = (bf16[256,2048]{1,0:T(8,128)(2,1)}, bf16[256,2048]{1,0:T(8,128)(2,1)}, u32[]{:S(2)}, u32[]{:S(2)}) collective-permute-start(bf16[256,2048]{1,0:T(8,128)(2,1)} %select_dynamic-update-slice_fusion.4), channel_id=1, source_target_pairs={{0,16},{4,20},{8,24},{12,28},{16,0},{20,4},{24,8},{28,12},{1,17},{... | collective-permute-start | bytes 3145736 | tf_op jit(solution)/shard_map/ppermute | solution.py:50
  252.8 35.4 %collective-permute-start.18 = (bf16[256,2048]{1,0:T(8,128)(2,1)}, bf16[256,2048]{1,0:T(8,128)(2,1)}, u32[]{:S(2)}, u32[]{:S(2)}) collective-permute-start(bf16[256,2048]{1,0:T(8,128)(2,1)} %select_dynamic-update-slice_fusion.4), channel_id=1, source_target_pairs={{0,8},{4,12},{8,0},{12,4},{16,24},{20,28},{24,16},{28,20},{1,9},{5... | collective-permute-start | bytes 3145736 | tf_op jit(solution)/shard_map/ppermute | solution.py:50
  278.6 88.7 %collective-permute-start.82 = (bf16[2752,256]{1,0:T(8,128)(2,1)}, bf16[2752,256]{1,0:T(8,128)(2,1)}, u32[]{:S(2)}, u32[]{:S(2)}) collective-permute-start(bf16[2752,256]{1,0:T(8,128)(2,1)} %param.27), channel_id=1, source_target_pairs={{0,4},{4,0},{8,12},{12,8},{16,20},{20,16},{24,28},{28,24},{1,5},{5... | collective-permute-start | bytes 4227080 | tf_op jit(solution)/shard_map/ppermute | solution.py:50
  278.6 35.1 %collective-permute-start.59 = (bf16[256,2048]{1,0:T(8,128)(2,1)}, bf16[256,2048]{1,0:T(8,128)(2,1)S(1)}, u32[]{:S(2)}, u32[]{:S(2)}) collective-permute-start(bf16[256,2048]{1,0:T(8,128)(2,1)} %collective-permute-done.58), channel_id=1, source_target_pairs={{1,0},{2,3},{5,4},{6,7},{9,8},{10,11},{13,12},{14,15},{17,16},{18,... | collective-permute-start | bytes 3145736 | tf_op jit(solution)/shard_map/ppermute | solution.py:95
  282.2 105.9 %collective-permute-start.48 = (bf16[2048,256]{1,0:T(8,128)(2,1)}, bf16[2048,256]{1,0:T(8,128)(2,1)}, u32[]{:S(2)}, u32[]{:S(2)}) collective-permute-start(bf16[2048,256]{1,0:T(8,128)(2,1)} %select_dynamic-update-slice_fusion), channel_id=1, source_target_pairs={{0,4},{4,0},{8,12},{12,8},{16,20},{20,16},{24,28},{28,24},{1,5},{5... | collective-permute-start | bytes 3145736 | tf_op jit(solution)/shard_map/ppermute | solution.py:50
  315.1 31.0 %collective-permute-start.65 = (bf16[128,2752]{0,1:T(8,128)(2,1)}, bf16[128,2752]{0,1:T(8,128)(2,1)}, u32[]{:S(2)}, u32[]{:S(2)}) collective-permute-start(bf16[128,2752]{0,1:T(8,128)(2,1)} %slice.587), channel_id=1, source_target_pairs={{0,16},{4,20},{8,24},{12,28},{16,0},{20,4},{24,8},{28,12},{1,17},{... | collective-permute-start | bytes 2113544 | tf_op jit(solution)/shard_map/ppermute | solution.py:50
  346.1 45.6 %collective-permute-start.76 = (bf16[256,2752]{0,1:T(8,128)(2,1)}, bf16[256,2752]{0,1:T(8,128)(2,1)}, u32[]{:S(2)}, u32[]{:S(2)}) collective-permute-start(bf16[256,2752]{0,1:T(8,128)(2,1)} %collective-permute-done.71), channel_id=1, source_target_pairs={{0,4},{4,0},{8,12},{12,8},{16,20},{20,16},{24,28},{28,24},{1,5},{5... | collective-permute-start | bytes 4227080 | tf_op jit(solution)/shard_map/ppermute | solution.py:50
  431.6 36.3 %collective-permute-start.60 = (bf16[256,2048]{1,0:T(8,128)(2,1)}, bf16[256,2048]{1,0:T(8,128)(2,1)S(1)}, u32[]{:S(2)}, u32[]{:S(2)}) collective-permute-start(bf16[256,2048]{1,0:T(8,128)(2,1)} %collective-permute-done.57), channel_id=1, source_target_pairs={{1,2},{2,1},{5,6},{6,5},{9,10},{10,9},{13,14},{14,13},{17,18},{18,... | collective-permute-start | bytes 3145736 | tf_op jit(solution)/shard_map/ppermute | solution.py:95
  466.9 36.7 %collective-permute-start.84 = (bf16[2752,256]{1,0:T(8,128)(2,1)}, bf16[2752,256]{1,0:T(8,128)(2,1)S(1)}, u32[]{:S(2)}, u32[]{:S(2)}) collective-permute-start(bf16[2752,256]{1,0:T(8,128)(2,1)} %collective-permute-done.79), channel_id=1, source_target_pairs={{0,4},{4,0},{8,12},{12,8},{16,20},{20,16},{24,28},{28,24},{1,5},{5... | collective-permute-start | bytes 4227080 | tf_op jit(solution)/shard_map/ppermute | solution.py:50
  468.0 34.4 %collective-permute-start.83 = (bf16[2752,256]{1,0:T(8,128)(2,1)}, bf16[2752,256]{1,0:T(8,128)(2,1)S(1)}, u32[]{:S(2)}, u32[]{:S(2)}) collective-permute-start(bf16[2752,256]{1,0:T(8,128)(2,1)} %collective-permute-done.78), channel_id=1, source_target_pairs={{0,4},{4,0},{8,12},{12,8},{16,20},{20,16},{24,28},{28,24},{1,5},{5... | collective-permute-start | bytes 4227080 | tf_op jit(solution)/shard_map/ppermute | solution.py:50
  468.5 38.2 %collective-permute-start.61 = (bf16[256,2048]{1,0:T(8,128)(2,1)S(1)}, bf16[256,2048]{1,0:T(8,128)(2,1)S(1)}, u32[]{:S(2)}, u32[]{:S(2)}) collective-permute-start(bf16[256,2048]{1,0:T(8,128)(2,1)S(1)} %collective-permute-done.60), channel_id=1, source_target_pairs={{1,0},{2,3},{5,4},{6,7},{9,8},{10,11},{13,12},{14,15},{17,16},{18,... | collective-permute-start | bytes 3145736 | tf_op jit(solution)/shard_map/ppermute | solution.py:95
  470.9 53.1 %collective-permute-start.69 = (bf16[256,2752]{0,1:T(8,128)(2,1)S(1)}, bf16[256,2752]{0,1:T(8,128)(2,1)}, u32[]{:S(2)}, u32[]{:S(2)}) collective-permute-start(bf16[256,2752]{0,1:T(8,128)(2,1)S(1)} %copy-done.50), channel_id=1, source_target_pairs={{0,4},{4,0},{8,12},{12,8},{16,20},{20,16},{24,28},{28,24},{1,5},{5... | collective-permute-start | bytes 4227080 | tf_op jit(solution)/shard_map/ppermute | solution.py:50
  533.1 46.0 %collective-permute-start.56 = (bf16[256,2048]{1,0:T(8,128)(2,1)}, bf16[256,2048]{1,0:T(8,128)(2,1)S(1)}, u32[]{:S(2)}, u32[]{:S(2)}) collective-permute-start(bf16[256,2048]{1,0:T(8,128)(2,1)} %collective-permute-done.55), channel_id=1, source_target_pairs={{1,0},{2,3},{5,4},{6,7},{9,8},{10,11},{13,12},{14,15},{17,16},{18,... | collective-permute-start | bytes 3145736 | tf_op jit(solution)/shard_map/ppermute | solution.py:95
  683.5 46.1 %collective-permute-start.86 = (bf16[256,2048]{1,0:T(8,128)(2,1)}, bf16[256,2048]{1,0:T(8,128)(2,1)S(1)}, u32[]{:S(2)}, u32[]{:S(2)}) collective-permute-start(bf16[256,2048]{1,0:T(8,128)(2,1)} %slice.594), channel_id=1, source_target_pairs={{0,1},{3,2},{4,5},{7,6},{8,9},{11,10},{12,13},{15,14},{16,17},{19,... | collective-permute-start | bytes 3145736 | tf_op jit(solution)/shard_map/ppermute | solution.py:95
  707.2 39.9 %collective-permute-start.92 = (bf16[256,2048]{1,0:T(8,128)(2,1)S(1)}, bf16[256,2048]{1,0:T(8,128)(2,1)S(1)}, u32[]{:S(2)}, u32[]{:S(2)}) collective-permute-start(bf16[256,2048]{1,0:T(8,128)(2,1)S(1)} %get-tuple-element.78), channel_id=1, source_target_pairs={{1,2},{2,1},{5,6},{6,5},{9,10},{10,9},{13,14},{14,13},{17,18},{18,... | collective-permute-start | bytes 3145736 | tf_op jit(solution)/shard_map/ppermute | solution.py:95
  707.9 44.0 %collective-permute-start.94 = (bf16[256,2048]{1,0:T(8,128)(2,1)S(1)}, bf16[256,2048]{1,0:T(8,128)(2,1)}, u32[]{:S(2)}, u32[]{:S(2)}) collective-permute-start(bf16[256,2048]{1,0:T(8,128)(2,1)S(1)} %get-tuple-element.79), channel_id=1, source_target_pairs={{0,1},{3,2},{4,5},{7,6},{8,9},{11,10},{12,13},{15,14},{16,17},{19,... | collective-permute-start | bytes 3145736 | tf_op jit(solution)/shard_map/ppermute | solution.py:95
  730.5 43.9 %collective-permute-start.89 = (bf16[256,2048]{1,0:T(8,128)(2,1)S(1)}, bf16[256,2048]{1,0:T(8,128)(2,1)S(1)}, u32[]{:S(2)}, u32[]{:S(2)}) collective-permute-start(bf16[256,2048]{1,0:T(8,128)(2,1)S(1)} %get-tuple-element.83), channel_id=1, source_target_pairs={{0,1},{3,2},{4,5},{7,6},{8,9},{11,10},{12,13},{15,14},{16,17},{19,... | collective-permute-start | bytes 3145736 | tf_op jit(solution)/shard_map/ppermute | solution.py:95
  747.1 134.6 %collective-permute-start.141 = (bf16[1024,2752]{0,1:T(8,128)(2,1)}, bf16[1024,2752]{0,1:T(8,128)(2,1)}, u32[]{:S(2)}, u32[]{:S(2)}) collective-permute-start(bf16[1024,2752]{0,1:T(8,128)(2,1)} %convolution_convert_fusion.1), channel_id=1, source_target_pairs={{0,4},{4,0},{8,12},{12,8},{16,20},{20,16},{24,28},{28,24},{1,5},{5... | collective-permute-start | bytes 16908296 | tf_op jit(solution)/shard_map/ppermute | solution.py:50
  754.3 42.6 %collective-permute-start.93 = (bf16[256,2048]{1,0:T(8,128)(2,1)}, bf16[256,2048]{1,0:T(8,128)(2,1)S(1)}, u32[]{:S(2)}, u32[]{:S(2)}) collective-permute-start(bf16[256,2048]{1,0:T(8,128)(2,1)} %get-tuple-element.76), channel_id=1, source_target_pairs={{0,1},{1,0},{2,3},{3,2},{4,5},{5,4},{6,7},{7,6},{8,9},{9,8},{10,11... | collective-permute-start | bytes 3145736 | tf_op jit(solution)/shard_map/ppermute | solution.py:95
  756.9 40.1 %collective-permute-start.95 = (bf16[256,2048]{1,0:T(8,128)(2,1)S(1)}, bf16[256,2048]{1,0:T(8,128)(2,1)S(1)}, u32[]{:S(2)}, u32[]{:S(2)}) collective-permute-start(bf16[256,2048]{1,0:T(8,128)(2,1)S(1)} %get-tuple-element.77), channel_id=1, source_target_pairs={{1,2},{2,1},{5,6},{6,5},{9,10},{10,9},{13,14},{14,13},{17,18},{18,... | collective-permute-start | bytes 3145736 | tf_op jit(solution)/shard_map/ppermute | solution.py:95
  775.9 41.6 %collective-permute-start.88 = (bf16[256,2048]{1,0:T(8,128)(2,1)}, bf16[256,2048]{1,0:T(8,128)(2,1)}, u32[]{:S(2)}, u32[]{:S(2)}) collective-permute-start(bf16[256,2048]{1,0:T(8,128)(2,1)} %get-tuple-element.80), channel_id=1, source_target_pairs={{0,1},{1,0},{2,3},{3,2},{4,5},{5,4},{6,7},{7,6},{8,9},{9,8},{10,11... | collective-permute-start | bytes 3145736 | tf_op jit(solution)/shard_map/ppermute | solution.py:95
  778.4 39.2 %collective-permute-start.90 = (bf16[256,2048]{1,0:T(8,128)(2,1)}, bf16[256,2048]{1,0:T(8,128)(2,1)}, u32[]{:S(2)}, u32[]{:S(2)}) collective-permute-start(bf16[256,2048]{1,0:T(8,128)(2,1)} %get-tuple-element.81), channel_id=1, source_target_pairs={{1,2},{2,1},{5,6},{6,5},{9,10},{10,9},{13,14},{14,13},{17,18},{18,... | collective-permute-start | bytes 3145736 | tf_op jit(solution)/shard_map/ppermute | solution.py:95
  797.0 131.2 %collective-permute-start.136 = (bf16[1024,2752]{0,1:T(8,128)(2,1)}, bf16[1024,2752]{0,1:T(8,128)(2,1)}, u32[]{:S(2)}, u32[]{:S(2)}) collective-permute-start(bf16[1024,2752]{0,1:T(8,128)(2,1)} %convolution_convert_fusion.2), channel_id=1, source_target_pairs={{0,4},{4,0},{8,12},{12,8},{16,20},{20,16},{24,28},{28,24},{1,5},{5... | collective-permute-start | bytes 16908296 | tf_op jit(solution)/shard_map/ppermute | solution.py:50
  797.0 99.9 %collective-permute-start.146 = (bf16[2752,1024]{1,0:T(8,128)(2,1)}, bf16[2752,1024]{1,0:T(8,128)(2,1)}, u32[]{:S(2)}, u32[]{:S(2)}) collective-permute-start(bf16[2752,1024]{1,0:T(8,128)(2,1)} %convolution_convert_fusion), channel_id=1, source_target_pairs={{0,4},{4,0},{8,12},{12,8},{16,20},{20,16},{24,28},{28,24},{1,5},{5... | collective-permute-start | bytes 16908296 | tf_op jit(solution)/shard_map/ppermute | solution.py:50
  879.6 109.9 %collective-permute-start.126 = (bf16[2048,1024]{1,0:T(8,128)(2,1)S(1)}, bf16[2048,1024]{1,0:T(8,128)(2,1)}, u32[]{:S(2)}, u32[]{:S(2)}) collective-permute-start(bf16[2048,1024]{1,0:T(8,128)(2,1)S(1)} %copy-done.19), channel_id=1, source_target_pairs={{0,4},{4,0},{8,12},{12,8},{16,20},{20,16},{24,28},{28,24},{1,5},{5... | collective-permute-start | bytes 12582920 | tf_op jit(solution)/shard_map/ppermute | solution.py:50
  881.6 118.7 %collective-permute-start.106 = (bf16[1024,2048]{1,0:T(8,128)(2,1)S(1)}, bf16[1024,2048]{1,0:T(8,128)(2,1)}, u32[]{:S(2)}, u32[]{:S(2)}) collective-permute-start(bf16[1024,2048]{1,0:T(8,128)(2,1)S(1)} %convolution_convert_fusion.5), channel_id=1, source_target_pairs={{0,4},{4,0},{8,12},{12,8},{16,20},{20,16},{24,28},{28,24},{1,5},{5... | collective-permute-start | bytes 12582920 | tf_op jit(solution)/shard_map/ppermute | solution.py:50
  881.7 112.7 %collective-permute-start.96 = (bf16[4096,512]{1,0:T(8,128)(2,1)}, bf16[4096,512]{1,0:T(8,128)(2,1)}, u32[]{:S(2)}, u32[]{:S(2)}) collective-permute-start(bf16[4096,512]{1,0:T(8,128)(2,1)} %slice.484), channel_id=1, source_target_pairs={{0,4},{4,0},{8,12},{12,8},{16,20},{20,16},{24,28},{28,24},{1,5},{5... | collective-permute-start | bytes 12582920 | tf_op jit(solution)/shard_map/ppermute | solution.py:50
  896.9 49.8 %collective-permute-start.144 = (bf16[128,2752]{0,1:T(8,128)(2,1)}, bf16[128,2752]{0,1:T(8,128)(2,1)}, u32[]{:S(2)}, u32[]{:S(2)}) collective-permute-start(bf16[128,2752]{0,1:T(8,128)(2,1)} %get-tuple-element.48), channel_id=1, source_target_pairs={{0,8},{4,12},{8,0},{12,4},{16,24},{20,28},{24,16},{28,20},{1,9},{5... | collective-permute-start | bytes 2113544 | tf_op jit(solution)/shard_map/ppermute | solution.py:50
  981.7 34.1 %collective-permute-start.145 = (bf16[256,2752]{0,1:T(8,128)(2,1)}, bf16[256,2752]{0,1:T(8,128)(2,1)}, u32[]{:S(2)}, u32[]{:S(2)}) collective-permute-start(bf16[256,2752]{0,1:T(8,128)(2,1)} %pad_maximum_fusion.9), channel_id=1, source_target_pairs={{0,16},{4,20},{8,24},{12,28},{16,0},{20,4},{24,8},{28,12},{1,17},{... | collective-permute-start | bytes 4227080 | tf_op jit(solution)/shard_map/ppermute | solution.py:50
  984.0 34.1 %collective-permute-start.143 = (bf16[256,2752]{0,1:T(8,128)(2,1)}, bf16[256,2752]{0,1:T(8,128)(2,1)}, u32[]{:S(2)}, u32[]{:S(2)}) collective-permute-start(bf16[256,2752]{0,1:T(8,128)(2,1)} %pad_maximum_fusion.8), channel_id=1, source_target_pairs={{0,8},{4,12},{8,0},{12,4},{16,24},{20,28},{24,16},{28,20},{1,9},{5... | collective-permute-start | bytes 4227080 | tf_op jit(solution)/shard_map/ppermute | solution.py:50
  989.5 196.0 %collective-permute-start.140 = (bf16[256,2752]{0,1:T(8,128)(2,1)}, bf16[256,2752]{0,1:T(8,128)(2,1)}, u32[]{:S(2)}, u32[]{:S(2)}) collective-permute-start(bf16[256,2752]{0,1:T(8,128)(2,1)} %pad_maximum_fusion.7), channel_id=1, source_target_pairs={{0,16},{4,20},{8,24},{12,28},{16,0},{20,4},{24,8},{28,12},{1,17},{... | collective-permute-start | bytes 4227080 | tf_op jit(solution)/shard_map/ppermute | solution.py:50
  994.4 73.6 %collective-permute-start.129 = (bf16[1024,256]{1,0:T(8,128)(2,1)S(1)}, bf16[1024,256]{1,0:T(8,128)(2,1)S(1)}, u32[]{:S(2)}, u32[]{:S(2)}) collective-permute-start(bf16[1024,256]{1,0:T(8,128)(2,1)S(1)} %get-tuple-element.60), channel_id=1, source_target_pairs={{0,8},{4,12},{8,0},{12,4},{16,24},{20,28},{24,16},{28,20},{1,9},{5... | collective-permute-start | bytes 1572872 | tf_op jit(solution)/shard_map/ppermute | solution.py:50
  1000.3 68.5 %collective-permute-start.127 = (bf16[1024,256]{1,0:T(8,128)(2,1)S(1)}, bf16[1024,256]{1,0:T(8,128)(2,1)S(1)}, u32[]{:S(2)}, u32[]{:S(2)}) collective-permute-start(bf16[1024,256]{1,0:T(8,128)(2,1)S(1)} %get-tuple-element.61), channel_id=1, source_target_pairs={{0,16},{4,20},{8,24},{12,28},{16,0},{20,4},{24,8},{28,12},{1,17},{... | collective-permute-start | bytes 1572872 | tf_op jit(solution)/shard_map/ppermute | solution.py:50
  1018.2 48.2 %collective-permute-start.97 = (bf16[512,512]{1,0:T(8,128)(2,1)S(1)}, bf16[512,512]{1,0:T(8,128)(2,1)S(1)}, u32[]{:S(2)}, u32[]{:S(2)}) collective-permute-start(bf16[512,512]{1,0:T(8,128)(2,1)S(1)} %get-tuple-element.73), channel_id=1, source_target_pairs={{0,16},{4,20},{8,24},{12,28},{16,0},{20,4},{24,8},{28,12},{1,17},{... | collective-permute-start | bytes 1572872 | tf_op jit(solution)/shard_map/ppermute | solution.py:50
  1037.6 32.7 %collective-permute-start.109 = (bf16[128,2048]{1,0:T(8,128)(2,1)S(1)}, bf16[128,2048]{1,0:T(8,128)(2,1)S(1)}, u32[]{:S(2)}, u32[]{:S(2)}) collective-permute-start(bf16[128,2048]{1,0:T(8,128)(2,1)S(1)} %get-tuple-element.66), channel_id=1, source_target_pairs={{0,8},{4,12},{8,0},{12,4},{16,24},{20,28},{24,16},{28,20},{1,9},{5... | collective-permute-start | bytes 1572872 | tf_op jit(solution)/shard_map/ppermute | solution.py:50
  1068.0 35.7 %collective-permute-start.100 = (bf16[1024,512]{1,0:T(8,128)(2,1)S(1)}, bf16[1024,512]{1,0:T(8,128)(2,1)S(1)}, u32[]{:S(2)}, u32[]{:S(2)}) collective-permute-start(bf16[1024,512]{1,0:T(8,128)(2,1)S(1)} %pad_maximum_fusion.16), channel_id=1, source_target_pairs={{0,16},{4,20},{8,24},{12,28},{16,0},{20,4},{24,8},{28,12},{1,17},{... | collective-permute-start | bytes 3145736 | tf_op jit(solution)/shard_map/ppermute | solution.py:50
  1068.8 34.9 %collective-permute-start.98 = (bf16[1024,512]{1,0:T(8,128)(2,1)S(1)}, bf16[1024,512]{1,0:T(8,128)(2,1)S(1)}, u32[]{:S(2)}, u32[]{:S(2)}) collective-permute-start(bf16[1024,512]{1,0:T(8,128)(2,1)S(1)} %pad_maximum_fusion.15), channel_id=1, source_target_pairs={{0,8},{4,12},{8,0},{12,4},{16,24},{20,28},{24,16},{28,20},{1,9},{5... | collective-permute-start | bytes 3145736 | tf_op jit(solution)/shard_map/ppermute | solution.py:50
  1070.4 55.8 %collective-permute-start.130 = (bf16[2048,256]{1,0:T(8,128)(2,1)S(1)}, bf16[2048,256]{1,0:T(8,128)(2,1)S(1)}, u32[]{:S(2)}, u32[]{:S(2)}) collective-permute-start(bf16[2048,256]{1,0:T(8,128)(2,1)S(1)} %pad_maximum_fusion.20), channel_id=1, source_target_pairs={{0,16},{4,20},{8,24},{12,28},{16,0},{20,4},{24,8},{28,12},{1,17},{... | collective-permute-start | bytes 3145736 | tf_op jit(solution)/shard_map/ppermute | solution.py:50
  1081.2 46.3 %collective-permute-start.128 = (bf16[2048,256]{1,0:T(8,128)(2,1)S(1)}, bf16[2048,256]{1,0:T(8,128)(2,1)S(1)}, u32[]{:S(2)}, u32[]{:S(2)}) collective-permute-start(bf16[2048,256]{1,0:T(8,128)(2,1)S(1)} %pad_maximum_fusion.19), channel_id=1, source_target_pairs={{0,8},{4,12},{8,0},{12,4},{16,24},{20,28},{24,16},{28,20},{1,9},{5... | collective-permute-start | bytes 3145736 | tf_op jit(solution)/shard_map/ppermute | solution.py:50
  1108.7 37.3 %collective-permute-start.110 = (bf16[256,2048]{1,0:T(8,128)(2,1)S(1)}, bf16[256,2048]{1,0:T(8,128)(2,1)S(1)}, u32[]{:S(2)}, u32[]{:S(2)}) collective-permute-start(bf16[256,2048]{1,0:T(8,128)(2,1)S(1)} %pad_maximum_fusion.18), channel_id=1, source_target_pairs={{0,16},{4,20},{8,24},{12,28},{16,0},{20,4},{24,8},{28,12},{1,17},{... | collective-permute-start | bytes 3145736 | tf_op jit(solution)/shard_map/ppermute | solution.py:50
  1112.5 37.9 %collective-permute-start.108 = (bf16[256,2048]{1,0:T(8,128)(2,1)S(1)}, bf16[256,2048]{1,0:T(8,128)(2,1)S(1)}, u32[]{:S(2)}, u32[]{:S(2)}) collective-permute-start(bf16[256,2048]{1,0:T(8,128)(2,1)S(1)} %pad_maximum_fusion.17), channel_id=1, source_target_pairs={{0,8},{4,12},{8,0},{12,4},{16,24},{20,28},{24,16},{28,20},{1,9},{5... | collective-permute-start | bytes 3145736 | tf_op jit(solution)/shard_map/ppermute | solution.py:50
  1126.2 60.7 %collective-permute-start.138 = (bf16[256,2752]{0,1:T(8,128)(2,1)}, bf16[256,2752]{0,1:T(8,128)(2,1)}, u32[]{:S(2)}, u32[]{:S(2)}) collective-permute-start(bf16[256,2752]{0,1:T(8,128)(2,1)} %pad_maximum_fusion.6), channel_id=1, source_target_pairs={{0,8},{4,12},{8,0},{12,4},{16,24},{20,28},{24,16},{28,20},{1,9},{5... | collective-permute-start | bytes 4227080 | tf_op jit(solution)/shard_map/ppermute | solution.py:50
  1128.7 29.3 %collective-permute-start.131 = (bf16[512,256]{1,0:T(8,128)(2,1)S(1)}, bf16[512,256]{1,0:T(8,128)(2,1)S(1)}, u32[]{:S(2)}, u32[]{:S(2)}) collective-permute-start(bf16[512,256]{1,0:T(8,128)(2,1)S(1)} %constant_dynamic-slice_fusion.1), channel_id=1, source_target_pairs={{0,1},{3,2},{4,5},{7,6},{8,9},{11,10},{12,13},{15,14},{16,17},{19,... | collective-permute-start | bytes 786440 | tf_op jit(solution)/shard_map/ppermute | solution.py:95
  1158.0 51.1 %collective-permute-start.150 = (bf16[2752,256]{1,0:T(8,128)(2,1)}, bf16[2752,256]{1,0:T(8,128)(2,1)}, u32[]{:S(2)}, u32[]{:S(2)}) collective-permute-start(bf16[2752,256]{1,0:T(8,128)(2,1)} %pad_maximum_fusion.11), channel_id=1, source_target_pairs={{0,16},{4,20},{8,24},{12,28},{16,0},{20,4},{24,8},{28,12},{1,17},{... | collective-permute-start | bytes 4227080 | tf_op jit(solution)/shard_map/ppermute | solution.py:50
  1160.9 48.6 %collective-permute-start.148 = (bf16[2752,256]{1,0:T(8,128)(2,1)}, bf16[2752,256]{1,0:T(8,128)(2,1)}, u32[]{:S(2)}, u32[]{:S(2)}) collective-permute-start(bf16[2752,256]{1,0:T(8,128)(2,1)} %pad_maximum_fusion.10), channel_id=1, source_target_pairs={{0,8},{4,12},{8,0},{12,4},{16,24},{20,28},{24,16},{28,20},{1,9},{5... | collective-permute-start | bytes 4227080 | tf_op jit(solution)/shard_map/ppermute | solution.py:50
  1161.3 30.1 %collective-permute-start.111 = (bf16[256,512]{1,0:T(8,128)(2,1)}, bf16[256,512]{1,0:T(8,128)(2,1)}, u32[]{:S(2)}, u32[]{:S(2)}) collective-permute-start(bf16[256,512]{1,0:T(8,128)(2,1)} %constant_dynamic-slice_fusion.5), channel_id=1, source_target_pairs={{0,1},{3,2},{4,5},{7,6},{8,9},{11,10},{12,13},{15,14},{16,17},{19,... | collective-permute-start | bytes 786440 | tf_op jit(solution)/shard_map/ppermute | solution.py:95
  (163 other events, 5721.4 us)

commit v2 on v1

v2 whole, which is shorter than its diff:
```python
import functools

import jax
import jax.numpy as jnp
from jax import lax
from jax.experimental import pallas as pl
from jax.experimental.pallas import tpu as pltpu
from jax.sharding import PartitionSpec as P

HEADS = 16
KV = 2
HD = 128
BLK = 512
GROUP = HEADS // KV
TILE = 512
BATCH = 8
ROWS = 1024
UNITS = 256
GRAD_UNITS = 512

EPSILON = 1e-06
ROPE_BASE = 1000000.0
NEGATIVE = -1e30
SCALE = HD**-0.5
LOG2E = 1.4426950408889634

F32 = jnp.float32
BF16 = jnp.bfloat16

ORDER = ((0, 2, 4, 6, 1, 5, 3, 7), (0, 4, 2, 6, 1, 3, 5, 7))
RELAY = ((0, 1, 2, 3), (1, 0, 2, 3), (2, 3, 1, 0), (3, 2, 1, 0))


def contract(left_side, right_side, left_dim, right_dim):
    return lax.dot_general(
        left_side,
        right_side,
        (((left_dim,), (right_dim,)), ((), ())),
        preferred_element_type=F32,
    )


def after(value, *others):
    return lax.optimization_barrier((value, *others))[0]


class Lane:
    def __init__(self, depth):
        self.depth = depth
        self.done = []

    def __call__(self, send, value):
        if len(self.done) >= self.depth:
            value = after(value, self.done[-self.depth])
        self.done.append(send(value))
        return self.done[-1]


class SeqAxis:
    def __init__(self):
        self.size = lax.axis_size("seq")
        self.me = lax.axis_index("seq")
        self.fast = self.size == 8
        self.lane = Lane(2)
        places = jnp.arange(self.size, dtype=jnp.int32)
        if self.fast:
            odd = self.me % 2 == 1
            self.order = self.me ^ jnp.where(odd, jnp.array(ORDER[1]), jnp.array(ORDER[0]))
        else:
            self.order = places
        self.place = jnp.sum(
            jnp.where(self.order[:, None] == places[None, :], places[:, None], 0), axis=0
        )

    def swap(self, value, even, odd, ordered=True):
        pairs = [(i, i ^ (odd if i % 2 else even)) for i in range(self.size)]

        def send(item):
            return lax.ppermute(item, "seq", pairs)

        return self.lane(send, value) if ordered else send(value)

    def begin(self, value, ordered=True):
        if not self.fast:
            return [value]
        return [value, self.swap(value, 2, 4, ordered), self.swap(value, 4, 2, ordered)]

    def finish(self, begun, axis=0, ordered=True):
        if not self.fast:
            whole = lax.all_gather(begun[0], "seq", axis=axis, tiled=True)
            half = whole.shape[axis] // 2
            return [
                lax.slice_in_dim(whole, i * half, (i + 1) * half, axis=axis) for i in range(2)
            ]
        value, one, two = begun
        mine = jnp.concatenate([value, one, two, self.swap(one, 4, 2, ordered)], axis=axis)
        return [mine, self.swap(mine, 1, 1, False)]

    def gather(self, value, axis=0, ordered=True):
        return self.finish(self.begin(value, ordered), axis, ordered)

    def reduce(self, mine, other):
        if not self.fast:
            whole = jnp.concatenate([jnp.stack(mine(None)), other], axis=0)
            return lax.psum_scatter(whole, "seq", scatter_dimension=0, tiled=False).astype(F32)
        here, one, two, corner = mine(self.swap(other, 1, 1, False))
        corner = self.swap(corner, 4, 2)
        two = self.swap(two, 4, 2)
        one = self.swap(one + corner, 2, 4)
        return here.astype(F32) + two.astype(F32) + one.astype(F32)


class HeadAxis:
    def __init__(self):
        self.size = lax.axis_size("head")
        self.me = lax.axis_index("head")
        self.fast = self.size == 4
        self.inner = (self.me == 1) | (self.me == 2)
        self.relay = jnp.array(RELAY, jnp.int32)[self.me] if self.fast else None
        self.direct = self.me ^ jnp.arange(self.size, dtype=jnp.int32)

    def send(self, value, pairs):
        return lax.ppermute(value, "head", pairs)

    def gather(self, value):
        if not self.fast:
            return lax.all_gather(value, "head", axis=0, tiled=True)
        pair = [(0, 1), (1, 0), (2, 3), (3, 2)]
        middle = [(1, 2), (2, 1)]
        outward = [(1, 0), (2, 3)]
        slot1 = self.send(value, pair)
        near = self.send(value, middle)
        far = self.send(slot1, middle)
        slot2 = jnp.where(self.inner, near, self.send(near, outward))
        slot3 = jnp.where(self.inner, far, self.send(far, outward))
        return place([value, slot1, slot2, slot3], self.relay, 0)

    def reduce(self, whole, beside):
        if not self.fast:
            return [lax.psum_scatter(whole, "head", scatter_dimension=0, tiled=True)]
        pair = [(0, 1), (1, 0), (2, 3), (3, 2)]
        middle = [(1, 2), (2, 1)]
        inward = [(0, 1), (3, 2)]
        rows = whole.shape[0] // self.size
        own, slot1, slot2, slot3 = (
            lax.dynamic_slice_in_dim(whole, self.relay[k] * rows, rows, 0) for k in range(4)
        )
        far = slot3 + after(self.send(slot3, inward), beside[0])
        near = self.send(after(slot2, far), inward)
        next_door = slot1 + after(self.send(far, middle), beside[1])
        near = slot2 + near
        return [own, after(self.send(next_door, pair), beside[2]), self.send(near, middle)]

    def gather_small(self, value, axis):
        if not self.fast:
            return lax.all_gather(value, "head", axis=axis, tiled=True)
        pieces = [value] + [
            self.send(value, [(i, i ^ k) for i in range(self.size)]) for k in range(1, 4)
        ]
        return place(pieces, self.direct, axis)

    def reduce_small(self, value, axis):
        if not self.fast:
            return lax.psum_scatter(value, "head", scatter_dimension=axis, tiled=True).astype(F32)
        width = value.shape[axis] // self.size
        total = None
        for k in range(self.size):
            part = lax.dynamic_slice_in_dim(value, (self.me ^ k) * width, width, axis)
            if k:
                part = self.send(part, [(i, i ^ k) for i in range(self.size)])
            total = part.astype(F32) if total is None else total + part.astype(F32)
        return total


def vmem():
    return pl.BlockSpec(memory_space=pltpu.VMEM)


def anywhere():
    return pl.BlockSpec(memory_space=pl.ANY)


def smem():
    return pl.BlockSpec(memory_space=pltpu.SMEM)


def place_kernel(axis, order_ref, *refs):
    out_ref = refs[-1]
    for k, piece_ref in enumerate(refs[:-1]):
        width = piece_ref.shape[axis]
        at = pl.ds(pl.multiple_of(order_ref[k] * width, width), width)
        if axis:
            out_ref[:, at] = piece_ref[...]
        else:
            out_ref[at, :] = piece_ref[...]


def place(pieces, order, axis):
    shape = list(pieces[0].shape)
    shape[axis] *= len(pieces)
    return pl.pallas_call(
        functools.partial(place_kernel, axis),
        out_shape=jax.ShapeDtypeStruct(shape, pieces[0].dtype),
        in_specs=[smem()] + [vmem()] * len(pieces),
        out_specs=vmem(),
        name="place",
    )(order, *pieces)


def shuffle_kernel(count, order_ref, *refs):
    for i in range(len(refs) // 2):
        in_ref, out_ref = refs[i], refs[len(refs) // 2 + i]
        width = in_ref.shape[1] // count
        for p in range(count):
            at = pl.ds(pl.multiple_of(order_ref[p] * width, width), width)
            out_ref[:, p * width : (p + 1) * width] = in_ref[:, at]


def shuffle(order, *values):
    return pl.pallas_call(
        functools.partial(shuffle_kernel, order.shape[0]),
        out_shape=[jax.ShapeDtypeStruct(v.shape, v.dtype) for v in values],
        in_specs=[smem()] + [vmem()] * len(values),
        out_specs=[vmem()] * len(values),
        name="shuffle",
    )(order, *values)


def turn(values, cosine, sine):
    return values * cosine + pltpu.roll(values, HD // 2, 1) * sine


def allowed_bias(tile, stream, first, shape):
    key = tile * TILE + lax.broadcasted_iota(jnp.int32, shape, 0)
    return jnp.where((key >= first) & (key <= stream), 0.0, NEGATIVE)


def fetch(half_a_ref, half_b_ref, whole_ref, sem_ref):
    half = half_a_ref.shape[0]
    copies = [
        pltpu.make_async_copy(ref, whole_ref.at[pl.ds(i * half, half)], sem_ref.at[i])
        for i, ref in enumerate((half_a_ref, half_b_ref))
    ]
    for copy in copies:
        copy.start()
    return copies


def forward_kernel(
    offset_ref, bound_ref, raw_ref, cos_ref, sin_ref, stream_ref, first_ref, half_a_ref, half_b_ref,
    query_ref, mixed_ref, lse_ref,
    top_ref, total_ref, sum_ref, bias_ref, turned_ref, kv_ref, sem_ref,
):
    copies = fetch(half_a_ref, half_b_ref, kv_ref, sem_ref)
    cosine, sine = cos_ref[...], sin_ref[...]
    for h in range(HEADS):
        query_ref[h] = turn(raw_ref[:, h * HD : (h + 1) * HD], cosine, sine).astype(BF16)
    top_ref[...] = jnp.full(top_ref.shape, NEGATIVE, F32)
    total_ref[...] = jnp.zeros(total_ref.shape, F32)
    sum_ref[...] = jnp.zeros(sum_ref.shape, F32)
    for copy in copies:
        copy.wait()

    def visit(tile, carry):
        start = pl.multiple_of(offset_ref[tile], TILE)
        bias_ref[...] = allowed_bias(tile, stream_ref[...], first_ref[...], bias_ref.shape)
        for g in range(KV):
            turned_ref[g] = kv_ref[pl.ds(start, TILE), (KV + g) * HD : (KV + g + 1) * HD].T
        for g in range(KV):
            keys = kv_ref[pl.ds(start, TILE), g * HD : (g + 1) * HD]

            def some(i, carry):
                heads = [g * GROUP + i * BATCH + b for b in range(BATCH)]
                old = [top_ref[h] for h in heads]
                total = [total_ref[h] for h in heads]
                summed = [sum_ref[h] for h in heads]
                scores = [contract(keys, query_ref[h], 1, 1) for h in heads]
                bias = bias_ref[...]
                turned = turned_ref[g]
                new, fresh, fades = [], [], []
                for b in range(BATCH):
                    score = scores[b] * (SCALE * LOG2E) + bias
                    peak = jnp.maximum(old[b], jnp.max(score, axis=0, keepdims=True))
                    weights = jnp.exp2(score - peak)
                    fade = jnp.exp2(old[b] - peak)
                    new.append(peak)
                    fades.append(fade)
                    total[b] = total[b] * fade + jnp.sum(weights, axis=0, keepdims=True)
                    fresh.append(contract(turned, weights.astype(BF16), 1, 0))
                for b, h in enumerate(heads):
                    top_ref[h] = new[b]
                    total_ref[h] = total[b]
                    sum_ref[h] = summed[b] * fades[b] + fresh[b]
                return carry

            lax.fori_loop(0, GROUP // BATCH, some, 0)
        return carry

    lax.fori_loop(bound_ref[0], bound_ref[1] + 1, visit, 0)
    for h in range(HEADS):
        lse_ref[h] = top_ref[h] + jnp.log2(total_ref[h])
        mixed_ref[:, h * HD : (h + 1) * HD] = (sum_ref[h] / total_ref[h]).T.astype(BF16)


def attention_forward(offsets, bounds, query_raw, cosine, sine, stream, first, kv_a, kv_b):
    rows = query_raw.shape[0]
    kv_shape = (2 * kv_a.shape[0], kv_a.shape[1])
    return pl.pallas_call(
        forward_kernel,
        out_shape=(
            jax.ShapeDtypeStruct((HEADS, rows, HD), BF16),
            jax.ShapeDtypeStruct((rows, HEADS * HD), BF16),
            jax.ShapeDtypeStruct((HEADS, 1, rows), F32),
        ),
        in_specs=[smem(), smem()] + [vmem()] * 5 + [anywhere()] * 2,
        out_specs=[vmem()] * 3,
        scratch_shapes=[
            pltpu.VMEM((HEADS, 1, rows), F32),
            pltpu.VMEM((HEADS, 1, rows), F32),
            pltpu.VMEM((HEADS, HD, rows), F32),
            pltpu.VMEM((TILE, rows), F32),
            pltpu.VMEM((KV, HD, TILE), BF16),
            pltpu.VMEM(kv_shape, BF16),
            pltpu.SemaphoreType.DMA((2,)),
        ],
        compiler_params=pltpu.CompilerParams(vmem_limit_bytes=48 << 20),
        cost_estimate=pl.CostEstimate(
            flops=4 * HEADS * rows * HD * 2048,
            transcendentals=HEADS * rows * 2048,
            bytes_accessed=kv_a.size * 4 + query_raw.size * 8,
        ),
        name="attention_forward",
    )(offsets, bounds, query_raw, cosine, sine, stream, first, kv_a, kv_b)


def backward_kernel(
    offset_ref, bound_ref, query_ref, cos_ref, sin_ref, stream_ref, first_ref,
    mixed_ref, grad_ref, lse_ref, half_a_ref, half_b_ref,
    d_query_ref, d_half_a_ref, d_half_b_ref,
    delta_ref, head_grad_ref, sum_ref, bias_ref, turned_ref, d_tile_ref, kv_ref, sem_ref,
):
    copies = fetch(half_a_ref, half_b_ref, kv_ref, sem_ref)
    half = half_a_ref.shape[0]
    for h in range(HEADS):
        part = grad_ref[:, h * HD : (h + 1) * HD]
        head_grad_ref[h] = part
        product = part.astype(F32) * mixed_ref[:, h * HD : (h + 1) * HD].astype(F32)
        delta_ref[h] = lax.dot_general(
            jnp.ones((8, HD), F32),
            product,
            (((1,), (1,)), ((), ())),
            precision=lax.Precision.HIGHEST,
            preferred_element_type=F32,
        )[:1]
    sum_ref[...] = jnp.zeros(sum_ref.shape, F32)
    d_half_a_ref[...] = jnp.zeros(d_half_a_ref.shape, BF16)
    d_half_b_ref[...] = jnp.zeros(d_half_b_ref.shape, BF16)
    for copy in copies:
        copy.wait()

    def visit(tile, carry):
        start = pl.multiple_of(offset_ref[tile], TILE)
        bias_ref[...] = allowed_bias(tile, stream_ref[...], first_ref[...], bias_ref.shape)
        d_tile_ref[...] = jnp.zeros(d_tile_ref.shape, F32)
        for g in range(KV):
            turned_ref[g] = kv_ref[pl.ds(start, TILE), g * HD : (g + 1) * HD].T
        for g in range(KV):
            keys = kv_ref[pl.ds(start, TILE), g * HD : (g + 1) * HD]
            values = kv_ref[pl.ds(start, TILE), (KV + g) * HD : (KV + g + 1) * HD]

            def some(i, carry):
                heads = [g * GROUP + i * BATCH + b for b in range(BATCH)]
                query = [query_ref[h] for h in heads]
                head_grad = [head_grad_ref[h] for h in heads]
                summed = [sum_ref[h] for h in heads]
                bias = bias_ref[...]
                turned = turned_ref[g]
                d_keys, d_values = d_tile_ref[g], d_tile_ref[KV + g]
                for b, h in enumerate(heads):
                    scores = contract(keys, query[b], 1, 1) * (SCALE * LOG2E) + bias
                    weights = jnp.exp2(scores - lse_ref[h])
                    d_weights = contract(values, head_grad[b], 1, 1)
                    d_scores = (weights * (d_weights - delta_ref[h])).astype(BF16)
                    d_keys += contract(d_scores, query[b], 1, 0)
                    d_values += contract(weights.astype(BF16), head_grad[b], 1, 0)
                    summed[b] += contract(turned, d_scores, 1, 0)
                for b, h in enumerate(heads):
                    sum_ref[h] = summed[b]
                d_tile_ref[g] = d_keys
                d_tile_ref[KV + g] = d_values
                return carry

            lax.fori_loop(0, GROUP // BATCH, some, 0)
        for i, d_ref in enumerate((d_half_a_ref, d_half_b_ref)):

            @pl.when(start // half == i)
            def _():
                at = pl.ds(pl.multiple_of(start - i * half, TILE), TILE)
                for g in range(KV):
                    d_ref[at, g * HD : (g + 1) * HD] = (d_tile_ref[g] * SCALE).astype(BF16)
                    d_ref[at, (KV + g) * HD : (KV + g + 1) * HD] = d_tile_ref[KV + g].astype(BF16)

        return carry

    lax.fori_loop(bound_ref[0], bound_ref[1] + 1, visit, 0)
    cosine, sine = cos_ref[...], -sin_ref[...]
    for h in range(HEADS):
        d_query_ref[:, h * HD : (h + 1) * HD] = turn(
            sum_ref[h].T * SCALE, cosine, sine
        ).astype(BF16)


def attention_backward(
    offsets, bounds, queries, cosine, sine, stream, first, mixed, d_mixed, lse, kv_a, kv_b
):
    rows = mixed.shape[0]
    kv_shape = (2 * kv_a.shape[0], kv_a.shape[1])
    return pl.pallas_call(
        backward_kernel,
        out_shape=(
            jax.ShapeDtypeStruct((rows, HEADS * HD), BF16),
            jax.ShapeDtypeStruct(kv_a.shape, BF16),
            jax.ShapeDtypeStruct(kv_b.shape, BF16),
        ),
        in_specs=[smem(), smem()] + [vmem()] * 8 + [anywhere()] * 2,
        out_specs=[vmem()] * 3,
        scratch_shapes=[
            pltpu.VMEM((HEADS, 1, rows), F32),
            pltpu.VMEM((HEADS, rows, HD), BF16),
            pltpu.VMEM((HEADS, HD, rows), F32),
            pltpu.VMEM((TILE, rows), F32),
            pltpu.VMEM((KV, HD, TILE), BF16),
            pltpu.VMEM((2 * KV, TILE, HD), F32),
            pltpu.VMEM(kv_shape, BF16),
            pltpu.SemaphoreType.DMA((2,)),
        ],
        compiler_params=pltpu.CompilerParams(vmem_limit_bytes=56 << 20),
        cost_estimate=pl.CostEstimate(
            flops=10 * HEADS * rows * HD * 2048,
            transcendentals=HEADS * rows * 2048,
            bytes_accessed=kv_a.size * 8 + mixed.size * 8,
        ),
        name="attention_backward",
    )(offsets, bounds, queries, cosine, sine, stream, first, mixed, d_mixed, lse, kv_a, kv_b)


def side_by_side(order_ref, weight_ref):
    return jnp.concatenate([weight_ref[order_ref[p]] for p in range(weight_ref.shape[0])], axis=1)


def ffn_kernel(
    order_ref, normed_ref, grad_ref, gate_ref, up_ref, down_a_ref, down_b_ref,
    act_ref, d_gate_ref, d_up_ref,
):
    step = ROWS

    def chunk(i, carry):
        at = pl.ds(pl.multiple_of(i * step, step), step)
        normed = normed_ref[at, :]
        gate = contract(normed, side_by_side(order_ref, gate_ref), 1, 1)
        up = contract(normed, side_by_side(order_ref, up_ref), 1, 1)
        down = [ref[p] for ref in (down_a_ref, down_b_ref) for p in range(ref.shape[0])]
        d_act = contract(grad_ref[at, :], jnp.concatenate(down, axis=1), 1, 1)
        sigmoid = jax.nn.sigmoid(gate)
        silu = gate * sigmoid
        act_ref[at, :] = (silu * up).astype(BF16)
        d_up_ref[at, :] = (d_act * silu).astype(BF16)
        d_gate_ref[at, :] = (d_act * up * (sigmoid + silu * (1.0 - sigmoid))).astype(BF16)
        return carry

    lax.fori_loop(0, normed_ref.shape[0] // step, chunk, 0)


def ffn_middle(order, normed, grad, gate, up, down_a, down_b):
    rows, depth = normed.shape
    pieces, units, piece = gate.shape
    width = UNITS
    whole = pl.BlockSpec((rows, depth), lambda i, order_ref: (0, 0), pipeline_mode=pl.Buffered(1))
    weight = pl.BlockSpec((pieces, width, piece), lambda i, order_ref: (0, i, 0))
    half = pl.BlockSpec((pieces // 2, width, piece), lambda i, order_ref: (0, i, 0))
    return pl.pallas_call(
        ffn_kernel,
        out_shape=(jax.ShapeDtypeStruct((rows, units), BF16),) * 3,
        grid_spec=pltpu.PrefetchScalarGridSpec(
            num_scalar_prefetch=1,
            grid=(pl.cdiv(units, width),),
            in_specs=[whole, whole, weight, weight, half, half],
            out_specs=[pl.BlockSpec((rows, width), lambda i, order_ref: (0, i))] * 3,
        ),
        compiler_params=pltpu.CompilerParams(vmem_limit_bytes=48 << 20),
        cost_estimate=pl.CostEstimate(
            flops=6 * rows * depth * units,
            transcendentals=rows * units,
            bytes_accessed=2 * (3 * depth * units + 3 * rows * units + 2 * rows * depth),
        ),
        name="ffn_middle",
    )(order, normed, grad, gate, up, down_a, down_b)


def back_kernel(order_ref, d_gate_ref, d_up_ref, gate_ref, up_ref, out_ref):
    out_ref[...] = (
        contract(d_gate_ref[...], gate_ref[0], 1, 0) + contract(d_up_ref[...], up_ref[0], 1, 0)
    ).astype(BF16)


def ffn_back(order, d_gate, d_up, gate, up):
    rows, units = d_gate.shape
    pieces, _, piece = gate.shape
    whole = pl.BlockSpec((rows, units), lambda i, order_ref: (0, 0), pipeline_mode=pl.Buffered(1))
    part = pl.BlockSpec((1, units, piece), lambda i, order_ref: (order_ref[i], 0, 0))
    return pl.pallas_call(
        back_kernel,
        out_shape=jax.ShapeDtypeStruct((rows, pieces * piece), BF16),
        grid_spec=pltpu.PrefetchScalarGridSpec(
            num_scalar_prefetch=1,
            grid=(pieces,),
            in_specs=[whole, whole, part, part],
            out_specs=pl.BlockSpec((rows, piece), lambda i, order_ref: (0, i)),
        ),
        compiler_params=pltpu.CompilerParams(vmem_limit_bytes=48 << 20),
        cost_estimate=pl.CostEstimate(
            flops=4 * rows * pieces * piece * units,
            transcendentals=0,
            bytes_accessed=2 * (2 * pieces * piece * units + 2 * rows * units),
        ),
        name="ffn_back",
    )(order, d_gate, d_up, gate, up)


def forth_kernel(act_ref, down_a_ref, down_b_ref, out_ref):
    count = pl.num_programs(0) // 2
    for i, down_ref in enumerate((down_a_ref, down_b_ref)):

        @pl.when(pl.program_id(0) // count == i)
        def _():
            out_ref[...] = contract(act_ref[...], down_ref[0], 1, 0).astype(BF16)


def ffn_forth(act, down_a, down_b):
    rows, units = act.shape
    count, _, piece = down_a.shape
    return pl.pallas_call(
        forth_kernel,
        out_shape=jax.ShapeDtypeStruct((rows, 2 * count * piece), BF16),
        grid=(2 * count,),
        in_specs=[
            pl.BlockSpec((rows, units), lambda i: (0, 0), pipeline_mode=pl.Buffered(1)),
            pl.BlockSpec((1, units, piece), lambda i: (jnp.minimum(i, count - 1), 0, 0)),
            pl.BlockSpec((1, units, piece), lambda i: (jnp.maximum(i - count, 0), 0, 0)),
        ],
        out_specs=pl.BlockSpec((rows, piece), lambda i: (0, i)),
        compiler_params=pltpu.CompilerParams(vmem_limit_bytes=48 << 20),
        cost_estimate=pl.CostEstimate(
            flops=4 * rows * count * piece * units,
            transcendentals=0,
            bytes_accessed=2 * (2 * count * piece * units + rows * units),
        ),
        name="ffn_forth",
    )(act, down_a, down_b)


def unit_grad_kernel(count, shift, added, stacked, order_ref, left_ref, right_ref, *refs):
    outs = refs[added:]
    piece = outs[0].shape[-1]
    turned = left_ref[...].T
    for p in range(count):
        at = pl.ds(pl.multiple_of(order_ref[shift + p] * piece, piece), piece)
        term = contract(turned, right_ref[:, at], 1, 0)
        if added:
            term = term + refs[0][p].astype(F32)
        if stacked:
            outs[0][p] = term.astype(BF16)
        else:
            outs[p][...] = term.astype(BF16)


def unit_grad(left, right, order, shift, count, piece, received=None, apart=False):
    rows, units = left.shape
    columns = right.shape[1]
    width = GRAD_UNITS if count <= 4 else UNITS
    stack = pl.BlockSpec((count, width, piece), lambda i, order_ref: (0, i, 0))
    single = pl.BlockSpec((width, piece), lambda i, order_ref: (i, 0))
    extra = [] if received is None else [received]
    if apart:
        out_shape = [jax.ShapeDtypeStruct((units, piece), BF16)] * count
        out_specs = [single] * count
    else:
        out_shape = jax.ShapeDtypeStruct((count, units, piece), BF16)
        out_specs = stack
    return pl.pallas_call(
        functools.partial(unit_grad_kernel, count, shift, len(extra), not apart),
        out_shape=out_shape,
        grid_spec=pltpu.PrefetchScalarGridSpec(
            num_scalar_prefetch=1,
            grid=(pl.cdiv(units, width),),
            in_specs=[
                pl.BlockSpec((rows, width), lambda i, order_ref: (0, i)),
                pl.BlockSpec(
                    (rows, columns), lambda i, order_ref: (0, 0), pipeline_mode=pl.Buffered(1)
                ),
            ]
            + [stack] * len(extra),
            out_specs=out_specs,
        ),
        compiler_params=pltpu.CompilerParams(vmem_limit_bytes=48 << 20),
        cost_estimate=pl.CostEstimate(
            flops=2 * rows * units * count * piece,
            transcendentals=0,
            bytes_accessed=2
            * (rows * units + rows * columns + (1 + len(extra)) * units * count * piece),
        ),
        name="unit_grad",
    )(order, left, right, *extra)


def rope_tables(position):
    half_width = HD // 2
    inverse = ROPE_BASE ** (-(jnp.arange(half_width, dtype=F32) * 2.0 / HD))
    angles = position.astype(F32)[:, None] * inverse[None, :]
    cosine, sine = jnp.cos(angles), jnp.sin(angles)
    return (
        jnp.concatenate([cosine, cosine], axis=1),
        jnp.concatenate([-sine, sine], axis=1),
    )


def rotate(values, cosine, sine):
    half_width = values.shape[-1] // 2
    swapped = jnp.concatenate([values[..., half_width:], values[..., :half_width]], axis=-1)
    return values * cosine + swapped * sine


def norm_forward(values, gain_vector):
    rms_scale = lax.rsqrt(jnp.mean(values * values, axis=1, keepdims=True) + EPSILON)
    return (values * rms_scale * gain_vector, rms_scale)


def norm_backward(values, rms_scale, gain_vector, gradient):
    weighted = gradient * gain_vector
    gain_grad = jnp.sum(gradient * values * rms_scale, axis=0)
    inner_mean = jnp.mean(weighted * values, axis=1, keepdims=True)
    return (rms_scale * weighted - values * rms_scale**3 * inner_mean, gain_grad)


def local(
    inputs,
    out_grad,
    q_weight,
    q_bias,
    kv_weight,
    kv_bias,
    out_weight,
    attn_gain,
    ffn_gain,
    gate_weight,
    up_weight,
    down_weight,
    block_order,
    long_docs,
    short_docs,
):
    seq, head = SeqAxis(), HeadAxis()
    local_rows, depth = inputs.shape
    span_rows = local_rows * head.size
    wide = KV * HD * 2
    half = depth // 2
    pieces = seq.size // 2

    inputs16, cotangent16 = shuffle(seq.order, inputs, out_grad)
    grad_all = lax.all_gather(cotangent16, "head", axis=0, tiled=True)
    q_a, q_b = seq.gather(head.gather_small(q_weight, 1))
    out_a, out_b = seq.gather(head.gather_small(out_weight, 0), axis=1)

    kv_rows_each = kv_weight.shape[0]
    sizes = [q_bias.shape[0], kv_bias.shape[0], attn_gain.shape[0], ffn_gain.shape[0]]
    cuts = [sum(sizes[:i]) for i in range(5)]
    padded = -(-(kv_rows_each + 1) // 16) * 16
    strip = jnp.concatenate([q_bias, kv_bias, attn_gain, ffn_gain])
    strip = jnp.pad(strip[None, :], ((0, padded - kv_rows_each - 1), (0, wide - strip.shape[0])))
    pack = jnp.concatenate([kv_weight, strip], axis=0)
    pack_all = jnp.concatenate(seq.gather(head.gather_small(pack, 0), ordered=False), axis=0)
    pack_all = pack_all.reshape(seq.size, head.size, padded, wide)
    kv_full = pack_all[:, :, :kv_rows_each].reshape(depth, wide)
    strips = pack_all[:, :, kv_rows_each].astype(F32)

    def part_of(i):
        return strips[:, :, cuts[i] : cuts[i + 1]].reshape(seq.size, -1)

    q_bias_full = part_of(0)[seq.place].reshape(1, -1)
    kv_bias_full = part_of(1)[seq.place].reshape(1, -1)
    attn_gain32 = part_of(2).reshape(1, -1)
    ffn_gain32 = part_of(3).reshape(1, -1)

    lengths = jnp.concatenate([long_docs, short_docs])
    index = jnp.arange(lengths.shape[0], dtype=jnp.int32)
    starts = jnp.sum(jnp.where(index[None, :] < index[:, None], lengths[None, :], 0), axis=1)
    long_total = starts[long_docs.shape[0]]
    row_start = (seq.me * head.size + head.me) * local_rows
    stream = (
        block_order[row_start // BLK] * BLK
        + row_start % BLK
        + jnp.arange(local_rows, dtype=jnp.int32)
    )
    position = jnp.where(stream >= long_total, stream - long_total, stream)
    first = jnp.max(jnp.where(starts[None, :] <= stream[:, None], starts[None, :], 0), axis=1)
    cosine, sine = rope_tables(position)
    blocks = jnp.arange(block_order.shape[0], dtype=jnp.int32)
    storage = jnp.sum(
        jnp.where(block_order[:, None] == blocks[None, :], blocks[:, None], 0), axis=0
    )
    span_blocks = span_rows // BLK
    base = seq.place[storage // span_blocks] * span_rows + storage % span_blocks * BLK
    per_block = BLK // TILE
    offsets = (base[:, None] + jnp.arange(per_block, dtype=jnp.int32)[None, :] * TILE).reshape(-1)
    bounds = jnp.stack([first[0] // TILE, stream[-1] // TILE]).astype(jnp.int32)
    where = (offsets.astype(jnp.int32), bounds)
    tables = (cosine, sine, stream[None, :], first[None, :])

    residual = inputs16.astype(F32)
    normed32, attn_scale = norm_forward(residual, attn_gain32)
    normed = normed32.astype(BF16)
    kv_raw = jnp.dot(normed, kv_full, preferred_element_type=F32) + kv_bias_full
    key_part = rotate(
        kv_raw[:, : KV * HD].reshape(local_rows, KV, HD), cosine[:, None, :], sine[:, None, :]
    )
    kv_rows = jnp.concatenate(
        [key_part.reshape(local_rows, KV * HD), kv_raw[:, KV * HD :]], axis=1
    ).astype(BF16)
    query_raw = (
        jnp.dot(normed[:, :half], q_a, preferred_element_type=F32)
        + jnp.dot(normed[:, half:], q_b, preferred_element_type=F32)
        + q_bias_full
    )
    kv_halves = seq.gather(head.gather_small(kv_rows, 0))
    queries, mixed, lse = attention_forward(*where, query_raw, *tables, *kv_halves)
    hidden = residual + jnp.concatenate(
        [jnp.dot(mixed, part, preferred_element_type=F32) for part in (out_a, out_b)], axis=1
    )
    normed2_32, ffn_scale = norm_forward(hidden, ffn_gain32)
    normed2 = normed2_32.astype(BF16)

    straight = jnp.arange(seq.size, dtype=jnp.int32)
    gate_own, up_own = after((gate_weight.T, up_weight.T), kv_halves[0])
    gate_all = lax.all_gather(gate_own, "seq", axis=0, tiled=False)
    up_all = lax.all_gather(up_own, "seq", axis=0, tiled=False)
    down = [
        half_of.reshape(pieces, -1, depth // seq.size)
        for half_of in seq.gather(after(down_weight, kv_halves[0]))
    ]
    normed2_all = head.gather(normed2)
    act, d_gate, d_up = ffn_middle(seq.order, normed2_all, grad_all, gate_all, up_all, *down)
    d_normed2_terms = ffn_back(seq.order, d_gate, d_up, gate_all, up_all)

    def total(parts):
        return sum(part.astype(F32) for part in parts)

    piece = depth // seq.size

    def by_lane(left, right):
        def mine(received):
            return unit_grad(left, right, straight, 0, pieces, piece, received, True)

        return seq.reduce(mine, unit_grad(left, right, straight, pieces, pieces, piece))

    def whole_grad(left, right):
        return unit_grad(after(left, d_normed2_terms), right, seq.place, 0, seq.size, piece)

    def scattered(whole):
        return lax.psum_scatter(whole, "seq", scatter_dimension=0, tiled=False).astype(F32)

    terms = [
        whole_grad(act, grad_all), whole_grad(d_gate, normed2_all), whole_grad(d_up, normed2_all)
    ]
    d_normed2 = total(head.reduce(d_normed2_terms, terms))
    down_grad, gate_grad, up_grad = (scattered(whole) for whole in terms)
    gate_grad, up_grad = gate_grad.T, up_grad.T

    d_hidden_norm, ffn_gain_grad = norm_backward(hidden, ffn_scale, ffn_gain32, d_normed2)
    d_hidden = cotangent16.astype(F32) + d_hidden_norm
    d_attn = d_hidden.astype(BF16)
    d_mixed = (
        contract(d_attn[:, :half], out_a, 1, 1) + contract(d_attn[:, half:], out_b, 1, 1)
    ).astype(BF16)
    d_queries, d_kv_a, d_kv_b = attention_backward(
        *where, queries, *tables, mixed, d_mixed, lse, *kv_halves
    )

    ffn_terms = ffn_forth(after(act, d_normed2), *down)
    beside = (d_queries, d_kv_a, d_kv_b)
    (output,) = shuffle(seq.place, hidden + total(head.reduce(ffn_terms, beside)))

    def stacked(value):
        return value.reshape(pieces, value.shape[0] // pieces, value.shape[1])

    def adding(value):
        def add(received):
            return list(value if received is None else value + received)

        return add

    d_kv_span = seq.reduce(adding(stacked(d_kv_a)), stacked(d_kv_b))
    d_kv_own = head.reduce_small(d_kv_span.astype(BF16), 0)
    key_back = rotate(
        d_kv_own[:, : KV * HD].reshape(local_rows, KV, HD), cosine[:, None, :], -sine[:, None, :]
    )
    d_kv = jnp.concatenate(
        [key_back.reshape(local_rows, KV * HD), d_kv_own[:, KV * HD :]], axis=1
    ).astype(BF16)
    d_normed = jnp.concatenate(
        [contract(d_queries, part, 1, 1) for part in (q_a, q_b)], axis=1
    ) + contract(d_kv, kv_full, 1, 1)
    d_input_norm, attn_gain_grad = norm_backward(residual, attn_scale, attn_gain32, d_normed)
    (input_grad,) = shuffle(seq.place, d_hidden + d_input_norm)

    out_span = by_lane(mixed, d_attn)
    out_weight_grad = head.reduce_small(out_span.astype(BF16), 0)
    rest = (straight, 0, 1, d_queries.shape[1])

    def q_part(i, received):
        columns = normed[:, i * half : (i + 1) * half]
        if received is not None:
            received = received.reshape(1, half, -1)
        return stacked(unit_grad(columns, d_queries, *rest, received)[0])

    q_span = seq.reduce(lambda received: list(q_part(0, received)), q_part(1, None))
    q_weight_grad = head.reduce_small(q_span.astype(BF16), 1)
    kv_part = contract(normed, d_kv, 0, 0).reshape(seq.size, head.size, kv_rows_each, wide)
    q_bias_part = jnp.sum(d_queries.astype(F32), axis=0).reshape(seq.size, -1)[seq.order]
    kv_bias_part = jnp.sum(d_kv.astype(F32), axis=0).reshape(seq.size, -1)[seq.order]
    strips = jnp.concatenate(
        [
            item.reshape(seq.size, head.size, 1, -1)
            for item in (q_bias_part, kv_bias_part, attn_gain_grad, ffn_gain_grad)
        ],
        axis=3,
    )
    strips = jnp.pad(
        strips,
        ((0, 0), (0, 0), (0, padded - kv_rows_each - 1), (0, wide - strips.shape[3])),
    )
    small = jnp.concatenate([kv_part, strips], axis=2).astype(BF16)
    small = small.reshape(seq.size, head.size * padded, wide)
    small = seq.reduce(adding(small[:pieces]), small[pieces:])
    small = head.reduce_small(small.astype(BF16), 0)
    kv_weight_grad = small[:kv_rows_each]
    tail = small[kv_rows_each]
    q_bias_grad, kv_bias_grad, attn_grad, ffn_grad = (
        tail[cuts[i] : cuts[i + 1]] for i in range(4)
    )
    return (
        output,
        input_grad,
        q_weight_grad,
        q_bias_grad,
        kv_weight_grad,
        kv_bias_grad,
        out_weight_grad,
        attn_grad,
        ffn_grad,
        gate_grad,
        up_grad,
        down_grad,
    )


def solution(mesh):
    in_specs = (
        P(("seq", "head"), None),
        P(("seq", "head"), None),
        P("seq", "head"),
        P(("seq", "head")),
        P(("seq", "head"), None),
        P(("seq", "head")),
        P("head", "seq"),
        P(("seq", "head")),
        P(("seq", "head")),
        P("seq", "head"),
        P("seq", "head"),
        P("head", "seq"),
        P(),
        P(),
        P(),
    )
    out_specs = (
        P(("seq", "head"), None),
        P(("seq", "head"), None),
        P("seq", "head"),
        P(("seq", "head")),
        P(("seq", "head"), None),
        P(("seq", "head")),
        P("head", "seq"),
        P(("seq", "head")),
        P(("seq", "head")),
        P("seq", "head"),
        P("seq", "head"),
        P("head", "seq"),
    )
    return jax.shard_map(local, mesh=mesh, in_specs=in_specs, out_specs=out_specs, check_vma=False)
```

time: 1270 us -> 1020 us (0.80); the launches traced: 1250 us -> 1010 us
  local copies, waits for them, and re-layouts: 197 us -> 56.8 us
  waiting for transfers between devices: 437 us -> 329 us
  matrix products: 126 us -> 38.5 us
  Pallas kernels: 155 us -> 209 us
  starting transfers between devices: 225 us -> 274 us
    ppermute x91 -> x36, waiting for transfers between devices: 257 us -> 124 us  [send(): return lax.ppermute(item, 'seq', pairs)]
    pallas_call x5 -> x17, Pallas kernels: 56.2 us -> 142 us  [the longest x7 69.7 us: unit_grad(): pl.pallas_call(functools.partial(unit_grad_kernel, count, shift, len(extr...]
    dot_general x14 -> x6, matrix products: 95.1 us -> 22.7 us  [contract(): lax.dot_general(left_side, right_side, (((left_dim,), (right_dim,)), ((),...]
    unnamed x212 -> x176, local copies, waits for them, and re-layouts: 93.2 us -> 30.1 us
    ppermute x16 -> x0, local copies, waits for them, and re-layouts: 38.5 us -> none  [swap(): return lax.ppermute(value, 'seq', [(i, i ^ bit) for i in range(self.size)])]
    slice x27 -> x6, local copies, waits for them, and re-layouts: 34.4 us -> 3.49 us  [the longest x1 1.23 us: local(): small = seq.reduce(adding(small[:pieces]), small[pieces:])]
    ppermute x60 -> x39, starting transfers between devices: 135 us -> 164 us  [send(): return lax.ppermute(value, 'head', pairs)]
    ppermute x60 -> x39, waiting for transfers between devices: 180 us -> 204 us  [send(): return lax.ppermute(value, 'head', pairs)]
  transfers between devices with their start and end apart: 151 -> 81, of which waited for: 52 -> 28; matrix products, arithmetic and copies ran while one was open for 31% -> 15% of each run, Pallas kernels for 6% -> 11%
where the time goes in v2:
time: 1020 us; the launch traced here: 1010 us
  waiting for transfers between devices  329 us (32%)
  starting transfers between devices  274 us (27%)
  Pallas kernels  209 us (20%)
  other arithmetic  82.2 us (8%)
  local copies, waits for them, and re-layouts  56.8 us (6%)
  matrix products  38.5 us (4%)
  between operations  24.5 us (2%)
    ppermute x39, waiting for transfers between devices, send(): return lax.ppermute(value, 'head', pairs)  204 us
    ppermute x39, starting transfers between devices, send(): return lax.ppermute(value, 'head', pairs)  164 us
    ppermute x36, waiting for transfers between devices, send(): return lax.ppermute(item, 'seq', pairs)  124 us
    ppermute x36, starting transfers between devices, send(): return lax.ppermute(item, 'seq', pairs)  110 us
    pallas_call x7, Pallas kernels, unit_grad(): pl.pallas_call(functools.partial(unit_grad_kernel, count, shift, len(extr...  69.7 us
    pallas_call x1, Pallas kernels, ffn_middle(): pl.pallas_call(ffn_kernel, out_shape=(jax.ShapeDtypeStruct((rows, units),...  44.2 us
    pallas_call x1, Pallas kernels, ffn_back(): pl.pallas_call(back_kernel, out_shape=jax.ShapeDtypeStruct((rows, pieces...  31.8 us
    unnamed x176, local copies, waits for them, and re-layouts  30.1 us
  transfers between devices with their start and end apart: 81, of which 28 were waited for; matrix products, arithmetic and copies ran while one was open for 15% of the time, Pallas kernels for 11%

profile of v2, /device:TPU:0, one launch (start us, length us, event | category | flops | bytes accessed | tf_op | source)
XLA Modules:
  0.0 1014.1 jit_solution(16922691032018189885)
XLA Ops:
  15.4 3.5 collective-permute-start.8
  34.2 7.5 collective-permute-done.3
  43.7 5.0 collective-permute-done.5
  66.6 32.3 %collective-permute-done.18.refs_2_ = bf16[512,256]{1,0:T(8,128)(2,1)} collective-permute-done((bf16[512,256]{1,0:T(8,128)(2,1)}, bf16[512,256]{1,0:T(8,128)(2,1)}, u32[]{:S(2)}, u32[]{:S(2)}) %collective-permute-start.18) | collective-permute-done | bytes 262176 | tf_op jit(solution)/shard_map/ppermute | solution.py:123
  116.3 4.9 collective-permute-done.12
  123.6 20.3 %collective-permute-start.14 = (bf16[256,512]{1,0:T(8,128)(2,1)S(1)}, bf16[256,512]{1,0:T(8,128)(2,1)S(1)}, u32[]{:S(2)}, u32[]{:S(2)}) collective-permute-start(bf16[256,512]{1,0:T(8,128)(2,1)S(1)} %pad_maximum_fusion.4.refs_0_), channel_id=1, source_target_pairs={{0,1},{1,0},{2,3},{3,2},{4,5},{5,4},{6,7},{7,6},{8,9},{9,8},{10,11... | collective-permute-start | bytes 786440 | tf_op jit(solution)/shard_map/ppermute | solution.py:123
  146.4 6.2 collective-permute-done.14.refs_1_
  152.7 9.4 collective-permute-done.15.refs_2_
  165.6 15.3 %collective-permute-done.23 = bf16[2048,256]{1,0:T(8,128)(2,1)} collective-permute-done((bf16[2048,256]{1,0:T(8,128)(2,1)}, bf16[2048,256]{1,0:T(8,128)(2,1)}, u32[]{:S(2)}, u32[]{:S(2)}) %collective-permute-start.23) | collective-permute-done | bytes 1048608 | tf_op jit(solution)/shard_map/ppermute | solution.py:79
  181.1 7.1 collective-permute-done.21
  188.3 5.0 collective-permute-start.25
  195.9 11.2 %collective-permute-done.25 = bf16[1024,512]{1,0:T(8,128)(2,1)S(1)} collective-permute-done((bf16[1024,512]{1,0:T(8,128)(2,1)S(1)}, bf16[1024,512]{1,0:T(8,128)(2,1)S(1)}, u32[]{:S(2)}, u32[]{:S(2)}) %collective-permute-start.25) | collective-permute-done | bytes 1048608 | tf_op jit(solution)/shard_map/ppermute | solution.py:79
  211.1 3.8 pad_maximum_fusion
  217.0 3.7 pad_maximum_fusion.2
  231.7 19.6 %collective-permute-done.33 = bf16[2752,256]{1,0:T(8,128)(2,1)} collective-permute-done((bf16[2752,256]{1,0:T(8,128)(2,1)}, bf16[2752,256]{1,0:T(8,128)(2,1)}, u32[]{:S(2)}, u32[]{:S(2)}) %collective-permute-start.33) | collective-permute-done | bytes 1409056 | tf_op jit(solution)/shard_map/ppermute | solution.py:79
  251.3 3.4 fusion.41
  254.8 3.5 fusion.2.raw_ref
  265.0 44.0 %collective-permute-done.35 = bf16[2752,256]{1,0:T(8,128)(2,1)S(1)} collective-permute-done((bf16[2752,256]{1,0:T(8,128)(2,1)}, bf16[2752,256]{1,0:T(8,128)(2,1)S(1)}, u32[]{:S(2)}, u32[]{:S(2)}) %collective-permute-start.35) | collective-permute-done | bytes 1409056 | tf_op jit(solution)/shard_map/ppermute | solution.py:79
  311.0 7.9 attention_forward.1
  319.0 4.7 fusion.53
  327.9 11.5 %collective-permute-start.28 = (bf16[256,2048]{1,0:T(8,128)(2,1)S(1)}, bf16[256,2048]{1,0:T(8,128)(2,1)S(1)}, u32[]{:S(2)}, u32[]{:S(2)}) collective-permute-start(bf16[256,2048]{1,0:T(8,128)(2,1)S(1)} %multiply_convert_fusion.refs_0_), channel_id=1, source_target_pairs={{0,1},{1,0},{2,3},{3,2},{4,5},{5,4},{6,7},{7,6},{8,9},{9,8},{10,11... | collective-permute-start | bytes 3145736 | tf_op jit(solution)/shard_map/ppermute | solution.py:123
  341.0 21.8 %collective-permute-done.28.refs_1_ = bf16[256,2048]{1,0:T(8,128)(2,1)S(1)} collective-permute-done((bf16[256,2048]{1,0:T(8,128)(2,1)S(1)}, bf16[256,2048]{1,0:T(8,128)(2,1)S(1)}, u32[]{:S(2)}, u32[]{:S(2)}) %collective-permute-start.28) | collective-permute-done | bytes 1048608 | tf_op jit(solution)/shard_map/ppermute | solution.py:123
  368.4 23.1 %collective-permute-done.30 = bf16[256,2048]{1,0:T(8,128)(2,1)} collective-permute-done((bf16[256,2048]{1,0:T(8,128)(2,1)}, bf16[256,2048]{1,0:T(8,128)(2,1)}, u32[]{:S(2)}, u32[]{:S(2)}) %collective-permute-start.30) | collective-permute-done | bytes 1048608 | tf_op jit(solution)/shard_map/ppermute | solution.py:123
  393.8 20.5 %collective-permute-done.32 = bf16[256,2048]{1,0:T(8,128)(2,1)} collective-permute-done((bf16[256,2048]{1,0:T(8,128)(2,1)}, bf16[256,2048]{1,0:T(8,128)(2,1)}, u32[]{:S(2)}, u32[]{:S(2)}) %collective-permute-start.32) | collective-permute-done | bytes 1048608 | tf_op jit(solution)/shard_map/ppermute | solution.py:123
  416.6 4.4 place.9.normed_ref.right_ref
  423.3 44.2 %ffn_middle.1 = (bf16[1024,2752]{1,0:T(8,128)(2,1)}, bf16[1024,2752]{1,0:T(8,128)(2,1)}, bf16[1024,2752]{1,0:T(8,128)(2,1)}) custom-call(s32[8]{0:T(128)S(1)} %copy-done.16, bf16[1024,2048]{1,0:T(8,128)(2,1)S(1)} %copy-done.8, bf16[1024,2048]{1,0:T(8,128)(2,1)} %all-gather.6.cloned.1.call-done.grad_ref.right_ref, bf16[8,2752,256]{2,1,0:T(8,128)(2,1)} %bitcast.162, ...), custom_call_target="tpu_custom_call" | custom-call | flops 34628173824 | bytes 59113472 | tf_op jit(solution)/shard_map/ffn_middle/pallas_call | solution.py:481
  467.4 31.8 %ffn_back.1 = bf16[1024,2048]{1,0:T(8,128)(2,1)S(1)} custom-call(s32[8]{0:T(128)S(1)} %copy-done.16, bf16[1024,2752]{1,0:T(8,128)(2,1)} %get-tuple-element.85.d_gate_ref.left_ref, bf16[1024,2752]{1,0:T(8,128)(2,1)} %get-tuple-element.87.d_up_ref.left_ref, bf16[8,2752,256]{2,1,0:T(8,128)(2,1)} %bitcast.163, bf16[8,2752,256]{2,1,0:T(8,128)(2,1)} %bitcast.165), custom_call_target="tpu_custom_call" | custom-call | flops 23085449216 | bytes 33816576 | tf_op jit(solution)/shard_map/ffn_back/pallas_call | solution.py:511
  501.2 17.5 %unit_grad.9 = bf16[8,2752,256]{2,1,0:T(8,128)(2,1)} custom-call(s32[8]{0:T(128)S(1)} %select_reduce_fusion.3.order_ref, bf16[1024,2752]{1,0:T(8,128)(2,1)} %get-tuple-element.87.d_up_ref.left_ref, bf16[1024,2048]{1,0:T(8,128)(2,1)S(1)} %copy-done.9), custom_call_target="tpu_custom_call" | custom-call | flops 11542724608 | bytes 21102592 | tf_op jit(solution)/shard_map/unit_grad/pallas_call | solution.py:590
  521.0 17.6 %unit_grad.8 = bf16[8,2752,256]{2,1,0:T(8,128)(2,1)} custom-call(s32[8]{0:T(128)S(1)} %select_reduce_fusion.3.order_ref, bf16[1024,2752]{1,0:T(8,128)(2,1)} %get-tuple-element.85.d_gate_ref.left_ref, bf16[1024,2048]{1,0:T(8,128)(2,1)S(1)} %copy-done.10), custom_call_target="tpu_custom_call" | custom-call | flops 11542724608 | bytes 21102592 | tf_op jit(solution)/shard_map/unit_grad/pallas_call | solution.py:590
  547.2 17.7 %unit_grad.7 = bf16[8,2752,256]{2,1,0:T(8,128)(2,1)} custom-call(s32[8]{0:T(128)S(1)} %select_reduce_fusion.3.order_ref, bf16[1024,2752]{1,0:T(8,128)(2,1)} %get-tuple-element.90.left_ref.act_ref, bf16[1024,2048]{1,0:T(8,128)(2,1)S(1)} %copy-done.18), custom_call_target="tpu_custom_call" | custom-call | flops 11542724608 | bytes 21102592 | tf_op jit(solution)/shard_map/unit_grad/pallas_call | solution.py:590
  573.1 24.1 %collective-permute-start.40 = (bf16[256,2048]{1,0:T(8,128)(2,1)S(1)}, bf16[256,2048]{1,0:T(8,128)(2,1)S(1)}, u32[]{:S(2)}, u32[]{:S(2)}) collective-permute-start(bf16[256,2048]{1,0:T(8,128)(2,1)S(1)} %get-tuple-element.89), channel_id=1, source_target_pairs={{0,1},{3,2},{4,5},{7,6},{8,9},{11,10},{12,13},{15,14},{16,17},{19,... | collective-permute-start | bytes 3145736 | tf_op jit(solution)/shard_map/ppermute | solution.py:123
  597.3 23.5 %collective-permute-done.40 = bf16[256,2048]{1,0:T(8,128)(2,1)S(1)} collective-permute-done((bf16[256,2048]{1,0:T(8,128)(2,1)S(1)}, bf16[256,2048]{1,0:T(8,128)(2,1)S(1)}, u32[]{:S(2)}, u32[]{:S(2)}) %collective-permute-start.40) | collective-permute-done | bytes 1048608 | tf_op jit(solution)/shard_map/ppermute | solution.py:123
  624.6 13.7 %collective-permute-done.39 = bf16[256,2048]{1,0:T(8,128)(2,1)S(1)} collective-permute-done((bf16[256,2048]{1,0:T(8,128)(2,1)}, bf16[256,2048]{1,0:T(8,128)(2,1)S(1)}, u32[]{:S(2)}, u32[]{:S(2)}) %collective-permute-start.39) | collective-permute-done | bytes 1048608 | tf_op jit(solution)/shard_map/ppermute | solution.py:123
  641.2 3.6 fusion.46
  644.9 3.8 fusion.21
  648.7 5.3 fusion.3.grad_ref
  654.0 15.0 %attention_backward.1 = (bf16[256,2048]{1,0:T(8,128)(2,1)}, bf16[4096,512]{1,0:T(8,128)(2,1)}, bf16[4096,512]{1,0:T(8,128)(2,1)}) custom-call(s32[16]{0:T(128)} %copy-done.21, s32[2]{0:T(128)} %copy-done.20, bf16[16,256,128]{2,1,0:T(8,128)(2,1)} %copy-done.22, f32[256,128]{1,0:T(8,128)} %copy-done.14, f32[256,128]{1,0:T(8,128)} %copy-done.15, ...), custom_call_target="tpu_custom_call" | custom-call | flops 10737418240 | bytes 20971520 | tf_op jit(solution)/shard_map/attention_backward/pallas_call | solution.py:418
  669.1 17.7 %ffn_forth.1 = bf16[1024,2048]{1,0:T(8,128)(2,1)S(1)} custom-call(bf16[1024,2752]{1,0:T(8,128)(2,1)} %get-tuple-element.90.left_ref.act_ref, bf16[4,2752,256]{2,1,0:T(8,128)(2,1)} %bitcast.18.down_a_ref, bf16[4,2752,256]{2,1,0:T(8,128)(2,1)} %bitcast.19.down_b_ref), custom_call_target="tpu_custom_call" | custom-call | flops 11542724608 | bytes 16908288 | tf_op jit(solution)/shard_map/ffn_forth/pallas_call | solution.py:542
  687.9 5.6 collective-permute-start.42
  694.4 4.0 unit_grad.12
  698.7 3.4 unit_grad.10
  702.5 13.5 %collective-permute-done.42 = bf16[256,2048]{1,0:T(8,128)(2,1)} collective-permute-done((bf16[256,2048]{1,0:T(8,128)(2,1)}, bf16[256,2048]{1,0:T(8,128)(2,1)}, u32[]{:S(2)}, u32[]{:S(2)}) %collective-permute-start.42) | collective-permute-done | bytes 1048608 | tf_op jit(solution)/shard_map/ppermute | solution.py:123
  718.3 3.4 add.375
  724.5 28.4 %collective-permute-start.49 = (bf16[1024,512]{1,0:T(8,128)(2,1)}, bf16[1024,512]{1,0:T(8,128)(2,1)}, u32[]{:S(2)}, u32[]{:S(2)}) collective-permute-start(bf16[1024,512]{1,0:T(8,128)(2,1)} %get-tuple-element.101), channel_id=1, source_target_pairs={{0,16},{4,12},{8,24},{12,4},{16,0},{20,28},{24,8},{28,20},{1,17},{... | collective-permute-start | bytes 3145736 | tf_op jit(solution)/shard_map/ppermute | solution.py:79
  754.4 43.8 %collective-permute-start.44 = (bf16[256,2048]{1,0:T(8,128)(2,1)}, bf16[256,2048]{1,0:T(8,128)(2,1)}, u32[]{:S(2)}, u32[]{:S(2)}) collective-permute-start(bf16[256,2048]{1,0:T(8,128)(2,1)} %get-tuple-element.133), channel_id=1, source_target_pairs={{0,1},{1,0},{2,3},{3,2},{4,5},{5,4},{6,7},{7,6},{8,9},{9,8},{10,11... | collective-permute-start | bytes 3145736 | tf_op jit(solution)/shard_map/ppermute | solution.py:123
  802.8 8.4 collective-permute-done.44
  811.3 9.3 collective-permute-start.50
  820.6 4.5 fusion.55
  825.1 4.4 fusion.56
  832.8 5.8 unit_grad.13
  839.6 10.8 %collective-permute-start.56 = (bf16[2048,256]{1,0:T(8,128)(2,1)S(1)}, bf16[2048,256]{1,0:T(8,128)(2,1)S(1)}, u32[]{:S(2)}, u32[]{:S(2)}) collective-permute-start(bf16[2048,256]{1,0:T(8,128)(2,1)S(1)} %get-tuple-element.105), channel_id=1, source_target_pairs={{0,16},{4,12},{8,24},{12,4},{16,0},{20,28},{24,8},{28,20},{1,17},{... | collective-permute-start | bytes 3145736 | tf_op jit(solution)/shard_map/ppermute | solution.py:79
  850.5 3.7 unit_grad.11
  856.7 4.8 collective-permute-start.51
  866.9 11.1 %collective-permute-start.57 = (bf16[2048,256]{1,0:T(8,128)(2,1)}, bf16[2048,256]{1,0:T(8,128)(2,1)}, u32[]{:S(2)}, u32[]{:S(2)}) collective-permute-start(bf16[2048,256]{1,0:T(8,128)(2,1)} %add.389), channel_id=1, source_target_pairs={{0,8},{4,20},{8,0},{12,28},{16,24},{20,4},{24,16},{28,12},{1,9},{5... | collective-permute-start | bytes 3145736 | tf_op jit(solution)/shard_map/ppermute | solution.py:79
  878.2 9.5 collective-permute-done.52
  889.9 3.9 fusion.12
  897.9 3.8 add_add_fusion.refs_0_
  911.1 3.8 collective-permute-start.72
  922.5 9.5 collective-permute-start.61
  946.0 15.4 %collective-permute-start.68 = (bf16[320,512]{1,0:T(8,128)(2,1)S(1)}, bf16[320,512]{1,0:T(8,128)(2,1)S(1)}, u32[]{:S(2)}, u32[]{:S(2)}) collective-permute-start(bf16[320,512]{1,0:T(8,128)(2,1)S(1)} %fusion.24), channel_id=1, source_target_pairs={{0,8},{4,20},{8,0},{12,28},{16,24},{20,4},{24,16},{28,12},{1,9},{5... | collective-permute-start | bytes 983048 | tf_op jit(solution)/shard_map/ppermute | solution.py:79
  963.6 3.5 collective-permute-start.62
  972.9 3.9 collective-permute-done.62
  979.2 10.8 %collective-permute-done.63 = bf16[256,512]{1,0:T(8,128)(2,1)S(1)} collective-permute-done((bf16[256,512]{1,0:T(8,128)(2,1)S(1)}, bf16[256,512]{1,0:T(8,128)(2,1)S(1)}, u32[]{:S(2)}, u32[]{:S(2)}) %collective-permute-start.63) | collective-permute-done | bytes 262176 | tf_op jit(solution)/shard_map/ppermute | solution.py:123
  990.9 4.6 collective-permute-done.70
  (438 shorter events, 220.7 us)
Async XLA Ops:
  7.2 413.8 %all-gather.6.cloned.1.call-start = ((), (), s32[]{:S(2)}) async-start(), calls=%async_computation.3 | async-start | bytes 5242880 | tf_op jit(solution)/shard_map/all_gather | solution.py:670
  8.9 18.8 %collective-permute-start = (bf16[80,512]{1,0:T(8,128)(2,1)S(1)}, bf16[80,512]{1,0:T(8,128)(2,1)S(1)}, u32[]{:S(2)}, u32[]{:S(2)}) collective-permute-start(bf16[80,512]{1,0:T(8,128)(2,1)S(1)} %fusion.28.refs_0_), channel_id=1, source_target_pairs={{0,1},{1,0},{2,3},{3,2},{4,5},{5,4},{6,7},{7,6},{8,9},{9,8},{10,11... | collective-permute-start | bytes 245768 | tf_op jit(solution)/shard_map/ppermute | solution.py:123
  14.5 37.6 %collective-permute-start.7 = (bf16[256,512]{1,0:T(8,128)(2,1)}, bf16[256,512]{1,0:T(8,128)(2,1)S(1)}, u32[]{:S(2)}, u32[]{:S(2)}) collective-permute-start(bf16[256,512]{1,0:T(8,128)(2,1)} %refs_0_.4), channel_id=1, source_target_pairs={{0,1},{1,0},{2,3},{3,2},{4,5},{5,4},{6,7},{7,6},{8,9},{9,8},{10,11... | collective-permute-start | bytes 786440 | tf_op jit(solution)/shard_map/ppermute | solution.py:123
  15.4 38.2 %collective-permute-start.8 = (bf16[256,512]{1,0:T(8,128)(2,1)}, bf16[256,512]{1,0:T(8,128)(2,1)S(1)}, u32[]{:S(2)}, u32[]{:S(2)}) collective-permute-start(bf16[256,512]{1,0:T(8,128)(2,1)} %refs_0_.4), channel_id=1, source_target_pairs={{0,2},{1,3},{2,0},{3,1},{4,6},{5,7},{6,4},{7,5},{8,10},{9,11},{10,... | collective-permute-start | bytes 786440 | tf_op jit(solution)/shard_map/ppermute | solution.py:123
  23.4 397.6 %all-gather.8.cloned.1.call-start = ((), (), s32[]{:S(2)}) async-start(), calls=%async_computation.7 | async-start | bytes 12681216 | tf_op jit(solution)/shard_map/all_gather | solution.py:744
  27.6 26.0 %collective-permute-start.9 = (bf16[256,512]{1,0:T(8,128)(2,1)S(1)}, bf16[256,512]{1,0:T(8,128)(2,1)S(1)}, u32[]{:S(2)}, u32[]{:S(2)}) collective-permute-start(bf16[256,512]{1,0:T(8,128)(2,1)S(1)} %copy-done.59), channel_id=1, source_target_pairs={{0,3},{1,2},{2,1},{3,0},{4,7},{5,6},{6,5},{7,4},{8,11},{9,10},{10,... | collective-permute-start | bytes 786440 | tf_op jit(solution)/shard_map/ppermute | solution.py:123
  43.2 19.4 %collective-permute-start.17 = (bf16[512,256]{1,0:T(8,128)(2,1)}, bf16[512,256]{1,0:T(8,128)(2,1)S(1)}, u32[]{:S(2)}, u32[]{:S(2)}) collective-permute-start(bf16[512,256]{1,0:T(8,128)(2,1)} %refs_0_.5), channel_id=1, source_target_pairs={{0,1},{1,0},{2,3},{3,2},{4,5},{5,4},{6,7},{7,6},{8,9},{9,8},{10,11... | collective-permute-start | bytes 786440 | tf_op jit(solution)/shard_map/ppermute | solution.py:123
  51.6 53.8 %collective-permute-start.6 = (bf16[1280,512]{1,0:T(8,128)(2,1)}, bf16[1280,512]{1,0:T(8,128)(2,1)}, u32[]{:S(2)}, u32[]{:S(2)}) collective-permute-start(bf16[1280,512]{1,0:T(8,128)(2,1)} %pad_maximum_fusion.3), channel_id=1, source_target_pairs={{0,4},{4,0},{8,12},{12,8},{16,20},{20,16},{24,28},{28,24},{1,5},{5... | collective-permute-start | bytes 3932168 | tf_op jit(solution)/shard_map/ppermute | solution.py:79
  52.2 46.8 %collective-permute-start.18 = (bf16[512,256]{1,0:T(8,128)(2,1)}, bf16[512,256]{1,0:T(8,128)(2,1)}, u32[]{:S(2)}, u32[]{:S(2)}) collective-permute-start(bf16[512,256]{1,0:T(8,128)(2,1)} %refs_0_.5), channel_id=1, source_target_pairs={{0,2},{1,3},{2,0},{3,1},{4,6},{5,7},{6,4},{7,5},{8,10},{9,11},{10,... | collective-permute-start | bytes 786440 | tf_op jit(solution)/shard_map/ppermute | solution.py:123
  57.3 45.0 %collective-permute-start.11 = (bf16[256,2048]{1,0:T(8,128)(2,1)}, bf16[256,2048]{1,0:T(8,128)(2,1)}, u32[]{:S(2)}, u32[]{:S(2)}) collective-permute-start(bf16[256,2048]{1,0:T(8,128)(2,1)} %place.6), channel_id=1, source_target_pairs={{0,16},{4,12},{8,24},{12,4},{16,0},{20,28},{24,8},{28,20},{1,17},{... | collective-permute-start | bytes 3145736 | tf_op jit(solution)/shard_map/ppermute | solution.py:79
  57.5 46.3 %collective-permute-start.10 = (bf16[256,2048]{1,0:T(8,128)(2,1)}, bf16[256,2048]{1,0:T(8,128)(2,1)}, u32[]{:S(2)}, u32[]{:S(2)}) collective-permute-start(bf16[256,2048]{1,0:T(8,128)(2,1)} %place.6), channel_id=1, source_target_pairs={{0,8},{4,20},{8,0},{12,28},{16,24},{20,4},{24,16},{28,12},{1,9},{5... | collective-permute-start | bytes 3145736 | tf_op jit(solution)/shard_map/ppermute | solution.py:79
  62.6 36.4 %collective-permute-start.19 = (bf16[512,256]{1,0:T(8,128)(2,1)}, bf16[512,256]{1,0:T(8,128)(2,1)}, u32[]{:S(2)}, u32[]{:S(2)}) collective-permute-start(bf16[512,256]{1,0:T(8,128)(2,1)} %refs_0_.5), channel_id=1, source_target_pairs={{0,3},{1,2},{2,1},{3,0},{4,7},{5,6},{6,5},{7,4},{8,11},{9,10},{10,... | collective-permute-start | bytes 786440 | tf_op jit(solution)/shard_map/ppermute | solution.py:123
  102.3 62.7 %collective-permute-start.22 = (bf16[2048,256]{1,0:T(8,128)(2,1)}, bf16[2048,256]{1,0:T(8,128)(2,1)}, u32[]{:S(2)}, u32[]{:S(2)}) collective-permute-start(bf16[2048,256]{1,0:T(8,128)(2,1)} %place.8), channel_id=1, source_target_pairs={{0,8},{4,20},{8,0},{12,28},{16,24},{20,4},{24,16},{28,12},{1,9},{5... | collective-permute-start | bytes 3145736 | tf_op jit(solution)/shard_map/ppermute | solution.py:79
  121.1 43.9 %collective-permute-start.20 = (bf16[2048,256]{1,0:T(8,128)(2,1)}, bf16[2048,256]{1,0:T(8,128)(2,1)}, u32[]{:S(2)}, u32[]{:S(2)}) collective-permute-start(bf16[2048,256]{1,0:T(8,128)(2,1)} %place.8), channel_id=1, source_target_pairs={{0,16},{4,12},{8,24},{12,4},{16,0},{20,28},{24,8},{28,20},{1,17},{... | collective-permute-start | bytes 3145736 | tf_op jit(solution)/shard_map/ppermute | solution.py:79
  123.6 29.1 %collective-permute-start.14 = (bf16[256,512]{1,0:T(8,128)(2,1)S(1)}, bf16[256,512]{1,0:T(8,128)(2,1)S(1)}, u32[]{:S(2)}, u32[]{:S(2)}) collective-permute-start(bf16[256,512]{1,0:T(8,128)(2,1)S(1)} %pad_maximum_fusion.4.refs_0_), channel_id=1, source_target_pairs={{0,1},{1,0},{2,3},{3,2},{4,5},{5,4},{6,7},{7,6},{8,9},{9,8},{10,11... | collective-permute-start | bytes 786440 | tf_op jit(solution)/shard_map/ppermute | solution.py:123
  143.9 18.2 %collective-permute-start.15 = (bf16[256,512]{1,0:T(8,128)(2,1)S(1)}, bf16[256,512]{1,0:T(8,128)(2,1)S(1)}, u32[]{:S(2)}, u32[]{:S(2)}) collective-permute-start(bf16[256,512]{1,0:T(8,128)(2,1)S(1)} %pad_maximum_fusion.4.refs_0_), channel_id=1, source_target_pairs={{0,2},{1,3},{2,0},{3,1},{4,6},{5,7},{6,4},{7,5},{8,10},{9,11},{10,... | collective-permute-start | bytes 786440 | tf_op jit(solution)/shard_map/ppermute | solution.py:123
  145.1 17.7 %collective-permute-start.16 = (bf16[256,512]{1,0:T(8,128)(2,1)S(1)}, bf16[256,512]{1,0:T(8,128)(2,1)}, u32[]{:S(2)}, u32[]{:S(2)}) collective-permute-start(bf16[256,512]{1,0:T(8,128)(2,1)S(1)} %pad_maximum_fusion.4.refs_0_), channel_id=1, source_target_pairs={{0,3},{1,2},{2,1},{3,0},{4,7},{5,6},{6,5},{7,4},{8,11},{9,10},{10,... | collective-permute-start | bytes 786440 | tf_op jit(solution)/shard_map/ppermute | solution.py:123
  165.0 23.3 %collective-permute-start.21 = (bf16[1024,512]{1,0:T(8,128)(2,1)}, bf16[1024,512]{1,0:T(8,128)(2,1)S(1)}, u32[]{:S(2)}, u32[]{:S(2)}) collective-permute-start(bf16[1024,512]{1,0:T(8,128)(2,1)} %place.7), channel_id=1, source_target_pairs={{0,8},{4,20},{8,0},{12,28},{16,24},{20,4},{24,16},{28,12},{1,9},{5... | collective-permute-start | bytes 3145736 | tf_op jit(solution)/shard_map/ppermute | solution.py:79
  188.3 18.8 %collective-permute-start.25 = (bf16[1024,512]{1,0:T(8,128)(2,1)S(1)}, bf16[1024,512]{1,0:T(8,128)(2,1)S(1)}, u32[]{:S(2)}, u32[]{:S(2)}) collective-permute-start(bf16[1024,512]{1,0:T(8,128)(2,1)S(1)} %collective-permute-done.21), channel_id=1, source_target_pairs={{0,16},{4,12},{8,24},{12,4},{16,0},{20,28},{24,8},{28,20},{1,17},{... | collective-permute-start | bytes 3145736 | tf_op jit(solution)/shard_map/ppermute | solution.py:79
  210.3 210.7 %all-gather.10.cloned.1.call-start = ((), (), s32[]{:S(2)}) async-start(), calls=%async_computation.8 | async-start | bytes 12681216 | tf_op jit(solution)/shard_map/all_gather | solution.py:745
  211.1 786.3 %reduce-scatter.6.cloned.1.call-start = ((), (), s32[]{:S(2)}) async-start(), calls=%async_computation.5 | async-start | bytes 12681216 | tf_op jit(solution)/shard_map/reduce_scatter | solution.py:769
  215.0 36.4 %collective-permute-start.13 = (bf16[1024,2048]{1,0:T(8,128)(2,1)}, bf16[1024,2048]{1,0:T(8,128)(2,1)}, u32[]{:S(2)}, u32[]{:S(2)}) collective-permute-start(bf16[1024,2048]{1,0:T(8,128)(2,1)} %pad_maximum_fusion), channel_id=1, source_target_pairs={{0,4},{4,0},{8,12},{12,8},{16,20},{20,16},{24,28},{28,24},{1,5},{5... | collective-permute-start | bytes 12582920 | tf_op jit(solution)/shard_map/ppermute | solution.py:79
  215.0 95.9 %collective-permute-start.26 = (bf16[4096,512]{1,0:T(8,128)(2,1)}, bf16[4096,512]{1,0:T(8,128)(2,1)}, u32[]{:S(2)}, u32[]{:S(2)}) collective-permute-start(bf16[4096,512]{1,0:T(8,128)(2,1)} %pad_maximum_fusion.1.half_a_ref), channel_id=1, source_target_pairs={{0,4},{4,0},{8,12},{12,8},{16,20},{20,16},{24,28},{28,24},{1,5},{5... | collective-permute-start | bytes 12582920 | tf_op jit(solution)/shard_map/ppermute | solution.py:79
  215.5 35.8 %collective-permute-start.33 = (bf16[2752,256]{1,0:T(8,128)(2,1)}, bf16[2752,256]{1,0:T(8,128)(2,1)}, u32[]{:S(2)}, u32[]{:S(2)}) collective-permute-start(bf16[2752,256]{1,0:T(8,128)(2,1)} %param.29), channel_id=1, source_target_pairs={{0,8},{4,20},{8,0},{12,28},{16,24},{20,4},{24,16},{28,12},{1,9},{5... | collective-permute-start | bytes 4227080 | tf_op jit(solution)/shard_map/ppermute | solution.py:79
  220.7 103.1 %collective-permute-start.27 = (bf16[2048,1024]{1,0:T(8,128)(2,1)}, bf16[2048,1024]{1,0:T(8,128)(2,1)}, u32[]{:S(2)}, u32[]{:S(2)}) collective-permute-start(bf16[2048,1024]{1,0:T(8,128)(2,1)} %pad_maximum_fusion.2), channel_id=1, source_target_pairs={{0,4},{4,0},{8,12},{12,8},{16,20},{20,16},{24,28},{28,24},{1,5},{5... | collective-permute-start | bytes 12582920 | tf_op jit(solution)/shard_map/ppermute | solution.py:79
  228.8 35.0 %collective-permute-start.34 = (bf16[2752,256]{1,0:T(8,128)(2,1)}, bf16[2752,256]{1,0:T(8,128)(2,1)S(1)}, u32[]{:S(2)}, u32[]{:S(2)}) collective-permute-start(bf16[2752,256]{1,0:T(8,128)(2,1)} %param.29), channel_id=1, source_target_pairs={{0,16},{4,12},{8,24},{12,4},{16,0},{20,28},{24,8},{28,20},{1,17},{... | collective-permute-start | bytes 4227080 | tf_op jit(solution)/shard_map/ppermute | solution.py:79
  251.3 57.7 %collective-permute-start.35 = (bf16[2752,256]{1,0:T(8,128)(2,1)}, bf16[2752,256]{1,0:T(8,128)(2,1)S(1)}, u32[]{:S(2)}, u32[]{:S(2)}) collective-permute-start(bf16[2752,256]{1,0:T(8,128)(2,1)} %collective-permute-done.33), channel_id=1, source_target_pairs={{0,16},{4,12},{8,24},{12,4},{16,0},{20,28},{24,8},{28,20},{1,17},{... | collective-permute-start | bytes 4227080 | tf_op jit(solution)/shard_map/ppermute | solution.py:79
  310.3 110.8 %collective-permute-start.36 = (bf16[11008,256]{1,0:T(8,128)(2,1)}, bf16[11008,256]{1,0:T(8,128)(2,1)}, u32[]{:S(2)}, u32[]{:S(2)}) collective-permute-start(bf16[11008,256]{1,0:T(8,128)(2,1)} %constant_dynamic-update-slice_fusion.5), channel_id=1, source_target_pairs={{0,4},{4,0},{8,12},{12,8},{16,20},{20,16},{24,28},{28,24},{1,5},{5... | collective-permute-start | bytes 16908296 | tf_op jit(solution)/shard_map/ppermute | solution.py:79
  327.9 34.9 %collective-permute-start.28 = (bf16[256,2048]{1,0:T(8,128)(2,1)S(1)}, bf16[256,2048]{1,0:T(8,128)(2,1)S(1)}, u32[]{:S(2)}, u32[]{:S(2)}) collective-permute-start(bf16[256,2048]{1,0:T(8,128)(2,1)S(1)} %multiply_convert_fusion.refs_0_), channel_id=1, source_target_pairs={{0,1},{1,0},{2,3},{3,2},{4,5},{5,4},{6,7},{7,6},{8,9},{9,8},{10,11... | collective-permute-start | bytes 3145736 | tf_op jit(solution)/shard_map/ppermute | solution.py:123
  339.4 25.1 %collective-permute-start.29 = (bf16[256,2048]{1,0:T(8,128)(2,1)S(1)}, bf16[256,2048]{1,0:T(8,128)(2,1)}, u32[]{:S(2)}, u32[]{:S(2)}) collective-permute-start(bf16[256,2048]{1,0:T(8,128)(2,1)S(1)} %multiply_convert_fusion.refs_0_), channel_id=1, source_target_pairs={{1,2},{2,1},{5,6},{6,5},{9,10},{10,9},{13,14},{14,13},{17,18},{18,... | collective-permute-start | bytes 3145736 | tf_op jit(solution)/shard_map/ppermute | solution.py:123
  364.5 26.9 %collective-permute-start.30 = (bf16[256,2048]{1,0:T(8,128)(2,1)}, bf16[256,2048]{1,0:T(8,128)(2,1)}, u32[]{:S(2)}, u32[]{:S(2)}) collective-permute-start(bf16[256,2048]{1,0:T(8,128)(2,1)} %collective-permute-done.29), channel_id=1, source_target_pairs={{1,0},{2,3},{5,4},{6,7},{9,8},{10,11},{13,12},{14,15},{17,16},{18,... | collective-permute-start | bytes 3145736 | tf_op jit(solution)/shard_map/ppermute | solution.py:123
  365.8 48.5 %collective-permute-start.32 = (bf16[256,2048]{1,0:T(8,128)(2,1)}, bf16[256,2048]{1,0:T(8,128)(2,1)}, u32[]{:S(2)}, u32[]{:S(2)}) collective-permute-start(bf16[256,2048]{1,0:T(8,128)(2,1)} %collective-permute-done.31), channel_id=1, source_target_pairs={{1,0},{2,3},{5,4},{6,7},{9,8},{10,11},{13,12},{14,15},{17,16},{18,... | collective-permute-start | bytes 3145736 | tf_op jit(solution)/shard_map/ppermute | solution.py:123
  518.8 481.8 %reduce-scatter.4.cloned.1.call-start = ((), (), s32[]{:S(2)}) async-start(), calls=%async_computation.4 | async-start | bytes 12681216 | tf_op jit(solution)/shard_map/reduce_scatter | solution.py:769
  538.6 465.1 %reduce-scatter.8.cloned.1.call-start = ((), (), s32[]{:S(2)}) async-start(), calls=%async_computation.6 | async-start | bytes 12681216 | tf_op jit(solution)/shard_map/reduce_scatter | solution.py:769
  541.4 23.6 %collective-permute-start.37 = (bf16[256,2048]{1,0:T(8,128)(2,1)S(1)}, bf16[256,2048]{1,0:T(8,128)(2,1)}, u32[]{:S(2)}, u32[]{:S(2)}) collective-permute-start(bf16[256,2048]{1,0:T(8,128)(2,1)S(1)} %constant_dynamic-slice_fusion.15), channel_id=1, source_target_pairs={{0,1},{3,2},{4,5},{7,6},{8,9},{11,10},{12,13},{15,14},{16,17},{19,... | collective-permute-start | bytes 3145736 | tf_op jit(solution)/shard_map/ppermute | solution.py:123
  573.1 47.6 %collective-permute-start.40 = (bf16[256,2048]{1,0:T(8,128)(2,1)S(1)}, bf16[256,2048]{1,0:T(8,128)(2,1)S(1)}, u32[]{:S(2)}, u32[]{:S(2)}) collective-permute-start(bf16[256,2048]{1,0:T(8,128)(2,1)S(1)} %get-tuple-element.89), channel_id=1, source_target_pairs={{0,1},{3,2},{4,5},{7,6},{8,9},{11,10},{12,13},{15,14},{16,17},{19,... | collective-permute-start | bytes 3145736 | tf_op jit(solution)/shard_map/ppermute | solution.py:123
  597.2 41.1 %collective-permute-start.39 = (bf16[256,2048]{1,0:T(8,128)(2,1)}, bf16[256,2048]{1,0:T(8,128)(2,1)S(1)}, u32[]{:S(2)}, u32[]{:S(2)}) collective-permute-start(bf16[256,2048]{1,0:T(8,128)(2,1)} %get-tuple-element.135), channel_id=1, source_target_pairs={{0,1},{1,0},{2,3},{3,2},{4,5},{5,4},{6,7},{7,6},{8,9},{9,8},{10,11... | collective-permute-start | bytes 3145736 | tf_op jit(solution)/shard_map/ppermute | solution.py:123
  669.0 49.3 %collective-permute-start.47 = (bf16[4,1024,512]{2,1,0:T(8,128)(2,1)}, bf16[4,1024,512]{2,1,0:T(8,128)(2,1)}, u32[]{:S(2)}, u32[]{:S(2)}) collective-permute-start(bf16[4,1024,512]{2,1,0:T(8,128)(2,1)} %bitcast.166), channel_id=1, source_target_pairs={{0,4},{4,0},{8,12},{12,8},{16,20},{20,16},{24,28},{28,24},{1,5},{5... | collective-permute-start | bytes 12582920 | tf_op jit(solution)/shard_map/ppermute | solution.py:79
  687.9 28.0 %collective-permute-start.42 = (bf16[256,2048]{1,0:T(8,128)(2,1)}, bf16[256,2048]{1,0:T(8,128)(2,1)}, u32[]{:S(2)}, u32[]{:S(2)}) collective-permute-start(bf16[256,2048]{1,0:T(8,128)(2,1)} %constant_dynamic-slice_fusion.13), channel_id=1, source_target_pairs={{0,1},{3,2},{4,5},{7,6},{8,9},{11,10},{12,13},{15,14},{16,17},{19,... | collective-permute-start | bytes 3145736 | tf_op jit(solution)/shard_map/ppermute | solution.py:123
  698.5 134.3 %collective-permute-start.55 = (bf16[4,2048,256]{2,1,0:T(8,128)(2,1)}, bf16[4,2048,256]{2,1,0:T(8,128)(2,1)}, u32[]{:S(2)}, u32[]{:S(2)}) collective-permute-start(bf16[4,2048,256]{2,1,0:T(8,128)(2,1)} %unit_grad.12), channel_id=1, source_target_pairs={{0,4},{4,0},{8,12},{12,8},{16,20},{20,16},{24,28},{28,24},{1,5},{5... | collective-permute-start | bytes 12582920 | tf_op jit(solution)/shard_map/ppermute | solution.py:79
  702.2 148.3 %collective-permute-start.54 = (bf16[4,256,2048]{2,1,0:T(8,128)(2,1)}, bf16[4,256,2048]{2,1,0:T(8,128)(2,1)}, u32[]{:S(2)}, u32[]{:S(2)}) collective-permute-start(bf16[4,256,2048]{2,1,0:T(8,128)(2,1)} %bitcast.30), channel_id=1, source_target_pairs={{0,4},{4,0},{8,12},{12,8},{16,20},{20,16},{24,28},{28,24},{1,5},{5... | collective-permute-start | bytes 12582920 | tf_op jit(solution)/shard_map/ppermute | solution.py:79
  724.5 76.6 %collective-permute-start.49 = (bf16[1024,512]{1,0:T(8,128)(2,1)}, bf16[1024,512]{1,0:T(8,128)(2,1)}, u32[]{:S(2)}, u32[]{:S(2)}) collective-permute-start(bf16[1024,512]{1,0:T(8,128)(2,1)} %get-tuple-element.101), channel_id=1, source_target_pairs={{0,16},{4,12},{8,24},{12,4},{16,0},{20,28},{24,8},{28,20},{1,17},{... | collective-permute-start | bytes 3145736 | tf_op jit(solution)/shard_map/ppermute | solution.py:79
  754.4 56.9 %collective-permute-start.44 = (bf16[256,2048]{1,0:T(8,128)(2,1)}, bf16[256,2048]{1,0:T(8,128)(2,1)}, u32[]{:S(2)}, u32[]{:S(2)}) collective-permute-start(bf16[256,2048]{1,0:T(8,128)(2,1)} %get-tuple-element.133), channel_id=1, source_target_pairs={{0,1},{1,0},{2,3},{3,2},{4,5},{5,4},{6,7},{7,6},{8,9},{9,8},{10,11... | collective-permute-start | bytes 3145736 | tf_op jit(solution)/shard_map/ppermute | solution.py:123
  799.1 30.4 %collective-permute-start.45 = (bf16[256,2048]{1,0:T(8,128)(2,1)S(1)}, bf16[256,2048]{1,0:T(8,128)(2,1)S(1)}, u32[]{:S(2)}, u32[]{:S(2)}) collective-permute-start(bf16[256,2048]{1,0:T(8,128)(2,1)S(1)} %get-tuple-element.99), channel_id=1, source_target_pairs={{0,1},{3,2},{4,5},{7,6},{8,9},{11,10},{12,13},{15,14},{16,17},{19,... | collective-permute-start | bytes 3145736 | tf_op jit(solution)/shard_map/ppermute | solution.py:123
  801.1 38.5 %collective-permute-start.48 = (bf16[1024,512]{1,0:T(8,128)(2,1)}, bf16[1024,512]{1,0:T(8,128)(2,1)S(1)}, u32[]{:S(2)}, u32[]{:S(2)}) collective-permute-start(bf16[1024,512]{1,0:T(8,128)(2,1)} %get-tuple-element.100), channel_id=1, source_target_pairs={{0,16},{4,12},{8,24},{12,4},{16,0},{20,28},{24,8},{28,20},{1,17},{... | collective-permute-start | bytes 3145736 | tf_op jit(solution)/shard_map/ppermute | solution.py:79
  811.3 42.9 %collective-permute-start.50 = (bf16[1024,512]{1,0:T(8,128)(2,1)S(1)}, bf16[1024,512]{1,0:T(8,128)(2,1)S(1)}, u32[]{:S(2)}, u32[]{:S(2)}) collective-permute-start(bf16[1024,512]{1,0:T(8,128)(2,1)S(1)} %fusion.18), channel_id=1, source_target_pairs={{0,8},{4,20},{8,0},{12,28},{16,24},{20,4},{24,16},{28,12},{1,9},{5... | collective-permute-start | bytes 3145736 | tf_op jit(solution)/shard_map/ppermute | solution.py:79
  830.9 66.2 %collective-permute-start.46 = (bf16[256,2048]{1,0:T(8,128)(2,1)}, bf16[256,2048]{1,0:T(8,128)(2,1)}, u32[]{:S(2)}, u32[]{:S(2)}) collective-permute-start(bf16[256,2048]{1,0:T(8,128)(2,1)} %add.372), channel_id=1, source_target_pairs={{1,2},{2,1},{5,6},{6,5},{9,10},{10,9},{13,14},{14,13},{17,18},{18,... | collective-permute-start | bytes 3145736 | tf_op jit(solution)/shard_map/ppermute | solution.py:123
  839.6 25.9 %collective-permute-start.56 = (bf16[2048,256]{1,0:T(8,128)(2,1)S(1)}, bf16[2048,256]{1,0:T(8,128)(2,1)S(1)}, u32[]{:S(2)}, u32[]{:S(2)}) collective-permute-start(bf16[2048,256]{1,0:T(8,128)(2,1)S(1)} %get-tuple-element.105), channel_id=1, source_target_pairs={{0,16},{4,12},{8,24},{12,4},{16,0},{20,28},{24,8},{28,20},{1,17},{... | collective-permute-start | bytes 3145736 | tf_op jit(solution)/shard_map/ppermute | solution.py:79
  856.7 21.3 %collective-permute-start.51 = (bf16[256,512]{1,0:T(8,128)(2,1)S(1)}, bf16[256,512]{1,0:T(8,128)(2,1)S(1)}, u32[]{:S(2)}, u32[]{:S(2)}) collective-permute-start(bf16[256,512]{1,0:T(8,128)(2,1)S(1)} %get-tuple-element.149), channel_id=1, source_target_pairs={{0,1},{1,0},{2,3},{3,2},{4,5},{5,4},{6,7},{7,6},{8,9},{9,8},{10,11... | collective-permute-start | bytes 786440 | tf_op jit(solution)/shard_map/ppermute | solution.py:123
  861.5 26.2 %collective-permute-start.52 = (bf16[256,512]{1,0:T(8,128)(2,1)S(1)}, bf16[256,512]{1,0:T(8,128)(2,1)S(1)}, u32[]{:S(2)}, u32[]{:S(2)}) collective-permute-start(bf16[256,512]{1,0:T(8,128)(2,1)S(1)} %get-tuple-element.151), channel_id=1, source_target_pairs={{0,2},{1,3},{2,0},{3,1},{4,6},{5,7},{6,4},{7,5},{8,10},{9,11},{10,... | collective-permute-start | bytes 786440 | tf_op jit(solution)/shard_map/ppermute | solution.py:123
  861.5 26.2 %collective-permute-start.53 = (bf16[256,512]{1,0:T(8,128)(2,1)S(1)}, bf16[256,512]{1,0:T(8,128)(2,1)S(1)}, u32[]{:S(2)}, u32[]{:S(2)}) collective-permute-start(bf16[256,512]{1,0:T(8,128)(2,1)S(1)} %get-tuple-element.150), channel_id=1, source_target_pairs={{0,3},{1,2},{2,1},{3,0},{4,7},{5,6},{6,5},{7,4},{8,11},{9,10},{10,... | collective-permute-start | bytes 786440 | tf_op jit(solution)/shard_map/ppermute | solution.py:123
  866.9 41.2 %collective-permute-start.57 = (bf16[2048,256]{1,0:T(8,128)(2,1)}, bf16[2048,256]{1,0:T(8,128)(2,1)}, u32[]{:S(2)}, u32[]{:S(2)}) collective-permute-start(bf16[2048,256]{1,0:T(8,128)(2,1)} %add.389), channel_id=1, source_target_pairs={{0,8},{4,20},{8,0},{12,28},{16,24},{20,4},{24,16},{28,12},{1,9},{5... | collective-permute-start | bytes 3145736 | tf_op jit(solution)/shard_map/ppermute | solution.py:79
  878.0 27.0 %collective-permute-start.59 = (bf16[2048,256]{1,0:T(8,128)(2,1)}, bf16[2048,256]{1,0:T(8,128)(2,1)}, u32[]{:S(2)}, u32[]{:S(2)}) collective-permute-start(bf16[2048,256]{1,0:T(8,128)(2,1)} %get-tuple-element.109), channel_id=1, source_target_pairs={{0,16},{4,12},{8,24},{12,4},{16,0},{20,28},{24,8},{28,20},{1,17},{... | collective-permute-start | bytes 3145736 | tf_op jit(solution)/shard_map/ppermute | solution.py:79
  897.1 20.2 %collective-permute-start.65 = (bf16[4,320,512]{2,1,0:T(8,128)(2,1)}, bf16[4,320,512]{2,1,0:T(8,128)(2,1)}, u32[]{:S(2)}, u32[]{:S(2)}) collective-permute-start(bf16[4,320,512]{2,1,0:T(8,128)(2,1)} %bitcast.38), channel_id=1, source_target_pairs={{0,4},{4,0},{8,12},{12,8},{16,20},{20,16},{24,28},{28,24},{1,5},{5... | collective-permute-start | bytes 3932168 | tf_op jit(solution)/shard_map/ppermute | solution.py:79
  911.1 30.1 %collective-permute-start.72 = (bf16[512,256]{1,0:T(8,128)(2,1)}, bf16[512,256]{1,0:T(8,128)(2,1)}, u32[]{:S(2)}, u32[]{:S(2)}) collective-permute-start(bf16[512,256]{1,0:T(8,128)(2,1)} %get-tuple-element.141), channel_id=1, source_target_pairs={{0,1},{1,0},{2,3},{3,2},{4,5},{5,4},{6,7},{7,6},{8,9},{9,8},{10,11... | collective-permute-start | bytes 786440 | tf_op jit(solution)/shard_map/ppermute | solution.py:123
  914.9 26.3 %collective-permute-start.73 = (bf16[512,256]{1,0:T(8,128)(2,1)}, bf16[512,256]{1,0:T(8,128)(2,1)}, u32[]{:S(2)}, u32[]{:S(2)}) collective-permute-start(bf16[512,256]{1,0:T(8,128)(2,1)} %get-tuple-element.143), channel_id=1, source_target_pairs={{0,2},{1,3},{2,0},{3,1},{4,6},{5,7},{6,4},{7,5},{8,10},{9,11},{10,... | collective-permute-start | bytes 786440 | tf_op jit(solution)/shard_map/ppermute | solution.py:123
  915.8 25.3 %collective-permute-start.74 = (bf16[512,256]{1,0:T(8,128)(2,1)}, bf16[512,256]{1,0:T(8,128)(2,1)}, u32[]{:S(2)}, u32[]{:S(2)}) collective-permute-start(bf16[512,256]{1,0:T(8,128)(2,1)} %get-tuple-element.142), channel_id=1, source_target_pairs={{0,3},{1,2},{2,1},{3,0},{4,7},{5,6},{6,5},{7,4},{8,11},{9,10},{10,... | collective-permute-start | bytes 786440 | tf_op jit(solution)/shard_map/ppermute | solution.py:123
  922.5 38.9 %collective-permute-start.61 = (bf16[256,2048]{1,0:T(8,128)(2,1)S(1)}, bf16[256,2048]{1,0:T(8,128)(2,1)}, u32[]{:S(2)}, u32[]{:S(2)}) collective-permute-start(bf16[256,2048]{1,0:T(8,128)(2,1)S(1)} %fusion.17), channel_id=1, source_target_pairs={{0,8},{4,20},{8,0},{12,28},{16,24},{20,4},{24,16},{28,12},{1,9},{5... | collective-permute-start | bytes 3145736 | tf_op jit(solution)/shard_map/ppermute | solution.py:79
  946.0 23.6 %collective-permute-start.68 = (bf16[320,512]{1,0:T(8,128)(2,1)S(1)}, bf16[320,512]{1,0:T(8,128)(2,1)S(1)}, u32[]{:S(2)}, u32[]{:S(2)}) collective-permute-start(bf16[320,512]{1,0:T(8,128)(2,1)S(1)} %fusion.24), channel_id=1, source_target_pairs={{0,8},{4,20},{8,0},{12,28},{16,24},{20,4},{24,16},{28,12},{1,9},{5... | collective-permute-start | bytes 983048 | tf_op jit(solution)/shard_map/ppermute | solution.py:79
  967.1 22.9 %collective-permute-start.63 = (bf16[256,512]{1,0:T(8,128)(2,1)S(1)}, bf16[256,512]{1,0:T(8,128)(2,1)S(1)}, u32[]{:S(2)}, u32[]{:S(2)}) collective-permute-start(bf16[256,512]{1,0:T(8,128)(2,1)S(1)} %get-tuple-element.146), channel_id=1, source_target_pairs={{0,2},{1,3},{2,0},{3,1},{4,6},{5,7},{6,4},{7,5},{8,10},{9,11},{10,... | collective-permute-start | bytes 786440 | tf_op jit(solution)/shard_map/ppermute | solution.py:123
  967.9 22.1 %collective-permute-start.64 = (bf16[256,512]{1,0:T(8,128)(2,1)S(1)}, bf16[256,512]{1,0:T(8,128)(2,1)S(1)}, u32[]{:S(2)}, u32[]{:S(2)}) collective-permute-start(bf16[256,512]{1,0:T(8,128)(2,1)S(1)} %get-tuple-element.145), channel_id=1, source_target_pairs={{0,3},{1,2},{2,1},{3,0},{4,7},{5,6},{6,5},{7,4},{8,11},{9,10},{10,... | collective-permute-start | bytes 786440 | tf_op jit(solution)/shard_map/ppermute | solution.py:123
  969.7 21.2 %collective-permute-start.69 = (bf16[80,512]{1,0:T(8,128)(2,1)S(1)}, bf16[80,512]{1,0:T(8,128)(2,1)S(1)}, u32[]{:S(2)}, u32[]{:S(2)}) collective-permute-start(bf16[80,512]{1,0:T(8,128)(2,1)S(1)} %get-tuple-element.152), channel_id=1, source_target_pairs={{0,1},{1,0},{2,3},{3,2},{4,5},{5,4},{6,7},{7,6},{8,9},{9,8},{10,11... | collective-permute-start | bytes 245768 | tf_op jit(solution)/shard_map/ppermute | solution.py:123
  972.1 23.4 %collective-permute-start.70 = (bf16[80,512]{1,0:T(8,128)(2,1)S(1)}, bf16[80,512]{1,0:T(8,128)(2,1)S(1)}, u32[]{:S(2)}, u32[]{:S(2)}) collective-permute-start(bf16[80,512]{1,0:T(8,128)(2,1)S(1)} %get-tuple-element.154), channel_id=1, source_target_pairs={{0,2},{1,3},{2,0},{3,1},{4,6},{5,7},{6,4},{7,5},{8,10},{9,11},{10,... | collective-permute-start | bytes 245768 | tf_op jit(solution)/shard_map/ppermute | solution.py:123
  976.8 18.7 %collective-permute-start.71 = (bf16[80,512]{1,0:T(8,128)(2,1)S(1)}, bf16[80,512]{1,0:T(8,128)(2,1)S(1)}, u32[]{:S(2)}, u32[]{:S(2)}) collective-permute-start(bf16[80,512]{1,0:T(8,128)(2,1)S(1)} %get-tuple-element.153), channel_id=1, source_target_pairs={{0,3},{1,2},{2,1},{3,0},{4,7},{5,6},{6,5},{7,4},{8,11},{9,10},{10,... | collective-permute-start | bytes 245768 | tf_op jit(solution)/shard_map/ppermute | solution.py:123
  (100 other events, 2951.7 us)
Sparse Core Ops, SparseCore 0:
  23.5 111.2 all-gather.5
  210.4 100.6 all-gather.7
  313.0 67.2 all-gather.9
  518.9 99.5 reduce-scatter.5
  622.4 85.3 reduce-scatter.3
  711.2 112.5 reduce-scatter.7

commit v3 on v2

--- a/solution.py
+++ b/solution.py
@@ -124,7 +124,7 @@
 
     def gather(self, value):
         if not self.fast:
-            return lax.all_gather(value, "head", axis=0, tiled=True)
+            return lax.all_gather(value, "head", axis=0, tiled=True), (value,)
         pair = [(0, 1), (1, 0), (2, 3), (3, 2)]
         middle = [(1, 2), (2, 1)]
         outward = [(1, 0), (2, 3)]
@@ -133,7 +133,7 @@
         far = self.send(slot1, middle)
         slot2 = jnp.where(self.inner, near, self.send(near, outward))
         slot3 = jnp.where(self.inner, far, self.send(far, outward))
-        return place([value, slot1, slot2, slot3], self.relay, 0)
+        return place([value, slot1, slot2, slot3], self.relay, 0), (slot1, near)
 
     def reduce(self, whole, beside):
         if not self.fast:
@@ -667,9 +667,10 @@
     pieces = seq.size // 2
 
     inputs16, cotangent16 = shuffle(seq.order, inputs, out_grad)
-    grad_all = lax.all_gather(cotangent16, "head", axis=0, tiled=True)
-    q_a, q_b = seq.gather(head.gather_small(q_weight, 1))
-    out_a, out_b = seq.gather(head.gather_small(out_weight, 0), axis=1)
+    gate_all = lax.all_gather(gate_weight.T, "seq", axis=0, tiled=False)
+    q_span = head.gather_small(q_weight, 1)
+    out_span = head.gather_small(out_weight, 0)
+    q_a, q_b = seq.gather(q_span)
 
     kv_rows_each = kv_weight.shape[0]
     sizes = [q_bias.shape[0], kv_bias.shape[0], attn_gain.shape[0], ffn_gain.shape[0]]
@@ -731,7 +732,12 @@
         + jnp.dot(normed[:, half:], q_b, preferred_element_type=F32)
         + q_bias_full
     )
-    kv_halves = seq.gather(head.gather_small(kv_rows, 0))
+    kv_span = head.gather_small(after(kv_rows, q_span, out_span), 0)
+    cotangent_late = after(cotangent16, kv_span, gate_all)
+    kv_halves = seq.gather(after(kv_span, cotangent_late))
+    out_a, out_b = seq.gather(out_span, axis=1)
+    grad_all = lax.all_gather(cotangent_late, "head", axis=0, tiled=True)
+    up_all = lax.all_gather(after(up_weight.T, kv_halves[0]), "seq", axis=0, tiled=False)
     queries, mixed, lse = attention_forward(*where, query_raw, *tables, *kv_halves)
     hidden = residual + jnp.concatenate(
         [jnp.dot(mixed, part, preferred_element_type=F32) for part in (out_a, out_b)], axis=1
@@ -740,14 +746,12 @@
     normed2 = normed2_32.astype(BF16)
 
     straight = jnp.arange(seq.size, dtype=jnp.int32)
-    gate_own, up_own = after((gate_weight.T, up_weight.T), kv_halves[0])
-    gate_all = lax.all_gather(gate_own, "seq", axis=0, tiled=False)
-    up_all = lax.all_gather(up_own, "seq", axis=0, tiled=False)
+    normed2_all, first_step = head.gather(normed2)
+    down_begun = seq.begin(after(down_weight, *first_step))
+    down_begun = [after(item, normed2_all) for item in down_begun]
     down = [
-        half_of.reshape(pieces, -1, depth // seq.size)
-        for half_of in seq.gather(after(down_weight, kv_halves[0]))
+        half_of.reshape(pieces, -1, depth // seq.size) for half_of in seq.finish(down_begun)
     ]
-    normed2_all = head.gather(normed2)
     act, d_gate, d_up = ffn_middle(seq.order, normed2_all, grad_all, gate_all, up_all, *down)
     d_normed2_terms = ffn_back(seq.order, d_gate, d_up, gate_all, up_all)
 

time: 1020 us -> 1040 us (1.020)
  starting transfers between devices: 274 us -> 179 us
  waiting for transfers between devices: 329 us -> 402 us
  Pallas kernels: 209 us -> 243 us
    ppermute x36, starting transfers between devices: 110 us -> 36.6 us  [send(): return lax.ppermute(item, 'seq', pairs)]
    ppermute x36, waiting for transfers between devices: 124 us -> 183 us  [send(): return lax.ppermute(item, 'seq', pairs)]
    ppermute x39, starting transfers between devices: 164 us -> 142 us  [send(): return lax.ppermute(value, 'head', pairs)]
    pallas_call x1, Pallas kernels: 15 us -> 35.6 us  [attention_backward(): pl.pallas_call(backward_kernel, out_shape=(jax.ShapeDtypeStruct((rows, HE...]
    ppermute x39, waiting for transfers between devices: 204 us -> 218 us  [send(): return lax.ppermute(value, 'head', pairs)]
    pallas_call x1, Pallas kernels: 7.95 us -> 20.9 us  [attention_forward(): pl.pallas_call(forward_kernel, out_shape=(jax.ShapeDtypeStruct((HEADS, ro...]
    unnamed x176 -> x171, local copies, waits for them, and re-layouts: 30.1 us -> 34.5 us
  transfers between devices with their start and end apart: 81 -> 81, of which waited for: 28 -> 32; matrix products, arithmetic and copies ran while one was open for 15% -> 15% of each run, Pallas kernels for 11% -> 15%
where the time goes in v3:
time: 1040 us; the launch traced here: 1030 us
  waiting for transfers between devices  402 us (39%)
  Pallas kernels  243 us (23%)
  starting transfers between devices  179 us (17%)
  other arithmetic  78.9 us (8%)
  local copies, waits for them, and re-layouts  62.7 us (6%)
  matrix products  37.3 us (4%)
  between operations  24.4 us (2%)
    ppermute x39, waiting for transfers between devices, send(): return lax.ppermute(value, 'head', pairs)  218 us
    ppermute x36, waiting for transfers between devices, send(): return lax.ppermute(item, 'seq', pairs)  183 us
    ppermute x39, starting transfers between devices, send(): return lax.ppermute(value, 'head', pairs)  142 us
    pallas_call x7, Pallas kernels, unit_grad(): pl.pallas_call(functools.partial(unit_grad_kernel, count, shift, len(extr...  70 us
    pallas_call x1, Pallas kernels, ffn_middle(): pl.pallas_call(ffn_kernel, out_shape=(jax.ShapeDtypeStruct((rows, units),...  44.1 us
    ppermute x36, starting transfers between devices, send(): return lax.ppermute(item, 'seq', pairs)  36.6 us
    pallas_call x1, Pallas kernels, attention_backward(): pl.pallas_call(backward_kernel, out_shape=(jax.ShapeDtypeStruct((rows, HE...  35.6 us
    unnamed x171, local copies, waits for them, and re-layouts  34.5 us
  transfers between devices with their start and end apart: 81, of which 32 were waited for; matrix products, arithmetic and copies ran while one was open for 15% of the time, Pallas kernels for 15%

profile of v3, /device:TPU:0, one launch (start us, length us, event | category | flops | bytes accessed | tf_op | source)
XLA Modules:
  0.0 1026.7 jit_solution(7505483108897185601)
XLA Ops:
  16.2 3.5 collective-permute-start.8
  36.1 9.5 collective-permute-done.3
  50.0 7.2 collective-permute-done.5
  67.7 14.6 %collective-permute-done.15.refs_2_ = bf16[512,256]{1,0:T(8,128)(2,1)} collective-permute-done((bf16[512,256]{1,0:T(8,128)(2,1)}, bf16[512,256]{1,0:T(8,128)(2,1)}, u32[]{:S(2)}, u32[]{:S(2)}) %collective-permute-start.15) | collective-permute-done | bytes 262176 | tf_op jit(solution)/shard_map/ppermute | solution.py:123
  98.6 5.9 collective-permute-start.17
  107.2 8.5 collective-permute-done.17.refs_1_
  115.7 10.1 collective-permute-done.18.refs_2_
  131.5 23.7 %collective-permute-done.10 = bf16[256,2048]{1,0:T(8,128)(2,1)S(1)} collective-permute-done((bf16[256,2048]{1,0:T(8,128)(2,1)}, bf16[256,2048]{1,0:T(8,128)(2,1)S(1)}, u32[]{:S(2)}, u32[]{:S(2)}) %collective-permute-start.10) | collective-permute-done | bytes 1048608 | tf_op jit(solution)/shard_map/ppermute | solution.py:79
  155.4 22.8 %collective-permute-done.12 = bf16[256,2048]{1,0:T(8,128)(2,1)S(1)} collective-permute-done((bf16[256,2048]{1,0:T(8,128)(2,1)S(1)}, bf16[256,2048]{1,0:T(8,128)(2,1)S(1)}, u32[]{:S(2)}, u32[]{:S(2)}) %collective-permute-start.12) | collective-permute-done | bytes 1048608 | tf_op jit(solution)/shard_map/ppermute | solution.py:79
  183.9 9.3 collective-permute-done.21
  194.3 11.3 %collective-permute-done.22 = bf16[1024,512]{1,0:T(8,128)(2,1)S(1)} collective-permute-done((bf16[1024,512]{1,0:T(8,128)(2,1)S(1)}, bf16[1024,512]{1,0:T(8,128)(2,1)S(1)}, u32[]{:S(2)}, u32[]{:S(2)}) %collective-permute-start.22) | collective-permute-done | bytes 1048608 | tf_op jit(solution)/shard_map/ppermute | solution.py:79
  207.9 3.7 pad_maximum_fusion
  211.7 14.4 %collective-permute-done.24 = bf16[2048,256]{1,0:T(8,128)(2,1)S(1)} collective-permute-done((bf16[2048,256]{1,0:T(8,128)(2,1)}, bf16[2048,256]{1,0:T(8,128)(2,1)S(1)}, u32[]{:S(2)}, u32[]{:S(2)}) %collective-permute-start.24) | collective-permute-done | bytes 1048608 | tf_op jit(solution)/shard_map/ppermute | solution.py:79
  228.1 23.2 %collective-permute-done.26 = bf16[2048,256]{1,0:T(8,128)(2,1)S(1)} collective-permute-done((bf16[2048,256]{1,0:T(8,128)(2,1)S(1)}, bf16[2048,256]{1,0:T(8,128)(2,1)S(1)}, u32[]{:S(2)}, u32[]{:S(2)}) %collective-permute-start.26) | collective-permute-done | bytes 1048608 | tf_op jit(solution)/shard_map/ppermute | solution.py:79
  251.3 21.1 %collective-permute-done.25 = bf16[2048,256]{1,0:T(8,128)(2,1)S(1)} collective-permute-done((bf16[2048,256]{1,0:T(8,128)(2,1)S(1)}, bf16[2048,256]{1,0:T(8,128)(2,1)S(1)}, u32[]{:S(2)}, u32[]{:S(2)}) %collective-permute-start.25) | collective-permute-done | bytes 1048608 | tf_op jit(solution)/shard_map/ppermute | solution.py:79
  282.8 3.4 fusion.41
  286.3 3.5 fusion.2.raw_ref
  289.8 20.9 %attention_forward.1 = (bf16[16,256,128]{2,1,0:T(8,128)(2,1)S(1)}, bf16[256,2048]{1,0:T(8,128)(2,1)S(1)}, f32[16,1,256]{2,1,0:T(1,128)S(1)}) custom-call(s32[16]{0:T(128)S(1)} %fusion.34.offset_ref, s32[2]{0:T(128)S(1)} %pad_add_fusion.1.bound_ref, f32[256,2048]{1,0:T(8,128)S(1)} %fusion.2.raw_ref, f32[256,128]{1,0:T(8,128)S(1)} %pad_maximum_fusion.5.cos_ref, ...), custom_call_target="tpu_custom_call" | custom-call | flops 4294967296 | bytes 12582912 | tf_op jit(solution)/shard_map/attention_forward/pallas_call | solution.py:308
  310.7 4.2 fusion.53
  315.0 3.4 fusion.54
  319.1 11.7 %collective-permute-start.28 = (bf16[256,2048]{1,0:T(8,128)(2,1)S(1)}, bf16[256,2048]{1,0:T(8,128)(2,1)S(1)}, u32[]{:S(2)}, u32[]{:S(2)}) collective-permute-start(bf16[256,2048]{1,0:T(8,128)(2,1)S(1)} %multiply_convert_fusion.refs_0_), channel_id=1, source_target_pairs={{0,1},{1,0},{2,3},{3,2},{4,5},{5,4},{6,7},{7,6},{8,9},{9,8},{10,11... | collective-permute-start | bytes 3145736 | tf_op jit(solution)/shard_map/ppermute | solution.py:123
  332.4 16.2 %collective-permute-done.28.refs_1_ = bf16[256,2048]{1,0:T(8,128)(2,1)S(1)} collective-permute-done((bf16[256,2048]{1,0:T(8,128)(2,1)S(1)}, bf16[256,2048]{1,0:T(8,128)(2,1)S(1)}, u32[]{:S(2)}, u32[]{:S(2)}) %collective-permute-start.28) | collective-permute-done | bytes 1048608 | tf_op jit(solution)/shard_map/ppermute | solution.py:123
  354.2 13.0 %collective-permute-done.30 = bf16[256,2048]{1,0:T(8,128)(2,1)} collective-permute-done((bf16[256,2048]{1,0:T(8,128)(2,1)}, bf16[256,2048]{1,0:T(8,128)(2,1)}, u32[]{:S(2)}, u32[]{:S(2)}) %collective-permute-start.30) | collective-permute-done | bytes 1048608 | tf_op jit(solution)/shard_map/ppermute | solution.py:123
  369.5 35.1 %collective-permute-done.32 = bf16[256,2048]{1,0:T(8,128)(2,1)} collective-permute-done((bf16[256,2048]{1,0:T(8,128)(2,1)}, bf16[256,2048]{1,0:T(8,128)(2,1)}, u32[]{:S(2)}, u32[]{:S(2)}) %collective-permute-start.32) | collective-permute-done | bytes 1048608 | tf_op jit(solution)/shard_map/ppermute | solution.py:123
  406.9 4.5 place.9.normed_ref.right_ref
  419.1 11.2 %collective-permute-done.35 = bf16[2752,256]{1,0:T(8,128)(2,1)S(1)} collective-permute-done((bf16[2752,256]{1,0:T(8,128)(2,1)}, bf16[2752,256]{1,0:T(8,128)(2,1)S(1)}, u32[]{:S(2)}, u32[]{:S(2)}) %collective-permute-start.35) | collective-permute-done | bytes 1409056 | tf_op jit(solution)/shard_map/ppermute | solution.py:79
  431.5 5.8 collective-permute-start.36
  437.3 9.2 collective-permute-done.36
  448.7 44.1 %ffn_middle.1 = (bf16[1024,2752]{1,0:T(8,128)(2,1)}, bf16[1024,2752]{1,0:T(8,128)(2,1)}, bf16[1024,2752]{1,0:T(8,128)(2,1)}) custom-call(s32[8]{0:T(128)S(1)} %copy-done.16, bf16[1024,2048]{1,0:T(8,128)(2,1)S(1)} %copy-done.8, bf16[1024,2048]{1,0:T(8,128)(2,1)} %all-gather.6.cloned.1.call-done.grad_ref.right_ref, bf16[8,2752,256]{2,1,0:T(8,128)(2,1)} %bitcast.162, ...), custom_call_target="tpu_custom_call" | custom-call | flops 34628173824 | bytes 59113472 | tf_op jit(solution)/shard_map/ffn_middle/pallas_call | solution.py:481
  492.8 31.8 %ffn_back.1 = bf16[1024,2048]{1,0:T(8,128)(2,1)S(1)} custom-call(s32[8]{0:T(128)S(1)} %copy-done.16, bf16[1024,2752]{1,0:T(8,128)(2,1)} %get-tuple-element.95.d_gate_ref.left_ref, bf16[1024,2752]{1,0:T(8,128)(2,1)} %get-tuple-element.97.d_up_ref.left_ref, bf16[8,2752,256]{2,1,0:T(8,128)(2,1)} %bitcast.163, bf16[8,2752,256]{2,1,0:T(8,128)(2,1)} %bitcast.165), custom_call_target="tpu_custom_call" | custom-call | flops 23085449216 | bytes 33816576 | tf_op jit(solution)/shard_map/ffn_back/pallas_call | solution.py:511
  526.5 17.6 %unit_grad.9 = bf16[8,2752,256]{2,1,0:T(8,128)(2,1)} custom-call(s32[8]{0:T(128)S(1)} %select_reduce_fusion.3.order_ref, bf16[1024,2752]{1,0:T(8,128)(2,1)} %get-tuple-element.97.d_up_ref.left_ref, bf16[1024,2048]{1,0:T(8,128)(2,1)S(1)} %copy-done.9), custom_call_target="tpu_custom_call" | custom-call | flops 11542724608 | bytes 21102592 | tf_op jit(solution)/shard_map/unit_grad/pallas_call | solution.py:590
  546.4 17.9 %unit_grad.8 = bf16[8,2752,256]{2,1,0:T(8,128)(2,1)} custom-call(s32[8]{0:T(128)S(1)} %select_reduce_fusion.3.order_ref, bf16[1024,2752]{1,0:T(8,128)(2,1)} %get-tuple-element.95.d_gate_ref.left_ref, bf16[1024,2048]{1,0:T(8,128)(2,1)S(1)} %copy-done.10), custom_call_target="tpu_custom_call" | custom-call | flops 11542724608 | bytes 21102592 | tf_op jit(solution)/shard_map/unit_grad/pallas_call | solution.py:590
  572.8 17.6 %unit_grad.7 = bf16[8,2752,256]{2,1,0:T(8,128)(2,1)} custom-call(s32[8]{0:T(128)S(1)} %select_reduce_fusion.3.order_ref, bf16[1024,2752]{1,0:T(8,128)(2,1)} %get-tuple-element.100.left_ref.act_ref, bf16[1024,2048]{1,0:T(8,128)(2,1)S(1)} %copy-done.18), custom_call_target="tpu_custom_call" | custom-call | flops 11542724608 | bytes 21102592 | tf_op jit(solution)/shard_map/unit_grad/pallas_call | solution.py:590
  596.6 3.4 dynamic-slice_add_fusion.1
  600.0 28.9 %collective-permute-start.40 = (bf16[256,2048]{1,0:T(8,128)(2,1)S(1)}, bf16[256,2048]{1,0:T(8,128)(2,1)S(1)}, u32[]{:S(2)}, u32[]{:S(2)}) collective-permute-start(bf16[256,2048]{1,0:T(8,128)(2,1)S(1)} %get-tuple-element.99), channel_id=1, source_target_pairs={{0,1},{3,2},{4,5},{7,6},{8,9},{11,10},{12,13},{15,14},{16,17},{19,... | collective-permute-start | bytes 3145736 | tf_op jit(solution)/shard_map/ppermute | solution.py:123
  628.9 23.5 %collective-permute-done.40 = bf16[256,2048]{1,0:T(8,128)(2,1)S(1)} collective-permute-done((bf16[256,2048]{1,0:T(8,128)(2,1)S(1)}, bf16[256,2048]{1,0:T(8,128)(2,1)S(1)}, u32[]{:S(2)}, u32[]{:S(2)}) %collective-permute-start.40) | collective-permute-done | bytes 1048608 | tf_op jit(solution)/shard_map/ppermute | solution.py:123
  656.3 16.6 %collective-permute-done.39 = bf16[256,2048]{1,0:T(8,128)(2,1)S(1)} collective-permute-done((bf16[256,2048]{1,0:T(8,128)(2,1)}, bf16[256,2048]{1,0:T(8,128)(2,1)S(1)}, u32[]{:S(2)}, u32[]{:S(2)}) %collective-permute-start.39) | collective-permute-done | bytes 1048608 | tf_op jit(solution)/shard_map/ppermute | solution.py:123
  675.5 3.6 fusion.46
  679.1 3.9 fusion.21
  683.0 4.4 fusion.3.grad_ref
  687.4 35.6 %attention_backward.1 = (bf16[256,2048]{1,0:T(8,128)(2,1)}, bf16[4096,512]{1,0:T(8,128)(2,1)}, bf16[4096,512]{1,0:T(8,128)(2,1)}) custom-call(s32[16]{0:T(128)} %copy-done.21, s32[2]{0:T(128)} %copy-done.20, bf16[16,256,128]{2,1,0:T(8,128)(2,1)} %copy-done.22, f32[256,128]{1,0:T(8,128)} %copy-done.14, f32[256,128]{1,0:T(8,128)} %copy-done.15, ...), custom_call_target="tpu_custom_call" | custom-call | flops 10737418240 | bytes 20971520 | tf_op jit(solution)/shard_map/attention_backward/pallas_call | solution.py:418
  723.0 9.3 collective-permute-start.47
  732.4 17.6 %ffn_forth.1 = bf16[1024,2048]{1,0:T(8,128)(2,1)S(1)} custom-call(bf16[1024,2752]{1,0:T(8,128)(2,1)} %get-tuple-element.100.left_ref.act_ref, bf16[4,2752,256]{2,1,0:T(8,128)(2,1)} %bitcast.18.down_a_ref, bf16[4,2752,256]{2,1,0:T(8,128)(2,1)} %bitcast.19.down_b_ref), custom_call_target="tpu_custom_call" | custom-call | flops 11542724608 | bytes 16908288 | tf_op jit(solution)/shard_map/ffn_forth/pallas_call | solution.py:542
  751.1 5.9 collective-permute-start.42
  758.0 4.0 unit_grad.12
  762.0 3.4 unit_grad.10
  765.9 13.1 %collective-permute-done.42 = bf16[256,2048]{1,0:T(8,128)(2,1)} collective-permute-done((bf16[256,2048]{1,0:T(8,128)(2,1)}, bf16[256,2048]{1,0:T(8,128)(2,1)}, u32[]{:S(2)}, u32[]{:S(2)}) %collective-permute-start.42) | collective-permute-done | bytes 1048608 | tf_op jit(solution)/shard_map/ppermute | solution.py:123
  781.4 3.5 add.375
  789.0 32.1 %collective-permute-start.44 = (bf16[256,2048]{1,0:T(8,128)(2,1)}, bf16[256,2048]{1,0:T(8,128)(2,1)}, u32[]{:S(2)}, u32[]{:S(2)}) collective-permute-start(bf16[256,2048]{1,0:T(8,128)(2,1)} %get-tuple-element.143), channel_id=1, source_target_pairs={{0,1},{1,0},{2,3},{3,2},{4,5},{5,4},{6,7},{7,6},{8,9},{9,8},{10,11... | collective-permute-start | bytes 3145736 | tf_op jit(solution)/shard_map/ppermute | solution.py:123
  827.7 17.3 %collective-permute-done.44 = bf16[256,2048]{1,0:T(8,128)(2,1)} collective-permute-done((bf16[256,2048]{1,0:T(8,128)(2,1)}, bf16[256,2048]{1,0:T(8,128)(2,1)}, u32[]{:S(2)}, u32[]{:S(2)}) %collective-permute-start.44) | collective-permute-done | bytes 1048608 | tf_op jit(solution)/shard_map/ppermute | solution.py:123
  845.0 4.6 fusion.55
  849.6 4.5 fusion.56
  854.0 10.6 %collective-permute-done.45 = bf16[256,2048]{1,0:T(8,128)(2,1)S(1)} collective-permute-done((bf16[256,2048]{1,0:T(8,128)(2,1)S(1)}, bf16[256,2048]{1,0:T(8,128)(2,1)S(1)}, u32[]{:S(2)}, u32[]{:S(2)}) %collective-permute-start.45) | collective-permute-done | bytes 1048608 | tf_op jit(solution)/shard_map/ppermute | solution.py:123
  868.0 5.8 unit_grad.13
  874.9 3.7 unit_grad.11
  881.1 4.2 collective-permute-start.51
  894.3 18.0 %collective-permute-done.52 = bf16[256,512]{1,0:T(8,128)(2,1)S(1)} collective-permute-done((bf16[256,512]{1,0:T(8,128)(2,1)S(1)}, bf16[256,512]{1,0:T(8,128)(2,1)S(1)}, u32[]{:S(2)}, u32[]{:S(2)}) %collective-permute-start.52) | collective-permute-done | bytes 262176 | tf_op jit(solution)/shard_map/ppermute | solution.py:123
  914.4 3.9 fusion.12
  922.5 3.8 add_add_fusion.refs_0_
  946.0 18.0 %collective-permute-done.58 = bf16[256,2048]{1,0:T(8,128)(2,1)S(1)} collective-permute-done((bf16[256,2048]{1,0:T(8,128)(2,1)S(1)}, bf16[256,2048]{1,0:T(8,128)(2,1)S(1)}, u32[]{:S(2)}, u32[]{:S(2)}) %collective-permute-start.58) | collective-permute-done | bytes 1048608 | tf_op jit(solution)/shard_map/ppermute | solution.py:79
  977.7 3.4 collective-permute-start.62
  986.4 4.1 collective-permute-done.62
  992.6 10.0 collective-permute-done.63
  1003.5 4.7 collective-permute-done.70
  (433 shorter events, 217.1 us)
Async XLA Ops:
  7.2 121.6 %all-gather.8.cloned.1.call-start = ((), (), s32[]{:S(2)}) async-start(), calls=%async_computation.7 | async-start | bytes 12681216 | tf_op jit(solution)/shard_map/all_gather | solution.py:670
  7.9 429.4 %all-gather.6.cloned.1.call-start = ((), (), s32[]{:S(2)}) async-start(), calls=%async_computation.3 | async-start | bytes 5242880 | tf_op jit(solution)/shard_map/all_gather | solution.py:739
  9.6 20.0 %collective-permute-start = (bf16[80,512]{1,0:T(8,128)(2,1)S(1)}, bf16[80,512]{1,0:T(8,128)(2,1)S(1)}, u32[]{:S(2)}, u32[]{:S(2)}) collective-permute-start(bf16[80,512]{1,0:T(8,128)(2,1)S(1)} %fusion.28.refs_0_), channel_id=1, source_target_pairs={{0,1},{1,0},{2,3},{3,2},{4,5},{5,4},{6,7},{7,6},{8,9},{9,8},{10,11... | collective-permute-start | bytes 245768 | tf_op jit(solution)/shard_map/ppermute | solution.py:123
  12.7 17.1 %collective-permute-start.1 = (bf16[80,512]{1,0:T(8,128)(2,1)S(1)}, bf16[80,512]{1,0:T(8,128)(2,1)S(1)}, u32[]{:S(2)}, u32[]{:S(2)}) collective-permute-start(bf16[80,512]{1,0:T(8,128)(2,1)S(1)} %fusion.28.refs_0_), channel_id=1, source_target_pairs={{0,2},{1,3},{2,0},{3,1},{4,6},{5,7},{6,4},{7,5},{8,10},{9,11},{10,... | collective-permute-start | bytes 245768 | tf_op jit(solution)/shard_map/ppermute | solution.py:123
  15.3 45.5 %collective-permute-start.7 = (bf16[256,512]{1,0:T(8,128)(2,1)}, bf16[256,512]{1,0:T(8,128)(2,1)S(1)}, u32[]{:S(2)}, u32[]{:S(2)}) collective-permute-start(bf16[256,512]{1,0:T(8,128)(2,1)} %refs_0_.4), channel_id=1, source_target_pairs={{0,1},{1,0},{2,3},{3,2},{4,5},{5,4},{6,7},{7,6},{8,9},{9,8},{10,11... | collective-permute-start | bytes 786440 | tf_op jit(solution)/shard_map/ppermute | solution.py:123
  16.2 46.4 %collective-permute-start.8 = (bf16[256,512]{1,0:T(8,128)(2,1)}, bf16[256,512]{1,0:T(8,128)(2,1)S(1)}, u32[]{:S(2)}, u32[]{:S(2)}) collective-permute-start(bf16[256,512]{1,0:T(8,128)(2,1)} %refs_0_.4), channel_id=1, source_target_pairs={{0,2},{1,3},{2,0},{3,1},{4,6},{5,7},{6,4},{7,5},{8,10},{9,11},{10,... | collective-permute-start | bytes 786440 | tf_op jit(solution)/shard_map/ppermute | solution.py:123
  29.6 35.8 %collective-permute-start.9 = (bf16[256,512]{1,0:T(8,128)(2,1)}, bf16[256,512]{1,0:T(8,128)(2,1)}, u32[]{:S(2)}, u32[]{:S(2)}) collective-permute-start(bf16[256,512]{1,0:T(8,128)(2,1)} %refs_0_.4), channel_id=1, source_target_pairs={{0,3},{1,2},{2,1},{3,0},{4,7},{5,6},{6,5},{7,4},{8,11},{9,10},{10,... | collective-permute-start | bytes 786440 | tf_op jit(solution)/shard_map/ppermute | solution.py:123
  48.4 19.3 %collective-permute-start.14 = (bf16[512,256]{1,0:T(8,128)(2,1)}, bf16[512,256]{1,0:T(8,128)(2,1)}, u32[]{:S(2)}, u32[]{:S(2)}) collective-permute-start(bf16[512,256]{1,0:T(8,128)(2,1)} %refs_0_.5), channel_id=1, source_target_pairs={{0,1},{1,0},{2,3},{3,2},{4,5},{5,4},{6,7},{7,6},{8,9},{9,8},{10,11... | collective-permute-start | bytes 786440 | tf_op jit(solution)/shard_map/ppermute | solution.py:123
  59.4 26.2 %collective-permute-start.6 = (bf16[1280,512]{1,0:T(8,128)(2,1)}, bf16[1280,512]{1,0:T(8,128)(2,1)}, u32[]{:S(2)}, u32[]{:S(2)}) collective-permute-start(bf16[1280,512]{1,0:T(8,128)(2,1)} %pad_maximum_fusion.2), channel_id=1, source_target_pairs={{0,4},{4,0},{8,12},{12,8},{16,20},{20,16},{24,28},{28,24},{1,5},{5... | collective-permute-start | bytes 3932168 | tf_op jit(solution)/shard_map/ppermute | solution.py:79
  60.8 21.5 %collective-permute-start.15 = (bf16[512,256]{1,0:T(8,128)(2,1)}, bf16[512,256]{1,0:T(8,128)(2,1)}, u32[]{:S(2)}, u32[]{:S(2)}) collective-permute-start(bf16[512,256]{1,0:T(8,128)(2,1)} %refs_0_.5), channel_id=1, source_target_pairs={{0,2},{1,3},{2,0},{3,1},{4,6},{5,7},{6,4},{7,5},{8,10},{9,11},{10,... | collective-permute-start | bytes 786440 | tf_op jit(solution)/shard_map/ppermute | solution.py:123
  62.6 19.7 %collective-permute-start.16 = (bf16[512,256]{1,0:T(8,128)(2,1)}, bf16[512,256]{1,0:T(8,128)(2,1)}, u32[]{:S(2)}, u32[]{:S(2)}) collective-permute-start(bf16[512,256]{1,0:T(8,128)(2,1)} %refs_0_.5), channel_id=1, source_target_pairs={{0,3},{1,2},{2,1},{3,0},{4,7},{5,6},{6,5},{7,4},{8,11},{9,10},{10,... | collective-permute-start | bytes 786440 | tf_op jit(solution)/shard_map/ppermute | solution.py:123
  98.6 17.2 %collective-permute-start.17 = (bf16[256,512]{1,0:T(8,128)(2,1)S(1)}, bf16[256,512]{1,0:T(8,128)(2,1)S(1)}, u32[]{:S(2)}, u32[]{:S(2)}) collective-permute-start(bf16[256,512]{1,0:T(8,128)(2,1)S(1)} %pad_maximum_fusion.3.refs_0_), channel_id=1, source_target_pairs={{0,1},{1,0},{2,3},{3,2},{4,5},{5,4},{6,7},{7,6},{8,9},{9,8},{10,11... | collective-permute-start | bytes 786440 | tf_op jit(solution)/shard_map/ppermute | solution.py:123
  104.4 21.4 %collective-permute-start.18 = (bf16[256,512]{1,0:T(8,128)(2,1)S(1)}, bf16[256,512]{1,0:T(8,128)(2,1)S(1)}, u32[]{:S(2)}, u32[]{:S(2)}) collective-permute-start(bf16[256,512]{1,0:T(8,128)(2,1)S(1)} %pad_maximum_fusion.3.refs_0_), channel_id=1, source_target_pairs={{0,2},{1,3},{2,0},{3,1},{4,6},{5,7},{6,4},{7,5},{8,10},{9,11},{10,... | collective-permute-start | bytes 786440 | tf_op jit(solution)/shard_map/ppermute | solution.py:123
  105.8 20.7 %collective-permute-start.19 = (bf16[256,512]{1,0:T(8,128)(2,1)S(1)}, bf16[256,512]{1,0:T(8,128)(2,1)}, u32[]{:S(2)}, u32[]{:S(2)}) collective-permute-start(bf16[256,512]{1,0:T(8,128)(2,1)S(1)} %pad_maximum_fusion.3.refs_0_), channel_id=1, source_target_pairs={{0,3},{1,2},{2,1},{3,0},{4,7},{5,6},{6,5},{7,4},{8,11},{9,10},{10,... | collective-permute-start | bytes 786440 | tf_op jit(solution)/shard_map/ppermute | solution.py:123
  128.8 317.7 %all-gather.10.cloned.1.call-start = ((), (), s32[]{:S(2)}) async-start(), calls=%async_computation.8 | async-start | bytes 12681216 | tf_op jit(solution)/shard_map/all_gather | solution.py:740
  128.9 26.3 %collective-permute-start.10 = (bf16[256,2048]{1,0:T(8,128)(2,1)}, bf16[256,2048]{1,0:T(8,128)(2,1)S(1)}, u32[]{:S(2)}, u32[]{:S(2)}) collective-permute-start(bf16[256,2048]{1,0:T(8,128)(2,1)} %place.6), channel_id=1, source_target_pairs={{0,8},{4,20},{8,0},{12,28},{16,24},{20,4},{24,16},{28,12},{1,9},{5... | collective-permute-start | bytes 3145736 | tf_op jit(solution)/shard_map/ppermute | solution.py:79
  129.0 26.3 %collective-permute-start.11 = (bf16[256,2048]{1,0:T(8,128)(2,1)}, bf16[256,2048]{1,0:T(8,128)(2,1)S(1)}, u32[]{:S(2)}, u32[]{:S(2)}) collective-permute-start(bf16[256,2048]{1,0:T(8,128)(2,1)} %place.6), channel_id=1, source_target_pairs={{0,16},{4,12},{8,24},{12,4},{16,0},{20,28},{24,8},{28,20},{1,17},{... | collective-permute-start | bytes 3145736 | tf_op jit(solution)/shard_map/ppermute | solution.py:79
  155.2 23.0 %collective-permute-start.12 = (bf16[256,2048]{1,0:T(8,128)(2,1)S(1)}, bf16[256,2048]{1,0:T(8,128)(2,1)S(1)}, u32[]{:S(2)}, u32[]{:S(2)}) collective-permute-start(bf16[256,2048]{1,0:T(8,128)(2,1)S(1)} %collective-permute-done.10), channel_id=1, source_target_pairs={{0,16},{4,12},{8,24},{12,4},{16,0},{20,28},{24,8},{28,20},{1,17},{... | collective-permute-start | bytes 3145736 | tf_op jit(solution)/shard_map/ppermute | solution.py:79
  155.2 23.3 %collective-permute-start.20 = (bf16[1024,512]{1,0:T(8,128)(2,1)}, bf16[1024,512]{1,0:T(8,128)(2,1)S(1)}, u32[]{:S(2)}, u32[]{:S(2)}) collective-permute-start(bf16[1024,512]{1,0:T(8,128)(2,1)} %place.8), channel_id=1, source_target_pairs={{0,8},{4,20},{8,0},{12,28},{16,24},{20,4},{24,16},{28,12},{1,9},{5... | collective-permute-start | bytes 3145736 | tf_op jit(solution)/shard_map/ppermute | solution.py:79
  179.2 26.5 %collective-permute-start.22 = (bf16[1024,512]{1,0:T(8,128)(2,1)S(1)}, bf16[1024,512]{1,0:T(8,128)(2,1)S(1)}, u32[]{:S(2)}, u32[]{:S(2)}) collective-permute-start(bf16[1024,512]{1,0:T(8,128)(2,1)S(1)} %collective-permute-done.20), channel_id=1, source_target_pairs={{0,16},{4,12},{8,24},{12,4},{16,0},{20,28},{24,8},{28,20},{1,17},{... | collective-permute-start | bytes 3145736 | tf_op jit(solution)/shard_map/ppermute | solution.py:79
  206.8 803.3 %reduce-scatter.6.cloned.1.call-start = ((), (), s32[]{:S(2)}) async-start(), calls=%async_computation.5 | async-start | bytes 12681216 | tf_op jit(solution)/shard_map/reduce_scatter | solution.py:773
  206.8 19.3 %collective-permute-start.24 = (bf16[2048,256]{1,0:T(8,128)(2,1)}, bf16[2048,256]{1,0:T(8,128)(2,1)S(1)}, u32[]{:S(2)}, u32[]{:S(2)}) collective-permute-start(bf16[2048,256]{1,0:T(8,128)(2,1)} %place.7), channel_id=1, source_target_pairs={{0,8},{4,20},{8,0},{12,28},{16,24},{20,4},{24,16},{28,12},{1,9},{5... | collective-permute-start | bytes 3145736 | tf_op jit(solution)/shard_map/ppermute | solution.py:79
  211.6 71.2 %collective-permute-start.13 = (bf16[1024,2048]{1,0:T(8,128)(2,1)}, bf16[1024,2048]{1,0:T(8,128)(2,1)}, u32[]{:S(2)}, u32[]{:S(2)}) collective-permute-start(bf16[1024,2048]{1,0:T(8,128)(2,1)} %pad_maximum_fusion), channel_id=1, source_target_pairs={{0,4},{4,0},{8,12},{12,8},{16,20},{20,16},{24,28},{28,24},{1,5},{5... | collective-permute-start | bytes 12582920 | tf_op jit(solution)/shard_map/ppermute | solution.py:79
  226.1 25.2 %collective-permute-start.26 = (bf16[2048,256]{1,0:T(8,128)(2,1)S(1)}, bf16[2048,256]{1,0:T(8,128)(2,1)S(1)}, u32[]{:S(2)}, u32[]{:S(2)}) collective-permute-start(bf16[2048,256]{1,0:T(8,128)(2,1)S(1)} %collective-permute-done.24), channel_id=1, source_target_pairs={{0,16},{4,12},{8,24},{12,4},{16,0},{20,28},{24,8},{28,20},{1,17},{... | collective-permute-start | bytes 3145736 | tf_op jit(solution)/shard_map/ppermute | solution.py:79
  226.1 46.3 %collective-permute-start.25 = (bf16[2048,256]{1,0:T(8,128)(2,1)S(1)}, bf16[2048,256]{1,0:T(8,128)(2,1)S(1)}, u32[]{:S(2)}, u32[]{:S(2)}) collective-permute-start(bf16[2048,256]{1,0:T(8,128)(2,1)S(1)} %copy-done.38), channel_id=1, source_target_pairs={{0,16},{4,12},{8,24},{12,4},{16,0},{20,28},{24,8},{28,20},{1,17},{... | collective-permute-start | bytes 3145736 | tf_op jit(solution)/shard_map/ppermute | solution.py:79
  228.1 61.6 %collective-permute-start.23 = (bf16[4096,512]{1,0:T(8,128)(2,1)}, bf16[4096,512]{1,0:T(8,128)(2,1)}, u32[]{:S(2)}, u32[]{:S(2)}) collective-permute-start(bf16[4096,512]{1,0:T(8,128)(2,1)} %constant_dynamic-update-slice_fusion.5.half_a_ref), channel_id=1, source_target_pairs={{0,4},{4,0},{8,12},{12,8},{16,20},{20,16},{24,28},{28,24},{1,5},{5... | collective-permute-start | bytes 12582920 | tf_op jit(solution)/shard_map/ppermute | solution.py:79
  274.7 40.2 %collective-permute-start.27 = (bf16[2048,1024]{1,0:T(8,128)(2,1)}, bf16[2048,1024]{1,0:T(8,128)(2,1)}, u32[]{:S(2)}, u32[]{:S(2)}) collective-permute-start(bf16[2048,1024]{1,0:T(8,128)(2,1)} %pad_maximum_fusion.1), channel_id=1, source_target_pairs={{0,4},{4,0},{8,12},{12,8},{16,20},{20,16},{24,28},{28,24},{1,5},{5... | collective-permute-start | bytes 12582920 | tf_op jit(solution)/shard_map/ppermute | solution.py:79
  319.1 29.5 %collective-permute-start.28 = (bf16[256,2048]{1,0:T(8,128)(2,1)S(1)}, bf16[256,2048]{1,0:T(8,128)(2,1)S(1)}, u32[]{:S(2)}, u32[]{:S(2)}) collective-permute-start(bf16[256,2048]{1,0:T(8,128)(2,1)S(1)} %multiply_convert_fusion.refs_0_), channel_id=1, source_target_pairs={{0,1},{1,0},{2,3},{3,2},{4,5},{5,4},{6,7},{7,6},{8,9},{9,8},{10,11... | collective-permute-start | bytes 3145736 | tf_op jit(solution)/shard_map/ppermute | solution.py:123
  330.7 19.5 %collective-permute-start.29 = (bf16[256,2048]{1,0:T(8,128)(2,1)S(1)}, bf16[256,2048]{1,0:T(8,128)(2,1)}, u32[]{:S(2)}, u32[]{:S(2)}) collective-permute-start(bf16[256,2048]{1,0:T(8,128)(2,1)S(1)} %multiply_convert_fusion.refs_0_), channel_id=1, source_target_pairs={{1,2},{2,1},{5,6},{6,5},{9,10},{10,9},{13,14},{14,13},{17,18},{18,... | collective-permute-start | bytes 3145736 | tf_op jit(solution)/shard_map/ppermute | solution.py:123
  350.2 17.0 %collective-permute-start.30 = (bf16[256,2048]{1,0:T(8,128)(2,1)}, bf16[256,2048]{1,0:T(8,128)(2,1)}, u32[]{:S(2)}, u32[]{:S(2)}) collective-permute-start(bf16[256,2048]{1,0:T(8,128)(2,1)} %collective-permute-done.29), channel_id=1, source_target_pairs={{1,0},{2,3},{5,4},{6,7},{9,8},{10,11},{13,12},{14,15},{17,16},{18,... | collective-permute-start | bytes 3145736 | tf_op jit(solution)/shard_map/ppermute | solution.py:123
  351.5 53.1 %collective-permute-start.32 = (bf16[256,2048]{1,0:T(8,128)(2,1)}, bf16[256,2048]{1,0:T(8,128)(2,1)}, u32[]{:S(2)}, u32[]{:S(2)}) collective-permute-start(bf16[256,2048]{1,0:T(8,128)(2,1)} %collective-permute-done.31), channel_id=1, source_target_pairs={{1,0},{2,3},{5,4},{6,7},{9,8},{10,11},{13,12},{14,15},{17,16},{18,... | collective-permute-start | bytes 3145736 | tf_op jit(solution)/shard_map/ppermute | solution.py:123
  352.8 58.6 %collective-permute-start.33 = (bf16[2752,256]{1,0:T(8,128)(2,1)}, bf16[2752,256]{1,0:T(8,128)(2,1)}, u32[]{:S(2)}, u32[]{:S(2)}) collective-permute-start(bf16[2752,256]{1,0:T(8,128)(2,1)} %param.29), channel_id=1, source_target_pairs={{0,8},{4,20},{8,0},{12,28},{16,24},{20,4},{24,16},{28,12},{1,9},{5... | collective-permute-start | bytes 4227080 | tf_op jit(solution)/shard_map/ppermute | solution.py:79
  352.9 58.5 %collective-permute-start.34 = (bf16[2752,256]{1,0:T(8,128)(2,1)}, bf16[2752,256]{1,0:T(8,128)(2,1)}, u32[]{:S(2)}, u32[]{:S(2)}) collective-permute-start(bf16[2752,256]{1,0:T(8,128)(2,1)} %param.29), channel_id=1, source_target_pairs={{0,16},{4,12},{8,24},{12,4},{16,0},{20,28},{24,8},{28,20},{1,17},{... | collective-permute-start | bytes 4227080 | tf_op jit(solution)/shard_map/ppermute | solution.py:79
  411.4 18.9 %collective-permute-start.35 = (bf16[2752,256]{1,0:T(8,128)(2,1)}, bf16[2752,256]{1,0:T(8,128)(2,1)S(1)}, u32[]{:S(2)}, u32[]{:S(2)}) collective-permute-start(bf16[2752,256]{1,0:T(8,128)(2,1)} %collective-permute-done.33), channel_id=1, source_target_pairs={{0,16},{4,12},{8,24},{12,4},{16,0},{20,28},{24,8},{28,20},{1,17},{... | collective-permute-start | bytes 4227080 | tf_op jit(solution)/shard_map/ppermute | solution.py:79
  544.1 469.0 %reduce-scatter.4.cloned.1.call-start = ((), (), s32[]{:S(2)}) async-start(), calls=%async_computation.4 | async-start | bytes 12681216 | tf_op jit(solution)/shard_map/reduce_scatter | solution.py:773
  564.3 452.0 %reduce-scatter.8.cloned.1.call-start = ((), (), s32[]{:S(2)}) async-start(), calls=%async_computation.6 | async-start | bytes 12681216 | tf_op jit(solution)/shard_map/reduce_scatter | solution.py:773
  566.9 24.7 %collective-permute-start.37 = (bf16[256,2048]{1,0:T(8,128)(2,1)S(1)}, bf16[256,2048]{1,0:T(8,128)(2,1)}, u32[]{:S(2)}, u32[]{:S(2)}) collective-permute-start(bf16[256,2048]{1,0:T(8,128)(2,1)S(1)} %constant_dynamic-slice_fusion.15), channel_id=1, source_target_pairs={{0,1},{3,2},{4,5},{7,6},{8,9},{11,10},{12,13},{15,14},{16,17},{19,... | collective-permute-start | bytes 3145736 | tf_op jit(solution)/shard_map/ppermute | solution.py:123
  600.0 52.4 %collective-permute-start.40 = (bf16[256,2048]{1,0:T(8,128)(2,1)S(1)}, bf16[256,2048]{1,0:T(8,128)(2,1)S(1)}, u32[]{:S(2)}, u32[]{:S(2)}) collective-permute-start(bf16[256,2048]{1,0:T(8,128)(2,1)S(1)} %get-tuple-element.99), channel_id=1, source_target_pairs={{0,1},{3,2},{4,5},{7,6},{8,9},{11,10},{12,13},{15,14},{16,17},{19,... | collective-permute-start | bytes 3145736 | tf_op jit(solution)/shard_map/ppermute | solution.py:123
  628.9 44.0 %collective-permute-start.39 = (bf16[256,2048]{1,0:T(8,128)(2,1)}, bf16[256,2048]{1,0:T(8,128)(2,1)S(1)}, u32[]{:S(2)}, u32[]{:S(2)}) collective-permute-start(bf16[256,2048]{1,0:T(8,128)(2,1)} %get-tuple-element.145), channel_id=1, source_target_pairs={{0,1},{1,0},{2,3},{3,2},{4,5},{5,4},{6,7},{7,6},{8,9},{9,8},{10,11... | collective-permute-start | bytes 3145736 | tf_op jit(solution)/shard_map/ppermute | solution.py:123
  653.8 19.2 %collective-permute-start.41 = (bf16[256,2048]{1,0:T(8,128)(2,1)}, bf16[256,2048]{1,0:T(8,128)(2,1)}, u32[]{:S(2)}, u32[]{:S(2)}) collective-permute-start(bf16[256,2048]{1,0:T(8,128)(2,1)} %add.365), channel_id=1, source_target_pairs={{1,2},{2,1},{5,6},{6,5},{9,10},{10,9},{13,14},{14,13},{17,18},{18,... | collective-permute-start | bytes 3145736 | tf_op jit(solution)/shard_map/ppermute | solution.py:123
  723.0 58.3 %collective-permute-start.47 = (bf16[4,1024,512]{2,1,0:T(8,128)(2,1)}, bf16[4,1024,512]{2,1,0:T(8,128)(2,1)}, u32[]{:S(2)}, u32[]{:S(2)}) collective-permute-start(bf16[4,1024,512]{2,1,0:T(8,128)(2,1)} %bitcast.166), channel_id=1, source_target_pairs={{0,4},{4,0},{8,12},{12,8},{16,20},{20,16},{24,28},{28,24},{1,5},{5... | collective-permute-start | bytes 12582920 | tf_op jit(solution)/shard_map/ppermute | solution.py:79
  751.1 27.9 %collective-permute-start.42 = (bf16[256,2048]{1,0:T(8,128)(2,1)}, bf16[256,2048]{1,0:T(8,128)(2,1)}, u32[]{:S(2)}, u32[]{:S(2)}) collective-permute-start(bf16[256,2048]{1,0:T(8,128)(2,1)} %constant_dynamic-slice_fusion.13), channel_id=1, source_target_pairs={{0,1},{3,2},{4,5},{7,6},{8,9},{11,10},{12,13},{15,14},{16,17},{19,... | collective-permute-start | bytes 3145736 | tf_op jit(solution)/shard_map/ppermute | solution.py:123
  762.0 106.0 %collective-permute-start.55 = (bf16[4,2048,256]{2,1,0:T(8,128)(2,1)}, bf16[4,2048,256]{2,1,0:T(8,128)(2,1)}, u32[]{:S(2)}, u32[]{:S(2)}) collective-permute-start(bf16[4,2048,256]{2,1,0:T(8,128)(2,1)} %unit_grad.12), channel_id=1, source_target_pairs={{0,4},{4,0},{8,12},{12,8},{16,20},{20,16},{24,28},{28,24},{1,5},{5... | collective-permute-start | bytes 12582920 | tf_op jit(solution)/shard_map/ppermute | solution.py:79
  765.4 109.4 %collective-permute-start.54 = (bf16[4,256,2048]{2,1,0:T(8,128)(2,1)}, bf16[4,256,2048]{2,1,0:T(8,128)(2,1)}, u32[]{:S(2)}, u32[]{:S(2)}) collective-permute-start(bf16[4,256,2048]{2,1,0:T(8,128)(2,1)} %bitcast.30), channel_id=1, source_target_pairs={{0,4},{4,0},{8,12},{12,8},{16,20},{20,16},{24,28},{28,24},{1,5},{5... | collective-permute-start | bytes 12582920 | tf_op jit(solution)/shard_map/ppermute | solution.py:79
  787.5 36.4 %collective-permute-start.49 = (bf16[1024,512]{1,0:T(8,128)(2,1)}, bf16[1024,512]{1,0:T(8,128)(2,1)}, u32[]{:S(2)}, u32[]{:S(2)}) collective-permute-start(bf16[1024,512]{1,0:T(8,128)(2,1)} %get-tuple-element.111), channel_id=1, source_target_pairs={{0,16},{4,12},{8,24},{12,4},{16,0},{20,28},{24,8},{28,20},{1,17},{... | collective-permute-start | bytes 3145736 | tf_op jit(solution)/shard_map/ppermute | solution.py:79
  789.0 56.0 %collective-permute-start.44 = (bf16[256,2048]{1,0:T(8,128)(2,1)}, bf16[256,2048]{1,0:T(8,128)(2,1)}, u32[]{:S(2)}, u32[]{:S(2)}) collective-permute-start(bf16[256,2048]{1,0:T(8,128)(2,1)} %get-tuple-element.143), channel_id=1, source_target_pairs={{0,1},{1,0},{2,3},{3,2},{4,5},{5,4},{6,7},{7,6},{8,9},{9,8},{10,11... | collective-permute-start | bytes 3145736 | tf_op jit(solution)/shard_map/ppermute | solution.py:123
  822.0 42.7 %collective-permute-start.45 = (bf16[256,2048]{1,0:T(8,128)(2,1)S(1)}, bf16[256,2048]{1,0:T(8,128)(2,1)S(1)}, u32[]{:S(2)}, u32[]{:S(2)}) collective-permute-start(bf16[256,2048]{1,0:T(8,128)(2,1)S(1)} %get-tuple-element.109), channel_id=1, source_target_pairs={{0,1},{3,2},{4,5},{7,6},{8,9},{11,10},{12,13},{15,14},{16,17},{19,... | collective-permute-start | bytes 3145736 | tf_op jit(solution)/shard_map/ppermute | solution.py:123
  824.0 50.9 %collective-permute-start.48 = (bf16[1024,512]{1,0:T(8,128)(2,1)}, bf16[1024,512]{1,0:T(8,128)(2,1)S(1)}, u32[]{:S(2)}, u32[]{:S(2)}) collective-permute-start(bf16[1024,512]{1,0:T(8,128)(2,1)} %get-tuple-element.110), channel_id=1, source_target_pairs={{0,16},{4,12},{8,24},{12,4},{16,0},{20,28},{24,8},{28,20},{1,17},{... | collective-permute-start | bytes 3145736 | tf_op jit(solution)/shard_map/ppermute | solution.py:79
  845.0 33.6 %collective-permute-start.50 = (bf16[1024,512]{1,0:T(8,128)(2,1)S(1)}, bf16[1024,512]{1,0:T(8,128)(2,1)S(1)}, u32[]{:S(2)}, u32[]{:S(2)}) collective-permute-start(bf16[1024,512]{1,0:T(8,128)(2,1)S(1)} %fusion.18), channel_id=1, source_target_pairs={{0,8},{4,20},{8,0},{12,28},{16,24},{20,4},{24,16},{28,12},{1,9},{5... | collective-permute-start | bytes 3145736 | tf_op jit(solution)/shard_map/ppermute | solution.py:79
  866.1 55.6 %collective-permute-start.46 = (bf16[256,2048]{1,0:T(8,128)(2,1)}, bf16[256,2048]{1,0:T(8,128)(2,1)}, u32[]{:S(2)}, u32[]{:S(2)}) collective-permute-start(bf16[256,2048]{1,0:T(8,128)(2,1)} %add.372), channel_id=1, source_target_pairs={{1,2},{2,1},{5,6},{6,5},{9,10},{10,9},{13,14},{14,13},{17,18},{18,... | collective-permute-start | bytes 3145736 | tf_op jit(solution)/shard_map/ppermute | solution.py:123
  885.3 26.9 %collective-permute-start.52 = (bf16[256,512]{1,0:T(8,128)(2,1)S(1)}, bf16[256,512]{1,0:T(8,128)(2,1)S(1)}, u32[]{:S(2)}, u32[]{:S(2)}) collective-permute-start(bf16[256,512]{1,0:T(8,128)(2,1)S(1)} %get-tuple-element.161), channel_id=1, source_target_pairs={{0,2},{1,3},{2,0},{3,1},{4,6},{5,7},{6,4},{7,5},{8,10},{9,11},{10,... | collective-permute-start | bytes 786440 | tf_op jit(solution)/shard_map/ppermute | solution.py:123
  885.4 26.8 %collective-permute-start.53 = (bf16[256,512]{1,0:T(8,128)(2,1)S(1)}, bf16[256,512]{1,0:T(8,128)(2,1)S(1)}, u32[]{:S(2)}, u32[]{:S(2)}) collective-permute-start(bf16[256,512]{1,0:T(8,128)(2,1)S(1)} %get-tuple-element.160), channel_id=1, source_target_pairs={{0,3},{1,2},{2,1},{3,0},{4,7},{5,6},{6,5},{7,4},{8,11},{9,10},{10,... | collective-permute-start | bytes 786440 | tf_op jit(solution)/shard_map/ppermute | solution.py:123
  890.9 38.6 %collective-permute-start.57 = (bf16[2048,256]{1,0:T(8,128)(2,1)}, bf16[2048,256]{1,0:T(8,128)(2,1)}, u32[]{:S(2)}, u32[]{:S(2)}) collective-permute-start(bf16[2048,256]{1,0:T(8,128)(2,1)} %add.389), channel_id=1, source_target_pairs={{0,8},{4,20},{8,0},{12,28},{16,24},{20,4},{24,16},{28,12},{1,9},{5... | collective-permute-start | bytes 3145736 | tf_op jit(solution)/shard_map/ppermute | solution.py:79
  892.1 37.4 %collective-permute-start.59 = (bf16[2048,256]{1,0:T(8,128)(2,1)}, bf16[2048,256]{1,0:T(8,128)(2,1)}, u32[]{:S(2)}, u32[]{:S(2)}) collective-permute-start(bf16[2048,256]{1,0:T(8,128)(2,1)} %get-tuple-element.119), channel_id=1, source_target_pairs={{0,16},{4,12},{8,24},{12,4},{16,0},{20,28},{24,8},{28,20},{1,17},{... | collective-permute-start | bytes 3145736 | tf_op jit(solution)/shard_map/ppermute | solution.py:79
  932.6 37.6 %collective-permute-start.72 = (bf16[512,256]{1,0:T(8,128)(2,1)}, bf16[512,256]{1,0:T(8,128)(2,1)}, u32[]{:S(2)}, u32[]{:S(2)}) collective-permute-start(bf16[512,256]{1,0:T(8,128)(2,1)} %get-tuple-element.151), channel_id=1, source_target_pairs={{0,1},{1,0},{2,3},{3,2},{4,5},{5,4},{6,7},{7,6},{8,9},{9,8},{10,11... | collective-permute-start | bytes 786440 | tf_op jit(solution)/shard_map/ppermute | solution.py:123
  935.9 34.2 %collective-permute-start.73 = (bf16[512,256]{1,0:T(8,128)(2,1)}, bf16[512,256]{1,0:T(8,128)(2,1)}, u32[]{:S(2)}, u32[]{:S(2)}) collective-permute-start(bf16[512,256]{1,0:T(8,128)(2,1)} %get-tuple-element.153), channel_id=1, source_target_pairs={{0,2},{1,3},{2,0},{3,1},{4,6},{5,7},{6,4},{7,5},{8,10},{9,11},{10,... | collective-permute-start | bytes 786440 | tf_op jit(solution)/shard_map/ppermute | solution.py:123
  936.5 33.6 %collective-permute-start.74 = (bf16[512,256]{1,0:T(8,128)(2,1)}, bf16[512,256]{1,0:T(8,128)(2,1)}, u32[]{:S(2)}, u32[]{:S(2)}) collective-permute-start(bf16[512,256]{1,0:T(8,128)(2,1)} %get-tuple-element.152), channel_id=1, source_target_pairs={{0,3},{1,2},{2,1},{3,0},{4,7},{5,6},{6,5},{7,4},{8,11},{9,10},{10,... | collective-permute-start | bytes 786440 | tf_op jit(solution)/shard_map/ppermute | solution.py:123
  938.3 25.6 %collective-permute-start.58 = (bf16[256,2048]{1,0:T(8,128)(2,1)S(1)}, bf16[256,2048]{1,0:T(8,128)(2,1)S(1)}, u32[]{:S(2)}, u32[]{:S(2)}) collective-permute-start(bf16[256,2048]{1,0:T(8,128)(2,1)S(1)} %copy-done.50), channel_id=1, source_target_pairs={{0,16},{4,12},{8,24},{12,4},{16,0},{20,28},{24,8},{28,20},{1,17},{... | collective-permute-start | bytes 3145736 | tf_op jit(solution)/shard_map/ppermute | solution.py:79
  945.9 27.6 %collective-permute-start.61 = (bf16[256,2048]{1,0:T(8,128)(2,1)S(1)}, bf16[256,2048]{1,0:T(8,128)(2,1)}, u32[]{:S(2)}, u32[]{:S(2)}) collective-permute-start(bf16[256,2048]{1,0:T(8,128)(2,1)S(1)} %fusion.17), channel_id=1, source_target_pairs={{0,8},{4,20},{8,0},{12,28},{16,24},{20,4},{24,16},{28,12},{1,9},{5... | collective-permute-start | bytes 3145736 | tf_op jit(solution)/shard_map/ppermute | solution.py:79
  981.1 21.4 %collective-permute-start.63 = (bf16[256,512]{1,0:T(8,128)(2,1)S(1)}, bf16[256,512]{1,0:T(8,128)(2,1)S(1)}, u32[]{:S(2)}, u32[]{:S(2)}) collective-permute-start(bf16[256,512]{1,0:T(8,128)(2,1)S(1)} %get-tuple-element.156), channel_id=1, source_target_pairs={{0,2},{1,3},{2,0},{3,1},{4,6},{5,7},{6,4},{7,5},{8,10},{9,11},{10,... | collective-permute-start | bytes 786440 | tf_op jit(solution)/shard_map/ppermute | solution.py:123
  981.8 20.7 %collective-permute-start.64 = (bf16[256,512]{1,0:T(8,128)(2,1)S(1)}, bf16[256,512]{1,0:T(8,128)(2,1)S(1)}, u32[]{:S(2)}, u32[]{:S(2)}) collective-permute-start(bf16[256,512]{1,0:T(8,128)(2,1)S(1)} %get-tuple-element.155), channel_id=1, source_target_pairs={{0,3},{1,2},{2,1},{3,0},{4,7},{5,6},{6,5},{7,4},{8,11},{9,10},{10,... | collective-permute-start | bytes 786440 | tf_op jit(solution)/shard_map/ppermute | solution.py:123
  983.7 19.7 %collective-permute-start.69 = (bf16[80,512]{1,0:T(8,128)(2,1)S(1)}, bf16[80,512]{1,0:T(8,128)(2,1)S(1)}, u32[]{:S(2)}, u32[]{:S(2)}) collective-permute-start(bf16[80,512]{1,0:T(8,128)(2,1)S(1)} %get-tuple-element.162), channel_id=1, source_target_pairs={{0,1},{1,0},{2,3},{3,2},{4,5},{5,4},{6,7},{7,6},{8,9},{9,8},{10,11... | collective-permute-start | bytes 245768 | tf_op jit(solution)/shard_map/ppermute | solution.py:123
  984.8 23.3 %collective-permute-start.70 = (bf16[80,512]{1,0:T(8,128)(2,1)S(1)}, bf16[80,512]{1,0:T(8,128)(2,1)S(1)}, u32[]{:S(2)}, u32[]{:S(2)}) collective-permute-start(bf16[80,512]{1,0:T(8,128)(2,1)S(1)} %get-tuple-element.164), channel_id=1, source_target_pairs={{0,2},{1,3},{2,0},{3,1},{4,6},{5,7},{6,4},{7,5},{8,10},{9,11},{10,... | collective-permute-start | bytes 245768 | tf_op jit(solution)/shard_map/ppermute | solution.py:123
  990.5 17.6 %collective-permute-start.71 = (bf16[80,512]{1,0:T(8,128)(2,1)S(1)}, bf16[80,512]{1,0:T(8,128)(2,1)S(1)}, u32[]{:S(2)}, u32[]{:S(2)}) collective-permute-start(bf16[80,512]{1,0:T(8,128)(2,1)S(1)} %get-tuple-element.163), channel_id=1, source_target_pairs={{0,3},{1,2},{2,1},{3,0},{4,7},{5,6},{6,5},{7,4},{8,11},{9,10},{10,... | collective-permute-start | bytes 245768 | tf_op jit(solution)/shard_map/ppermute | solution.py:123
  (96 other events, 2841.5 us)
Sparse Core Ops, SparseCore 0:
  9.9 75.1 all-gather.7
  128.9 84.1 all-gather.5
  215.0 79.9 all-gather.9
  544.2 84.6 reduce-scatter.5
  632.8 85.3 reduce-scatter.3
  732.5 113.7 reduce-scatter.7

commit v4 on v3

--- a/solution.py
+++ b/solution.py
@@ -147,7 +147,7 @@
         )
         far = slot3 + after(self.send(slot3, inward), beside[0])
         near = self.send(after(slot2, far), inward)
-        next_door = slot1 + after(self.send(far, middle), beside[1])
+        next_door = slot1 + after(self.send(far, middle), near, beside[1])
         near = slot2 + near
         return [own, after(self.send(next_door, pair), beside[2]), self.send(near, middle)]
 
@@ -671,6 +671,7 @@
     q_span = head.gather_small(q_weight, 1)
     out_span = head.gather_small(out_weight, 0)
     q_a, q_b = seq.gather(q_span)
+    out_a, out_b = seq.gather(out_span, axis=1)
 
     kv_rows_each = kv_weight.shape[0]
     sizes = [q_bias.shape[0], kv_bias.shape[0], attn_gain.shape[0], ffn_gain.shape[0]]
@@ -732,10 +733,9 @@
         + jnp.dot(normed[:, half:], q_b, preferred_element_type=F32)
         + q_bias_full
     )
-    kv_span = head.gather_small(after(kv_rows, q_span, out_span), 0)
+    kv_span = head.gather_small(after(kv_rows, q_a, out_span), 0)
     cotangent_late = after(cotangent16, kv_span, gate_all)
     kv_halves = seq.gather(after(kv_span, cotangent_late))
-    out_a, out_b = seq.gather(out_span, axis=1)
     grad_all = lax.all_gather(cotangent_late, "head", axis=0, tiled=True)
     up_all = lax.all_gather(after(up_weight.T, kv_halves[0]), "seq", axis=0, tiled=False)
     queries, mixed, lse = attention_forward(*where, query_raw, *tables, *kv_halves)
@@ -776,7 +776,7 @@
         whole_grad(act, grad_all), whole_grad(d_gate, normed2_all), whole_grad(d_up, normed2_all)
     ]
     d_normed2 = total(head.reduce(d_normed2_terms, terms))
-    down_grad, gate_grad, up_grad = (scattered(whole) for whole in terms)
+    down_grad, gate_grad, up_grad = (scattered(after(whole, d_normed2)) for whole in terms)
     gate_grad, up_grad = gate_grad.T, up_grad.T
 
     d_hidden_norm, ffn_gain_grad = norm_backward(hidden, ffn_scale, ffn_gain32, d_normed2)

time: 1040 us -> 968 us (0.931)
  waiting for transfers between devices: 402 us -> 372 us
  Pallas kernels: 243 us -> 221 us
  starting transfers between devices: 179 us -> 161 us
  other arithmetic: 78.9 us -> 90.5 us
    ppermute x39, waiting for transfers between devices: 218 us -> 142 us  [send(): return lax.ppermute(value, 'head', pairs)]
    ppermute x39, starting transfers between devices: 142 us -> 96.6 us  [send(): return lax.ppermute(value, 'head', pairs)]
    ppermute x36, waiting for transfers between devices: 183 us -> 228 us  [send(): return lax.ppermute(item, 'seq', pairs)]
    ppermute x36, starting transfers between devices: 36.6 us -> 64.3 us  [send(): return lax.ppermute(item, 'seq', pairs)]
    pallas_call x1, Pallas kernels: 35.6 us -> 22.3 us  [attention_backward(): pl.pallas_call(backward_kernel, out_shape=(jax.ShapeDtypeStruct((rows, HE...]
    unnamed x171 -> x159, local copies, waits for them, and re-layouts: 34.5 us -> 27.3 us
  transfers between devices with their start and end apart: 81 -> 81, of which waited for: 32 -> 31; matrix products, arithmetic and copies ran while one was open for 15% -> 16% of each run, Pallas kernels for 15% -> 15%
where the time goes in v4:
time: 968 us; the launch traced here: 960 us
  waiting for transfers between devices  372 us (38%)
  Pallas kernels  221 us (23%)
  starting transfers between devices  161 us (17%)
  other arithmetic  90.5 us (9%)
  local copies, waits for them, and re-layouts  54.2 us (6%)
  matrix products  36.8 us (4%)
  between operations  24.3 us (3%)
    ppermute x36, waiting for transfers between devices, send(): return lax.ppermute(item, 'seq', pairs)  228 us
    ppermute x39, waiting for transfers between devices, send(): return lax.ppermute(value, 'head', pairs)  142 us
    ppermute x39, starting transfers between devices, send(): return lax.ppermute(value, 'head', pairs)  96.6 us
    pallas_call x7, Pallas kernels, unit_grad(): pl.pallas_call(functools.partial(unit_grad_kernel, count, shift, len(extr...  70.6 us
    ppermute x36, starting transfers between devices, send(): return lax.ppermute(item, 'seq', pairs)  64.3 us
    pallas_call x1, Pallas kernels, ffn_middle(): pl.pallas_call(ffn_kernel, out_shape=(jax.ShapeDtypeStruct((rows, units),...  44.1 us
    pallas_call x1, Pallas kernels, ffn_back(): pl.pallas_call(back_kernel, out_shape=jax.ShapeDtypeStruct((rows, pieces...  31.5 us
    unnamed x159, local copies, waits for them, and re-layouts  27.3 us
  transfers between devices with their start and end apart: 81, of which 31 were waited for; matrix products, arithmetic and copies ran while one was open for 16% of the time, Pallas kernels for 15%

profile of v4, /device:TPU:0, one launch (start us, length us, event | category | flops | bytes accessed | tf_op | source)
XLA Modules:
  0.0 959.5 jit_solution(17171825828194128866)
XLA Ops:
  16.2 3.5 collective-permute-start.8
  36.2 9.5 collective-permute-done.3
  49.4 7.9 collective-permute-done.5
  70.3 11.3 %collective-permute-done.15.refs_2_ = bf16[512,256]{1,0:T(8,128)(2,1)} collective-permute-done((bf16[512,256]{1,0:T(8,128)(2,1)}, bf16[512,256]{1,0:T(8,128)(2,1)}, u32[]{:S(2)}, u32[]{:S(2)}) %collective-permute-start.15) | collective-permute-done | bytes 262176 | tf_op jit(solution)/shard_map/ppermute | solution.py:123
  86.0 16.8 %collective-permute-done.10 = bf16[256,2048]{1,0:T(8,128)(2,1)} collective-permute-done((bf16[256,2048]{1,0:T(8,128)(2,1)}, bf16[256,2048]{1,0:T(8,128)(2,1)}, u32[]{:S(2)}, u32[]{:S(2)}) %collective-permute-start.10) | collective-permute-done | bytes 1048608 | tf_op jit(solution)/shard_map/ppermute | solution.py:79
  118.1 3.6 pad_maximum_fusion
  126.1 9.5 collective-permute-done.17.refs_1_
  135.6 8.9 collective-permute-done.18.refs_2_
  150.3 23.3 %collective-permute-done.22 = bf16[2048,256]{1,0:T(8,128)(2,1)S(1)} collective-permute-done((bf16[2048,256]{1,0:T(8,128)(2,1)S(1)}, bf16[2048,256]{1,0:T(8,128)(2,1)S(1)}, u32[]{:S(2)}, u32[]{:S(2)}) %collective-permute-start.22) | collective-permute-done | bytes 1048608 | tf_op jit(solution)/shard_map/ppermute | solution.py:79
  174.9 20.5 %collective-permute-done.23 = bf16[2048,256]{1,0:T(8,128)(2,1)S(1)} collective-permute-done((bf16[2048,256]{1,0:T(8,128)(2,1)S(1)}, bf16[2048,256]{1,0:T(8,128)(2,1)S(1)}, u32[]{:S(2)}, u32[]{:S(2)}) %collective-permute-start.23) | collective-permute-done | bytes 1048608 | tf_op jit(solution)/shard_map/ppermute | solution.py:79
  200.4 10.0 %collective-permute-done.24 = bf16[1024,512]{1,0:T(8,128)(2,1)S(1)} collective-permute-done((bf16[1024,512]{1,0:T(8,128)(2,1)}, bf16[1024,512]{1,0:T(8,128)(2,1)S(1)}, u32[]{:S(2)}, u32[]{:S(2)}) %collective-permute-start.24) | collective-permute-done | bytes 1048608 | tf_op jit(solution)/shard_map/ppermute | solution.py:79
  210.4 11.2 %collective-permute-done.25 = bf16[1024,512]{1,0:T(8,128)(2,1)S(1)} collective-permute-done((bf16[1024,512]{1,0:T(8,128)(2,1)S(1)}, bf16[1024,512]{1,0:T(8,128)(2,1)S(1)}, u32[]{:S(2)}, u32[]{:S(2)}) %collective-permute-start.25) | collective-permute-done | bytes 1048608 | tf_op jit(solution)/shard_map/ppermute | solution.py:79
  224.3 3.6 pad_maximum_fusion.1
  236.0 3.8 fusion.41
  241.5 11.2 %attention_forward.1 = (bf16[16,256,128]{2,1,0:T(8,128)(2,1)S(1)}, bf16[256,2048]{1,0:T(8,128)(2,1)S(1)}, f32[16,1,256]{2,1,0:T(1,128)S(1)}) custom-call(s32[16]{0:T(128)S(1)} %fusion.34.offset_ref, s32[2]{0:T(128)S(1)} %pad_add_fusion.1.bound_ref, f32[256,2048]{1,0:T(8,128)S(1)} %fusion.2.raw_ref, f32[256,128]{1,0:T(8,128)S(1)} %pad_maximum_fusion.5.cos_ref, ...), custom_call_target="tpu_custom_call" | custom-call | flops 4294967296 | bytes 12582912 | tf_op jit(solution)/shard_map/attention_forward/pallas_call | solution.py:308
  252.7 4.2 fusion.53
  257.0 3.5 fusion.54
  261.1 7.4 collective-permute-start.28
  270.2 22.3 %collective-permute-done.28.refs_1_ = bf16[256,2048]{1,0:T(8,128)(2,1)S(1)} collective-permute-done((bf16[256,2048]{1,0:T(8,128)(2,1)S(1)}, bf16[256,2048]{1,0:T(8,128)(2,1)S(1)}, u32[]{:S(2)}, u32[]{:S(2)}) %collective-permute-start.28) | collective-permute-done | bytes 1048608 | tf_op jit(solution)/shard_map/ppermute | solution.py:123
  298.1 23.9 %collective-permute-done.30 = bf16[256,2048]{1,0:T(8,128)(2,1)} collective-permute-done((bf16[256,2048]{1,0:T(8,128)(2,1)}, bf16[256,2048]{1,0:T(8,128)(2,1)}, u32[]{:S(2)}, u32[]{:S(2)}) %collective-permute-start.30) | collective-permute-done | bytes 1048608 | tf_op jit(solution)/shard_map/ppermute | solution.py:123
  324.4 20.8 %collective-permute-done.32 = bf16[256,2048]{1,0:T(8,128)(2,1)} collective-permute-done((bf16[256,2048]{1,0:T(8,128)(2,1)}, bf16[256,2048]{1,0:T(8,128)(2,1)}, u32[]{:S(2)}, u32[]{:S(2)}) %collective-permute-start.32) | collective-permute-done | bytes 1048608 | tf_op jit(solution)/shard_map/ppermute | solution.py:123
  347.5 4.4 place.9.normed_ref.right_ref
  359.6 11.2 %collective-permute-done.35 = bf16[2752,256]{1,0:T(8,128)(2,1)S(1)} collective-permute-done((bf16[2752,256]{1,0:T(8,128)(2,1)}, bf16[2752,256]{1,0:T(8,128)(2,1)S(1)}, u32[]{:S(2)}, u32[]{:S(2)}) %collective-permute-start.35) | collective-permute-done | bytes 1409056 | tf_op jit(solution)/shard_map/ppermute | solution.py:79
  375.3 6.3 collective-permute-done.36
  383.8 44.1 %ffn_middle.1 = (bf16[1024,2752]{1,0:T(8,128)(2,1)}, bf16[1024,2752]{1,0:T(8,128)(2,1)}, bf16[1024,2752]{1,0:T(8,128)(2,1)}) custom-call(s32[8]{0:T(128)S(1)} %copy-done.18, bf16[1024,2048]{1,0:T(8,128)(2,1)S(1)} %copy-done.8, bf16[1024,2048]{1,0:T(8,128)(2,1)} %all-gather.6.cloned.1.call-done.grad_ref.right_ref, bf16[8,2752,256]{2,1,0:T(8,128)(2,1)} %bitcast.163, ...), custom_call_target="tpu_custom_call" | custom-call | flops 34628173824 | bytes 59113472 | tf_op jit(solution)/shard_map/ffn_middle/pallas_call | solution.py:481
  428.0 31.5 %ffn_back.1 = bf16[1024,2048]{1,0:T(8,128)(2,1)S(1)} custom-call(s32[8]{0:T(128)S(1)} %copy-done.18, bf16[1024,2752]{1,0:T(8,128)(2,1)} %get-tuple-element.99.d_gate_ref.left_ref, bf16[1024,2752]{1,0:T(8,128)(2,1)} %get-tuple-element.101.d_up_ref.left_ref, bf16[8,2752,256]{2,1,0:T(8,128)(2,1)} %bitcast.164, bf16[8,2752,256]{2,1,0:T(8,128)(2,1)} %bitcast.166), custom_call_target="tpu_custom_call" | custom-call | flops 23085449216 | bytes 33816576 | tf_op jit(solution)/shard_map/ffn_back/pallas_call | solution.py:511
  462.6 15.0 %collective-permute-start.37 = (bf16[256,2048]{1,0:T(8,128)(2,1)}, bf16[256,2048]{1,0:T(8,128)(2,1)}, u32[]{:S(2)}, u32[]{:S(2)}) collective-permute-start(bf16[256,2048]{1,0:T(8,128)(2,1)} %get-tuple-element.151), channel_id=1, source_target_pairs={{0,1},{3,2},{4,5},{7,6},{8,9},{11,10},{12,13},{15,14},{16,17},{19,... | collective-permute-start | bytes 3145736 | tf_op jit(solution)/shard_map/ppermute | solution.py:123
  477.6 17.5 %unit_grad.7 = bf16[8,2752,256]{2,1,0:T(8,128)(2,1)} custom-call(s32[8]{0:T(128)S(1)} %select_reduce_fusion.3.order_ref, bf16[1024,2752]{1,0:T(8,128)(2,1)} %get-tuple-element.103.left_ref.act_ref, bf16[1024,2048]{1,0:T(8,128)(2,1)S(1)} %copy-done.20), custom_call_target="tpu_custom_call" | custom-call | flops 11542724608 | bytes 21102592 | tf_op jit(solution)/shard_map/unit_grad/pallas_call | solution.py:590
  495.1 4.6 collective-permute-done.37
  504.2 7.3 collective-permute-start.39
  513.8 17.5 %unit_grad.8 = bf16[8,2752,256]{2,1,0:T(8,128)(2,1)} custom-call(s32[8]{0:T(128)S(1)} %select_reduce_fusion.3.order_ref, bf16[1024,2752]{1,0:T(8,128)(2,1)} %get-tuple-element.99.d_gate_ref.left_ref, bf16[1024,2048]{1,0:T(8,128)(2,1)S(1)} %copy-done.9), custom_call_target="tpu_custom_call" | custom-call | flops 11542724608 | bytes 21102592 | tf_op jit(solution)/shard_map/unit_grad/pallas_call | solution.py:590
  542.6 17.5 %unit_grad.9 = bf16[8,2752,256]{2,1,0:T(8,128)(2,1)} custom-call(s32[8]{0:T(128)S(1)} %select_reduce_fusion.3.order_ref, bf16[1024,2752]{1,0:T(8,128)(2,1)} %get-tuple-element.101.d_up_ref.left_ref, bf16[1024,2048]{1,0:T(8,128)(2,1)S(1)} %copy-done.10), custom_call_target="tpu_custom_call" | custom-call | flops 11542724608 | bytes 21102592 | tf_op jit(solution)/shard_map/unit_grad/pallas_call | solution.py:590
  560.1 3.7 multiply_reduce_fusion
  564.7 3.8 fusion.46
  568.6 3.8 fusion.21
  572.4 4.6 fusion.3.grad_ref
  577.0 22.3 %attention_backward.1 = (bf16[256,2048]{1,0:T(8,128)(2,1)}, bf16[4096,512]{1,0:T(8,128)(2,1)}, bf16[4096,512]{1,0:T(8,128)(2,1)}) custom-call(s32[16]{0:T(128)} %copy-done.25, s32[2]{0:T(128)} %copy-done.24, bf16[16,256,128]{2,1,0:T(8,128)(2,1)} %copy-done.26, f32[256,128]{1,0:T(8,128)} %copy-done.16, f32[256,128]{1,0:T(8,128)} %copy-done.17, ...), custom_call_target="tpu_custom_call" | custom-call | flops 10737418240 | bytes 20971520 | tf_op jit(solution)/shard_map/attention_backward/pallas_call | solution.py:418
  599.4 18.0 %ffn_forth.1 = bf16[1024,2048]{1,0:T(8,128)(2,1)S(1)} custom-call(bf16[1024,2752]{1,0:T(8,128)(2,1)} %get-tuple-element.103.left_ref.act_ref, bf16[4,2752,256]{2,1,0:T(8,128)(2,1)} %bitcast.18.down_a_ref, bf16[4,2752,256]{2,1,0:T(8,128)(2,1)} %bitcast.19.down_b_ref), custom_call_target="tpu_custom_call" | custom-call | flops 11542724608 | bytes 16908288 | tf_op jit(solution)/shard_map/ffn_forth/pallas_call | solution.py:542
  618.7 7.7 collective-permute-start.42
  626.4 4.0 unit_grad.12
  630.7 18.7 %collective-permute-done.42 = bf16[256,2048]{1,0:T(8,128)(2,1)S(1)} collective-permute-done((bf16[256,2048]{1,0:T(8,128)(2,1)S(1)}, bf16[256,2048]{1,0:T(8,128)(2,1)S(1)}, u32[]{:S(2)}, u32[]{:S(2)}) %collective-permute-start.42) | collective-permute-done | bytes 1048608 | tf_op jit(solution)/shard_map/ppermute | solution.py:123
  652.4 5.7 collective-permute-start.44
  661.7 5.7 add.375
  669.1 23.6 %collective-permute-start.49 = (bf16[1024,512]{1,0:T(8,128)(2,1)}, bf16[1024,512]{1,0:T(8,128)(2,1)}, u32[]{:S(2)}, u32[]{:S(2)}) collective-permute-start(bf16[1024,512]{1,0:T(8,128)(2,1)} %get-tuple-element.114), channel_id=1, source_target_pairs={{0,16},{4,12},{8,24},{12,4},{16,0},{20,28},{24,8},{28,20},{1,17},{... | collective-permute-start | bytes 3145736 | tf_op jit(solution)/shard_map/ppermute | solution.py:79
  695.3 13.0 %collective-permute-start.48 = (bf16[1024,512]{1,0:T(8,128)(2,1)}, bf16[1024,512]{1,0:T(8,128)(2,1)}, u32[]{:S(2)}, u32[]{:S(2)}) collective-permute-start(bf16[1024,512]{1,0:T(8,128)(2,1)} %get-tuple-element.113), channel_id=1, source_target_pairs={{0,16},{4,12},{8,24},{12,4},{16,0},{20,28},{24,8},{28,20},{1,17},{... | collective-permute-start | bytes 3145736 | tf_op jit(solution)/shard_map/ppermute | solution.py:79
  708.4 19.9 %collective-permute-done.49 = bf16[1024,512]{1,0:T(8,128)(2,1)} collective-permute-done((bf16[1024,512]{1,0:T(8,128)(2,1)}, bf16[1024,512]{1,0:T(8,128)(2,1)}, u32[]{:S(2)}, u32[]{:S(2)}) %collective-permute-start.49) | collective-permute-done | bytes 1048608 | tf_op jit(solution)/shard_map/ppermute | solution.py:79
  730.9 4.1 collective-permute-start.50
  735.0 4.4 fusion.55
  745.3 4.5 fusion.56
  749.8 6.1 unit_grad.13
  756.1 16.5 %collective-permute-done.50 = bf16[1024,512]{1,0:T(8,128)(2,1)} collective-permute-done((bf16[1024,512]{1,0:T(8,128)(2,1)}, bf16[1024,512]{1,0:T(8,128)(2,1)}, u32[]{:S(2)}, u32[]{:S(2)}) %collective-permute-start.50) | collective-permute-done | bytes 1048608 | tf_op jit(solution)/shard_map/ppermute | solution.py:79
  780.2 3.8 add_add_fusion.refs_0_
  784.1 3.6 shuffle.4
  787.7 4.5 unit_grad.11
  792.2 3.6 add.389
  803.3 5.2 fusion.12
  812.3 23.8 %collective-permute-done.59 = bf16[2048,256]{1,0:T(8,128)(2,1)} collective-permute-done((bf16[2048,256]{1,0:T(8,128)(2,1)S(1)}, bf16[2048,256]{1,0:T(8,128)(2,1)}, u32[]{:S(2)}, u32[]{:S(2)}) %collective-permute-start.59) | collective-permute-done | bytes 1048608 | tf_op jit(solution)/shard_map/ppermute | solution.py:79
  840.1 3.6 collective-permute-start.73
  846.7 14.3 %collective-permute-done.60 = bf16[256,2048]{1,0:T(8,128)(2,1)S(1)} collective-permute-done((bf16[256,2048]{1,0:T(8,128)(2,1)S(1)}, bf16[256,2048]{1,0:T(8,128)(2,1)S(1)}, u32[]{:S(2)}, u32[]{:S(2)}) %collective-permute-start.60) | collective-permute-done | bytes 1048608 | tf_op jit(solution)/shard_map/ppermute | solution.py:79
  863.5 28.1 %collective-permute-done.58 = bf16[256,2048]{1,0:T(8,128)(2,1)} collective-permute-done((bf16[256,2048]{1,0:T(8,128)(2,1)S(1)}, bf16[256,2048]{1,0:T(8,128)(2,1)}, u32[]{:S(2)}, u32[]{:S(2)}) %collective-permute-start.58) | collective-permute-done | bytes 1048608 | tf_op jit(solution)/shard_map/ppermute | solution.py:79
  908.2 3.5 collective-permute-start.63
  917.6 4.3 collective-permute-done.62
  923.8 6.3 collective-permute-done.63
  931.0 9.9 %collective-permute-done.70 = bf16[80,512]{1,0:T(8,128)(2,1)S(1)} collective-permute-done((bf16[80,512]{1,0:T(8,128)(2,1)S(1)}, bf16[80,512]{1,0:T(8,128)(2,1)S(1)}, u32[]{:S(2)}, u32[]{:S(2)}) %collective-permute-start.70) | collective-permute-done | bytes 81952 | tf_op jit(solution)/shard_map/ppermute | solution.py:123
  (421 shorter events, 216.8 us)
Async XLA Ops:
  7.2 140.2 %all-gather.8.cloned.1.call-start = ((), (), s32[]{:S(2)}) async-start(), calls=%async_computation.7 | async-start | bytes 12681216 | tf_op jit(solution)/shard_map/all_gather | solution.py:670
  7.9 367.4 %all-gather.6.cloned.1.call-start = ((), (), s32[]{:S(2)}) async-start(), calls=%async_computation.3 | async-start | bytes 5242880 | tf_op jit(solution)/shard_map/all_gather | solution.py:739
  9.6 20.0 %collective-permute-start = (bf16[80,512]{1,0:T(8,128)(2,1)S(1)}, bf16[80,512]{1,0:T(8,128)(2,1)S(1)}, u32[]{:S(2)}, u32[]{:S(2)}) collective-permute-start(bf16[80,512]{1,0:T(8,128)(2,1)S(1)} %fusion.28.refs_0_), channel_id=1, source_target_pairs={{0,1},{1,0},{2,3},{3,2},{4,5},{5,4},{6,7},{7,6},{8,9},{9,8},{10,11... | collective-permute-start | bytes 245768 | tf_op jit(solution)/shard_map/ppermute | solution.py:123
  15.3 44.7 %collective-permute-start.7 = (bf16[256,512]{1,0:T(8,128)(2,1)}, bf16[256,512]{1,0:T(8,128)(2,1)}, u32[]{:S(2)}, u32[]{:S(2)}) collective-permute-start(bf16[256,512]{1,0:T(8,128)(2,1)} %refs_0_.4), channel_id=1, source_target_pairs={{0,1},{1,0},{2,3},{3,2},{4,5},{5,4},{6,7},{7,6},{8,9},{9,8},{10,11... | collective-permute-start | bytes 786440 | tf_op jit(solution)/shard_map/ppermute | solution.py:123
  16.2 45.7 %collective-permute-start.8 = (bf16[256,512]{1,0:T(8,128)(2,1)}, bf16[256,512]{1,0:T(8,128)(2,1)}, u32[]{:S(2)}, u32[]{:S(2)}) collective-permute-start(bf16[256,512]{1,0:T(8,128)(2,1)} %refs_0_.4), channel_id=1, source_target_pairs={{0,2},{1,3},{2,0},{3,1},{4,6},{5,7},{6,4},{7,5},{8,10},{9,11},{10,... | collective-permute-start | bytes 786440 | tf_op jit(solution)/shard_map/ppermute | solution.py:123
  29.6 33.7 %collective-permute-start.9 = (bf16[256,512]{1,0:T(8,128)(2,1)S(1)}, bf16[256,512]{1,0:T(8,128)(2,1)}, u32[]{:S(2)}, u32[]{:S(2)}) collective-permute-start(bf16[256,512]{1,0:T(8,128)(2,1)S(1)} %copy-done.58), channel_id=1, source_target_pairs={{0,3},{1,2},{2,1},{3,0},{4,7},{5,6},{6,5},{7,4},{8,11},{9,10},{10,... | collective-permute-start | bytes 786440 | tf_op jit(solution)/shard_map/ppermute | solution.py:123
  47.8 19.9 %collective-permute-start.14 = (bf16[512,256]{1,0:T(8,128)(2,1)}, bf16[512,256]{1,0:T(8,128)(2,1)}, u32[]{:S(2)}, u32[]{:S(2)}) collective-permute-start(bf16[512,256]{1,0:T(8,128)(2,1)} %refs_0_.5), channel_id=1, source_target_pairs={{0,1},{1,0},{2,3},{3,2},{4,5},{5,4},{6,7},{7,6},{8,9},{9,8},{10,11... | collective-permute-start | bytes 786440 | tf_op jit(solution)/shard_map/ppermute | solution.py:123
  59.4 45.7 %collective-permute-start.6 = (bf16[1280,512]{1,0:T(8,128)(2,1)}, bf16[1280,512]{1,0:T(8,128)(2,1)S(1)}, u32[]{:S(2)}, u32[]{:S(2)}) collective-permute-start(bf16[1280,512]{1,0:T(8,128)(2,1)} %pad_maximum_fusion.2), channel_id=1, source_target_pairs={{0,4},{4,0},{8,12},{12,8},{16,20},{20,16},{24,28},{28,24},{1,5},{5... | collective-permute-start | bytes 3932168 | tf_op jit(solution)/shard_map/ppermute | solution.py:79
  59.9 21.6 %collective-permute-start.15 = (bf16[512,256]{1,0:T(8,128)(2,1)}, bf16[512,256]{1,0:T(8,128)(2,1)}, u32[]{:S(2)}, u32[]{:S(2)}) collective-permute-start(bf16[512,256]{1,0:T(8,128)(2,1)} %refs_0_.5), channel_id=1, source_target_pairs={{0,2},{1,3},{2,0},{3,1},{4,6},{5,7},{6,4},{7,5},{8,10},{9,11},{10,... | collective-permute-start | bytes 786440 | tf_op jit(solution)/shard_map/ppermute | solution.py:123
  61.9 19.7 %collective-permute-start.16 = (bf16[512,256]{1,0:T(8,128)(2,1)}, bf16[512,256]{1,0:T(8,128)(2,1)}, u32[]{:S(2)}, u32[]{:S(2)}) collective-permute-start(bf16[512,256]{1,0:T(8,128)(2,1)} %refs_0_.5), channel_id=1, source_target_pairs={{0,3},{1,2},{2,1},{3,0},{4,7},{5,6},{6,5},{7,4},{8,11},{9,10},{10,... | collective-permute-start | bytes 786440 | tf_op jit(solution)/shard_map/ppermute | solution.py:123
  65.5 37.3 %collective-permute-start.10 = (bf16[256,2048]{1,0:T(8,128)(2,1)}, bf16[256,2048]{1,0:T(8,128)(2,1)}, u32[]{:S(2)}, u32[]{:S(2)}) collective-permute-start(bf16[256,2048]{1,0:T(8,128)(2,1)} %place.6), channel_id=1, source_target_pairs={{0,8},{4,20},{8,0},{12,28},{16,24},{20,4},{24,16},{28,12},{1,9},{5... | collective-permute-start | bytes 3145736 | tf_op jit(solution)/shard_map/ppermute | solution.py:79
  67.8 48.6 %collective-permute-start.11 = (bf16[256,2048]{1,0:T(8,128)(2,1)}, bf16[256,2048]{1,0:T(8,128)(2,1)}, u32[]{:S(2)}, u32[]{:S(2)}) collective-permute-start(bf16[256,2048]{1,0:T(8,128)(2,1)} %place.6), channel_id=1, source_target_pairs={{0,16},{4,12},{8,24},{12,4},{16,0},{20,28},{24,8},{28,20},{1,17},{... | collective-permute-start | bytes 3145736 | tf_op jit(solution)/shard_map/ppermute | solution.py:79
  123.1 21.3 %collective-permute-start.18 = (bf16[256,512]{1,0:T(8,128)(2,1)S(1)}, bf16[256,512]{1,0:T(8,128)(2,1)S(1)}, u32[]{:S(2)}, u32[]{:S(2)}) collective-permute-start(bf16[256,512]{1,0:T(8,128)(2,1)S(1)} %pad_maximum_fusion.3.refs_0_), channel_id=1, source_target_pairs={{0,2},{1,3},{2,0},{3,1},{4,6},{5,7},{6,4},{7,5},{8,10},{9,11},{10,... | collective-permute-start | bytes 786440 | tf_op jit(solution)/shard_map/ppermute | solution.py:123
  125.6 18.9 %collective-permute-start.19 = (bf16[256,512]{1,0:T(8,128)(2,1)S(1)}, bf16[256,512]{1,0:T(8,128)(2,1)}, u32[]{:S(2)}, u32[]{:S(2)}) collective-permute-start(bf16[256,512]{1,0:T(8,128)(2,1)S(1)} %pad_maximum_fusion.3.refs_0_), channel_id=1, source_target_pairs={{0,3},{1,2},{2,1},{3,0},{4,7},{5,6},{6,5},{7,4},{8,11},{9,10},{10,... | collective-permute-start | bytes 786440 | tf_op jit(solution)/shard_map/ppermute | solution.py:123
  147.4 234.2 %all-gather.10.cloned.1.call-start = ((), (), s32[]{:S(2)}) async-start(), calls=%async_computation.8 | async-start | bytes 12681216 | tf_op jit(solution)/shard_map/all_gather | solution.py:740
  147.5 26.2 %collective-permute-start.22 = (bf16[2048,256]{1,0:T(8,128)(2,1)S(1)}, bf16[2048,256]{1,0:T(8,128)(2,1)S(1)}, u32[]{:S(2)}, u32[]{:S(2)}) collective-permute-start(bf16[2048,256]{1,0:T(8,128)(2,1)S(1)} %copy-done.41), channel_id=1, source_target_pairs={{0,8},{4,20},{8,0},{12,28},{16,24},{20,4},{24,16},{28,12},{1,9},{5... | collective-permute-start | bytes 3145736 | tf_op jit(solution)/shard_map/ppermute | solution.py:79
  148.9 25.6 %collective-permute-start.20 = (bf16[2048,256]{1,0:T(8,128)(2,1)S(1)}, bf16[2048,256]{1,0:T(8,128)(2,1)S(1)}, u32[]{:S(2)}, u32[]{:S(2)}) collective-permute-start(bf16[2048,256]{1,0:T(8,128)(2,1)S(1)} %copy-done.41), channel_id=1, source_target_pairs={{0,16},{4,12},{8,24},{12,4},{16,0},{20,28},{24,8},{28,20},{1,17},{... | collective-permute-start | bytes 3145736 | tf_op jit(solution)/shard_map/ppermute | solution.py:79
  173.6 21.7 %collective-permute-start.23 = (bf16[2048,256]{1,0:T(8,128)(2,1)S(1)}, bf16[2048,256]{1,0:T(8,128)(2,1)S(1)}, u32[]{:S(2)}, u32[]{:S(2)}) collective-permute-start(bf16[2048,256]{1,0:T(8,128)(2,1)S(1)} %collective-permute-done.22), channel_id=1, source_target_pairs={{0,16},{4,12},{8,24},{12,4},{16,0},{20,28},{24,8},{28,20},{1,17},{... | collective-permute-start | bytes 3145736 | tf_op jit(solution)/shard_map/ppermute | solution.py:79
  174.6 23.2 %collective-permute-start.21 = (bf16[1024,512]{1,0:T(8,128)(2,1)}, bf16[1024,512]{1,0:T(8,128)(2,1)S(1)}, u32[]{:S(2)}, u32[]{:S(2)}) collective-permute-start(bf16[1024,512]{1,0:T(8,128)(2,1)} %place.8), channel_id=1, source_target_pairs={{0,8},{4,20},{8,0},{12,28},{16,24},{20,4},{24,16},{28,12},{1,9},{5... | collective-permute-start | bytes 3145736 | tf_op jit(solution)/shard_map/ppermute | solution.py:79
  197.8 23.8 %collective-permute-start.25 = (bf16[1024,512]{1,0:T(8,128)(2,1)S(1)}, bf16[1024,512]{1,0:T(8,128)(2,1)S(1)}, u32[]{:S(2)}, u32[]{:S(2)}) collective-permute-start(bf16[1024,512]{1,0:T(8,128)(2,1)S(1)} %collective-permute-done.21), channel_id=1, source_target_pairs={{0,16},{4,12},{8,24},{12,4},{16,0},{20,28},{24,8},{28,20},{1,17},{... | collective-permute-start | bytes 3145736 | tf_op jit(solution)/shard_map/ppermute | solution.py:79
  223.7 719.2 %reduce-scatter.8.cloned.1.call-start = ((), (), s32[]{:S(2)}) async-start(), calls=%async_computation.6 | async-start | bytes 12681216 | tf_op jit(solution)/shard_map/reduce_scatter | solution.py:773
  227.9 29.0 %collective-permute-start.27 = (bf16[2048,1024]{1,0:T(8,128)(2,1)}, bf16[2048,1024]{1,0:T(8,128)(2,1)}, u32[]{:S(2)}, u32[]{:S(2)}) collective-permute-start(bf16[2048,1024]{1,0:T(8,128)(2,1)} %pad_maximum_fusion.1), channel_id=1, source_target_pairs={{0,4},{4,0},{8,12},{12,8},{16,20},{20,16},{24,28},{28,24},{1,5},{5... | collective-permute-start | bytes 12582920 | tf_op jit(solution)/shard_map/ppermute | solution.py:79
  261.1 31.4 %collective-permute-start.28 = (bf16[256,2048]{1,0:T(8,128)(2,1)S(1)}, bf16[256,2048]{1,0:T(8,128)(2,1)S(1)}, u32[]{:S(2)}, u32[]{:S(2)}) collective-permute-start(bf16[256,2048]{1,0:T(8,128)(2,1)S(1)} %multiply_convert_fusion.refs_0_), channel_id=1, source_target_pairs={{0,1},{1,0},{2,3},{3,2},{4,5},{5,4},{6,7},{7,6},{8,9},{9,8},{10,11... | collective-permute-start | bytes 3145736 | tf_op jit(solution)/shard_map/ppermute | solution.py:123
  268.5 25.6 %collective-permute-start.29 = (bf16[256,2048]{1,0:T(8,128)(2,1)S(1)}, bf16[256,2048]{1,0:T(8,128)(2,1)}, u32[]{:S(2)}, u32[]{:S(2)}) collective-permute-start(bf16[256,2048]{1,0:T(8,128)(2,1)S(1)} %multiply_convert_fusion.refs_0_), channel_id=1, source_target_pairs={{1,2},{2,1},{5,6},{6,5},{9,10},{10,9},{13,14},{14,13},{17,18},{18,... | collective-permute-start | bytes 3145736 | tf_op jit(solution)/shard_map/ppermute | solution.py:123
  294.2 27.9 %collective-permute-start.30 = (bf16[256,2048]{1,0:T(8,128)(2,1)}, bf16[256,2048]{1,0:T(8,128)(2,1)}, u32[]{:S(2)}, u32[]{:S(2)}) collective-permute-start(bf16[256,2048]{1,0:T(8,128)(2,1)} %collective-permute-done.29), channel_id=1, source_target_pairs={{1,0},{2,3},{5,4},{6,7},{9,8},{10,11},{13,12},{14,15},{17,16},{18,... | collective-permute-start | bytes 3145736 | tf_op jit(solution)/shard_map/ppermute | solution.py:123
  295.5 49.7 %collective-permute-start.32 = (bf16[256,2048]{1,0:T(8,128)(2,1)}, bf16[256,2048]{1,0:T(8,128)(2,1)}, u32[]{:S(2)}, u32[]{:S(2)}) collective-permute-start(bf16[256,2048]{1,0:T(8,128)(2,1)} %collective-permute-done.31), channel_id=1, source_target_pairs={{1,0},{2,3},{5,4},{6,7},{9,8},{10,11},{13,12},{14,15},{17,16},{18,... | collective-permute-start | bytes 3145736 | tf_op jit(solution)/shard_map/ppermute | solution.py:123
  296.8 55.2 %collective-permute-start.33 = (bf16[2752,256]{1,0:T(8,128)(2,1)}, bf16[2752,256]{1,0:T(8,128)(2,1)}, u32[]{:S(2)}, u32[]{:S(2)}) collective-permute-start(bf16[2752,256]{1,0:T(8,128)(2,1)} %param.29), channel_id=1, source_target_pairs={{0,8},{4,20},{8,0},{12,28},{16,24},{20,4},{24,16},{28,12},{1,9},{5... | collective-permute-start | bytes 4227080 | tf_op jit(solution)/shard_map/ppermute | solution.py:79
  296.8 55.1 %collective-permute-start.34 = (bf16[2752,256]{1,0:T(8,128)(2,1)}, bf16[2752,256]{1,0:T(8,128)(2,1)}, u32[]{:S(2)}, u32[]{:S(2)}) collective-permute-start(bf16[2752,256]{1,0:T(8,128)(2,1)} %param.29), channel_id=1, source_target_pairs={{0,16},{4,12},{8,24},{12,4},{16,0},{20,28},{24,8},{28,20},{1,17},{... | collective-permute-start | bytes 4227080 | tf_op jit(solution)/shard_map/ppermute | solution.py:79
  351.9 18.9 %collective-permute-start.35 = (bf16[2752,256]{1,0:T(8,128)(2,1)}, bf16[2752,256]{1,0:T(8,128)(2,1)S(1)}, u32[]{:S(2)}, u32[]{:S(2)}) collective-permute-start(bf16[2752,256]{1,0:T(8,128)(2,1)} %collective-permute-done.33), channel_id=1, source_target_pairs={{0,16},{4,12},{8,24},{12,4},{16,0},{20,28},{24,8},{28,20},{1,17},{... | collective-permute-start | bytes 4227080 | tf_op jit(solution)/shard_map/ppermute | solution.py:79
  462.6 37.1 %collective-permute-start.37 = (bf16[256,2048]{1,0:T(8,128)(2,1)}, bf16[256,2048]{1,0:T(8,128)(2,1)}, u32[]{:S(2)}, u32[]{:S(2)}) collective-permute-start(bf16[256,2048]{1,0:T(8,128)(2,1)} %get-tuple-element.151), channel_id=1, source_target_pairs={{0,1},{3,2},{4,5},{7,6},{8,9},{11,10},{12,13},{15,14},{16,17},{19,... | collective-permute-start | bytes 3145736 | tf_op jit(solution)/shard_map/ppermute | solution.py:123
  502.6 30.0 %collective-permute-start.38 = (bf16[256,2048]{1,0:T(8,128)(2,1)}, bf16[256,2048]{1,0:T(8,128)(2,1)}, u32[]{:S(2)}, u32[]{:S(2)}) collective-permute-start(bf16[256,2048]{1,0:T(8,128)(2,1)} %add.361), channel_id=1, source_target_pairs={{1,2},{2,1},{5,6},{6,5},{9,10},{10,9},{13,14},{14,13},{17,18},{18,... | collective-permute-start | bytes 3145736 | tf_op jit(solution)/shard_map/ppermute | solution.py:123
  504.2 28.3 %collective-permute-start.39 = (bf16[256,2048]{1,0:T(8,128)(2,1)}, bf16[256,2048]{1,0:T(8,128)(2,1)}, u32[]{:S(2)}, u32[]{:S(2)}) collective-permute-start(bf16[256,2048]{1,0:T(8,128)(2,1)} %get-tuple-element.98), channel_id=1, source_target_pairs={{0,1},{3,2},{4,5},{7,6},{8,9},{11,10},{12,13},{15,14},{16,17},{19,... | collective-permute-start | bytes 3145736 | tf_op jit(solution)/shard_map/ppermute | solution.py:123
  535.6 24.6 %collective-permute-start.40 = (bf16[256,2048]{1,0:T(8,128)(2,1)}, bf16[256,2048]{1,0:T(8,128)(2,1)}, u32[]{:S(2)}, u32[]{:S(2)}) collective-permute-start(bf16[256,2048]{1,0:T(8,128)(2,1)} %dynamic-slice_add_fusion.1), channel_id=1, source_target_pairs={{0,1},{1,0},{2,3},{3,2},{4,5},{5,4},{6,7},{7,6},{8,9},{9,8},{10,11... | collective-permute-start | bytes 3145736 | tf_op jit(solution)/shard_map/ppermute | solution.py:123
  541.0 19.2 %collective-permute-start.41 = (bf16[256,2048]{1,0:T(8,128)(2,1)}, bf16[256,2048]{1,0:T(8,128)(2,1)}, u32[]{:S(2)}, u32[]{:S(2)}) collective-permute-start(bf16[256,2048]{1,0:T(8,128)(2,1)} %add.365), channel_id=1, source_target_pairs={{1,2},{2,1},{5,6},{6,5},{9,10},{10,9},{13,14},{14,13},{17,18},{18,... | collective-permute-start | bytes 3145736 | tf_op jit(solution)/shard_map/ppermute | solution.py:123
  563.9 382.1 %reduce-scatter.6.cloned.1.call-start = ((), (), s32[]{:S(2)}) async-start(), calls=%async_computation.5 | async-start | bytes 12681216 | tf_op jit(solution)/shard_map/reduce_scatter | solution.py:773
  564.5 384.6 %reduce-scatter.4.cloned.1.call-start = ((), (), s32[]{:S(2)}) async-start(), calls=%async_computation.4 | async-start | bytes 12681216 | tf_op jit(solution)/shard_map/reduce_scatter | solution.py:773
  599.3 62.4 %collective-permute-start.47 = (bf16[4,1024,512]{2,1,0:T(8,128)(2,1)}, bf16[4,1024,512]{2,1,0:T(8,128)(2,1)}, u32[]{:S(2)}, u32[]{:S(2)}) collective-permute-start(bf16[4,1024,512]{2,1,0:T(8,128)(2,1)} %bitcast.167), channel_id=1, source_target_pairs={{0,4},{4,0},{8,12},{12,8},{16,20},{20,16},{24,28},{28,24},{1,5},{5... | collective-permute-start | bytes 12582920 | tf_op jit(solution)/shard_map/ppermute | solution.py:79
  618.7 30.7 %collective-permute-start.42 = (bf16[256,2048]{1,0:T(8,128)(2,1)S(1)}, bf16[256,2048]{1,0:T(8,128)(2,1)S(1)}, u32[]{:S(2)}, u32[]{:S(2)}) collective-permute-start(bf16[256,2048]{1,0:T(8,128)(2,1)S(1)} %get-tuple-element.149), channel_id=1, source_target_pairs={{0,1},{3,2},{4,5},{7,6},{8,9},{11,10},{12,13},{15,14},{16,17},{19,... | collective-permute-start | bytes 3145736 | tf_op jit(solution)/shard_map/ppermute | solution.py:123
  630.4 119.3 %collective-permute-start.55 = (bf16[4,2048,256]{2,1,0:T(8,128)(2,1)}, bf16[4,2048,256]{2,1,0:T(8,128)(2,1)}, u32[]{:S(2)}, u32[]{:S(2)}) collective-permute-start(bf16[4,2048,256]{2,1,0:T(8,128)(2,1)} %unit_grad.12), channel_id=1, source_target_pairs={{0,4},{4,0},{8,12},{12,8},{16,20},{20,16},{24,28},{28,24},{1,5},{5... | collective-permute-start | bytes 12582920 | tf_op jit(solution)/shard_map/ppermute | solution.py:79
  650.8 41.9 %collective-permute-start.43 = (bf16[256,2048]{1,0:T(8,128)(2,1)}, bf16[256,2048]{1,0:T(8,128)(2,1)}, u32[]{:S(2)}, u32[]{:S(2)}) collective-permute-start(bf16[256,2048]{1,0:T(8,128)(2,1)} %add.369), channel_id=1, source_target_pairs={{1,2},{2,1},{5,6},{6,5},{9,10},{10,9},{13,14},{14,13},{17,18},{18,... | collective-permute-start | bytes 3145736 | tf_op jit(solution)/shard_map/ppermute | solution.py:123
  652.4 40.3 %collective-permute-start.44 = (bf16[256,2048]{1,0:T(8,128)(2,1)}, bf16[256,2048]{1,0:T(8,128)(2,1)}, u32[]{:S(2)}, u32[]{:S(2)}) collective-permute-start(bf16[256,2048]{1,0:T(8,128)(2,1)} %get-tuple-element.108), channel_id=1, source_target_pairs={{0,1},{3,2},{4,5},{7,6},{8,9},{11,10},{12,13},{15,14},{16,17},{19,... | collective-permute-start | bytes 3145736 | tf_op jit(solution)/shard_map/ppermute | solution.py:123
  661.7 125.9 %collective-permute-start.54 = (bf16[4,256,2048]{2,1,0:T(8,128)(2,1)}, bf16[4,256,2048]{2,1,0:T(8,128)(2,1)}, u32[]{:S(2)}, u32[]{:S(2)}) collective-permute-start(bf16[4,256,2048]{2,1,0:T(8,128)(2,1)} %bitcast.30), channel_id=1, source_target_pairs={{0,4},{4,0},{8,12},{12,8},{16,20},{20,16},{24,28},{28,24},{1,5},{5... | collective-permute-start | bytes 12582920 | tf_op jit(solution)/shard_map/ppermute | solution.py:79
  669.1 59.1 %collective-permute-start.49 = (bf16[1024,512]{1,0:T(8,128)(2,1)}, bf16[1024,512]{1,0:T(8,128)(2,1)}, u32[]{:S(2)}, u32[]{:S(2)}) collective-permute-start(bf16[1024,512]{1,0:T(8,128)(2,1)} %get-tuple-element.114), channel_id=1, source_target_pairs={{0,16},{4,12},{8,24},{12,4},{16,0},{20,28},{24,8},{28,20},{1,17},{... | collective-permute-start | bytes 3145736 | tf_op jit(solution)/shard_map/ppermute | solution.py:79
  695.3 47.3 %collective-permute-start.45 = (bf16[256,2048]{1,0:T(8,128)(2,1)}, bf16[256,2048]{1,0:T(8,128)(2,1)}, u32[]{:S(2)}, u32[]{:S(2)}) collective-permute-start(bf16[256,2048]{1,0:T(8,128)(2,1)} %dynamic-slice_add_fusion), channel_id=1, source_target_pairs={{0,1},{1,0},{2,3},{3,2},{4,5},{5,4},{6,7},{7,6},{8,9},{9,8},{10,11... | collective-permute-start | bytes 3145736 | tf_op jit(solution)/shard_map/ppermute | solution.py:123
  695.3 60.5 %collective-permute-start.48 = (bf16[1024,512]{1,0:T(8,128)(2,1)}, bf16[1024,512]{1,0:T(8,128)(2,1)}, u32[]{:S(2)}, u32[]{:S(2)}) collective-permute-start(bf16[1024,512]{1,0:T(8,128)(2,1)} %get-tuple-element.113), channel_id=1, source_target_pairs={{0,16},{4,12},{8,24},{12,4},{16,0},{20,28},{24,8},{28,20},{1,17},{... | collective-permute-start | bytes 3145736 | tf_op jit(solution)/shard_map/ppermute | solution.py:79
  730.9 41.8 %collective-permute-start.50 = (bf16[1024,512]{1,0:T(8,128)(2,1)}, bf16[1024,512]{1,0:T(8,128)(2,1)}, u32[]{:S(2)}, u32[]{:S(2)}) collective-permute-start(bf16[1024,512]{1,0:T(8,128)(2,1)} %fusion.18), channel_id=1, source_target_pairs={{0,8},{4,20},{8,0},{12,28},{16,24},{20,4},{24,16},{28,12},{1,9},{5... | collective-permute-start | bytes 3145736 | tf_op jit(solution)/shard_map/ppermute | solution.py:79
  742.6 37.1 %collective-permute-start.46 = (bf16[256,2048]{1,0:T(8,128)(2,1)}, bf16[256,2048]{1,0:T(8,128)(2,1)}, u32[]{:S(2)}, u32[]{:S(2)}) collective-permute-start(bf16[256,2048]{1,0:T(8,128)(2,1)} %add.372), channel_id=1, source_target_pairs={{1,2},{2,1},{5,6},{6,5},{9,10},{10,9},{13,14},{14,13},{17,18},{18,... | collective-permute-start | bytes 3145736 | tf_op jit(solution)/shard_map/ppermute | solution.py:123
  755.9 36.3 %collective-permute-start.56 = (bf16[2048,256]{1,0:T(8,128)(2,1)}, bf16[2048,256]{1,0:T(8,128)(2,1)}, u32[]{:S(2)}, u32[]{:S(2)}) collective-permute-start(bf16[2048,256]{1,0:T(8,128)(2,1)} %get-tuple-element.118), channel_id=1, source_target_pairs={{0,16},{4,12},{8,24},{12,4},{16,0},{20,28},{24,8},{28,20},{1,17},{... | collective-permute-start | bytes 3145736 | tf_op jit(solution)/shard_map/ppermute | solution.py:79
  775.9 21.9 %collective-permute-start.51 = (bf16[256,512]{1,0:T(8,128)(2,1)}, bf16[256,512]{1,0:T(8,128)(2,1)}, u32[]{:S(2)}, u32[]{:S(2)}) collective-permute-start(bf16[256,512]{1,0:T(8,128)(2,1)} %get-tuple-element.165), channel_id=1, source_target_pairs={{0,1},{1,0},{2,3},{3,2},{4,5},{5,4},{6,7},{7,6},{8,9},{9,8},{10,11... | collective-permute-start | bytes 786440 | tf_op jit(solution)/shard_map/ppermute | solution.py:123
  776.9 21.5 %collective-permute-start.52 = (bf16[256,512]{1,0:T(8,128)(2,1)S(1)}, bf16[256,512]{1,0:T(8,128)(2,1)}, u32[]{:S(2)}, u32[]{:S(2)}) collective-permute-start(bf16[256,512]{1,0:T(8,128)(2,1)S(1)} %get-tuple-element.167), channel_id=1, source_target_pairs={{0,2},{1,3},{2,0},{3,1},{4,6},{5,7},{6,4},{7,5},{8,10},{9,11},{10,... | collective-permute-start | bytes 786440 | tf_op jit(solution)/shard_map/ppermute | solution.py:123
  779.7 18.6 %collective-permute-start.53 = (bf16[256,512]{1,0:T(8,128)(2,1)S(1)}, bf16[256,512]{1,0:T(8,128)(2,1)}, u32[]{:S(2)}, u32[]{:S(2)}) collective-permute-start(bf16[256,512]{1,0:T(8,128)(2,1)S(1)} %get-tuple-element.166), channel_id=1, source_target_pairs={{0,3},{1,2},{2,1},{3,0},{4,7},{5,6},{6,5},{7,4},{8,11},{9,10},{10,... | collective-permute-start | bytes 786440 | tf_op jit(solution)/shard_map/ppermute | solution.py:123
  795.8 41.4 %collective-permute-start.57 = (bf16[2048,256]{1,0:T(8,128)(2,1)}, bf16[2048,256]{1,0:T(8,128)(2,1)}, u32[]{:S(2)}, u32[]{:S(2)}) collective-permute-start(bf16[2048,256]{1,0:T(8,128)(2,1)} %add.389), channel_id=1, source_target_pairs={{0,8},{4,20},{8,0},{12,28},{16,24},{20,4},{24,16},{28,12},{1,9},{5... | collective-permute-start | bytes 3145736 | tf_op jit(solution)/shard_map/ppermute | solution.py:79
  796.6 39.5 %collective-permute-start.59 = (bf16[2048,256]{1,0:T(8,128)(2,1)S(1)}, bf16[2048,256]{1,0:T(8,128)(2,1)}, u32[]{:S(2)}, u32[]{:S(2)}) collective-permute-start(bf16[2048,256]{1,0:T(8,128)(2,1)S(1)} %copy-done.22), channel_id=1, source_target_pairs={{0,16},{4,12},{8,24},{12,4},{16,0},{20,28},{24,8},{28,20},{1,17},{... | collective-permute-start | bytes 3145736 | tf_op jit(solution)/shard_map/ppermute | solution.py:79
  810.1 34.4 %collective-permute-start.65 = (bf16[4,320,512]{2,1,0:T(8,128)(2,1)S(1)}, bf16[4,320,512]{2,1,0:T(8,128)(2,1)S(1)}, u32[]{:S(2)}, u32[]{:S(2)}) collective-permute-start(bf16[4,320,512]{2,1,0:T(8,128)(2,1)S(1)} %bitcast.156), channel_id=1, source_target_pairs={{0,4},{4,0},{8,12},{12,8},{16,20},{20,16},{24,28},{28,24},{1,5},{5... | collective-permute-start | bytes 3932168 | tf_op jit(solution)/shard_map/ppermute | solution.py:79
  836.1 24.8 %collective-permute-start.60 = (bf16[256,2048]{1,0:T(8,128)(2,1)S(1)}, bf16[256,2048]{1,0:T(8,128)(2,1)S(1)}, u32[]{:S(2)}, u32[]{:S(2)}) collective-permute-start(bf16[256,2048]{1,0:T(8,128)(2,1)S(1)} %get-tuple-element.123), channel_id=1, source_target_pairs={{0,16},{4,12},{8,24},{12,4},{16,0},{20,28},{24,8},{28,20},{1,17},{... | collective-permute-start | bytes 3145736 | tf_op jit(solution)/shard_map/ppermute | solution.py:79
  840.1 56.5 %collective-permute-start.72 = (bf16[512,256]{1,0:T(8,128)(2,1)}, bf16[512,256]{1,0:T(8,128)(2,1)}, u32[]{:S(2)}, u32[]{:S(2)}) collective-permute-start(bf16[512,256]{1,0:T(8,128)(2,1)} %get-tuple-element.157), channel_id=1, source_target_pairs={{0,1},{1,0},{2,3},{3,2},{4,5},{5,4},{6,7},{7,6},{8,9},{9,8},{10,11... | collective-permute-start | bytes 786440 | tf_op jit(solution)/shard_map/ppermute | solution.py:123
  840.1 56.5 %collective-permute-start.73 = (bf16[512,256]{1,0:T(8,128)(2,1)}, bf16[512,256]{1,0:T(8,128)(2,1)}, u32[]{:S(2)}, u32[]{:S(2)}) collective-permute-start(bf16[512,256]{1,0:T(8,128)(2,1)} %get-tuple-element.159), channel_id=1, source_target_pairs={{0,2},{1,3},{2,0},{3,1},{4,6},{5,7},{6,4},{7,5},{8,10},{9,11},{10,... | collective-permute-start | bytes 786440 | tf_op jit(solution)/shard_map/ppermute | solution.py:123
  843.8 52.9 %collective-permute-start.74 = (bf16[512,256]{1,0:T(8,128)(2,1)}, bf16[512,256]{1,0:T(8,128)(2,1)}, u32[]{:S(2)}, u32[]{:S(2)}) collective-permute-start(bf16[512,256]{1,0:T(8,128)(2,1)} %get-tuple-element.158), channel_id=1, source_target_pairs={{0,3},{1,2},{2,1},{3,0},{4,7},{5,6},{6,5},{7,4},{8,11},{9,10},{10,... | collective-permute-start | bytes 786440 | tf_op jit(solution)/shard_map/ppermute | solution.py:123
  844.5 47.1 %collective-permute-start.58 = (bf16[256,2048]{1,0:T(8,128)(2,1)S(1)}, bf16[256,2048]{1,0:T(8,128)(2,1)}, u32[]{:S(2)}, u32[]{:S(2)}) collective-permute-start(bf16[256,2048]{1,0:T(8,128)(2,1)S(1)} %get-tuple-element.120), channel_id=1, source_target_pairs={{0,16},{4,12},{8,24},{12,4},{16,0},{20,28},{24,8},{28,20},{1,17},{... | collective-permute-start | bytes 3145736 | tf_op jit(solution)/shard_map/ppermute | solution.py:79
  862.0 42.7 %collective-permute-start.61 = (bf16[256,2048]{1,0:T(8,128)(2,1)}, bf16[256,2048]{1,0:T(8,128)(2,1)}, u32[]{:S(2)}, u32[]{:S(2)}) collective-permute-start(bf16[256,2048]{1,0:T(8,128)(2,1)} %fusion.17), channel_id=1, source_target_pairs={{0,8},{4,20},{8,0},{12,28},{16,24},{20,4},{24,16},{28,12},{1,9},{5... | collective-permute-start | bytes 3145736 | tf_op jit(solution)/shard_map/ppermute | solution.py:79
  908.2 21.9 %collective-permute-start.63 = (bf16[256,512]{1,0:T(8,128)(2,1)S(1)}, bf16[256,512]{1,0:T(8,128)(2,1)S(1)}, u32[]{:S(2)}, u32[]{:S(2)}) collective-permute-start(bf16[256,512]{1,0:T(8,128)(2,1)S(1)} %get-tuple-element.162), channel_id=1, source_target_pairs={{0,2},{1,3},{2,0},{3,1},{4,6},{5,7},{6,4},{7,5},{8,10},{9,11},{10,... | collective-permute-start | bytes 786440 | tf_op jit(solution)/shard_map/ppermute | solution.py:123
  911.7 18.4 %collective-permute-start.64 = (bf16[256,512]{1,0:T(8,128)(2,1)S(1)}, bf16[256,512]{1,0:T(8,128)(2,1)S(1)}, u32[]{:S(2)}, u32[]{:S(2)}) collective-permute-start(bf16[256,512]{1,0:T(8,128)(2,1)S(1)} %get-tuple-element.161), channel_id=1, source_target_pairs={{0,3},{1,2},{2,1},{3,0},{4,7},{5,6},{6,5},{7,4},{8,11},{9,10},{10,... | collective-permute-start | bytes 786440 | tf_op jit(solution)/shard_map/ppermute | solution.py:123
  914.4 26.6 %collective-permute-start.70 = (bf16[80,512]{1,0:T(8,128)(2,1)S(1)}, bf16[80,512]{1,0:T(8,128)(2,1)S(1)}, u32[]{:S(2)}, u32[]{:S(2)}) collective-permute-start(bf16[80,512]{1,0:T(8,128)(2,1)S(1)} %get-tuple-element.170), channel_id=1, source_target_pairs={{0,2},{1,3},{2,0},{3,1},{4,6},{5,7},{6,4},{7,5},{8,10},{9,11},{10,... | collective-permute-start | bytes 245768 | tf_op jit(solution)/shard_map/ppermute | solution.py:123
  921.9 19.0 %collective-permute-start.71 = (bf16[80,512]{1,0:T(8,128)(2,1)S(1)}, bf16[80,512]{1,0:T(8,128)(2,1)S(1)}, u32[]{:S(2)}, u32[]{:S(2)}) collective-permute-start(bf16[80,512]{1,0:T(8,128)(2,1)S(1)} %get-tuple-element.169), channel_id=1, source_target_pairs={{0,3},{1,2},{2,1},{3,0},{4,7},{5,6},{6,5},{7,4},{8,11},{9,10},{10,... | collective-permute-start | bytes 245768 | tf_op jit(solution)/shard_map/ppermute | solution.py:123
  (90 other events, 2447.5 us)
Sparse Core Ops, SparseCore 0:
  9.9 88.1 all-gather.7
  147.5 83.4 all-gather.5
  232.9 65.1 all-gather.9
  564.0 88.4 reduce-scatter.7
  656.4 116.3 reduce-scatter.5
  776.3 121.7 reduce-scatter.3

commit v5 on v4

--- a/solution.py
+++ b/solution.py
@@ -116,6 +116,7 @@
         self.me = lax.axis_index("head")
         self.fast = self.size == 4
         self.inner = (self.me == 1) | (self.me == 2)
+        self.steps = None
         self.relay = jnp.array(RELAY, jnp.int32)[self.me] if self.fast else None
         self.direct = self.me ^ jnp.arange(self.size, dtype=jnp.int32)
 
@@ -149,6 +150,7 @@
         near = self.send(after(slot2, far), inward)
         next_door = slot1 + after(self.send(far, middle), near, beside[1])
         near = slot2 + near
+        self.steps = [far, next_door]
         return [own, after(self.send(next_door, pair), beside[2]), self.send(near, middle)]
 
     def gather_small(self, value, axis):
@@ -776,7 +778,10 @@
         whole_grad(act, grad_all), whole_grad(d_gate, normed2_all), whole_grad(d_up, normed2_all)
     ]
     d_normed2 = total(head.reduce(d_normed2_terms, terms))
-    down_grad, gate_grad, up_grad = (scattered(after(whole, d_normed2)) for whole in terms)
+    gates = [*(head.steps or [d_normed2] * 2), d_normed2]
+    down_grad, gate_grad, up_grad = (
+        scattered(after(whole, step)) for whole, step in zip(terms, gates, strict=True)
+    )
     gate_grad, up_grad = gate_grad.T, up_grad.T
 
     d_hidden_norm, ffn_gain_grad = norm_backward(hidden, ffn_scale, ffn_gain32, d_normed2)
@@ -789,10 +794,6 @@
         *where, queries, *tables, mixed, d_mixed, lse, *kv_halves
     )
 
-    ffn_terms = ffn_forth(after(act, d_normed2), *down)
-    beside = (d_queries, d_kv_a, d_kv_b)
-    (output,) = shuffle(seq.place, hidden + total(head.reduce(ffn_terms, beside)))
-
     def stacked(value):
         return value.reshape(pieces, value.shape[0] // pieces, value.shape[1])
 
@@ -803,6 +804,9 @@
         return add
 
     d_kv_span = seq.reduce(adding(stacked(d_kv_a)), stacked(d_kv_b))
+    ffn_terms = ffn_forth(after(act, d_kv_span), *down)
+    beside = (d_kv_span, d_kv_span, d_kv_span)
+    (output,) = shuffle(seq.place, hidden + total(head.reduce(ffn_terms, beside)))
     d_kv_own = head.reduce_small(d_kv_span.astype(BF16), 0)
     key_back = rotate(
         d_kv_own[:, : KV * HD].reshape(local_rows, KV, HD), cosine[:, None, :], -sine[:, None, :]

time: 968 us -> 932 us (0.963)
  starting transfers between devices: 161 us -> 139 us
  waiting for transfers between devices: 372 us -> 352 us
  other arithmetic: 90.5 us -> 74.2 us
  local copies, waits for them, and re-layouts: 54.2 us -> 64.9 us
    ppermute x36, starting transfers between devices: 64.3 us -> 26 us  [send(): return lax.ppermute(item, 'seq', pairs)]
    ppermute x39, starting transfers between devices: 96.6 us -> 113 us  [send(): return lax.ppermute(value, 'head', pairs)]
    ppermute x39, waiting for transfers between devices: 142 us -> 132 us  [send(): return lax.ppermute(value, 'head', pairs)]
    unnamed x159 -> x183, local copies, waits for them, and re-layouts: 27.3 us -> 33.8 us
  transfers between devices with their start and end apart: 81 -> 81, of which waited for: 31 -> 25; matrix products, arithmetic and copies ran while one was open for 16% -> 16% of each run, Pallas kernels for 15% -> 17%
where the time goes in v5:
time: 932 us; the launch traced here: 923 us
  waiting for transfers between devices  352 us (38%)
  Pallas kernels  230 us (25%)
  starting transfers between devices  139 us (15%)
  other arithmetic  74.2 us (8%)
  local copies, waits for them, and re-layouts  64.9 us (7%)
  matrix products  38.3 us (4%)
  between operations  24.4 us (3%)
    ppermute x36, waiting for transfers between devices, send(): return lax.ppermute(item, 'seq', pairs)  220 us
    ppermute x39, waiting for transfers between devices, send(): return lax.ppermute(value, 'head', pairs)  132 us
    ppermute x39, starting transfers between devices, send(): return lax.ppermute(value, 'head', pairs)  113 us
    pallas_call x7, Pallas kernels, unit_grad(): pl.pallas_call(functools.partial(unit_grad_kernel, count, shift, len(extr...  71 us
    pallas_call x1, Pallas kernels, ffn_middle(): pl.pallas_call(ffn_kernel, out_shape=(jax.ShapeDtypeStruct((rows, units),...  44.2 us
    unnamed x183, local copies, waits for them, and re-layouts  33.8 us
    pallas_call x1, Pallas kernels, ffn_back(): pl.pallas_call(back_kernel, out_shape=jax.ShapeDtypeStruct((rows, pieces...  31.5 us
    pallas_call x1, Pallas kernels, attention_backward(): pl.pallas_call(backward_kernel, out_shape=(jax.ShapeDtypeStruct((rows, HE...  26.8 us
  transfers between devices with their start and end apart: 81, of which 25 were waited for; matrix products, arithmetic and copies ran while one was open for 16% of the time, Pallas kernels for 17%

profile of v5, /device:TPU:0, one launch (start us, length us, event | category | flops | bytes accessed | tf_op | source)
XLA Modules:
  0.0 923.2 jit_solution(16278634820485701826)
XLA Ops:
  16.2 3.5 collective-permute-start.8
  24.2 3.2 shuffle.3
  36.3 9.4 %collective-permute-done.3 = bf16[320,512]{1,0:T(8,128)(2,1)S(1)} collective-permute-done((bf16[320,512]{1,0:T(8,128)(2,1)}, bf16[320,512]{1,0:T(8,128)(2,1)S(1)}, u32[]{:S(2)}, u32[]{:S(2)}) %collective-permute-start.3) | collective-permute-done | bytes 327712 | tf_op jit(solution)/shard_map/ppermute | solution.py:79
  49.9 7.5 collective-permute-done.5
  71.9 10.6 %collective-permute-done.15.refs_2_ = bf16[512,256]{1,0:T(8,128)(2,1)} collective-permute-done((bf16[512,256]{1,0:T(8,128)(2,1)}, bf16[512,256]{1,0:T(8,128)(2,1)}, u32[]{:S(2)}, u32[]{:S(2)}) %collective-permute-start.15) | collective-permute-done | bytes 262176 | tf_op jit(solution)/shard_map/ppermute | solution.py:124
  85.8 16.9 %collective-permute-done.10 = bf16[256,2048]{1,0:T(8,128)(2,1)} collective-permute-done((bf16[256,2048]{1,0:T(8,128)(2,1)}, bf16[256,2048]{1,0:T(8,128)(2,1)}, u32[]{:S(2)}, u32[]{:S(2)}) %collective-permute-start.10) | collective-permute-done | bytes 1048608 | tf_op jit(solution)/shard_map/ppermute | solution.py:79
  107.8 3.2 slice.188
  121.9 3.6 pad_maximum_fusion
  129.9 8.3 collective-permute-done.17.refs_1_
  138.2 10.1 %collective-permute-done.18.refs_2_ = bf16[256,512]{1,0:T(8,128)(2,1)S(1)} collective-permute-done((bf16[256,512]{1,0:T(8,128)(2,1)S(1)}, bf16[256,512]{1,0:T(8,128)(2,1)S(1)}, u32[]{:S(2)}, u32[]{:S(2)}) %collective-permute-start.18) | collective-permute-done | bytes 262176 | tf_op jit(solution)/shard_map/ppermute | solution.py:124
  152.5 24.9 %collective-permute-done.22 = bf16[2048,256]{1,0:T(8,128)(2,1)S(1)} collective-permute-done((bf16[2048,256]{1,0:T(8,128)(2,1)S(1)}, bf16[2048,256]{1,0:T(8,128)(2,1)S(1)}, u32[]{:S(2)}, u32[]{:S(2)}) %collective-permute-start.22) | collective-permute-done | bytes 1048608 | tf_op jit(solution)/shard_map/ppermute | solution.py:79
  178.4 22.2 %collective-permute-done.23 = bf16[2048,256]{1,0:T(8,128)(2,1)S(1)} collective-permute-done((bf16[2048,256]{1,0:T(8,128)(2,1)S(1)}, bf16[2048,256]{1,0:T(8,128)(2,1)S(1)}, u32[]{:S(2)}, u32[]{:S(2)}) %collective-permute-start.23) | collective-permute-done | bytes 1048608 | tf_op jit(solution)/shard_map/ppermute | solution.py:79
  204.1 11.5 %collective-permute-done.24 = bf16[1024,512]{1,0:T(8,128)(2,1)S(1)} collective-permute-done((bf16[1024,512]{1,0:T(8,128)(2,1)}, bf16[1024,512]{1,0:T(8,128)(2,1)S(1)}, u32[]{:S(2)}, u32[]{:S(2)}) %collective-permute-start.24) | collective-permute-done | bytes 1048608 | tf_op jit(solution)/shard_map/ppermute | solution.py:79
  215.7 11.2 %collective-permute-done.25 = bf16[1024,512]{1,0:T(8,128)(2,1)S(1)} collective-permute-done((bf16[1024,512]{1,0:T(8,128)(2,1)S(1)}, bf16[1024,512]{1,0:T(8,128)(2,1)S(1)}, u32[]{:S(2)}, u32[]{:S(2)}) %collective-permute-start.25) | collective-permute-done | bytes 1048608 | tf_op jit(solution)/shard_map/ppermute | solution.py:79
  229.6 3.7 pad_maximum_fusion.1
  241.4 4.2 fusion.40
  247.4 14.3 %attention_forward.1 = (bf16[16,256,128]{2,1,0:T(8,128)(2,1)S(1)}, bf16[256,2048]{1,0:T(8,128)(2,1)S(1)}, f32[16,1,256]{2,1,0:T(1,128)S(1)}) custom-call(s32[16]{0:T(128)S(1)} %fusion.33.offset_ref, s32[2]{0:T(128)S(1)} %pad_add_fusion.1.bound_ref, f32[256,2048]{1,0:T(8,128)S(1)} %fusion.2.raw_ref, f32[256,128]{1,0:T(8,128)S(1)} %pad_maximum_fusion.5.cos_ref, ...), custom_call_target="tpu_custom_call" | custom-call | flops 4294967296 | bytes 12582912 | tf_op jit(solution)/shard_map/attention_forward/pallas_call | solution.py:310
  261.7 4.2 fusion.52
  266.0 4.3 fusion.53
  270.9 5.8 collective-permute-start.28
  278.4 20.3 %collective-permute-done.28.refs_1_ = bf16[256,2048]{1,0:T(8,128)(2,1)S(1)} collective-permute-done((bf16[256,2048]{1,0:T(8,128)(2,1)S(1)}, bf16[256,2048]{1,0:T(8,128)(2,1)S(1)}, u32[]{:S(2)}, u32[]{:S(2)}) %collective-permute-start.28) | collective-permute-done | bytes 1048608 | tf_op jit(solution)/shard_map/ppermute | solution.py:124
  305.2 28.3 %collective-permute-done.30 = bf16[256,2048]{1,0:T(8,128)(2,1)} collective-permute-done((bf16[256,2048]{1,0:T(8,128)(2,1)}, bf16[256,2048]{1,0:T(8,128)(2,1)}, u32[]{:S(2)}, u32[]{:S(2)}) %collective-permute-start.30) | collective-permute-done | bytes 1048608 | tf_op jit(solution)/shard_map/ppermute | solution.py:124
  335.8 19.1 %collective-permute-done.32 = bf16[256,2048]{1,0:T(8,128)(2,1)} collective-permute-done((bf16[256,2048]{1,0:T(8,128)(2,1)}, bf16[256,2048]{1,0:T(8,128)(2,1)}, u32[]{:S(2)}, u32[]{:S(2)}) %collective-permute-start.32) | collective-permute-done | bytes 1048608 | tf_op jit(solution)/shard_map/ppermute | solution.py:124
  357.2 4.4 place.9.normed_ref.right_ref
  369.4 11.2 %collective-permute-done.35 = bf16[2752,256]{1,0:T(8,128)(2,1)S(1)} collective-permute-done((bf16[2752,256]{1,0:T(8,128)(2,1)}, bf16[2752,256]{1,0:T(8,128)(2,1)S(1)}, u32[]{:S(2)}, u32[]{:S(2)}) %collective-permute-start.35) | collective-permute-done | bytes 1409056 | tf_op jit(solution)/shard_map/ppermute | solution.py:79
  383.8 7.6 collective-permute-done.36
  393.6 44.2 %ffn_middle.1 = (bf16[1024,2752]{1,0:T(8,128)(2,1)}, bf16[1024,2752]{1,0:T(8,128)(2,1)}, bf16[1024,2752]{1,0:T(8,128)(2,1)}) custom-call(s32[8]{0:T(128)S(1)} %copy-done.17, bf16[1024,2048]{1,0:T(8,128)(2,1)S(1)} %copy-done.8, bf16[1024,2048]{1,0:T(8,128)(2,1)} %all-gather.6.cloned.1.call-done.grad_ref.right_ref, bf16[8,2752,256]{2,1,0:T(8,128)(2,1)} %bitcast.162, ...), custom_call_target="tpu_custom_call" | custom-call | flops 34628173824 | bytes 59113472 | tf_op jit(solution)/shard_map/ffn_middle/pallas_call | solution.py:483
  437.7 31.5 %ffn_back.1 = bf16[1024,2048]{1,0:T(8,128)(2,1)S(1)} custom-call(s32[8]{0:T(128)S(1)} %copy-done.17, bf16[1024,2752]{1,0:T(8,128)(2,1)} %get-tuple-element.100.d_gate_ref.left_ref, bf16[1024,2752]{1,0:T(8,128)(2,1)} %get-tuple-element.102.d_up_ref.left_ref, bf16[8,2752,256]{2,1,0:T(8,128)(2,1)} %bitcast.163, bf16[8,2752,256]{2,1,0:T(8,128)(2,1)} %bitcast.165), custom_call_target="tpu_custom_call" | custom-call | flops 23085449216 | bytes 33816576 | tf_op jit(solution)/shard_map/ffn_back/pallas_call | solution.py:513
  471.9 9.2 collective-permute-start.37
  481.1 17.5 %unit_grad.7 = bf16[8,2752,256]{2,1,0:T(8,128)(2,1)} custom-call(s32[8]{0:T(128)S(1)} %select_reduce_fusion.3.order_ref, bf16[1024,2752]{1,0:T(8,128)(2,1)} %get-tuple-element.110.left_ref.act_ref, bf16[1024,2048]{1,0:T(8,128)(2,1)S(1)} %copy-done.19), custom_call_target="tpu_custom_call" | custom-call | flops 11542724608 | bytes 21102592 | tf_op jit(solution)/shard_map/unit_grad/pallas_call | solution.py:592
  498.6 4.5 collective-permute-done.37
  508.4 7.4 collective-permute-start.39
  515.8 3.2 copy-done.9
  519.0 17.7 %unit_grad.8 = bf16[8,2752,256]{2,1,0:T(8,128)(2,1)} custom-call(s32[8]{0:T(128)S(1)} %select_reduce_fusion.3.order_ref, bf16[1024,2752]{1,0:T(8,128)(2,1)} %get-tuple-element.100.d_gate_ref.left_ref, bf16[1024,2048]{1,0:T(8,128)(2,1)S(1)} %copy-done.9), custom_call_target="tpu_custom_call" | custom-call | flops 11542724608 | bytes 21102592 | tf_op jit(solution)/shard_map/unit_grad/pallas_call | solution.py:592
  548.5 17.6 %unit_grad.9 = bf16[8,2752,256]{2,1,0:T(8,128)(2,1)} custom-call(s32[8]{0:T(128)S(1)} %select_reduce_fusion.3.order_ref, bf16[1024,2752]{1,0:T(8,128)(2,1)} %get-tuple-element.102.d_up_ref.left_ref, bf16[1024,2048]{1,0:T(8,128)(2,1)S(1)} %copy-done.10), custom_call_target="tpu_custom_call" | custom-call | flops 11542724608 | bytes 21102592 | tf_op jit(solution)/shard_map/unit_grad/pallas_call | solution.py:592
  570.9 4.6 fusion.20
  575.5 4.4 fusion.3.grad_ref
  580.0 26.8 %attention_backward.1 = (bf16[256,2048]{1,0:T(8,128)(2,1)}, bf16[4096,512]{1,0:T(8,128)(2,1)}, bf16[4096,512]{1,0:T(8,128)(2,1)}) custom-call(s32[16]{0:T(128)} %copy-done.22, s32[2]{0:T(128)} %copy-done.21, bf16[16,256,128]{2,1,0:T(8,128)(2,1)} %copy-done.23, f32[256,128]{1,0:T(8,128)} %copy-done.15, f32[256,128]{1,0:T(8,128)} %copy-done.16, ...), custom_call_target="tpu_custom_call" | custom-call | flops 10737418240 | bytes 20971520 | tf_op jit(solution)/shard_map/attention_backward/pallas_call | solution.py:420
  609.4 4.0 unit_grad.12
  614.8 3.4 unit_grad.10
  618.7 3.4 add.369
  627.7 4.5 fusion.54
  632.3 7.0 unit_grad.13
  639.3 9.7 %collective-permute-done.43 = bf16[1024,512]{1,0:T(8,128)(2,1)} collective-permute-done((bf16[1024,512]{1,0:T(8,128)(2,1)}, bf16[1024,512]{1,0:T(8,128)(2,1)}, u32[]{:S(2)}, u32[]{:S(2)}) %collective-permute-start.43) | collective-permute-done | bytes 1048608 | tf_op jit(solution)/shard_map/ppermute | solution.py:79
  648.9 32.4 %collective-permute-done.44 = bf16[1024,512]{1,0:T(8,128)(2,1)} collective-permute-done((bf16[1024,512]{1,0:T(8,128)(2,1)}, bf16[1024,512]{1,0:T(8,128)(2,1)}, u32[]{:S(2)}, u32[]{:S(2)}) %collective-permute-start.44) | collective-permute-done | bytes 1048608 | tf_op jit(solution)/shard_map/ppermute | solution.py:79
  682.8 4.4 fusion.55
  687.3 3.7 unit_grad.11
  693.6 18.5 %collective-permute-done.56 = bf16[2048,256]{1,0:T(8,128)(2,1)S(1)} collective-permute-done((bf16[2048,256]{1,0:T(8,128)(2,1)S(1)}, bf16[2048,256]{1,0:T(8,128)(2,1)S(1)}, u32[]{:S(2)}, u32[]{:S(2)}) %collective-permute-start.56) | collective-permute-done | bytes 1048608 | tf_op jit(solution)/shard_map/ppermute | solution.py:79
  713.4 4.4 collective-permute-done.45
  719.6 4.8 collective-permute-start.51
  724.3 7.9 collective-permute-start.52
  732.5 19.7 %ffn_forth.1 = bf16[1024,2048]{1,0:T(8,128)(2,1)S(1)} custom-call(bf16[1024,2752]{1,0:T(8,128)(2,1)} %get-tuple-element.110.left_ref.act_ref, bf16[4,2752,256]{2,1,0:T(8,128)(2,1)} %bitcast.18.down_a_ref, bf16[4,2752,256]{2,1,0:T(8,128)(2,1)} %bitcast.19.down_b_ref), custom_call_target="tpu_custom_call" | custom-call | flops 11542724608 | bytes 16908288 | tf_op jit(solution)/shard_map/ffn_forth/pallas_call | solution.py:544
  754.6 3.9 collective-permute-start.46
  762.2 4.8 fusion.12
  773.1 3.3 shuffle.5
  782.3 8.0 collective-permute-start.48
  791.8 3.3 collective-permute-done.60
  798.1 29.0 %collective-permute-done.58 = bf16[256,2048]{1,0:T(8,128)(2,1)S(1)} collective-permute-done((bf16[256,2048]{1,0:T(8,128)(2,1)S(1)}, bf16[256,2048]{1,0:T(8,128)(2,1)S(1)}, u32[]{:S(2)}, u32[]{:S(2)}) %collective-permute-start.58) | collective-permute-done | bytes 1048608 | tf_op jit(solution)/shard_map/ppermute | solution.py:79
  832.2 16.1 %collective-permute-done.73 = bf16[512,256]{1,0:T(8,128)(2,1)S(1)} collective-permute-done((bf16[512,256]{1,0:T(8,128)(2,1)S(1)}, bf16[512,256]{1,0:T(8,128)(2,1)S(1)}, u32[]{:S(2)}, u32[]{:S(2)}) %collective-permute-start.73) | collective-permute-done | bytes 262176 | tf_op jit(solution)/shard_map/ppermute | solution.py:124
  852.8 5.5 collective-permute-start.62
  858.3 10.1 %collective-permute-done.49 = bf16[256,2048]{1,0:T(8,128)(2,1)S(1)} collective-permute-done((bf16[256,2048]{1,0:T(8,128)(2,1)S(1)}, bf16[256,2048]{1,0:T(8,128)(2,1)S(1)}, u32[]{:S(2)}, u32[]{:S(2)}) %collective-permute-start.49) | collective-permute-done | bytes 1048608 | tf_op jit(solution)/shard_map/ppermute | solution.py:124
  877.9 18.1 %collective-permute-start.69 = (bf16[80,512]{1,0:T(8,128)(2,1)S(1)}, bf16[80,512]{1,0:T(8,128)(2,1)S(1)}, u32[]{:S(2)}, u32[]{:S(2)}) collective-permute-start(bf16[80,512]{1,0:T(8,128)(2,1)S(1)} %get-tuple-element.168), channel_id=1, source_target_pairs={{0,1},{1,0},{2,3},{3,2},{4,5},{5,4},{6,7},{7,6},{8,9},{9,8},{10,11... | collective-permute-start | bytes 245768 | tf_op jit(solution)/shard_map/ppermute | solution.py:124
  900.3 4.3 collective-permute-done.70
  906.5 3.1 bitcast_convert_fusion
  (445 shorter events, 199.2 us)
Async XLA Ops:
  7.2 144.0 %all-gather.8.cloned.1.call-start = ((), (), s32[]{:S(2)}) async-start(), calls=%async_computation.7 | async-start | bytes 12681216 | tf_op jit(solution)/shard_map/all_gather | solution.py:672
  7.9 375.8 %all-gather.6.cloned.1.call-start = ((), (), s32[]{:S(2)}) async-start(), calls=%async_computation.3 | async-start | bytes 5242880 | tf_op jit(solution)/shard_map/all_gather | solution.py:741
  9.6 20.0 %collective-permute-start = (bf16[80,512]{1,0:T(8,128)(2,1)S(1)}, bf16[80,512]{1,0:T(8,128)(2,1)S(1)}, u32[]{:S(2)}, u32[]{:S(2)}) collective-permute-start(bf16[80,512]{1,0:T(8,128)(2,1)S(1)} %fusion.27.refs_0_), channel_id=1, source_target_pairs={{0,1},{1,0},{2,3},{3,2},{4,5},{5,4},{6,7},{7,6},{8,9},{9,8},{10,11... | collective-permute-start | bytes 245768 | tf_op jit(solution)/shard_map/ppermute | solution.py:124
  15.3 45.6 %collective-permute-start.7 = (bf16[256,512]{1,0:T(8,128)(2,1)}, bf16[256,512]{1,0:T(8,128)(2,1)S(1)}, u32[]{:S(2)}, u32[]{:S(2)}) collective-permute-start(bf16[256,512]{1,0:T(8,128)(2,1)} %refs_0_.4), channel_id=1, source_target_pairs={{0,1},{1,0},{2,3},{3,2},{4,5},{5,4},{6,7},{7,6},{8,9},{9,8},{10,11... | collective-permute-start | bytes 786440 | tf_op jit(solution)/shard_map/ppermute | solution.py:124
  16.2 46.6 %collective-permute-start.8 = (bf16[256,512]{1,0:T(8,128)(2,1)}, bf16[256,512]{1,0:T(8,128)(2,1)S(1)}, u32[]{:S(2)}, u32[]{:S(2)}) collective-permute-start(bf16[256,512]{1,0:T(8,128)(2,1)} %refs_0_.4), channel_id=1, source_target_pairs={{0,2},{1,3},{2,0},{3,1},{4,6},{5,7},{6,4},{7,5},{8,10},{9,11},{10,... | collective-permute-start | bytes 786440 | tf_op jit(solution)/shard_map/ppermute | solution.py:124
  29.7 34.6 %collective-permute-start.9 = (bf16[256,512]{1,0:T(8,128)(2,1)S(1)}, bf16[256,512]{1,0:T(8,128)(2,1)S(1)}, u32[]{:S(2)}, u32[]{:S(2)}) collective-permute-start(bf16[256,512]{1,0:T(8,128)(2,1)S(1)} %copy-done.61), channel_id=1, source_target_pairs={{0,3},{1,2},{2,1},{3,0},{4,7},{5,6},{6,5},{7,4},{8,11},{9,10},{10,... | collective-permute-start | bytes 786440 | tf_op jit(solution)/shard_map/ppermute | solution.py:124
  48.4 21.0 %collective-permute-start.14 = (bf16[512,256]{1,0:T(8,128)(2,1)}, bf16[512,256]{1,0:T(8,128)(2,1)}, u32[]{:S(2)}, u32[]{:S(2)}) collective-permute-start(bf16[512,256]{1,0:T(8,128)(2,1)} %refs_0_.5), channel_id=1, source_target_pairs={{0,1},{1,0},{2,3},{3,2},{4,5},{5,4},{6,7},{7,6},{8,9},{9,8},{10,11... | collective-permute-start | bytes 786440 | tf_op jit(solution)/shard_map/ppermute | solution.py:124
  60.3 44.6 %collective-permute-start.6 = (bf16[1280,512]{1,0:T(8,128)(2,1)}, bf16[1280,512]{1,0:T(8,128)(2,1)}, u32[]{:S(2)}, u32[]{:S(2)}) collective-permute-start(bf16[1280,512]{1,0:T(8,128)(2,1)} %pad_maximum_fusion.2), channel_id=1, source_target_pairs={{0,4},{4,0},{8,12},{12,8},{16,20},{20,16},{24,28},{28,24},{1,5},{5... | collective-permute-start | bytes 3932168 | tf_op jit(solution)/shard_map/ppermute | solution.py:79
  60.9 21.6 %collective-permute-start.15 = (bf16[512,256]{1,0:T(8,128)(2,1)}, bf16[512,256]{1,0:T(8,128)(2,1)}, u32[]{:S(2)}, u32[]{:S(2)}) collective-permute-start(bf16[512,256]{1,0:T(8,128)(2,1)} %refs_0_.5), channel_id=1, source_target_pairs={{0,2},{1,3},{2,0},{3,1},{4,6},{5,7},{6,4},{7,5},{8,10},{9,11},{10,... | collective-permute-start | bytes 786440 | tf_op jit(solution)/shard_map/ppermute | solution.py:124
  62.8 19.7 %collective-permute-start.16 = (bf16[512,256]{1,0:T(8,128)(2,1)}, bf16[512,256]{1,0:T(8,128)(2,1)}, u32[]{:S(2)}, u32[]{:S(2)}) collective-permute-start(bf16[512,256]{1,0:T(8,128)(2,1)} %refs_0_.5), channel_id=1, source_target_pairs={{0,3},{1,2},{2,1},{3,0},{4,7},{5,6},{6,5},{7,4},{8,11},{9,10},{10,... | collective-permute-start | bytes 786440 | tf_op jit(solution)/shard_map/ppermute | solution.py:124
  67.2 35.5 %collective-permute-start.10 = (bf16[256,2048]{1,0:T(8,128)(2,1)}, bf16[256,2048]{1,0:T(8,128)(2,1)}, u32[]{:S(2)}, u32[]{:S(2)}) collective-permute-start(bf16[256,2048]{1,0:T(8,128)(2,1)} %place.6), channel_id=1, source_target_pairs={{0,8},{4,20},{8,0},{12,28},{16,24},{20,4},{24,16},{28,12},{1,9},{5... | collective-permute-start | bytes 3145736 | tf_op jit(solution)/shard_map/ppermute | solution.py:79
  69.4 52.5 %collective-permute-start.11 = (bf16[256,2048]{1,0:T(8,128)(2,1)}, bf16[256,2048]{1,0:T(8,128)(2,1)}, u32[]{:S(2)}, u32[]{:S(2)}) collective-permute-start(bf16[256,2048]{1,0:T(8,128)(2,1)} %place.6), channel_id=1, source_target_pairs={{0,16},{4,12},{8,24},{12,4},{16,0},{20,28},{24,8},{28,20},{1,17},{... | collective-permute-start | bytes 3145736 | tf_op jit(solution)/shard_map/ppermute | solution.py:79
  102.7 19.1 %collective-permute-start.12 = (bf16[256,2048]{1,0:T(8,128)(2,1)}, bf16[256,2048]{1,0:T(8,128)(2,1)}, u32[]{:S(2)}, u32[]{:S(2)}) collective-permute-start(bf16[256,2048]{1,0:T(8,128)(2,1)} %collective-permute-done.10), channel_id=1, source_target_pairs={{0,16},{4,12},{8,24},{12,4},{16,0},{20,28},{24,8},{28,20},{1,17},{... | collective-permute-start | bytes 3145736 | tf_op jit(solution)/shard_map/ppermute | solution.py:79
  126.9 21.4 %collective-permute-start.18 = (bf16[256,512]{1,0:T(8,128)(2,1)S(1)}, bf16[256,512]{1,0:T(8,128)(2,1)S(1)}, u32[]{:S(2)}, u32[]{:S(2)}) collective-permute-start(bf16[256,512]{1,0:T(8,128)(2,1)S(1)} %pad_maximum_fusion.3.refs_0_), channel_id=1, source_target_pairs={{0,2},{1,3},{2,0},{3,1},{4,6},{5,7},{6,4},{7,5},{8,10},{9,11},{10,... | collective-permute-start | bytes 786440 | tf_op jit(solution)/shard_map/ppermute | solution.py:124
  129.4 19.6 %collective-permute-start.19 = (bf16[256,512]{1,0:T(8,128)(2,1)S(1)}, bf16[256,512]{1,0:T(8,128)(2,1)}, u32[]{:S(2)}, u32[]{:S(2)}) collective-permute-start(bf16[256,512]{1,0:T(8,128)(2,1)S(1)} %pad_maximum_fusion.3.refs_0_), channel_id=1, source_target_pairs={{0,3},{1,2},{2,1},{3,0},{4,7},{5,6},{6,5},{7,4},{8,11},{9,10},{10,... | collective-permute-start | bytes 786440 | tf_op jit(solution)/shard_map/ppermute | solution.py:124
  151.2 240.1 %all-gather.10.cloned.1.call-start = ((), (), s32[]{:S(2)}) async-start(), calls=%async_computation.8 | async-start | bytes 12681216 | tf_op jit(solution)/shard_map/all_gather | solution.py:742
  151.3 26.1 %collective-permute-start.22 = (bf16[2048,256]{1,0:T(8,128)(2,1)S(1)}, bf16[2048,256]{1,0:T(8,128)(2,1)S(1)}, u32[]{:S(2)}, u32[]{:S(2)}) collective-permute-start(bf16[2048,256]{1,0:T(8,128)(2,1)S(1)} %copy-done.39), channel_id=1, source_target_pairs={{0,8},{4,20},{8,0},{12,28},{16,24},{20,4},{24,16},{28,12},{1,9},{5... | collective-permute-start | bytes 3145736 | tf_op jit(solution)/shard_map/ppermute | solution.py:79
  152.0 25.4 %collective-permute-start.20 = (bf16[2048,256]{1,0:T(8,128)(2,1)S(1)}, bf16[2048,256]{1,0:T(8,128)(2,1)S(1)}, u32[]{:S(2)}, u32[]{:S(2)}) collective-permute-start(bf16[2048,256]{1,0:T(8,128)(2,1)S(1)} %copy-done.39), channel_id=1, source_target_pairs={{0,16},{4,12},{8,24},{12,4},{16,0},{20,28},{24,8},{28,20},{1,17},{... | collective-permute-start | bytes 3145736 | tf_op jit(solution)/shard_map/ppermute | solution.py:79
  177.4 23.2 %collective-permute-start.23 = (bf16[2048,256]{1,0:T(8,128)(2,1)S(1)}, bf16[2048,256]{1,0:T(8,128)(2,1)S(1)}, u32[]{:S(2)}, u32[]{:S(2)}) collective-permute-start(bf16[2048,256]{1,0:T(8,128)(2,1)S(1)} %collective-permute-done.22), channel_id=1, source_target_pairs={{0,16},{4,12},{8,24},{12,4},{16,0},{20,28},{24,8},{28,20},{1,17},{... | collective-permute-start | bytes 3145736 | tf_op jit(solution)/shard_map/ppermute | solution.py:79
  177.4 24.1 %collective-permute-start.21 = (bf16[1024,512]{1,0:T(8,128)(2,1)}, bf16[1024,512]{1,0:T(8,128)(2,1)S(1)}, u32[]{:S(2)}, u32[]{:S(2)}) collective-permute-start(bf16[1024,512]{1,0:T(8,128)(2,1)} %place.8), channel_id=1, source_target_pairs={{0,8},{4,20},{8,0},{12,28},{16,24},{20,4},{24,16},{28,12},{1,9},{5... | collective-permute-start | bytes 3145736 | tf_op jit(solution)/shard_map/ppermute | solution.py:79
  201.6 25.2 %collective-permute-start.25 = (bf16[1024,512]{1,0:T(8,128)(2,1)S(1)}, bf16[1024,512]{1,0:T(8,128)(2,1)S(1)}, u32[]{:S(2)}, u32[]{:S(2)}) collective-permute-start(bf16[1024,512]{1,0:T(8,128)(2,1)S(1)} %collective-permute-done.21), channel_id=1, source_target_pairs={{0,16},{4,12},{8,24},{12,4},{16,0},{20,28},{24,8},{28,20},{1,17},{... | collective-permute-start | bytes 3145736 | tf_op jit(solution)/shard_map/ppermute | solution.py:79
  228.9 677.6 %reduce-scatter.8.cloned.1.call-start = ((), (), s32[]{:S(2)}) async-start(), calls=%async_computation.6 | async-start | bytes 12681216 | tf_op jit(solution)/shard_map/reduce_scatter | solution.py:775
  233.3 32.7 %collective-permute-start.27 = (bf16[2048,1024]{1,0:T(8,128)(2,1)}, bf16[2048,1024]{1,0:T(8,128)(2,1)}, u32[]{:S(2)}, u32[]{:S(2)}) collective-permute-start(bf16[2048,1024]{1,0:T(8,128)(2,1)} %pad_maximum_fusion.1), channel_id=1, source_target_pairs={{0,4},{4,0},{8,12},{12,8},{16,20},{20,16},{24,28},{28,24},{1,5},{5... | collective-permute-start | bytes 12582920 | tf_op jit(solution)/shard_map/ppermute | solution.py:79
  270.9 27.8 %collective-permute-start.28 = (bf16[256,2048]{1,0:T(8,128)(2,1)S(1)}, bf16[256,2048]{1,0:T(8,128)(2,1)S(1)}, u32[]{:S(2)}, u32[]{:S(2)}) collective-permute-start(bf16[256,2048]{1,0:T(8,128)(2,1)S(1)} %multiply_convert_fusion.refs_0_), channel_id=1, source_target_pairs={{0,1},{1,0},{2,3},{3,2},{4,5},{5,4},{6,7},{7,6},{8,9},{9,8},{10,11... | collective-permute-start | bytes 3145736 | tf_op jit(solution)/shard_map/ppermute | solution.py:124
  276.8 23.6 %collective-permute-start.29 = (bf16[256,2048]{1,0:T(8,128)(2,1)S(1)}, bf16[256,2048]{1,0:T(8,128)(2,1)}, u32[]{:S(2)}, u32[]{:S(2)}) collective-permute-start(bf16[256,2048]{1,0:T(8,128)(2,1)S(1)} %multiply_convert_fusion.refs_0_), channel_id=1, source_target_pairs={{1,2},{2,1},{5,6},{6,5},{9,10},{10,9},{13,14},{14,13},{17,18},{18,... | collective-permute-start | bytes 3145736 | tf_op jit(solution)/shard_map/ppermute | solution.py:124
  300.4 33.1 %collective-permute-start.30 = (bf16[256,2048]{1,0:T(8,128)(2,1)}, bf16[256,2048]{1,0:T(8,128)(2,1)}, u32[]{:S(2)}, u32[]{:S(2)}) collective-permute-start(bf16[256,2048]{1,0:T(8,128)(2,1)} %collective-permute-done.29), channel_id=1, source_target_pairs={{1,0},{2,3},{5,4},{6,7},{9,8},{10,11},{13,12},{14,15},{17,16},{18,... | collective-permute-start | bytes 3145736 | tf_op jit(solution)/shard_map/ppermute | solution.py:124
  301.7 53.2 %collective-permute-start.32 = (bf16[256,2048]{1,0:T(8,128)(2,1)}, bf16[256,2048]{1,0:T(8,128)(2,1)}, u32[]{:S(2)}, u32[]{:S(2)}) collective-permute-start(bf16[256,2048]{1,0:T(8,128)(2,1)} %collective-permute-done.31), channel_id=1, source_target_pairs={{1,0},{2,3},{5,4},{6,7},{9,8},{10,11},{13,12},{14,15},{17,16},{18,... | collective-permute-start | bytes 3145736 | tf_op jit(solution)/shard_map/ppermute | solution.py:124
  303.4 58.3 %collective-permute-start.33 = (bf16[2752,256]{1,0:T(8,128)(2,1)}, bf16[2752,256]{1,0:T(8,128)(2,1)}, u32[]{:S(2)}, u32[]{:S(2)}) collective-permute-start(bf16[2752,256]{1,0:T(8,128)(2,1)} %param.29), channel_id=1, source_target_pairs={{0,8},{4,20},{8,0},{12,28},{16,24},{20,4},{24,16},{28,12},{1,9},{5... | collective-permute-start | bytes 4227080 | tf_op jit(solution)/shard_map/ppermute | solution.py:79
  303.5 58.2 %collective-permute-start.34 = (bf16[2752,256]{1,0:T(8,128)(2,1)}, bf16[2752,256]{1,0:T(8,128)(2,1)}, u32[]{:S(2)}, u32[]{:S(2)}) collective-permute-start(bf16[2752,256]{1,0:T(8,128)(2,1)} %param.29), channel_id=1, source_target_pairs={{0,16},{4,12},{8,24},{12,4},{16,0},{20,28},{24,8},{28,20},{1,17},{... | collective-permute-start | bytes 4227080 | tf_op jit(solution)/shard_map/ppermute | solution.py:79
  471.9 31.3 %collective-permute-start.37 = (bf16[256,2048]{1,0:T(8,128)(2,1)}, bf16[256,2048]{1,0:T(8,128)(2,1)}, u32[]{:S(2)}, u32[]{:S(2)}) collective-permute-start(bf16[256,2048]{1,0:T(8,128)(2,1)} %get-tuple-element.151), channel_id=1, source_target_pairs={{0,1},{3,2},{4,5},{7,6},{8,9},{11,10},{12,13},{15,14},{16,17},{19,... | collective-permute-start | bytes 3145736 | tf_op jit(solution)/shard_map/ppermute | solution.py:124
  506.1 403.6 %reduce-scatter.4.cloned.1.call-start = ((), (), s32[]{:S(2)}) async-start(), calls=%async_computation.4 | async-start | bytes 12681216 | tf_op jit(solution)/shard_map/reduce_scatter | solution.py:775
  506.7 30.0 %collective-permute-start.38 = (bf16[256,2048]{1,0:T(8,128)(2,1)}, bf16[256,2048]{1,0:T(8,128)(2,1)}, u32[]{:S(2)}, u32[]{:S(2)}) collective-permute-start(bf16[256,2048]{1,0:T(8,128)(2,1)} %add.361), channel_id=1, source_target_pairs={{1,2},{2,1},{5,6},{6,5},{9,10},{10,9},{13,14},{14,13},{17,18},{18,... | collective-permute-start | bytes 3145736 | tf_op jit(solution)/shard_map/ppermute | solution.py:124
  508.4 28.3 %collective-permute-start.39 = (bf16[256,2048]{1,0:T(8,128)(2,1)S(1)}, bf16[256,2048]{1,0:T(8,128)(2,1)}, u32[]{:S(2)}, u32[]{:S(2)}) collective-permute-start(bf16[256,2048]{1,0:T(8,128)(2,1)S(1)} %get-tuple-element.99), channel_id=1, source_target_pairs={{0,1},{3,2},{4,5},{7,6},{8,9},{11,10},{12,13},{15,14},{16,17},{19,... | collective-permute-start | bytes 3145736 | tf_op jit(solution)/shard_map/ppermute | solution.py:124
  539.6 373.1 %reduce-scatter.6.cloned.1.call-start = ((), (), s32[]{:S(2)}) async-start(), calls=%async_computation.5 | async-start | bytes 12681216 | tf_op jit(solution)/shard_map/reduce_scatter | solution.py:775
  540.3 25.8 %collective-permute-start.40 = (bf16[256,2048]{1,0:T(8,128)(2,1)}, bf16[256,2048]{1,0:T(8,128)(2,1)}, u32[]{:S(2)}, u32[]{:S(2)}) collective-permute-start(bf16[256,2048]{1,0:T(8,128)(2,1)} %dynamic-slice_add_fusion.1), channel_id=1, source_target_pairs={{0,1},{1,0},{2,3},{3,2},{4,5},{5,4},{6,7},{7,6},{8,9},{9,8},{10,11... | collective-permute-start | bytes 3145736 | tf_op jit(solution)/shard_map/ppermute | solution.py:124
  545.3 20.9 %collective-permute-start.41 = (bf16[256,2048]{1,0:T(8,128)(2,1)}, bf16[256,2048]{1,0:T(8,128)(2,1)S(1)}, u32[]{:S(2)}, u32[]{:S(2)}) collective-permute-start(bf16[256,2048]{1,0:T(8,128)(2,1)} %add.365), channel_id=1, source_target_pairs={{1,2},{2,1},{5,6},{6,5},{9,10},{10,9},{13,14},{14,13},{17,18},{18,... | collective-permute-start | bytes 3145736 | tf_op jit(solution)/shard_map/ppermute | solution.py:124
  618.2 69.0 %collective-permute-start.54 = (bf16[4,256,2048]{2,1,0:T(8,128)(2,1)}, bf16[4,256,2048]{2,1,0:T(8,128)(2,1)}, u32[]{:S(2)}, u32[]{:S(2)}) collective-permute-start(bf16[4,256,2048]{2,1,0:T(8,128)(2,1)} %bitcast.30), channel_id=1, source_target_pairs={{0,4},{4,0},{8,12},{12,8},{16,20},{20,16},{24,28},{28,24},{1,5},{5... | collective-permute-start | bytes 12582920 | tf_op jit(solution)/shard_map/ppermute | solution.py:79
  624.8 24.2 %collective-permute-start.43 = (bf16[1024,512]{1,0:T(8,128)(2,1)}, bf16[1024,512]{1,0:T(8,128)(2,1)}, u32[]{:S(2)}, u32[]{:S(2)}) collective-permute-start(bf16[1024,512]{1,0:T(8,128)(2,1)} %get-tuple-element.107), channel_id=1, source_target_pairs={{0,16},{4,12},{8,24},{12,4},{16,0},{20,28},{24,8},{28,20},{1,17},{... | collective-permute-start | bytes 3145736 | tf_op jit(solution)/shard_map/ppermute | solution.py:79
  624.8 56.5 %collective-permute-start.44 = (bf16[1024,512]{1,0:T(8,128)(2,1)}, bf16[1024,512]{1,0:T(8,128)(2,1)}, u32[]{:S(2)}, u32[]{:S(2)}) collective-permute-start(bf16[1024,512]{1,0:T(8,128)(2,1)} %get-tuple-element.108), channel_id=1, source_target_pairs={{0,16},{4,12},{8,24},{12,4},{16,0},{20,28},{24,8},{28,20},{1,17},{... | collective-permute-start | bytes 3145736 | tf_op jit(solution)/shard_map/ppermute | solution.py:79
  648.9 63.2 %collective-permute-start.56 = (bf16[2048,256]{1,0:T(8,128)(2,1)S(1)}, bf16[2048,256]{1,0:T(8,128)(2,1)S(1)}, u32[]{:S(2)}, u32[]{:S(2)}) collective-permute-start(bf16[2048,256]{1,0:T(8,128)(2,1)S(1)} %get-tuple-element.118), channel_id=1, source_target_pairs={{0,16},{4,12},{8,24},{12,4},{16,0},{20,28},{24,8},{28,20},{1,17},{... | collective-permute-start | bytes 3145736 | tf_op jit(solution)/shard_map/ppermute | solution.py:79
  682.7 35.1 %collective-permute-start.45 = (bf16[1024,512]{1,0:T(8,128)(2,1)S(1)}, bf16[1024,512]{1,0:T(8,128)(2,1)S(1)}, u32[]{:S(2)}, u32[]{:S(2)}) collective-permute-start(bf16[1024,512]{1,0:T(8,128)(2,1)S(1)} %fusion.17), channel_id=1, source_target_pairs={{0,8},{4,20},{8,0},{12,28},{16,24},{20,4},{24,16},{28,12},{1,9},{5... | collective-permute-start | bytes 3145736 | tf_op jit(solution)/shard_map/ppermute | solution.py:79
  713.4 62.9 %collective-permute-start.57 = (bf16[2048,256]{1,0:T(8,128)(2,1)}, bf16[2048,256]{1,0:T(8,128)(2,1)}, u32[]{:S(2)}, u32[]{:S(2)}) collective-permute-start(bf16[2048,256]{1,0:T(8,128)(2,1)} %add.389), channel_id=1, source_target_pairs={{0,8},{4,20},{8,0},{12,28},{16,24},{20,4},{24,16},{28,12},{1,9},{5... | collective-permute-start | bytes 3145736 | tf_op jit(solution)/shard_map/ppermute | solution.py:79
  717.8 51.7 %collective-permute-start.59 = (bf16[2048,256]{1,0:T(8,128)(2,1)}, bf16[2048,256]{1,0:T(8,128)(2,1)}, u32[]{:S(2)}, u32[]{:S(2)}) collective-permute-start(bf16[2048,256]{1,0:T(8,128)(2,1)} %get-tuple-element.122), channel_id=1, source_target_pairs={{0,16},{4,12},{8,24},{12,4},{16,0},{20,28},{24,8},{28,20},{1,17},{... | collective-permute-start | bytes 3145736 | tf_op jit(solution)/shard_map/ppermute | solution.py:79
  719.6 35.0 %collective-permute-start.51 = (bf16[256,512]{1,0:T(8,128)(2,1)S(1)}, bf16[256,512]{1,0:T(8,128)(2,1)S(1)}, u32[]{:S(2)}, u32[]{:S(2)}) collective-permute-start(bf16[256,512]{1,0:T(8,128)(2,1)S(1)} %get-tuple-element.165), channel_id=1, source_target_pairs={{0,1},{1,0},{2,3},{3,2},{4,5},{5,4},{6,7},{7,6},{8,9},{9,8},{10,11... | collective-permute-start | bytes 786440 | tf_op jit(solution)/shard_map/ppermute | solution.py:124
  724.3 34.2 %collective-permute-start.52 = (bf16[256,512]{1,0:T(8,128)(2,1)S(1)}, bf16[256,512]{1,0:T(8,128)(2,1)S(1)}, u32[]{:S(2)}, u32[]{:S(2)}) collective-permute-start(bf16[256,512]{1,0:T(8,128)(2,1)S(1)} %get-tuple-element.166), channel_id=1, source_target_pairs={{0,2},{1,3},{2,0},{3,1},{4,6},{5,7},{6,4},{7,5},{8,10},{9,11},{10,... | collective-permute-start | bytes 786440 | tf_op jit(solution)/shard_map/ppermute | solution.py:124
  732.3 26.2 %collective-permute-start.53 = (bf16[256,512]{1,0:T(8,128)(2,1)S(1)}, bf16[256,512]{1,0:T(8,128)(2,1)S(1)}, u32[]{:S(2)}, u32[]{:S(2)}) collective-permute-start(bf16[256,512]{1,0:T(8,128)(2,1)S(1)} %get-tuple-element.167), channel_id=1, source_target_pairs={{0,3},{1,2},{2,1},{3,0},{4,7},{5,6},{6,5},{7,4},{8,11},{9,10},{10,... | collective-permute-start | bytes 786440 | tf_op jit(solution)/shard_map/ppermute | solution.py:124
  754.6 24.8 %collective-permute-start.46 = (bf16[256,2048]{1,0:T(8,128)(2,1)}, bf16[256,2048]{1,0:T(8,128)(2,1)}, u32[]{:S(2)}, u32[]{:S(2)}) collective-permute-start(bf16[256,2048]{1,0:T(8,128)(2,1)} %get-tuple-element.147), channel_id=1, source_target_pairs={{0,1},{3,2},{4,5},{7,6},{8,9},{11,10},{12,13},{15,14},{16,17},{19,... | collective-permute-start | bytes 3145736 | tf_op jit(solution)/shard_map/ppermute | solution.py:124
  769.6 25.6 %collective-permute-start.60 = (bf16[256,2048]{1,0:T(8,128)(2,1)}, bf16[256,2048]{1,0:T(8,128)(2,1)}, u32[]{:S(2)}, u32[]{:S(2)}) collective-permute-start(bf16[256,2048]{1,0:T(8,128)(2,1)} %get-tuple-element.123), channel_id=1, source_target_pairs={{0,16},{4,12},{8,24},{12,4},{16,0},{20,28},{24,8},{28,20},{1,17},{... | collective-permute-start | bytes 3145736 | tf_op jit(solution)/shard_map/ppermute | solution.py:79
  778.5 53.5 %collective-permute-start.72 = (bf16[512,256]{1,0:T(8,128)(2,1)S(1)}, bf16[512,256]{1,0:T(8,128)(2,1)S(1)}, u32[]{:S(2)}, u32[]{:S(2)}) collective-permute-start(bf16[512,256]{1,0:T(8,128)(2,1)S(1)} %get-tuple-element.157), channel_id=1, source_target_pairs={{0,1},{1,0},{2,3},{3,2},{4,5},{5,4},{6,7},{7,6},{8,9},{9,8},{10,11... | collective-permute-start | bytes 786440 | tf_op jit(solution)/shard_map/ppermute | solution.py:124
  778.5 48.5 %collective-permute-start.58 = (bf16[256,2048]{1,0:T(8,128)(2,1)S(1)}, bf16[256,2048]{1,0:T(8,128)(2,1)S(1)}, u32[]{:S(2)}, u32[]{:S(2)}) collective-permute-start(bf16[256,2048]{1,0:T(8,128)(2,1)S(1)} %copy-done.53), channel_id=1, source_target_pairs={{0,16},{4,12},{8,24},{12,4},{16,0},{20,28},{24,8},{28,20},{1,17},{... | collective-permute-start | bytes 3145736 | tf_op jit(solution)/shard_map/ppermute | solution.py:79
  781.5 49.4 %collective-permute-start.47 = (bf16[256,2048]{1,0:T(8,128)(2,1)S(1)}, bf16[256,2048]{1,0:T(8,128)(2,1)S(1)}, u32[]{:S(2)}, u32[]{:S(2)}) collective-permute-start(bf16[256,2048]{1,0:T(8,128)(2,1)S(1)} %add.373), channel_id=1, source_target_pairs={{1,2},{2,1},{5,6},{6,5},{9,10},{10,9},{13,14},{14,13},{17,18},{18,... | collective-permute-start | bytes 3145736 | tf_op jit(solution)/shard_map/ppermute | solution.py:124
  782.3 47.2 %collective-permute-start.48 = (bf16[256,2048]{1,0:T(8,128)(2,1)S(1)}, bf16[256,2048]{1,0:T(8,128)(2,1)S(1)}, u32[]{:S(2)}, u32[]{:S(2)}) collective-permute-start(bf16[256,2048]{1,0:T(8,128)(2,1)S(1)} %get-tuple-element.112), channel_id=1, source_target_pairs={{0,1},{3,2},{4,5},{7,6},{8,9},{11,10},{12,13},{15,14},{16,17},{19,... | collective-permute-start | bytes 3145736 | tf_op jit(solution)/shard_map/ppermute | solution.py:124
  796.5 53.7 %collective-permute-start.61 = (bf16[256,2048]{1,0:T(8,128)(2,1)S(1)}, bf16[256,2048]{1,0:T(8,128)(2,1)S(1)}, u32[]{:S(2)}, u32[]{:S(2)}) collective-permute-start(bf16[256,2048]{1,0:T(8,128)(2,1)S(1)} %fusion.16), channel_id=1, source_target_pairs={{0,8},{4,20},{8,0},{12,28},{16,24},{20,4},{24,16},{28,12},{1,9},{5... | collective-permute-start | bytes 3145736 | tf_op jit(solution)/shard_map/ppermute | solution.py:79
  827.1 21.3 %collective-permute-start.73 = (bf16[512,256]{1,0:T(8,128)(2,1)S(1)}, bf16[512,256]{1,0:T(8,128)(2,1)S(1)}, u32[]{:S(2)}, u32[]{:S(2)}) collective-permute-start(bf16[512,256]{1,0:T(8,128)(2,1)S(1)} %get-tuple-element.159), channel_id=1, source_target_pairs={{0,2},{1,3},{2,0},{3,1},{4,6},{5,7},{6,4},{7,5},{8,10},{9,11},{10,... | collective-permute-start | bytes 786440 | tf_op jit(solution)/shard_map/ppermute | solution.py:124
  829.5 19.6 %collective-permute-start.74 = (bf16[512,256]{1,0:T(8,128)(2,1)S(1)}, bf16[512,256]{1,0:T(8,128)(2,1)S(1)}, u32[]{:S(2)}, u32[]{:S(2)}) collective-permute-start(bf16[512,256]{1,0:T(8,128)(2,1)S(1)} %get-tuple-element.158), channel_id=1, source_target_pairs={{0,3},{1,2},{2,1},{3,0},{4,7},{5,6},{6,5},{7,4},{8,11},{9,10},{10,... | collective-permute-start | bytes 786440 | tf_op jit(solution)/shard_map/ppermute | solution.py:124
  830.9 19.1 %collective-permute-start.67 = (bf16[320,512]{1,0:T(8,128)(2,1)S(1)}, bf16[320,512]{1,0:T(8,128)(2,1)S(1)}, u32[]{:S(2)}, u32[]{:S(2)}) collective-permute-start(bf16[320,512]{1,0:T(8,128)(2,1)S(1)} %get-tuple-element.126), channel_id=1, source_target_pairs={{0,16},{4,12},{8,24},{12,4},{16,0},{20,28},{24,8},{28,20},{1,17},{... | collective-permute-start | bytes 983048 | tf_op jit(solution)/shard_map/ppermute | solution.py:79
  832.0 36.4 %collective-permute-start.49 = (bf16[256,2048]{1,0:T(8,128)(2,1)S(1)}, bf16[256,2048]{1,0:T(8,128)(2,1)S(1)}, u32[]{:S(2)}, u32[]{:S(2)}) collective-permute-start(bf16[256,2048]{1,0:T(8,128)(2,1)S(1)} %dynamic-slice_add_fusion), channel_id=1, source_target_pairs={{0,1},{1,0},{2,3},{3,2},{4,5},{5,4},{6,7},{7,6},{8,9},{9,8},{10,11... | collective-permute-start | bytes 3145736 | tf_op jit(solution)/shard_map/ppermute | solution.py:124
  848.3 21.4 %collective-permute-start.50 = (bf16[256,2048]{1,0:T(8,128)(2,1)S(1)}, bf16[256,2048]{1,0:T(8,128)(2,1)S(1)}, u32[]{:S(2)}, u32[]{:S(2)}) collective-permute-start(bf16[256,2048]{1,0:T(8,128)(2,1)S(1)} %add.376), channel_id=1, source_target_pairs={{1,2},{2,1},{5,6},{6,5},{9,10},{10,9},{13,14},{14,13},{17,18},{18,... | collective-permute-start | bytes 3145736 | tf_op jit(solution)/shard_map/ppermute | solution.py:124
  850.0 26.7 %collective-permute-start.68 = (bf16[320,512]{1,0:T(8,128)(2,1)S(1)}, bf16[320,512]{1,0:T(8,128)(2,1)S(1)}, u32[]{:S(2)}, u32[]{:S(2)}) collective-permute-start(bf16[320,512]{1,0:T(8,128)(2,1)S(1)} %fusion.23), channel_id=1, source_target_pairs={{0,8},{4,20},{8,0},{12,28},{16,24},{20,4},{24,16},{28,12},{1,9},{5... | collective-permute-start | bytes 983048 | tf_op jit(solution)/shard_map/ppermute | solution.py:79
  850.2 26.5 %collective-permute-start.66 = (bf16[320,512]{1,0:T(8,128)(2,1)S(1)}, bf16[320,512]{1,0:T(8,128)(2,1)S(1)}, u32[]{:S(2)}, u32[]{:S(2)}) collective-permute-start(bf16[320,512]{1,0:T(8,128)(2,1)S(1)} %get-tuple-element.125), channel_id=1, source_target_pairs={{0,16},{4,12},{8,24},{12,4},{16,0},{20,28},{24,8},{28,20},{1,17},{... | collective-permute-start | bytes 983048 | tf_op jit(solution)/shard_map/ppermute | solution.py:79
  852.8 43.2 %collective-permute-start.62 = (bf16[256,512]{1,0:T(8,128)(2,1)S(1)}, bf16[256,512]{1,0:T(8,128)(2,1)S(1)}, u32[]{:S(2)}, u32[]{:S(2)}) collective-permute-start(bf16[256,512]{1,0:T(8,128)(2,1)S(1)} %get-tuple-element.160), channel_id=1, source_target_pairs={{0,1},{1,0},{2,3},{3,2},{4,5},{5,4},{6,7},{7,6},{8,9},{9,8},{10,11... | collective-permute-start | bytes 786440 | tf_op jit(solution)/shard_map/ppermute | solution.py:124
  868.4 30.0 %collective-permute-start.63 = (bf16[256,512]{1,0:T(8,128)(2,1)S(1)}, bf16[256,512]{1,0:T(8,128)(2,1)}, u32[]{:S(2)}, u32[]{:S(2)}) collective-permute-start(bf16[256,512]{1,0:T(8,128)(2,1)S(1)} %get-tuple-element.162), channel_id=1, source_target_pairs={{0,2},{1,3},{2,0},{3,1},{4,6},{5,7},{6,4},{7,5},{8,10},{9,11},{10,... | collective-permute-start | bytes 786440 | tf_op jit(solution)/shard_map/ppermute | solution.py:124
  869.8 28.6 %collective-permute-start.64 = (bf16[256,512]{1,0:T(8,128)(2,1)S(1)}, bf16[256,512]{1,0:T(8,128)(2,1)}, u32[]{:S(2)}, u32[]{:S(2)}) collective-permute-start(bf16[256,512]{1,0:T(8,128)(2,1)S(1)} %get-tuple-element.161), channel_id=1, source_target_pairs={{0,3},{1,2},{2,1},{3,0},{4,7},{5,6},{6,5},{7,4},{8,11},{9,10},{10,... | collective-permute-start | bytes 786440 | tf_op jit(solution)/shard_map/ppermute | solution.py:124
  877.9 22.5 %collective-permute-start.69 = (bf16[80,512]{1,0:T(8,128)(2,1)S(1)}, bf16[80,512]{1,0:T(8,128)(2,1)S(1)}, u32[]{:S(2)}, u32[]{:S(2)}) collective-permute-start(bf16[80,512]{1,0:T(8,128)(2,1)S(1)} %get-tuple-element.168), channel_id=1, source_target_pairs={{0,1},{1,0},{2,3},{3,2},{4,5},{5,4},{6,7},{7,6},{8,9},{9,8},{10,11... | collective-permute-start | bytes 245768 | tf_op jit(solution)/shard_map/ppermute | solution.py:124
  (102 other events, 2417.0 us)
Sparse Core Ops, SparseCore 0:
  9.9 86.4 all-gather.7
  151.4 83.2 all-gather.5
  236.6 65.1 all-gather.9
  506.2 84.7 reduce-scatter.7
  594.9 124.6 reduce-scatter.3
  723.0 107.6 reduce-scatter.5

commit v6 on v5

--- a/solution.py
+++ b/solution.py
@@ -80,10 +80,11 @@
 
         return self.lane(send, value) if ordered else send(value)
 
-    def begin(self, value, ordered=True):
+    def begin(self, value, ordered=True, corner=False):
         if not self.fast:
             return [value]
-        return [value, self.swap(value, 2, 4, ordered), self.swap(value, 4, 2, ordered)]
+        begun = [value, self.swap(value, 2, 4, ordered), self.swap(value, 4, 2, ordered)]
+        return begun + [self.swap(value, 6, 6, ordered)] if corner else begun
 
     def finish(self, begun, axis=0, ordered=True):
         if not self.fast:
@@ -92,8 +93,9 @@
             return [
                 lax.slice_in_dim(whole, i * half, (i + 1) * half, axis=axis) for i in range(2)
             ]
-        value, one, two = begun
-        mine = jnp.concatenate([value, one, two, self.swap(one, 4, 2, ordered)], axis=axis)
+        if len(begun) == 3:
+            begun = [*begun, self.swap(begun[1], 4, 2, ordered)]
+        mine = jnp.concatenate(begun, axis=axis)
         return [mine, self.swap(mine, 1, 1, False)]
 
     def gather(self, value, axis=0, ordered=True):
@@ -749,7 +751,7 @@
 
     straight = jnp.arange(seq.size, dtype=jnp.int32)
     normed2_all, first_step = head.gather(normed2)
-    down_begun = seq.begin(after(down_weight, *first_step))
+    down_begun = seq.begin(after(down_weight, *first_step), corner=True)
     down_begun = [after(item, normed2_all) for item in down_begun]
     down = [
         half_of.reshape(pieces, -1, depth // seq.size) for half_of in seq.finish(down_begun)

time: 932 us -> 937 us (level)
  starting transfers between devices: 139 us -> 214 us
  waiting for transfers between devices: 352 us -> 300 us
  Pallas kernels: 230 us -> 212 us
    ppermute x36, starting transfers between devices: 26 us -> 105 us  [send(): return lax.ppermute(item, 'seq', pairs)]
    ppermute x39, waiting for transfers between devices: 132 us -> 91 us  [send(): return lax.ppermute(value, 'head', pairs)]
    pallas_call x1, Pallas kernels: 26.8 us -> 14.9 us  [attention_backward(): pl.pallas_call(backward_kernel, out_shape=(jax.ShapeDtypeStruct((rows, HE...]
    ppermute x36, waiting for transfers between devices: 220 us -> 209 us  [send(): return lax.ppermute(item, 'seq', pairs)]
  transfers between devices with their start and end apart: 81 -> 81, of which waited for: 25 -> 27; matrix products, arithmetic and copies ran while one was open for 16% -> 16% of each run, Pallas kernels for 17% -> 15%
where the time goes in v6:
time: 937 us; the launch traced here: 927 us
  waiting for transfers between devices  300 us (32%)
  starting transfers between devices  214 us (23%)
  Pallas kernels  212 us (23%)
  other arithmetic  74.8 us (8%)
  local copies, waits for them, and re-layouts  65.3 us (7%)
  matrix products  36.6 us (4%)
  between operations  24.4 us (3%)
    ppermute x36, waiting for transfers between devices, send(): return lax.ppermute(item, 'seq', pairs)  209 us
    ppermute x39, starting transfers between devices, send(): return lax.ppermute(value, 'head', pairs)  108 us
    ppermute x36, starting transfers between devices, send(): return lax.ppermute(item, 'seq', pairs)  105 us
    ppermute x39, waiting for transfers between devices, send(): return lax.ppermute(value, 'head', pairs)  91 us
    pallas_call x7, Pallas kernels, unit_grad(): pl.pallas_call(functools.partial(unit_grad_kernel, count, shift, len(extr...  71.3 us
    pallas_call x1, Pallas kernels, ffn_middle(): pl.pallas_call(ffn_kernel, out_shape=(jax.ShapeDtypeStruct((rows, units),...  44.2 us
    unnamed x183, local copies, waits for them, and re-layouts  32.9 us
    pallas_call x1, Pallas kernels, ffn_back(): pl.pallas_call(back_kernel, out_shape=jax.ShapeDtypeStruct((rows, pieces...  31.5 us
  transfers between devices with their start and end apart: 81, of which 27 were waited for; matrix products, arithmetic and copies ran while one was open for 16% of the time, Pallas kernels for 15%

profile of v6, /device:TPU:0, one launch (start us, length us, event | category | flops | bytes accessed | tf_op | source)
XLA Modules:
  0.0 927.0 jit_solution(14990673529929414136)
XLA Ops:
  16.2 3.5 collective-permute-start.8
  24.2 3.2 shuffle.3
  36.3 9.4 %collective-permute-done.3 = bf16[320,512]{1,0:T(8,128)(2,1)S(1)} collective-permute-done((bf16[320,512]{1,0:T(8,128)(2,1)}, bf16[320,512]{1,0:T(8,128)(2,1)S(1)}, u32[]{:S(2)}, u32[]{:S(2)}) %collective-permute-start.3) | collective-permute-done | bytes 327712 | tf_op jit(solution)/shard_map/ppermute | solution.py:79
  49.9 7.5 collective-permute-done.5
  71.9 10.6 %collective-permute-done.15.refs_2_ = bf16[512,256]{1,0:T(8,128)(2,1)} collective-permute-done((bf16[512,256]{1,0:T(8,128)(2,1)}, bf16[512,256]{1,0:T(8,128)(2,1)}, u32[]{:S(2)}, u32[]{:S(2)}) %collective-permute-start.15) | collective-permute-done | bytes 262176 | tf_op jit(solution)/shard_map/ppermute | solution.py:126
  85.8 16.9 %collective-permute-done.10 = bf16[256,2048]{1,0:T(8,128)(2,1)} collective-permute-done((bf16[256,2048]{1,0:T(8,128)(2,1)}, bf16[256,2048]{1,0:T(8,128)(2,1)}, u32[]{:S(2)}, u32[]{:S(2)}) %collective-permute-start.10) | collective-permute-done | bytes 1048608 | tf_op jit(solution)/shard_map/ppermute | solution.py:79
  107.8 3.2 slice.188
  121.9 3.6 pad_maximum_fusion
  129.9 8.3 collective-permute-done.17.refs_1_
  138.2 10.1 %collective-permute-done.18.refs_2_ = bf16[256,512]{1,0:T(8,128)(2,1)S(1)} collective-permute-done((bf16[256,512]{1,0:T(8,128)(2,1)S(1)}, bf16[256,512]{1,0:T(8,128)(2,1)S(1)}, u32[]{:S(2)}, u32[]{:S(2)}) %collective-permute-start.18) | collective-permute-done | bytes 262176 | tf_op jit(solution)/shard_map/ppermute | solution.py:126
  152.5 24.9 %collective-permute-done.22 = bf16[2048,256]{1,0:T(8,128)(2,1)S(1)} collective-permute-done((bf16[2048,256]{1,0:T(8,128)(2,1)S(1)}, bf16[2048,256]{1,0:T(8,128)(2,1)S(1)}, u32[]{:S(2)}, u32[]{:S(2)}) %collective-permute-start.22) | collective-permute-done | bytes 1048608 | tf_op jit(solution)/shard_map/ppermute | solution.py:79
  178.4 22.2 %collective-permute-done.23 = bf16[2048,256]{1,0:T(8,128)(2,1)S(1)} collective-permute-done((bf16[2048,256]{1,0:T(8,128)(2,1)S(1)}, bf16[2048,256]{1,0:T(8,128)(2,1)S(1)}, u32[]{:S(2)}, u32[]{:S(2)}) %collective-permute-start.23) | collective-permute-done | bytes 1048608 | tf_op jit(solution)/shard_map/ppermute | solution.py:79
  204.1 11.5 %collective-permute-done.24 = bf16[1024,512]{1,0:T(8,128)(2,1)S(1)} collective-permute-done((bf16[1024,512]{1,0:T(8,128)(2,1)}, bf16[1024,512]{1,0:T(8,128)(2,1)S(1)}, u32[]{:S(2)}, u32[]{:S(2)}) %collective-permute-start.24) | collective-permute-done | bytes 1048608 | tf_op jit(solution)/shard_map/ppermute | solution.py:79
  215.7 11.2 %collective-permute-done.25 = bf16[1024,512]{1,0:T(8,128)(2,1)S(1)} collective-permute-done((bf16[1024,512]{1,0:T(8,128)(2,1)S(1)}, bf16[1024,512]{1,0:T(8,128)(2,1)S(1)}, u32[]{:S(2)}, u32[]{:S(2)}) %collective-permute-start.25) | collective-permute-done | bytes 1048608 | tf_op jit(solution)/shard_map/ppermute | solution.py:79
  229.6 3.7 pad_maximum_fusion.1
  241.4 4.2 fusion.40
  247.4 7.8 attention_forward.1
  255.3 4.2 fusion.52
  259.5 3.5 fusion.53
  263.7 5.7 collective-permute-start.28
  271.0 12.9 %collective-permute-done.28.refs_1_ = bf16[256,2048]{1,0:T(8,128)(2,1)S(1)} collective-permute-done((bf16[256,2048]{1,0:T(8,128)(2,1)S(1)}, bf16[256,2048]{1,0:T(8,128)(2,1)S(1)}, u32[]{:S(2)}, u32[]{:S(2)}) %collective-permute-start.28) | collective-permute-done | bytes 1048608 | tf_op jit(solution)/shard_map/ppermute | solution.py:126
  286.8 26.8 %collective-permute-start.33 = (bf16[2752,256]{1,0:T(8,128)(2,1)}, bf16[2752,256]{1,0:T(8,128)(2,1)}, u32[]{:S(2)}, u32[]{:S(2)}) collective-permute-start(bf16[2752,256]{1,0:T(8,128)(2,1)} %param.29), channel_id=1, source_target_pairs={{0,8},{4,20},{8,0},{12,28},{16,24},{20,4},{24,16},{28,12},{1,9},{5... | collective-permute-start | bytes 4227080 | tf_op jit(solution)/shard_map/ppermute | solution.py:79
  316.6 10.4 %collective-permute-done.30 = bf16[256,2048]{1,0:T(8,128)(2,1)} collective-permute-done((bf16[256,2048]{1,0:T(8,128)(2,1)}, bf16[256,2048]{1,0:T(8,128)(2,1)}, u32[]{:S(2)}, u32[]{:S(2)}) %collective-permute-start.30) | collective-permute-done | bytes 1048608 | tf_op jit(solution)/shard_map/ppermute | solution.py:126
  329.4 16.4 %collective-permute-done.33 = bf16[2752,256]{1,0:T(8,128)(2,1)} collective-permute-done((bf16[2752,256]{1,0:T(8,128)(2,1)}, bf16[2752,256]{1,0:T(8,128)(2,1)}, u32[]{:S(2)}, u32[]{:S(2)}) %collective-permute-start.33) | collective-permute-done | bytes 1409056 | tf_op jit(solution)/shard_map/ppermute | solution.py:79
  345.8 4.2 collective-permute-done.32
  352.3 4.4 place.9.normed_ref.right_ref
  364.4 8.7 collective-permute-done.35
  377.6 7.6 collective-permute-done.36
  387.4 44.2 %ffn_middle.1 = (bf16[1024,2752]{1,0:T(8,128)(2,1)}, bf16[1024,2752]{1,0:T(8,128)(2,1)}, bf16[1024,2752]{1,0:T(8,128)(2,1)}) custom-call(s32[8]{0:T(128)S(1)} %copy-done.17, bf16[1024,2048]{1,0:T(8,128)(2,1)S(1)} %copy-done.8, bf16[1024,2048]{1,0:T(8,128)(2,1)} %all-gather.6.cloned.1.call-done.grad_ref.right_ref, bf16[8,2752,256]{2,1,0:T(8,128)(2,1)} %bitcast.162, ...), custom_call_target="tpu_custom_call" | custom-call | flops 34628173824 | bytes 59113472 | tf_op jit(solution)/shard_map/ffn_middle/pallas_call | solution.py:485
  431.6 31.5 %ffn_back.1 = bf16[1024,2048]{1,0:T(8,128)(2,1)S(1)} custom-call(s32[8]{0:T(128)S(1)} %copy-done.17, bf16[1024,2752]{1,0:T(8,128)(2,1)} %get-tuple-element.102.d_gate_ref.left_ref, bf16[1024,2752]{1,0:T(8,128)(2,1)} %get-tuple-element.104.d_up_ref.left_ref, bf16[8,2752,256]{2,1,0:T(8,128)(2,1)} %bitcast.163, bf16[8,2752,256]{2,1,0:T(8,128)(2,1)} %bitcast.165), custom_call_target="tpu_custom_call" | custom-call | flops 23085449216 | bytes 33816576 | tf_op jit(solution)/shard_map/ffn_back/pallas_call | solution.py:515
  465.7 15.3 %collective-permute-start.37 = (bf16[256,2048]{1,0:T(8,128)(2,1)}, bf16[256,2048]{1,0:T(8,128)(2,1)}, u32[]{:S(2)}, u32[]{:S(2)}) collective-permute-start(bf16[256,2048]{1,0:T(8,128)(2,1)} %get-tuple-element.153), channel_id=1, source_target_pairs={{0,1},{3,2},{4,5},{7,6},{8,9},{11,10},{12,13},{15,14},{16,17},{19,... | collective-permute-start | bytes 3145736 | tf_op jit(solution)/shard_map/ppermute | solution.py:126
  481.1 17.5 %unit_grad.7 = bf16[8,2752,256]{2,1,0:T(8,128)(2,1)} custom-call(s32[8]{0:T(128)S(1)} %select_reduce_fusion.3.order_ref, bf16[1024,2752]{1,0:T(8,128)(2,1)} %get-tuple-element.112.left_ref.act_ref, bf16[1024,2048]{1,0:T(8,128)(2,1)S(1)} %copy-done.19), custom_call_target="tpu_custom_call" | custom-call | flops 11542724608 | bytes 21102592 | tf_op jit(solution)/shard_map/unit_grad/pallas_call | solution.py:594
  498.6 4.5 collective-permute-done.37
  508.3 7.4 collective-permute-start.39
  517.9 18.0 %unit_grad.8 = bf16[8,2752,256]{2,1,0:T(8,128)(2,1)} custom-call(s32[8]{0:T(128)S(1)} %select_reduce_fusion.3.order_ref, bf16[1024,2752]{1,0:T(8,128)(2,1)} %get-tuple-element.102.d_gate_ref.left_ref, bf16[1024,2048]{1,0:T(8,128)(2,1)S(1)} %copy-done.9), custom_call_target="tpu_custom_call" | custom-call | flops 11542724608 | bytes 21102592 | tf_op jit(solution)/shard_map/unit_grad/pallas_call | solution.py:594
  548.3 17.7 %unit_grad.9 = bf16[8,2752,256]{2,1,0:T(8,128)(2,1)} custom-call(s32[8]{0:T(128)S(1)} %select_reduce_fusion.3.order_ref, bf16[1024,2752]{1,0:T(8,128)(2,1)} %get-tuple-element.104.d_up_ref.left_ref, bf16[1024,2048]{1,0:T(8,128)(2,1)S(1)} %copy-done.10), custom_call_target="tpu_custom_call" | custom-call | flops 11542724608 | bytes 21102592 | tf_op jit(solution)/shard_map/unit_grad/pallas_call | solution.py:594
  570.8 4.0 fusion.20
  574.8 4.6 fusion.3.grad_ref
  579.4 14.9 %attention_backward.1 = (bf16[256,2048]{1,0:T(8,128)(2,1)}, bf16[4096,512]{1,0:T(8,128)(2,1)}, bf16[4096,512]{1,0:T(8,128)(2,1)}) custom-call(s32[16]{0:T(128)} %copy-done.22, s32[2]{0:T(128)} %copy-done.21, bf16[16,256,128]{2,1,0:T(8,128)(2,1)} %copy-done.23, f32[256,128]{1,0:T(8,128)} %copy-done.15, f32[256,128]{1,0:T(8,128)} %copy-done.16, ...), custom_call_target="tpu_custom_call" | custom-call | flops 10737418240 | bytes 20971520 | tf_op jit(solution)/shard_map/attention_backward/pallas_call | solution.py:422
  594.3 13.9 %collective-permute-start.42 = (bf16[4,1024,512]{2,1,0:T(8,128)(2,1)}, bf16[4,1024,512]{2,1,0:T(8,128)(2,1)}, u32[]{:S(2)}, u32[]{:S(2)}) collective-permute-start(bf16[4,1024,512]{2,1,0:T(8,128)(2,1)} %bitcast.166), channel_id=1, source_target_pairs={{0,4},{4,0},{8,12},{12,8},{16,20},{20,16},{24,28},{28,24},{1,5},{5... | collective-permute-start | bytes 12582920 | tf_op jit(solution)/shard_map/ppermute | solution.py:79
  608.2 4.0 unit_grad.12
  613.6 3.4 unit_grad.10
  617.5 4.1 add.369
  624.7 8.9 collective-permute-start.43
  634.6 4.5 fusion.54
  639.1 7.0 unit_grad.13
  646.2 11.8 %collective-permute-done.43 = bf16[1024,512]{1,0:T(8,128)(2,1)} collective-permute-done((bf16[1024,512]{1,0:T(8,128)(2,1)}, bf16[1024,512]{1,0:T(8,128)(2,1)}, u32[]{:S(2)}, u32[]{:S(2)}) %collective-permute-start.43) | collective-permute-done | bytes 1048608 | tf_op jit(solution)/shard_map/ppermute | solution.py:79
  660.5 27.6 %collective-permute-done.44 = bf16[1024,512]{1,0:T(8,128)(2,1)} collective-permute-done((bf16[1024,512]{1,0:T(8,128)(2,1)}, bf16[1024,512]{1,0:T(8,128)(2,1)}, u32[]{:S(2)}, u32[]{:S(2)}) %collective-permute-start.44) | collective-permute-done | bytes 1048608 | tf_op jit(solution)/shard_map/ppermute | solution.py:79
  689.5 8.7 collective-permute-start.45
  698.2 4.4 fusion.55
  702.7 3.7 unit_grad.11
  711.6 21.7 %collective-permute-start.57 = (bf16[2048,256]{1,0:T(8,128)(2,1)}, bf16[2048,256]{1,0:T(8,128)(2,1)}, u32[]{:S(2)}, u32[]{:S(2)}) collective-permute-start(bf16[2048,256]{1,0:T(8,128)(2,1)} %add.389), channel_id=1, source_target_pairs={{0,8},{4,20},{8,0},{12,28},{16,24},{20,4},{24,16},{28,12},{1,9},{5... | collective-permute-start | bytes 3145736 | tf_op jit(solution)/shard_map/ppermute | solution.py:79
  740.1 19.7 %ffn_forth.1 = bf16[1024,2048]{1,0:T(8,128)(2,1)S(1)} custom-call(bf16[1024,2752]{1,0:T(8,128)(2,1)} %get-tuple-element.112.left_ref.act_ref, bf16[4,2752,256]{2,1,0:T(8,128)(2,1)} %bitcast.18.down_a_ref, bf16[4,2752,256]{2,1,0:T(8,128)(2,1)} %bitcast.19.down_b_ref), custom_call_target="tpu_custom_call" | custom-call | flops 11542724608 | bytes 16908288 | tf_op jit(solution)/shard_map/ffn_forth/pallas_call | solution.py:546
  762.1 3.7 collective-permute-start.46
  769.5 4.5 fusion.12
  780.2 3.2 shuffle.5
  790.7 5.6 collective-permute-start.48
  797.8 3.5 collective-permute-done.60
  804.3 28.0 %collective-permute-done.58 = bf16[256,2048]{1,0:T(8,128)(2,1)S(1)} collective-permute-done((bf16[256,2048]{1,0:T(8,128)(2,1)S(1)}, bf16[256,2048]{1,0:T(8,128)(2,1)S(1)}, u32[]{:S(2)}, u32[]{:S(2)}) %collective-permute-start.58) | collective-permute-done | bytes 1048608 | tf_op jit(solution)/shard_map/ppermute | solution.py:79
  837.2 15.0 %collective-permute-done.73 = bf16[512,256]{1,0:T(8,128)(2,1)S(1)} collective-permute-done((bf16[512,256]{1,0:T(8,128)(2,1)S(1)}, bf16[512,256]{1,0:T(8,128)(2,1)S(1)}, u32[]{:S(2)}, u32[]{:S(2)}) %collective-permute-start.73) | collective-permute-done | bytes 262176 | tf_op jit(solution)/shard_map/ppermute | solution.py:126
  857.3 5.5 collective-permute-start.62
  862.8 9.3 %collective-permute-done.49 = bf16[256,2048]{1,0:T(8,128)(2,1)S(1)} collective-permute-done((bf16[256,2048]{1,0:T(8,128)(2,1)S(1)}, bf16[256,2048]{1,0:T(8,128)(2,1)S(1)}, u32[]{:S(2)}, u32[]{:S(2)}) %collective-permute-start.49) | collective-permute-done | bytes 1048608 | tf_op jit(solution)/shard_map/ppermute | solution.py:126
  881.7 18.1 %collective-permute-start.69 = (bf16[80,512]{1,0:T(8,128)(2,1)S(1)}, bf16[80,512]{1,0:T(8,128)(2,1)S(1)}, u32[]{:S(2)}, u32[]{:S(2)}) collective-permute-start(bf16[80,512]{1,0:T(8,128)(2,1)S(1)} %get-tuple-element.170), channel_id=1, source_target_pairs={{0,1},{1,0},{2,3},{3,2},{4,5},{5,4},{6,7},{7,6},{8,9},{9,8},{10,11... | collective-permute-start | bytes 245768 | tf_op jit(solution)/shard_map/ppermute | solution.py:126
  904.1 4.3 collective-permute-done.70
  (445 shorter events, 212.2 us)
Async XLA Ops:
  7.2 144.0 %all-gather.8.cloned.1.call-start = ((), (), s32[]{:S(2)}) async-start(), calls=%async_computation.7 | async-start | bytes 12681216 | tf_op jit(solution)/shard_map/all_gather | solution.py:674
  7.9 369.7 %all-gather.6.cloned.1.call-start = ((), (), s32[]{:S(2)}) async-start(), calls=%async_computation.3 | async-start | bytes 5242880 | tf_op jit(solution)/shard_map/all_gather | solution.py:743
  9.6 20.0 %collective-permute-start = (bf16[80,512]{1,0:T(8,128)(2,1)S(1)}, bf16[80,512]{1,0:T(8,128)(2,1)S(1)}, u32[]{:S(2)}, u32[]{:S(2)}) collective-permute-start(bf16[80,512]{1,0:T(8,128)(2,1)S(1)} %fusion.27.refs_0_), channel_id=1, source_target_pairs={{0,1},{1,0},{2,3},{3,2},{4,5},{5,4},{6,7},{7,6},{8,9},{9,8},{10,11... | collective-permute-start | bytes 245768 | tf_op jit(solution)/shard_map/ppermute | solution.py:126
  15.3 45.6 %collective-permute-start.7 = (bf16[256,512]{1,0:T(8,128)(2,1)}, bf16[256,512]{1,0:T(8,128)(2,1)S(1)}, u32[]{:S(2)}, u32[]{:S(2)}) collective-permute-start(bf16[256,512]{1,0:T(8,128)(2,1)} %refs_0_.4), channel_id=1, source_target_pairs={{0,1},{1,0},{2,3},{3,2},{4,5},{5,4},{6,7},{7,6},{8,9},{9,8},{10,11... | collective-permute-start | bytes 786440 | tf_op jit(solution)/shard_map/ppermute | solution.py:126
  16.2 46.6 %collective-permute-start.8 = (bf16[256,512]{1,0:T(8,128)(2,1)}, bf16[256,512]{1,0:T(8,128)(2,1)S(1)}, u32[]{:S(2)}, u32[]{:S(2)}) collective-permute-start(bf16[256,512]{1,0:T(8,128)(2,1)} %refs_0_.4), channel_id=1, source_target_pairs={{0,2},{1,3},{2,0},{3,1},{4,6},{5,7},{6,4},{7,5},{8,10},{9,11},{10,... | collective-permute-start | bytes 786440 | tf_op jit(solution)/shard_map/ppermute | solution.py:126
  29.7 34.6 %collective-permute-start.9 = (bf16[256,512]{1,0:T(8,128)(2,1)S(1)}, bf16[256,512]{1,0:T(8,128)(2,1)S(1)}, u32[]{:S(2)}, u32[]{:S(2)}) collective-permute-start(bf16[256,512]{1,0:T(8,128)(2,1)S(1)} %copy-done.61), channel_id=1, source_target_pairs={{0,3},{1,2},{2,1},{3,0},{4,7},{5,6},{6,5},{7,4},{8,11},{9,10},{10,... | collective-permute-start | bytes 786440 | tf_op jit(solution)/shard_map/ppermute | solution.py:126
  48.4 21.0 %collective-permute-start.14 = (bf16[512,256]{1,0:T(8,128)(2,1)}, bf16[512,256]{1,0:T(8,128)(2,1)}, u32[]{:S(2)}, u32[]{:S(2)}) collective-permute-start(bf16[512,256]{1,0:T(8,128)(2,1)} %refs_0_.5), channel_id=1, source_target_pairs={{0,1},{1,0},{2,3},{3,2},{4,5},{5,4},{6,7},{7,6},{8,9},{9,8},{10,11... | collective-permute-start | bytes 786440 | tf_op jit(solution)/shard_map/ppermute | solution.py:126
  60.3 44.6 %collective-permute-start.6 = (bf16[1280,512]{1,0:T(8,128)(2,1)}, bf16[1280,512]{1,0:T(8,128)(2,1)}, u32[]{:S(2)}, u32[]{:S(2)}) collective-permute-start(bf16[1280,512]{1,0:T(8,128)(2,1)} %pad_maximum_fusion.2), channel_id=1, source_target_pairs={{0,4},{4,0},{8,12},{12,8},{16,20},{20,16},{24,28},{28,24},{1,5},{5... | collective-permute-start | bytes 3932168 | tf_op jit(solution)/shard_map/ppermute | solution.py:79
  60.9 21.6 %collective-permute-start.15 = (bf16[512,256]{1,0:T(8,128)(2,1)}, bf16[512,256]{1,0:T(8,128)(2,1)}, u32[]{:S(2)}, u32[]{:S(2)}) collective-permute-start(bf16[512,256]{1,0:T(8,128)(2,1)} %refs_0_.5), channel_id=1, source_target_pairs={{0,2},{1,3},{2,0},{3,1},{4,6},{5,7},{6,4},{7,5},{8,10},{9,11},{10,... | collective-permute-start | bytes 786440 | tf_op jit(solution)/shard_map/ppermute | solution.py:126
  62.8 19.7 %collective-permute-start.16 = (bf16[512,256]{1,0:T(8,128)(2,1)}, bf16[512,256]{1,0:T(8,128)(2,1)}, u32[]{:S(2)}, u32[]{:S(2)}) collective-permute-start(bf16[512,256]{1,0:T(8,128)(2,1)} %refs_0_.5), channel_id=1, source_target_pairs={{0,3},{1,2},{2,1},{3,0},{4,7},{5,6},{6,5},{7,4},{8,11},{9,10},{10,... | collective-permute-start | bytes 786440 | tf_op jit(solution)/shard_map/ppermute | solution.py:126
  67.2 35.5 %collective-permute-start.10 = (bf16[256,2048]{1,0:T(8,128)(2,1)}, bf16[256,2048]{1,0:T(8,128)(2,1)}, u32[]{:S(2)}, u32[]{:S(2)}) collective-permute-start(bf16[256,2048]{1,0:T(8,128)(2,1)} %place.6), channel_id=1, source_target_pairs={{0,8},{4,20},{8,0},{12,28},{16,24},{20,4},{24,16},{28,12},{1,9},{5... | collective-permute-start | bytes 3145736 | tf_op jit(solution)/shard_map/ppermute | solution.py:79
  69.4 52.5 %collective-permute-start.11 = (bf16[256,2048]{1,0:T(8,128)(2,1)}, bf16[256,2048]{1,0:T(8,128)(2,1)}, u32[]{:S(2)}, u32[]{:S(2)}) collective-permute-start(bf16[256,2048]{1,0:T(8,128)(2,1)} %place.6), channel_id=1, source_target_pairs={{0,16},{4,12},{8,24},{12,4},{16,0},{20,28},{24,8},{28,20},{1,17},{... | collective-permute-start | bytes 3145736 | tf_op jit(solution)/shard_map/ppermute | solution.py:79
  126.9 21.4 %collective-permute-start.18 = (bf16[256,512]{1,0:T(8,128)(2,1)S(1)}, bf16[256,512]{1,0:T(8,128)(2,1)S(1)}, u32[]{:S(2)}, u32[]{:S(2)}) collective-permute-start(bf16[256,512]{1,0:T(8,128)(2,1)S(1)} %pad_maximum_fusion.3.refs_0_), channel_id=1, source_target_pairs={{0,2},{1,3},{2,0},{3,1},{4,6},{5,7},{6,4},{7,5},{8,10},{9,11},{10,... | collective-permute-start | bytes 786440 | tf_op jit(solution)/shard_map/ppermute | solution.py:126
  129.4 19.6 %collective-permute-start.19 = (bf16[256,512]{1,0:T(8,128)(2,1)S(1)}, bf16[256,512]{1,0:T(8,128)(2,1)}, u32[]{:S(2)}, u32[]{:S(2)}) collective-permute-start(bf16[256,512]{1,0:T(8,128)(2,1)S(1)} %pad_maximum_fusion.3.refs_0_), channel_id=1, source_target_pairs={{0,3},{1,2},{2,1},{3,0},{4,7},{5,6},{6,5},{7,4},{8,11},{9,10},{10,... | collective-permute-start | bytes 786440 | tf_op jit(solution)/shard_map/ppermute | solution.py:126
  151.2 234.0 %all-gather.10.cloned.1.call-start = ((), (), s32[]{:S(2)}) async-start(), calls=%async_computation.8 | async-start | bytes 12681216 | tf_op jit(solution)/shard_map/all_gather | solution.py:744
  151.3 26.1 %collective-permute-start.22 = (bf16[2048,256]{1,0:T(8,128)(2,1)S(1)}, bf16[2048,256]{1,0:T(8,128)(2,1)S(1)}, u32[]{:S(2)}, u32[]{:S(2)}) collective-permute-start(bf16[2048,256]{1,0:T(8,128)(2,1)S(1)} %copy-done.39), channel_id=1, source_target_pairs={{0,8},{4,20},{8,0},{12,28},{16,24},{20,4},{24,16},{28,12},{1,9},{5... | collective-permute-start | bytes 3145736 | tf_op jit(solution)/shard_map/ppermute | solution.py:79
  152.0 25.4 %collective-permute-start.20 = (bf16[2048,256]{1,0:T(8,128)(2,1)S(1)}, bf16[2048,256]{1,0:T(8,128)(2,1)S(1)}, u32[]{:S(2)}, u32[]{:S(2)}) collective-permute-start(bf16[2048,256]{1,0:T(8,128)(2,1)S(1)} %copy-done.39), channel_id=1, source_target_pairs={{0,16},{4,12},{8,24},{12,4},{16,0},{20,28},{24,8},{28,20},{1,17},{... | collective-permute-start | bytes 3145736 | tf_op jit(solution)/shard_map/ppermute | solution.py:79
  177.4 23.2 %collective-permute-start.23 = (bf16[2048,256]{1,0:T(8,128)(2,1)S(1)}, bf16[2048,256]{1,0:T(8,128)(2,1)S(1)}, u32[]{:S(2)}, u32[]{:S(2)}) collective-permute-start(bf16[2048,256]{1,0:T(8,128)(2,1)S(1)} %collective-permute-done.22), channel_id=1, source_target_pairs={{0,16},{4,12},{8,24},{12,4},{16,0},{20,28},{24,8},{28,20},{1,17},{... | collective-permute-start | bytes 3145736 | tf_op jit(solution)/shard_map/ppermute | solution.py:79
  177.4 24.1 %collective-permute-start.21 = (bf16[1024,512]{1,0:T(8,128)(2,1)}, bf16[1024,512]{1,0:T(8,128)(2,1)S(1)}, u32[]{:S(2)}, u32[]{:S(2)}) collective-permute-start(bf16[1024,512]{1,0:T(8,128)(2,1)} %place.8), channel_id=1, source_target_pairs={{0,8},{4,20},{8,0},{12,28},{16,24},{20,4},{24,16},{28,12},{1,9},{5... | collective-permute-start | bytes 3145736 | tf_op jit(solution)/shard_map/ppermute | solution.py:79
  201.6 25.2 %collective-permute-start.25 = (bf16[1024,512]{1,0:T(8,128)(2,1)S(1)}, bf16[1024,512]{1,0:T(8,128)(2,1)S(1)}, u32[]{:S(2)}, u32[]{:S(2)}) collective-permute-start(bf16[1024,512]{1,0:T(8,128)(2,1)S(1)} %collective-permute-done.21), channel_id=1, source_target_pairs={{0,16},{4,12},{8,24},{12,4},{16,0},{20,28},{24,8},{28,20},{1,17},{... | collective-permute-start | bytes 3145736 | tf_op jit(solution)/shard_map/ppermute | solution.py:79
  228.9 681.4 %reduce-scatter.8.cloned.1.call-start = ((), (), s32[]{:S(2)}) async-start(), calls=%async_computation.6 | async-start | bytes 12681216 | tf_op jit(solution)/shard_map/reduce_scatter | solution.py:777
  233.3 26.2 %collective-permute-start.27 = (bf16[2048,1024]{1,0:T(8,128)(2,1)}, bf16[2048,1024]{1,0:T(8,128)(2,1)}, u32[]{:S(2)}, u32[]{:S(2)}) collective-permute-start(bf16[2048,1024]{1,0:T(8,128)(2,1)} %pad_maximum_fusion.1), channel_id=1, source_target_pairs={{0,4},{4,0},{8,12},{12,8},{16,20},{20,16},{24,28},{28,24},{1,5},{5... | collective-permute-start | bytes 12582920 | tf_op jit(solution)/shard_map/ppermute | solution.py:79
  263.7 20.2 %collective-permute-start.28 = (bf16[256,2048]{1,0:T(8,128)(2,1)S(1)}, bf16[256,2048]{1,0:T(8,128)(2,1)S(1)}, u32[]{:S(2)}, u32[]{:S(2)}) collective-permute-start(bf16[256,2048]{1,0:T(8,128)(2,1)S(1)} %multiply_convert_fusion.refs_0_), channel_id=1, source_target_pairs={{0,1},{1,0},{2,3},{3,2},{4,5},{5,4},{6,7},{7,6},{8,9},{9,8},{10,11... | collective-permute-start | bytes 3145736 | tf_op jit(solution)/shard_map/ppermute | solution.py:126
  283.8 29.8 %collective-permute-start.31 = (bf16[256,2048]{1,0:T(8,128)(2,1)S(1)}, bf16[256,2048]{1,0:T(8,128)(2,1)}, u32[]{:S(2)}, u32[]{:S(2)}) collective-permute-start(bf16[256,2048]{1,0:T(8,128)(2,1)S(1)} %collective-permute-done.28.refs_1_), channel_id=1, source_target_pairs={{1,2},{2,1},{5,6},{6,5},{9,10},{10,9},{13,14},{14,13},{17,18},{18,... | collective-permute-start | bytes 3145736 | tf_op jit(solution)/shard_map/ppermute | solution.py:126
  285.5 41.5 %collective-permute-start.30 = (bf16[256,2048]{1,0:T(8,128)(2,1)}, bf16[256,2048]{1,0:T(8,128)(2,1)}, u32[]{:S(2)}, u32[]{:S(2)}) collective-permute-start(bf16[256,2048]{1,0:T(8,128)(2,1)} %collective-permute-done.29), channel_id=1, source_target_pairs={{1,0},{2,3},{5,4},{6,7},{9,8},{10,11},{13,12},{14,15},{17,16},{18,... | collective-permute-start | bytes 3145736 | tf_op jit(solution)/shard_map/ppermute | solution.py:126
  286.8 59.0 %collective-permute-start.33 = (bf16[2752,256]{1,0:T(8,128)(2,1)}, bf16[2752,256]{1,0:T(8,128)(2,1)}, u32[]{:S(2)}, u32[]{:S(2)}) collective-permute-start(bf16[2752,256]{1,0:T(8,128)(2,1)} %param.29), channel_id=1, source_target_pairs={{0,8},{4,20},{8,0},{12,28},{16,24},{20,4},{24,16},{28,12},{1,9},{5... | collective-permute-start | bytes 4227080 | tf_op jit(solution)/shard_map/ppermute | solution.py:79
  313.7 36.3 %collective-permute-start.32 = (bf16[256,2048]{1,0:T(8,128)(2,1)}, bf16[256,2048]{1,0:T(8,128)(2,1)}, u32[]{:S(2)}, u32[]{:S(2)}) collective-permute-start(bf16[256,2048]{1,0:T(8,128)(2,1)} %collective-permute-done.31), channel_id=1, source_target_pairs={{1,0},{2,3},{5,4},{6,7},{9,8},{10,11},{13,12},{14,15},{17,16},{18,... | collective-permute-start | bytes 3145736 | tf_op jit(solution)/shard_map/ppermute | solution.py:126
  315.3 41.3 %collective-permute-start.34 = (bf16[2752,256]{1,0:T(8,128)(2,1)}, bf16[2752,256]{1,0:T(8,128)(2,1)}, u32[]{:S(2)}, u32[]{:S(2)}) collective-permute-start(bf16[2752,256]{1,0:T(8,128)(2,1)} %param.29), channel_id=1, source_target_pairs={{0,16},{4,12},{8,24},{12,4},{16,0},{20,28},{24,8},{28,20},{1,17},{... | collective-permute-start | bytes 4227080 | tf_op jit(solution)/shard_map/ppermute | solution.py:79
  345.8 27.3 %collective-permute-start.35 = (bf16[2752,256]{1,0:T(8,128)(2,1)}, bf16[2752,256]{1,0:T(8,128)(2,1)}, u32[]{:S(2)}, u32[]{:S(2)}) collective-permute-start(bf16[2752,256]{1,0:T(8,128)(2,1)} %param.29), channel_id=1, source_target_pairs={{0,24},{4,28},{8,16},{12,20},{16,8},{20,12},{24,0},{28,4},{1,25},{... | collective-permute-start | bytes 4227080 | tf_op jit(solution)/shard_map/ppermute | solution.py:79
  465.7 37.4 %collective-permute-start.37 = (bf16[256,2048]{1,0:T(8,128)(2,1)}, bf16[256,2048]{1,0:T(8,128)(2,1)}, u32[]{:S(2)}, u32[]{:S(2)}) collective-permute-start(bf16[256,2048]{1,0:T(8,128)(2,1)} %get-tuple-element.153), channel_id=1, source_target_pairs={{0,1},{3,2},{4,5},{7,6},{8,9},{11,10},{12,13},{15,14},{16,17},{19,... | collective-permute-start | bytes 3145736 | tf_op jit(solution)/shard_map/ppermute | solution.py:126
  506.0 407.4 %reduce-scatter.4.cloned.1.call-start = ((), (), s32[]{:S(2)}) async-start(), calls=%async_computation.4 | async-start | bytes 12681216 | tf_op jit(solution)/shard_map/reduce_scatter | solution.py:777
  506.7 29.6 %collective-permute-start.38 = (bf16[256,2048]{1,0:T(8,128)(2,1)}, bf16[256,2048]{1,0:T(8,128)(2,1)}, u32[]{:S(2)}, u32[]{:S(2)}) collective-permute-start(bf16[256,2048]{1,0:T(8,128)(2,1)} %add.361), channel_id=1, source_target_pairs={{1,2},{2,1},{5,6},{6,5},{9,10},{10,9},{13,14},{14,13},{17,18},{18,... | collective-permute-start | bytes 3145736 | tf_op jit(solution)/shard_map/ppermute | solution.py:126
  508.3 28.0 %collective-permute-start.39 = (bf16[256,2048]{1,0:T(8,128)(2,1)S(1)}, bf16[256,2048]{1,0:T(8,128)(2,1)}, u32[]{:S(2)}, u32[]{:S(2)}) collective-permute-start(bf16[256,2048]{1,0:T(8,128)(2,1)S(1)} %get-tuple-element.101), channel_id=1, source_target_pairs={{0,1},{3,2},{4,5},{7,6},{8,9},{11,10},{12,13},{15,14},{16,17},{19,... | collective-permute-start | bytes 3145736 | tf_op jit(solution)/shard_map/ppermute | solution.py:126
  539.3 377.3 %reduce-scatter.6.cloned.1.call-start = ((), (), s32[]{:S(2)}) async-start(), calls=%async_computation.5 | async-start | bytes 12681216 | tf_op jit(solution)/shard_map/reduce_scatter | solution.py:777
  540.0 26.1 %collective-permute-start.40 = (bf16[256,2048]{1,0:T(8,128)(2,1)}, bf16[256,2048]{1,0:T(8,128)(2,1)}, u32[]{:S(2)}, u32[]{:S(2)}) collective-permute-start(bf16[256,2048]{1,0:T(8,128)(2,1)} %dynamic-slice_add_fusion.1), channel_id=1, source_target_pairs={{0,1},{1,0},{2,3},{3,2},{4,5},{5,4},{6,7},{7,6},{8,9},{9,8},{10,11... | collective-permute-start | bytes 3145736 | tf_op jit(solution)/shard_map/ppermute | solution.py:126
  545.2 20.8 %collective-permute-start.41 = (bf16[256,2048]{1,0:T(8,128)(2,1)}, bf16[256,2048]{1,0:T(8,128)(2,1)S(1)}, u32[]{:S(2)}, u32[]{:S(2)}) collective-permute-start(bf16[256,2048]{1,0:T(8,128)(2,1)} %add.365), channel_id=1, source_target_pairs={{1,2},{2,1},{5,6},{6,5},{9,10},{10,9},{13,14},{14,13},{17,18},{18,... | collective-permute-start | bytes 3145736 | tf_op jit(solution)/shard_map/ppermute | solution.py:126
  594.3 23.2 %collective-permute-start.42 = (bf16[4,1024,512]{2,1,0:T(8,128)(2,1)}, bf16[4,1024,512]{2,1,0:T(8,128)(2,1)}, u32[]{:S(2)}, u32[]{:S(2)}) collective-permute-start(bf16[4,1024,512]{2,1,0:T(8,128)(2,1)} %bitcast.166), channel_id=1, source_target_pairs={{0,4},{4,0},{8,12},{12,8},{16,20},{20,16},{24,28},{28,24},{1,5},{5... | collective-permute-start | bytes 12582920 | tf_op jit(solution)/shard_map/ppermute | solution.py:79
  612.2 26.9 %collective-permute-start.55 = (bf16[4,2048,256]{2,1,0:T(8,128)(2,1)}, bf16[4,2048,256]{2,1,0:T(8,128)(2,1)}, u32[]{:S(2)}, u32[]{:S(2)}) collective-permute-start(bf16[4,2048,256]{2,1,0:T(8,128)(2,1)} %unit_grad.12), channel_id=1, source_target_pairs={{0,4},{4,0},{8,12},{12,8},{16,20},{20,16},{24,28},{28,24},{1,5},{5... | collective-permute-start | bytes 12582920 | tf_op jit(solution)/shard_map/ppermute | solution.py:79
  617.0 85.6 %collective-permute-start.54 = (bf16[4,256,2048]{2,1,0:T(8,128)(2,1)}, bf16[4,256,2048]{2,1,0:T(8,128)(2,1)}, u32[]{:S(2)}, u32[]{:S(2)}) collective-permute-start(bf16[4,256,2048]{2,1,0:T(8,128)(2,1)} %bitcast.30), channel_id=1, source_target_pairs={{0,4},{4,0},{8,12},{12,8},{16,20},{20,16},{24,28},{28,24},{1,5},{5... | collective-permute-start | bytes 12582920 | tf_op jit(solution)/shard_map/ppermute | solution.py:79
  624.7 33.3 %collective-permute-start.43 = (bf16[1024,512]{1,0:T(8,128)(2,1)}, bf16[1024,512]{1,0:T(8,128)(2,1)}, u32[]{:S(2)}, u32[]{:S(2)}) collective-permute-start(bf16[1024,512]{1,0:T(8,128)(2,1)} %get-tuple-element.109), channel_id=1, source_target_pairs={{0,16},{4,12},{8,24},{12,4},{16,0},{20,28},{24,8},{28,20},{1,17},{... | collective-permute-start | bytes 3145736 | tf_op jit(solution)/shard_map/ppermute | solution.py:79
  633.6 54.5 %collective-permute-start.44 = (bf16[1024,512]{1,0:T(8,128)(2,1)}, bf16[1024,512]{1,0:T(8,128)(2,1)}, u32[]{:S(2)}, u32[]{:S(2)}) collective-permute-start(bf16[1024,512]{1,0:T(8,128)(2,1)} %get-tuple-element.110), channel_id=1, source_target_pairs={{0,16},{4,12},{8,24},{12,4},{16,0},{20,28},{24,8},{28,20},{1,17},{... | collective-permute-start | bytes 3145736 | tf_op jit(solution)/shard_map/ppermute | solution.py:79
  658.0 52.2 %collective-permute-start.56 = (bf16[2048,256]{1,0:T(8,128)(2,1)S(1)}, bf16[2048,256]{1,0:T(8,128)(2,1)S(1)}, u32[]{:S(2)}, u32[]{:S(2)}) collective-permute-start(bf16[2048,256]{1,0:T(8,128)(2,1)S(1)} %get-tuple-element.120), channel_id=1, source_target_pairs={{0,16},{4,12},{8,24},{12,4},{16,0},{20,28},{24,8},{28,20},{1,17},{... | collective-permute-start | bytes 3145736 | tf_op jit(solution)/shard_map/ppermute | solution.py:79
  689.5 43.7 %collective-permute-start.45 = (bf16[1024,512]{1,0:T(8,128)(2,1)S(1)}, bf16[1024,512]{1,0:T(8,128)(2,1)S(1)}, u32[]{:S(2)}, u32[]{:S(2)}) collective-permute-start(bf16[1024,512]{1,0:T(8,128)(2,1)S(1)} %fusion.17), channel_id=1, source_target_pairs={{0,8},{4,20},{8,0},{12,28},{16,24},{20,4},{24,16},{28,12},{1,9},{5... | collective-permute-start | bytes 3145736 | tf_op jit(solution)/shard_map/ppermute | solution.py:79
  711.6 71.8 %collective-permute-start.57 = (bf16[2048,256]{1,0:T(8,128)(2,1)}, bf16[2048,256]{1,0:T(8,128)(2,1)}, u32[]{:S(2)}, u32[]{:S(2)}) collective-permute-start(bf16[2048,256]{1,0:T(8,128)(2,1)} %add.389), channel_id=1, source_target_pairs={{0,8},{4,20},{8,0},{12,28},{16,24},{20,4},{24,16},{28,12},{1,9},{5... | collective-permute-start | bytes 3145736 | tf_op jit(solution)/shard_map/ppermute | solution.py:79
  733.2 43.3 %collective-permute-start.59 = (bf16[2048,256]{1,0:T(8,128)(2,1)}, bf16[2048,256]{1,0:T(8,128)(2,1)}, u32[]{:S(2)}, u32[]{:S(2)}) collective-permute-start(bf16[2048,256]{1,0:T(8,128)(2,1)} %get-tuple-element.124), channel_id=1, source_target_pairs={{0,16},{4,12},{8,24},{12,4},{16,0},{20,28},{24,8},{28,20},{1,17},{... | collective-permute-start | bytes 3145736 | tf_op jit(solution)/shard_map/ppermute | solution.py:79
  735.6 26.5 %collective-permute-start.51 = (bf16[256,512]{1,0:T(8,128)(2,1)S(1)}, bf16[256,512]{1,0:T(8,128)(2,1)S(1)}, u32[]{:S(2)}, u32[]{:S(2)}) collective-permute-start(bf16[256,512]{1,0:T(8,128)(2,1)S(1)} %get-tuple-element.167), channel_id=1, source_target_pairs={{0,1},{1,0},{2,3},{3,2},{4,5},{5,4},{6,7},{7,6},{8,9},{9,8},{10,11... | collective-permute-start | bytes 786440 | tf_op jit(solution)/shard_map/ppermute | solution.py:126
  737.0 28.8 %collective-permute-start.52 = (bf16[256,512]{1,0:T(8,128)(2,1)S(1)}, bf16[256,512]{1,0:T(8,128)(2,1)S(1)}, u32[]{:S(2)}, u32[]{:S(2)}) collective-permute-start(bf16[256,512]{1,0:T(8,128)(2,1)S(1)} %get-tuple-element.168), channel_id=1, source_target_pairs={{0,2},{1,3},{2,0},{3,1},{4,6},{5,7},{6,4},{7,5},{8,10},{9,11},{10,... | collective-permute-start | bytes 786440 | tf_op jit(solution)/shard_map/ppermute | solution.py:126
  737.0 28.8 %collective-permute-start.53 = (bf16[256,512]{1,0:T(8,128)(2,1)S(1)}, bf16[256,512]{1,0:T(8,128)(2,1)S(1)}, u32[]{:S(2)}, u32[]{:S(2)}) collective-permute-start(bf16[256,512]{1,0:T(8,128)(2,1)S(1)} %get-tuple-element.169), channel_id=1, source_target_pairs={{0,3},{1,2},{2,1},{3,0},{4,7},{5,6},{6,5},{7,4},{8,11},{9,10},{10,... | collective-permute-start | bytes 786440 | tf_op jit(solution)/shard_map/ppermute | solution.py:126
  762.1 25.8 %collective-permute-start.46 = (bf16[256,2048]{1,0:T(8,128)(2,1)}, bf16[256,2048]{1,0:T(8,128)(2,1)}, u32[]{:S(2)}, u32[]{:S(2)}) collective-permute-start(bf16[256,2048]{1,0:T(8,128)(2,1)} %get-tuple-element.149), channel_id=1, source_target_pairs={{0,1},{3,2},{4,5},{7,6},{8,9},{11,10},{12,13},{15,14},{16,17},{19,... | collective-permute-start | bytes 3145736 | tf_op jit(solution)/shard_map/ppermute | solution.py:126
  776.5 24.8 %collective-permute-start.60 = (bf16[256,2048]{1,0:T(8,128)(2,1)}, bf16[256,2048]{1,0:T(8,128)(2,1)}, u32[]{:S(2)}, u32[]{:S(2)}) collective-permute-start(bf16[256,2048]{1,0:T(8,128)(2,1)} %get-tuple-element.125), channel_id=1, source_target_pairs={{0,16},{4,12},{8,24},{12,4},{16,0},{20,28},{24,8},{28,20},{1,17},{... | collective-permute-start | bytes 3145736 | tf_op jit(solution)/shard_map/ppermute | solution.py:79
  785.5 51.5 %collective-permute-start.72 = (bf16[512,256]{1,0:T(8,128)(2,1)S(1)}, bf16[512,256]{1,0:T(8,128)(2,1)S(1)}, u32[]{:S(2)}, u32[]{:S(2)}) collective-permute-start(bf16[512,256]{1,0:T(8,128)(2,1)S(1)} %get-tuple-element.159), channel_id=1, source_target_pairs={{0,1},{1,0},{2,3},{3,2},{4,5},{5,4},{6,7},{7,6},{8,9},{9,8},{10,11... | collective-permute-start | bytes 786440 | tf_op jit(solution)/shard_map/ppermute | solution.py:126
  785.6 46.7 %collective-permute-start.58 = (bf16[256,2048]{1,0:T(8,128)(2,1)S(1)}, bf16[256,2048]{1,0:T(8,128)(2,1)S(1)}, u32[]{:S(2)}, u32[]{:S(2)}) collective-permute-start(bf16[256,2048]{1,0:T(8,128)(2,1)S(1)} %copy-done.53), channel_id=1, source_target_pairs={{0,16},{4,12},{8,24},{12,4},{16,0},{20,28},{24,8},{28,20},{1,17},{... | collective-permute-start | bytes 3145736 | tf_op jit(solution)/shard_map/ppermute | solution.py:79
  789.9 46.2 %collective-permute-start.47 = (bf16[256,2048]{1,0:T(8,128)(2,1)S(1)}, bf16[256,2048]{1,0:T(8,128)(2,1)S(1)}, u32[]{:S(2)}, u32[]{:S(2)}) collective-permute-start(bf16[256,2048]{1,0:T(8,128)(2,1)S(1)} %add.373), channel_id=1, source_target_pairs={{1,2},{2,1},{5,6},{6,5},{9,10},{10,9},{13,14},{14,13},{17,18},{18,... | collective-permute-start | bytes 3145736 | tf_op jit(solution)/shard_map/ppermute | solution.py:126
  790.7 44.0 %collective-permute-start.48 = (bf16[256,2048]{1,0:T(8,128)(2,1)S(1)}, bf16[256,2048]{1,0:T(8,128)(2,1)S(1)}, u32[]{:S(2)}, u32[]{:S(2)}) collective-permute-start(bf16[256,2048]{1,0:T(8,128)(2,1)S(1)} %get-tuple-element.114), channel_id=1, source_target_pairs={{0,1},{3,2},{4,5},{7,6},{8,9},{11,10},{12,13},{15,14},{16,17},{19,... | collective-permute-start | bytes 3145736 | tf_op jit(solution)/shard_map/ppermute | solution.py:126
  802.7 51.4 %collective-permute-start.61 = (bf16[256,2048]{1,0:T(8,128)(2,1)S(1)}, bf16[256,2048]{1,0:T(8,128)(2,1)S(1)}, u32[]{:S(2)}, u32[]{:S(2)}) collective-permute-start(bf16[256,2048]{1,0:T(8,128)(2,1)S(1)} %fusion.16), channel_id=1, source_target_pairs={{0,8},{4,20},{8,0},{12,28},{16,24},{20,4},{24,16},{28,12},{1,9},{5... | collective-permute-start | bytes 3145736 | tf_op jit(solution)/shard_map/ppermute | solution.py:79
  832.3 19.9 %collective-permute-start.73 = (bf16[512,256]{1,0:T(8,128)(2,1)S(1)}, bf16[512,256]{1,0:T(8,128)(2,1)S(1)}, u32[]{:S(2)}, u32[]{:S(2)}) collective-permute-start(bf16[512,256]{1,0:T(8,128)(2,1)S(1)} %get-tuple-element.161), channel_id=1, source_target_pairs={{0,2},{1,3},{2,0},{3,1},{4,6},{5,7},{6,4},{7,5},{8,10},{9,11},{10,... | collective-permute-start | bytes 786440 | tf_op jit(solution)/shard_map/ppermute | solution.py:126
  837.0 35.2 %collective-permute-start.49 = (bf16[256,2048]{1,0:T(8,128)(2,1)S(1)}, bf16[256,2048]{1,0:T(8,128)(2,1)S(1)}, u32[]{:S(2)}, u32[]{:S(2)}) collective-permute-start(bf16[256,2048]{1,0:T(8,128)(2,1)S(1)} %dynamic-slice_add_fusion), channel_id=1, source_target_pairs={{0,1},{1,0},{2,3},{3,2},{4,5},{5,4},{6,7},{7,6},{8,9},{9,8},{10,11... | collective-permute-start | bytes 3145736 | tf_op jit(solution)/shard_map/ppermute | solution.py:126
  852.2 21.4 %collective-permute-start.50 = (bf16[256,2048]{1,0:T(8,128)(2,1)S(1)}, bf16[256,2048]{1,0:T(8,128)(2,1)S(1)}, u32[]{:S(2)}, u32[]{:S(2)}) collective-permute-start(bf16[256,2048]{1,0:T(8,128)(2,1)S(1)} %add.376), channel_id=1, source_target_pairs={{1,2},{2,1},{5,6},{6,5},{9,10},{10,9},{13,14},{14,13},{17,18},{18,... | collective-permute-start | bytes 3145736 | tf_op jit(solution)/shard_map/ppermute | solution.py:126
  853.9 26.6 %collective-permute-start.68 = (bf16[320,512]{1,0:T(8,128)(2,1)S(1)}, bf16[320,512]{1,0:T(8,128)(2,1)S(1)}, u32[]{:S(2)}, u32[]{:S(2)}) collective-permute-start(bf16[320,512]{1,0:T(8,128)(2,1)S(1)} %fusion.23), channel_id=1, source_target_pairs={{0,8},{4,20},{8,0},{12,28},{16,24},{20,4},{24,16},{28,12},{1,9},{5... | collective-permute-start | bytes 983048 | tf_op jit(solution)/shard_map/ppermute | solution.py:79
  854.0 26.5 %collective-permute-start.66 = (bf16[320,512]{1,0:T(8,128)(2,1)S(1)}, bf16[320,512]{1,0:T(8,128)(2,1)S(1)}, u32[]{:S(2)}, u32[]{:S(2)}) collective-permute-start(bf16[320,512]{1,0:T(8,128)(2,1)S(1)} %get-tuple-element.127), channel_id=1, source_target_pairs={{0,16},{4,12},{8,24},{12,4},{16,0},{20,28},{24,8},{28,20},{1,17},{... | collective-permute-start | bytes 983048 | tf_op jit(solution)/shard_map/ppermute | solution.py:79
  857.3 42.5 %collective-permute-start.62 = (bf16[256,512]{1,0:T(8,128)(2,1)S(1)}, bf16[256,512]{1,0:T(8,128)(2,1)S(1)}, u32[]{:S(2)}, u32[]{:S(2)}) collective-permute-start(bf16[256,512]{1,0:T(8,128)(2,1)S(1)} %get-tuple-element.162), channel_id=1, source_target_pairs={{0,1},{1,0},{2,3},{3,2},{4,5},{5,4},{6,7},{7,6},{8,9},{9,8},{10,11... | collective-permute-start | bytes 786440 | tf_op jit(solution)/shard_map/ppermute | solution.py:126
  872.2 30.0 %collective-permute-start.63 = (bf16[256,512]{1,0:T(8,128)(2,1)S(1)}, bf16[256,512]{1,0:T(8,128)(2,1)}, u32[]{:S(2)}, u32[]{:S(2)}) collective-permute-start(bf16[256,512]{1,0:T(8,128)(2,1)S(1)} %get-tuple-element.164), channel_id=1, source_target_pairs={{0,2},{1,3},{2,0},{3,1},{4,6},{5,7},{6,4},{7,5},{8,10},{9,11},{10,... | collective-permute-start | bytes 786440 | tf_op jit(solution)/shard_map/ppermute | solution.py:126
  873.6 28.6 %collective-permute-start.64 = (bf16[256,512]{1,0:T(8,128)(2,1)S(1)}, bf16[256,512]{1,0:T(8,128)(2,1)}, u32[]{:S(2)}, u32[]{:S(2)}) collective-permute-start(bf16[256,512]{1,0:T(8,128)(2,1)S(1)} %get-tuple-element.163), channel_id=1, source_target_pairs={{0,3},{1,2},{2,1},{3,0},{4,7},{5,6},{6,5},{7,4},{8,11},{9,10},{10,... | collective-permute-start | bytes 786440 | tf_op jit(solution)/shard_map/ppermute | solution.py:126
  881.7 22.5 %collective-permute-start.69 = (bf16[80,512]{1,0:T(8,128)(2,1)S(1)}, bf16[80,512]{1,0:T(8,128)(2,1)S(1)}, u32[]{:S(2)}, u32[]{:S(2)}) collective-permute-start(bf16[80,512]{1,0:T(8,128)(2,1)S(1)} %get-tuple-element.170), channel_id=1, source_target_pairs={{0,1},{1,0},{2,3},{3,2},{4,5},{5,4},{6,7},{7,6},{8,9},{9,8},{10,11... | collective-permute-start | bytes 245768 | tf_op jit(solution)/shard_map/ppermute | solution.py:126
  (102 other events, 2460.3 us)
Sparse Core Ops, SparseCore 0:
  9.9 86.4 all-gather.7
  151.4 83.2 all-gather.5
  236.6 65.2 all-gather.9
  506.2 94.0 reduce-scatter.7
  604.2 123.6 reduce-scatter.3
  731.3 105.9 reduce-scatter.5
